TPU v7x, 256 devices: a whole 4x4x8 slice. The times are simulated.
256 devices in a mesh: tm: 4 (over z_lo, core), mesh: 64 (over z_hi, x, y).
Axes of the slice: x: 4, y: 4, z: 8 (z_hi: 4, z_lo: 2; z = z_hi * 2 + z_lo), core: 2. Of those that a mesh axis runs over, the one named last changes fastest.
Arguments:
- states: bfloat16 [32, 8192, 256], P('tm', 'mesh'), may hold values from -6 to 6
- increment: float32 [32, 8192, 256], P('tm', 'mesh'), may hold values from -6 to 6
- window_slots: int32 [64, 4], P('mesh'), may hold values from 0 to 2, as said below
- edge_weights: bfloat16 [2, 64, 4, 128, 128], P(None, 'mesh'), may hold values from -0.125 to 0.125
- inner_weight: bfloat16 [2, 256, 1024], replicated, may hold values from -0.375 to 0.375
- inner_bias: float32 [2, 1024], replicated, may hold values from -5 to 5
- outer_weight: bfloat16 [2, 1024, 256], replicated, may hold values from -0.1875 to 0.1875
Outputs:
- misfit: float32 [32, 8192, 256], P('tm', 'mesh')
- normal_product: float32 [32, 8192, 256], P('tm', 'mesh')
Inputs may be any that keep to these rules, and one draw needn't show every extreme that they name: `window_slots`: slot 0 of a block's window is the block of the previous partition along mesh (cyclically), slot 1 the partition's own block, slot 2 the block of the next partition; every block's list names slot 0 and slot 2 at least once, and may name a slot twice.
All inputs are finite; a program needn't handle non-finite values.
Results may differ from a plain program's by a relative error of at most 0.007.
Values may be sent and summed in bfloat16 or wider, within the bound.
No kernel may reach another device: no remote copies, remote signals or barrier semaphores. Data moves between devices by JAX's collectives and lax.ppermute only.
A program may use at most 64 MiB of HBM per device.

v0:
```python
import jax
import jax.numpy as jnp
from jax import lax
from jax.sharding import PartitionSpec as P

LAYERS = 2


HALF_ROOT = 0.7071067811865476
DENSITY_NORM = 0.3989422804014327


def shifted(value, axis, steps):
    count = lax.axis_size(axis)
    pairs = [(source, (source + steps) % count) for source in range(count)]
    return lax.ppermute(value, axis, pairs)


def extended(cells, sides, width):
    for axis, dim in sides:
        count = lax.axis_size(axis)
        head = lax.slice_in_dim(cells, 0, width, axis=dim)
        tail = lax.slice_in_dim(cells, cells.shape[dim] - width, cells.shape[dim], axis=dim)
        cells = jnp.concatenate(
            [
                lax.ppermute(tail, axis, [(i, (i + 1) % count) for i in range(count)]),
                cells,
                lax.ppermute(head, axis, [((i + 1) % count, i) for i in range(count)]),
            ],
            axis=dim,
        )
    return cells


def shifted_2(array, axis, by):
    count = lax.axis_size(axis)
    pairs = [(i, i + by) for i in range(count) if 0 <= i + by < count]
    return lax.ppermute(array, axis, pairs)


def smooth_gate(values):
    return 0.5 * values * (1.0 + lax.erf(values * HALF_ROOT))


def smooth_slope(values):
    return (
        0.5 * (1.0 + lax.erf(values * HALF_ROOT))
        + values * jnp.exp(-0.5 * values * values) * DENSITY_NORM
    )


def aggregate(window, window_slots, weights):
    windows, total_rows, features = window.shape
    blocks = weights.shape[0]
    fanout = weights.shape[1]
    block_rows = weights.shape[2]
    block_view = window.reshape(windows, total_rows // block_rows, block_rows, features)
    picked = jnp.take(block_view, window_slots.reshape(-1), axis=1)
    picked = picked.reshape(windows, blocks, fanout, block_rows, features)
    summed = jnp.einsum("bkmn,tbknd->tbmd", weights, picked, preferred_element_type=jnp.float32)
    return summed.reshape(windows, blocks * block_rows, features)


def transpose_aggregate(source, window_slots, weights):
    windows, node_rows, features = source.shape
    blocks = weights.shape[0]
    block_rows = weights.shape[2]
    block_view = source.reshape(windows, blocks, block_rows, features)
    pieces = jnp.einsum("bkmn,tbmd->tbknd", weights, block_view, preferred_element_type=jnp.float32)
    selector = (
        window_slots[:, :, None] == jnp.arange(blocks + 2, dtype=jnp.int32)[None, None, :]
    ).astype(jnp.float32)
    collected = jnp.einsum("tbknd,bkw->twnd", pieces, selector, precision=lax.Precision.HIGHEST)
    from_right = shifted(collected[:, 0].astype(jnp.bfloat16), "mesh", -1).astype(jnp.float32)
    from_left = shifted(collected[:, blocks + 1].astype(jnp.bfloat16), "mesh", 1).astype(
        jnp.float32
    )
    own_blocks = collected[:, 1 : blocks + 1]
    own_blocks = own_blocks.at[:, 0].add(from_left)
    own_blocks = own_blocks.at[:, blocks - 1].add(from_right)
    return own_blocks.reshape(windows, node_rows, features)


def forward_pass(
    linear_states, source_field, window_slots, edge_weights, inner_weight, inner_bias, outer_weight
):
    windows = linear_states.shape[0]
    block_rows = edge_weights.shape[-1]
    base_state = linear_states
    tangent = source_field
    slopes = []
    for layer_index in range(LAYERS):
        stacked = jnp.concatenate([base_state, tangent.astype(jnp.bfloat16)], axis=0)
        window = extended(stacked, (("mesh", 1),), block_rows)
        blended = aggregate(window, window_slots, edge_weights[layer_index])
        base_sum = base_state.astype(jnp.float32) + blended[:windows]
        tangent_sum = tangent + blended[windows:]
        activation = (
            jnp.einsum(
                "tnd,dh->tnh",
                base_sum.astype(jnp.bfloat16),
                inner_weight[layer_index],
                preferred_element_type=jnp.float32,
            )
            + inner_bias[layer_index]
        )
        derivative = smooth_slope(activation)
        slopes.append(derivative)
        lifted = (
            derivative
            * jnp.einsum(
                "tnd,dh->tnh",
                tangent_sum.astype(jnp.bfloat16),
                inner_weight[layer_index],
                preferred_element_type=jnp.float32,
            )
        ).astype(jnp.bfloat16)
        tangent = tangent_sum + jnp.einsum(
            "tnh,hd->tnd", lifted, outer_weight[layer_index], preferred_element_type=jnp.float32
        )
        if layer_index + 1 < LAYERS:
            gated = smooth_gate(activation).astype(jnp.bfloat16)
            base_state = (
                base_sum
                + jnp.einsum(
                    "tnh,hd->tnd",
                    gated,
                    outer_weight[layer_index],
                    preferred_element_type=jnp.float32,
                )
            ).astype(jnp.bfloat16)
    return (slopes, tangent)


def adjoint_pass(slopes, cotangent, window_slots, edge_weights, inner_weight, outer_weight):
    current = cotangent
    for layer_index in range(LAYERS - 1, -1, -1):
        narrow = current.astype(jnp.bfloat16)
        spread = jnp.einsum(
            "tnd,hd->tnh", narrow, outer_weight[layer_index], preferred_element_type=jnp.float32
        )
        pulled = (slopes[layer_index] * spread).astype(jnp.bfloat16)
        returned = current + jnp.einsum(
            "tnh,dh->tnd", pulled, inner_weight[layer_index], preferred_element_type=jnp.float32
        )
        current = returned + transpose_aggregate(
            returned.astype(jnp.bfloat16), window_slots, edge_weights[layer_index]
        )
    return current


def local(states, increment, window_slots, edge_weights, inner_weight, inner_bias, outer_weight):
    windows = states.shape[0]
    previous_state = shifted_2(states[windows - 1 :], "tm", 1)
    previous_field = shifted_2(increment[windows - 1 :].astype(jnp.bfloat16), "tm", 1).astype(
        jnp.float32
    )
    linear_states = jnp.concatenate([previous_state, states[: windows - 1]], axis=0)
    linear_field = jnp.concatenate([previous_field, increment[: windows - 1]], axis=0)
    kept_slopes, images = forward_pass(
        linear_states,
        linear_field,
        window_slots,
        edge_weights,
        inner_weight,
        inner_bias,
        outer_weight,
    )
    misfit = increment - images
    pulled_back = adjoint_pass(
        kept_slopes, misfit, window_slots, edge_weights, inner_weight, outer_weight
    )
    carried = shifted_2(pulled_back[:1].astype(jnp.bfloat16), "tm", -1).astype(jnp.float32)
    normal = misfit - jnp.concatenate([pulled_back[1:], carried], axis=0)
    return (misfit, normal)


def solution(mesh):
    placed = (
        P("tm", "mesh", None),
        P("tm", "mesh", None),
        P("mesh", None),
        P(None, "mesh", None, None, None),
        P(),
        P(),
        P(),
    )
    return jax.shard_map(
        local,
        mesh=mesh,
        in_specs=placed,
        out_specs=(P("tm", "mesh", None), P("tm", "mesh", None)),
        check_vma=False,
    )
```

profile of v0, /device:TPU:1, one launch (start us, length us, event | category | flops | bytes accessed | tf_op | source)
XLA Modules:
  0.0 258.1 jit_solution(9635283123671334539)
XLA Ops:
  1.6 4.9 %collective-permute-start = (bf16[1,128,256]{2,1,0:T(8,128)(2,1)S(1)}, bf16[1,128,256]{2,1,0:T(8,128)(2,1)S(1)}, u32[]{:S(2)}, u32[]{:S(2)}) collective-permute-start(bf16[1,128,256]{2,1,0:T(8,128)(2,1)S(1)} %slice.363), channel_id=1, source_target_pairs={{0,64},{64,128},{128,192},{1,65},{65,129},{129,193},{2,66},{66,130... | collective-permute-start | bytes 196616 | tf_op jit(solution)/shard_map/ppermute | solution.py:38
  9.3 2.3 slice_bitcast_fusion.7
  13.9 9.8 %collective-permute-start.3 = (bf16[16,128,256]{2,1,0:T(8,128)(2,1)S(1)}, bf16[16,128,256]{2,1,0:T(8,128)(2,1)S(1)}, u32[]{:S(2)}, u32[]{:S(2)}) collective-permute-start(bf16[16,128,256]{2,1,0:T(8,128)(2,1)S(1)} %pad_maximum_fusion.3), channel_id=1, source_target_pairs={{1,0},{2,1},{3,2},{4,3},{5,4},{6,5},{7,6},{8,7},{9,8},{10,9},{11,1... | collective-permute-start | bytes 3145736 | tf_op jit(solution)/shard_map/ppermute | solution.py:28
  23.9 40.4 %collective-permute-done.3 = bf16[16,128,256]{2,1,0:T(8,128)(2,1)S(1)} collective-permute-done((bf16[16,128,256]{2,1,0:T(8,128)(2,1)S(1)}, bf16[16,128,256]{2,1,0:T(8,128)(2,1)S(1)}, u32[]{:S(2)}, u32[]{:S(2)}) %collective-permute-start.3) | collective-permute-done | bytes 1048608 | tf_op jit(solution)/shard_map/ppermute | solution.py:28
  64.2 10.4 %collective-permute-done.2 = bf16[16,128,256]{2,1,0:T(8,128)(2,1)S(1)} collective-permute-done((bf16[16,128,256]{2,1,0:T(8,128)(2,1)S(1)}, bf16[16,128,256]{2,1,0:T(8,128)(2,1)S(1)}, u32[]{:S(2)}, u32[]{:S(2)}) %collective-permute-start.2) | collective-permute-done | bytes 1048608 | tf_op jit(solution)/shard_map/ppermute | solution.py:26
  75.2 2.8 %gather_fusion = bf16[4,16,128,256]{3,2,1,0:T(8,128)(2,1)} fusion(bf16[16,3,128,256]{3,2,1,0:T(8,128)(2,1)S(1)} %bitcast.223, s32[1024]{0:T(1024)S(1)} %pad_clamp_fusion), kind=kCustom, calls=%fused_computation.clone | custom fusion | bytes 8388624 | tf_op jit(solution)/shard_map/jit(_take)/gather | solution.py:58
  78.0 3.3 %fusion.21 = f32[16,1,128,256]{3,2,0,1:T(8,128)S(1)} fusion(bf16[4,16,128,256]{3,2,1,0:T(8,128)(2,1)} %gather_fusion, pred[4]{0:T(512)(128)(4,1)S(1)} %compare_and_fusion, bf16[2,1,4,128,128]{4,3,2,1,0:T(8,128)(2,1)} %param.20), kind=kOutput, calls=%fused_computation.37 | convolution fusion | flops 538968064 | bytes 6422532 | tf_op jit(solution)/shard_map/bkmn,tbknd->tbmd/dot_general | solution.py:60
  81.4 2.7 %fusion.50 = f32[8,128,1024]{2,1,0:T(8,128)} fusion(f32[16,1,128,256]{3,2,0,1:T(8,128)S(1)} %fusion.21, bf16[7,1,128,256]{3,2,0,1:T(8,128)(2,1)S(1)} %copy-done.11, bf16[1,1,128,256]{3,2,0,1:T(8,128)(2,1)S(1)} %bitcast.224, bf16[2,256,1024]{2,1,0:T(8,128)(2,1)S(1)} %copy-done.6), kind=kOutput, calls=%fused_computation.74 | convolution fusion | flops 537919488 | bytes 6291456 | tf_op jit(solution)/shard_map/tnd,dh->tnh/dot_general | solution.py:99
  84.1 6.3 %fusion.139 = (bf16[8,128,256]{2,1,0:T(8,128)(2,1)S(1)}, f32[8,128,256]{2,1,0:T(8,128)}) fusion(bf16[2,1024,256]{2,1,0:T(8,128)(2,1)} %param.23, f32[16,1,128,256]{3,2,0,1:T(8,128)} %copy-done.13, f32[7,1,128,256]{3,2,0,1:T(8,128)} %get-tuple-element.59, f32[1,1,128,256]{3,2,0,1:T(8,128)S(1)} %get-tuple-element.63, ...), kind=kOutput, calls=%fused_computation.148 | convolution fusion | flops 1087111168 | bytes 11014144 | tf_op jit(solution)/shard_map/tnh,hd->tnd/dot_general | solution.py:118
  90.4 4.0 %fusion.46 = bf16[8,128,256]{2,1,0:T(8,128)(2,1)S(1)} fusion(f32[16,1,128,256]{3,2,0,1:T(8,128)} %copy-done.13, bf16[7,128,256]{2,1,0:T(8,128)(2,1)S(1)} %copy-done.2, bf16[1,128,256]{2,1,0:T(8,128)(2,1)S(1)} %collective-permute-done.1, f32[8,128,1024]{2,1,0:T(8,128)} %fusion.50, f32[1024]{0:T(1024)S(1)} %bitcast.226, bf16[2,1024,256]{2,1,0:T(8,128)(2,1)} %param.23), kind=kOutput, calls=%fused_computation.68 | convolution fusion | flops 544473088 | bytes 6819840 | tf_op jit(solution)/shard_map/tnh,hd->tnd/dot_general | solution.py:125
  96.0 23.9 %collective-permute-done.5 = bf16[16,128,256]{2,1,0:T(8,128)(2,1)S(1)} collective-permute-done((bf16[16,128,256]{2,1,0:T(8,128)(2,1)S(1)}, bf16[16,128,256]{2,1,0:T(8,128)(2,1)S(1)}, u32[]{:S(2)}, u32[]{:S(2)}) %collective-permute-start.5) | collective-permute-done | bytes 1048608 | tf_op jit(solution)/shard_map/ppermute | solution.py:28
  119.9 10.9 %collective-permute-done.4 = bf16[16,128,256]{2,1,0:T(8,128)(2,1)S(1)} collective-permute-done((bf16[16,128,256]{2,1,0:T(8,128)(2,1)S(1)}, bf16[16,128,256]{2,1,0:T(8,128)(2,1)S(1)}, u32[]{:S(2)}, u32[]{:S(2)}) %collective-permute-start.4) | collective-permute-done | bytes 1048608 | tf_op jit(solution)/shard_map/ppermute | solution.py:26
  132.5 2.8 %gather_fusion.1 = bf16[4,16,128,256]{3,2,1,0:T(8,128)(2,1)} fusion(bf16[16,3,128,256]{3,2,1,0:T(8,128)(2,1)S(1)} %bitcast.222, s32[1024]{0:T(1024)S(1)} %pad_clamp_fusion), kind=kCustom, calls=%fused_computation.1.clone | custom fusion | bytes 8388624 | tf_op jit(solution)/shard_map/jit(_take)/gather | solution.py:58
  135.3 3.3 %fusion.24 = f32[16,1,128,256]{3,2,0,1:T(8,128)S(1)} fusion(bf16[4,16,128,256]{3,2,1,0:T(8,128)(2,1)} %gather_fusion.1, pred[4]{0:T(512)(128)(4,1)S(1)} %compare_and_fusion, bf16[2,1,4,128,128]{4,3,2,1,0:T(8,128)(2,1)S(1)} %copy-done.14), kind=kOutput, calls=%fused_computation.38 | convolution fusion | flops 538968064 | bytes 6423040 | tf_op jit(solution)/shard_map/bkmn,tbknd->tbmd/dot_general | solution.py:60
  138.6 3.4 %fusion.7 = f32[8,128,1024]{2,1,0:T(8,128)} fusion(f32[1024]{0:T(1024)S(1)} %bitcast.228, f32[16,1,128,256]{3,2,0,1:T(8,128)S(1)} %fusion.24, bf16[8,128,256]{2,1,0:T(8,128)(2,1)S(1)} %copy-done.9, bf16[2,256,1024]{2,1,0:T(8,128)(2,1)S(1)} %copy-done.7), kind=kOutput, calls=%fused_computation.11 | convolution fusion | flops 547094528 | bytes 6295552 | tf_op jit(solution)/shard_map/tnd,dh->tnh/dot_general | solution.py:99
  142.0 5.0 %fusion.34 = f32[8,128,256]{2,1,0:T(8,128)S(1)} fusion(f32[8,128,256]{2,1,0:T(8,128)S(1)} %copy-done.3, f32[8,128,1024]{2,1,0:T(8,128)} %fusion.7, f32[8,128,256]{2,1,0:T(8,128)} %get-tuple-element.68, f32[16,1,128,256]{3,2,0,1:T(8,128)} %copy-done.12, bf16[2,1024,256]{2,1,0:T(8,128)(2,1)} %param.23, bf16[2,256,1024]{2,1,0:T(8,128)(2,1)S(1)} %copy-done.7), kind=kOutput, calls=%fused_computation.46 | convolution fusion | flops 1077149696 | bytes 11534336 | tf_op jit(solution)/shard_map/tnh,hd->tnd/dot_general | solution.py:118
  147.0 4.1 %fusion.32 = f32[8,128,256]{2,1,0:T(8,128)S(1)} fusion(f32[8,128,256]{2,1,0:T(8,128)S(1)} %fusion.34, f32[8,128,1024]{2,1,0:T(8,128)} %fusion.7, bf16[2,1024,256]{2,1,0:T(8,128)(2,1)} %param.23, bf16[2,256,1024]{2,1,0:T(8,128)(2,1)S(1)} %copy-done.7), kind=kOutput, calls=%fused_computation.44 | convolution fusion | flops 1076363264 | bytes 8388608 | tf_op jit(solution)/shard_map/tnh,dh->tnd/dot_general | solution.py:143
  151.1 2.7 %convolution_bitcast_fusion.1 = f32[8,4,128,256]{2,3,1,0:T(8,128)} fusion(f32[8,128,256]{2,1,0:T(8,128)S(1)} %fusion.32, bf16[2,1,4,128,128]{4,3,2,1,0:T(8,128)(2,1)S(1)} %copy-done.14), kind=kOutput, calls=%fused_computation.31 | convolution fusion | flops 268697600 | bytes 5373952 | tf_op jit(solution)/shard_map/bkmn,tbmd->tbknd/dot_general | solution.py:69
  153.9 5.3 %copy.27 = f32[8,4,128,256]{3,1,2,0:T(4,128)} copy(f32[8,4,128,256]{2,3,1,0:T(8,128)} %convolution_bitcast_fusion.1) | data formatting | bytes 8388608 | tf_op jit(solution)/shard_map/reshape.147
  159.2 6.9 %fusion.120 = f32[3,8,128,256]{3,0,2,1:T(4,128)S(1)} fusion(f32[8,4,128,256]{3,1,2,0:T(4,128)} %copy.27, s32[4]{0:T(128)S(1)} %bitcast.229), kind=kOutput, calls=%fused_computation.128 | convolution fusion | flops 37748748 | bytes 7340048 | tf_op jit(solution)/shard_map/tbknd,bkw->twnd/dot_general | solution.py:73
  166.0 2.3 fusion.137
  168.5 7.8 %collective-permute-start.7 = (bf16[8,128,256]{2,1,0:T(8,128)(2,1)S(1)}, bf16[8,128,256]{2,1,0:T(8,128)(2,1)S(1)}, u32[]{:S(2)}, u32[]{:S(2)}) collective-permute-start(bf16[8,128,256]{2,1,0:T(8,128)(2,1)S(1)} %get-tuple-element.58), channel_id=1, source_target_pairs={{0,63},{1,0},{2,1},{3,2},{4,3},{5,4},{6,5},{7,6},{8,7},{9,8},{10,9... | collective-permute-start | bytes 1572872 | tf_op jit(solution)/shard_map/ppermute | solution.py:16
  176.3 21.7 %collective-permute-done.6 = bf16[8,128,256]{2,1,0:T(8,128)(2,1)S(1)} collective-permute-done((bf16[8,128,256]{2,1,0:T(8,128)(2,1)S(1)}, bf16[8,128,256]{2,1,0:T(8,128)(2,1)S(1)}, u32[]{:S(2)}, u32[]{:S(2)}) %collective-permute-start.6) | collective-permute-done | bytes 524320 | tf_op jit(solution)/shard_map/ppermute | solution.py:16
  199.7 6.0 %fusion.31 = f32[8,128,256]{2,1,0:T(8,128)S(1)} fusion(f32[8,128,256]{2,1,0:T(8,128)S(1)} %fusion.32, bf16[8,128,256]{2,1,0:T(8,128)(2,1)} %copy-done.18, bf16[8,128,256]{2,1,0:T(8,128)(2,1)} %copy-done.17, f32[8,3,128,256]{3,2,0,1:T(8,128)} %get-tuple-element.54, bf16[2,1024,256]{2,1,0:T(8,128)(2,1)} %param.23, bf16[2,256,1024]{2,1,0:T(8,128)(2,1)} %param.21, ...), kind=kOutput, calls=%fused_computation.43 | convolution fusion | flops 1088421888 | bytes 12587008 | tf_op jit(solution)/shard_map/tnh,dh->tnd/dot_general | solution.py:143
  205.7 2.7 %convolution_bitcast_fusion = f32[8,4,128,256]{2,3,1,0:T(8,128)} fusion(f32[8,128,256]{2,1,0:T(8,128)S(1)} %fusion.31, bf16[2,1,4,128,128]{4,3,2,1,0:T(8,128)(2,1)S(1)} %copy-done.14), kind=kOutput, calls=%fused_computation.30 | convolution fusion | flops 268697600 | bytes 5373952 | tf_op jit(solution)/shard_map/bkmn,tbmd->tbknd/dot_general | solution.py:69
  208.4 5.3 %copy.31 = f32[8,4,128,256]{3,1,2,0:T(4,128)} copy(f32[8,4,128,256]{2,3,1,0:T(8,128)} %convolution_bitcast_fusion) | data formatting | bytes 8388608 | tf_op jit(solution)/shard_map/reshape.162
  213.7 6.9 %fusion.118 = f32[3,8,128,256]{3,0,2,1:T(4,128)S(1)} fusion(f32[8,4,128,256]{3,1,2,0:T(4,128)} %copy.31, s32[4]{0:T(128)S(1)} %bitcast.230), kind=kOutput, calls=%fused_computation.127 | convolution fusion | flops 37748748 | bytes 7340048 | tf_op jit(solution)/shard_map/tbknd,bkw->twnd/dot_general | solution.py:73
  221.5 7.8 %collective-permute-start.9 = (bf16[8,128,256]{2,1,0:T(8,128)(2,1)S(1)}, bf16[8,128,256]{2,1,0:T(8,128)(2,1)S(1)}, u32[]{:S(2)}, u32[]{:S(2)}) collective-permute-start(bf16[8,128,256]{2,1,0:T(8,128)(2,1)S(1)} %get-tuple-element.56), channel_id=1, source_target_pairs={{0,63},{1,0},{2,1},{3,2},{4,3},{5,4},{6,5},{7,6},{8,7},{9,8},{10,9... | collective-permute-start | bytes 1572872 | tf_op jit(solution)/shard_map/ppermute | solution.py:16
  229.3 16.2 %collective-permute-done.8 = bf16[8,128,256]{2,1,0:T(8,128)(2,1)S(1)} collective-permute-done((bf16[8,128,256]{2,1,0:T(8,128)(2,1)S(1)}, bf16[8,128,256]{2,1,0:T(8,128)(2,1)S(1)}, u32[]{:S(2)}, u32[]{:S(2)}) %collective-permute-start.8) | collective-permute-done | bytes 524320 | tf_op jit(solution)/shard_map/ppermute | solution.py:16
  245.5 5.6 %collective-permute-done.9 = bf16[8,128,256]{2,1,0:T(8,128)(2,1)S(1)} collective-permute-done((bf16[8,128,256]{2,1,0:T(8,128)(2,1)S(1)}, bf16[8,128,256]{2,1,0:T(8,128)(2,1)S(1)}, u32[]{:S(2)}, u32[]{:S(2)}) %collective-permute-start.9) | collective-permute-done | bytes 524320 | tf_op jit(solution)/shard_map/ppermute | solution.py:16
  251.3 2.4 collective-permute-start.10
  253.8 3.1 %collective-permute-done.10 = bf16[1,128,256]{2,1,0:T(8,128)(2,1)S(1)} collective-permute-done((bf16[1,128,256]{2,1,0:T(8,128)(2,1)S(1)}, bf16[1,128,256]{2,1,0:T(8,128)(2,1)S(1)}, u32[]{:S(2)}, u32[]{:S(2)}) %collective-permute-start.10) | collective-permute-done | bytes 65568 | tf_op jit(solution)/shard_map/ppermute | solution.py:38
  (68 shorter events, 14.1 us)
Async XLA Ops:
  0.6 23.2 %copy-start.16 = (s32[1,4]{1,0:T(1,128)S(1)}, s32[1,4]{1,0:T(1,128)}, u32[]{:S(2)}) copy-start(s32[1,4]{1,0:T(1,128)} %param.19) | copy-start | bytes 52
  0.6 23.2 %copy-start.15 = (f32[2,1024]{1,0:T(2,128)S(1)}, f32[2,1024]{1,0:T(2,128)}, u32[]{:S(2)}) copy-start(f32[2,1024]{1,0:T(2,128)} %param.22) | copy-start | bytes 24580
  1.6 12.1 %collective-permute-start = (bf16[1,128,256]{2,1,0:T(8,128)(2,1)S(1)}, bf16[1,128,256]{2,1,0:T(8,128)(2,1)S(1)}, u32[]{:S(2)}, u32[]{:S(2)}) collective-permute-start(bf16[1,128,256]{2,1,0:T(8,128)(2,1)S(1)} %slice.363), channel_id=1, source_target_pairs={{0,64},{64,128},{128,192},{1,65},{65,129},{129,193},{2,66},{66,130... | collective-permute-start | bytes 196616 | tf_op jit(solution)/shard_map/ppermute | solution.py:38
  7.4 6.5 %collective-permute-start.1 = (bf16[1,128,256]{2,1,0:T(8,128)(2,1)S(1)}, bf16[1,128,256]{2,1,0:T(8,128)(2,1)S(1)}, u32[]{:S(2)}, u32[]{:S(2)}) collective-permute-start(bf16[1,128,256]{2,1,0:T(8,128)(2,1)S(1)} %slice.197), channel_id=1, source_target_pairs={{0,64},{64,128},{128,192},{1,65},{65,129},{129,193},{2,66},{66,130... | collective-permute-start | bytes 196616 | tf_op jit(solution)/shard_map/ppermute | solution.py:38
  11.6 2.2 copy-start.4
  13.7 61.5 %copy-start.1 = (bf16[7,128,256]{2,1,0:T(8,128)(2,1)}, bf16[7,128,256]{2,1,0:T(8,128)(2,1)S(1)}, u32[]{:S(2)}) copy-start(bf16[7,128,256]{2,1,0:T(8,128)(2,1)S(1)} %get-tuple-element.62) | copy-start | bytes 1376260
  13.9 50.3 %collective-permute-start.3 = (bf16[16,128,256]{2,1,0:T(8,128)(2,1)S(1)}, bf16[16,128,256]{2,1,0:T(8,128)(2,1)S(1)}, u32[]{:S(2)}, u32[]{:S(2)}) collective-permute-start(bf16[16,128,256]{2,1,0:T(8,128)(2,1)S(1)} %pad_maximum_fusion.3), channel_id=1, source_target_pairs={{1,0},{2,1},{3,2},{4,3},{5,4},{6,5},{7,6},{8,7},{9,8},{10,9},{11,1... | collective-permute-start | bytes 3145736 | tf_op jit(solution)/shard_map/ppermute | solution.py:28
  23.8 50.8 %collective-permute-start.2 = (bf16[16,128,256]{2,1,0:T(8,128)(2,1)S(1)}, bf16[16,128,256]{2,1,0:T(8,128)(2,1)S(1)}, u32[]{:S(2)}, u32[]{:S(2)}) collective-permute-start(bf16[16,128,256]{2,1,0:T(8,128)(2,1)S(1)} %pad_maximum_fusion.3), channel_id=1, source_target_pairs={{0,1},{1,2},{2,3},{3,4},{4,5},{5,6},{6,7},{7,8},{8,9},{9,10},{10,1... | collective-permute-start | bytes 3145736 | tf_op jit(solution)/shard_map/ppermute | solution.py:26
  78.0 3.4 %copy-start.6 = (bf16[2,256,1024]{2,1,0:T(8,128)(2,1)S(1)}, bf16[2,256,1024]{2,1,0:T(8,128)(2,1)}, u32[]{:S(2)}) copy-start(bf16[2,256,1024]{2,1,0:T(8,128)(2,1)} %param.21) | copy-start | bytes 3145732
  78.0 3.4 %copy-start.11 = (bf16[7,1,128,256]{3,2,0,1:T(8,128)(2,1)S(1)}, bf16[7,1,128,256]{3,2,0,1:T(8,128)(2,1)}, u32[]{:S(2)}) copy-start(bf16[7,1,128,256]{3,2,0,1:T(8,128)(2,1)} %get-tuple-element.61) | copy-start | bytes 1376260
  81.3 2.7 %copy-start.13 = (f32[16,1,128,256]{3,2,0,1:T(8,128)}, f32[16,1,128,256]{3,2,0,1:T(8,128)S(1)}, u32[]{:S(2)}) copy-start(f32[16,1,128,256]{3,2,0,1:T(8,128)S(1)} %fusion.21) | copy-start | bytes 6291460
  81.3 2.7 %copy-start.5 = (f32[7,128,256]{2,1,0:T(8,128)S(1)}, f32[7,128,256]{2,1,0:T(8,128)}, u32[]{:S(2)}) copy-start(f32[7,128,256]{2,1,0:T(8,128)} %copy-done.4) | copy-start | bytes 2752516
  84.1 6.3 %copy-start.2 = (bf16[7,128,256]{2,1,0:T(8,128)(2,1)S(1)}, bf16[7,128,256]{2,1,0:T(8,128)(2,1)}, u32[]{:S(2)}) copy-start(bf16[7,128,256]{2,1,0:T(8,128)(2,1)} %copy-done.1) | copy-start | bytes 1376260
  90.4 4.0 %copy-start.10 = (bf16[8,128,256]{2,1,0:T(8,128)(2,1)}, bf16[8,128,256]{2,1,0:T(8,128)(2,1)S(1)}, u32[]{:S(2)}) copy-start(bf16[8,128,256]{2,1,0:T(8,128)(2,1)S(1)} %get-tuple-element.67) | copy-start | bytes 1572868
  94.4 38.1 %copy-start.8 = (bf16[8,128,256]{2,1,0:T(8,128)(2,1)}, bf16[8,128,256]{2,1,0:T(8,128)(2,1)S(1)}, u32[]{:S(2)}) copy-start(bf16[8,128,256]{2,1,0:T(8,128)(2,1)S(1)} %fusion.46) | copy-start | bytes 1572868
  94.5 25.4 %collective-permute-start.5 = (bf16[16,128,256]{2,1,0:T(8,128)(2,1)S(1)}, bf16[16,128,256]{2,1,0:T(8,128)(2,1)S(1)}, u32[]{:S(2)}, u32[]{:S(2)}) collective-permute-start(bf16[16,128,256]{2,1,0:T(8,128)(2,1)S(1)} %pad_maximum_fusion.4), channel_id=1, source_target_pairs={{1,0},{2,1},{3,2},{4,3},{5,4},{6,5},{7,6},{8,7},{9,8},{10,9},{11,1... | collective-permute-start | bytes 3145736 | tf_op jit(solution)/shard_map/ppermute | solution.py:28
  94.6 36.3 %collective-permute-start.4 = (bf16[16,128,256]{2,1,0:T(8,128)(2,1)S(1)}, bf16[16,128,256]{2,1,0:T(8,128)(2,1)S(1)}, u32[]{:S(2)}, u32[]{:S(2)}) collective-permute-start(bf16[16,128,256]{2,1,0:T(8,128)(2,1)S(1)} %pad_maximum_fusion.4), channel_id=1, source_target_pairs={{0,1},{1,2},{2,3},{3,4},{4,5},{5,6},{6,7},{7,8},{8,9},{9,10},{10,1... | collective-permute-start | bytes 3145736 | tf_op jit(solution)/shard_map/ppermute | solution.py:26
  132.5 2.8 %copy-start.14 = (bf16[2,1,4,128,128]{4,3,2,1,0:T(8,128)(2,1)S(1)}, bf16[2,1,4,128,128]{4,3,2,1,0:T(8,128)(2,1)}, u32[]{:S(2)}) copy-start(bf16[2,1,4,128,128]{4,3,2,1,0:T(8,128)(2,1)} %param.20) | copy-start | bytes 786436
  135.3 3.3 %copy-start.7 = (bf16[2,256,1024]{2,1,0:T(8,128)(2,1)S(1)}, bf16[2,256,1024]{2,1,0:T(8,128)(2,1)}, u32[]{:S(2)}) copy-start(bf16[2,256,1024]{2,1,0:T(8,128)(2,1)} %param.21) | copy-start | bytes 3145732
  135.3 3.3 %copy-start.9 = (bf16[8,128,256]{2,1,0:T(8,128)(2,1)S(1)}, bf16[8,128,256]{2,1,0:T(8,128)(2,1)}, u32[]{:S(2)}) copy-start(bf16[8,128,256]{2,1,0:T(8,128)(2,1)} %copy-done.8) | copy-start | bytes 1572868
  138.6 3.4 %copy-start.12 = (f32[16,1,128,256]{3,2,0,1:T(8,128)}, f32[16,1,128,256]{3,2,0,1:T(8,128)S(1)}, u32[]{:S(2)}) copy-start(f32[16,1,128,256]{3,2,0,1:T(8,128)S(1)} %fusion.24) | copy-start | bytes 6291460
  138.6 3.4 %copy-start.3 = (f32[8,128,256]{2,1,0:T(8,128)S(1)}, f32[8,128,256]{2,1,0:T(8,128)}, u32[]{:S(2)}) copy-start(f32[8,128,256]{2,1,0:T(8,128)} %param.18) | copy-start | bytes 3145732
  147.0 109.9 %copy-start = (f32[8,128,256]{2,1,0:T(8,128)}, f32[8,128,256]{2,1,0:T(8,128)S(1)}, u32[]{:S(2)}) copy-start(f32[8,128,256]{2,1,0:T(8,128)S(1)} %fusion.34) | copy-start | bytes 3145732
  168.4 29.6 %collective-permute-start.6 = (bf16[8,128,256]{2,1,0:T(8,128)(2,1)S(1)}, bf16[8,128,256]{2,1,0:T(8,128)(2,1)S(1)}, u32[]{:S(2)}, u32[]{:S(2)}) collective-permute-start(bf16[8,128,256]{2,1,0:T(8,128)(2,1)S(1)} %get-tuple-element.57), channel_id=1, source_target_pairs={{0,1},{1,2},{2,3},{3,4},{4,5},{5,6},{6,7},{7,8},{8,9},{9,10},{10,1... | collective-permute-start | bytes 1572872 | tf_op jit(solution)/shard_map/ppermute | solution.py:16
  168.5 29.5 %collective-permute-start.7 = (bf16[8,128,256]{2,1,0:T(8,128)(2,1)S(1)}, bf16[8,128,256]{2,1,0:T(8,128)(2,1)S(1)}, u32[]{:S(2)}, u32[]{:S(2)}) collective-permute-start(bf16[8,128,256]{2,1,0:T(8,128)(2,1)S(1)} %get-tuple-element.58), channel_id=1, source_target_pairs={{0,63},{1,0},{2,1},{3,2},{4,3},{5,4},{6,5},{7,6},{8,7},{9,8},{10,9... | collective-permute-start | bytes 1572872 | tf_op jit(solution)/shard_map/ppermute | solution.py:16
  198.0 0.8 copy-start.17
  198.9 0.8 copy-start.18
  221.4 24.1 %collective-permute-start.8 = (bf16[8,128,256]{2,1,0:T(8,128)(2,1)S(1)}, bf16[8,128,256]{2,1,0:T(8,128)(2,1)S(1)}, u32[]{:S(2)}, u32[]{:S(2)}) collective-permute-start(bf16[8,128,256]{2,1,0:T(8,128)(2,1)S(1)} %get-tuple-element.55), channel_id=1, source_target_pairs={{0,1},{1,2},{2,3},{3,4},{4,5},{5,6},{6,7},{7,8},{8,9},{9,10},{10,1... | collective-permute-start | bytes 1572872 | tf_op jit(solution)/shard_map/ppermute | solution.py:16
  221.5 29.5 %collective-permute-start.9 = (bf16[8,128,256]{2,1,0:T(8,128)(2,1)S(1)}, bf16[8,128,256]{2,1,0:T(8,128)(2,1)S(1)}, u32[]{:S(2)}, u32[]{:S(2)}) collective-permute-start(bf16[8,128,256]{2,1,0:T(8,128)(2,1)S(1)} %get-tuple-element.56), channel_id=1, source_target_pairs={{0,63},{1,0},{2,1},{3,2},{4,3},{5,4},{6,5},{7,6},{8,7},{9,8},{10,9... | collective-permute-start | bytes 1572872 | tf_op jit(solution)/shard_map/ppermute | solution.py:16
  251.3 5.6 %collective-permute-start.10 = (bf16[1,128,256]{2,1,0:T(8,128)(2,1)S(1)}, bf16[1,128,256]{2,1,0:T(8,128)(2,1)S(1)}, u32[]{:S(2)}, u32[]{:S(2)}) collective-permute-start(bf16[1,128,256]{2,1,0:T(8,128)(2,1)S(1)} %slice.362), channel_id=1, source_target_pairs={{64,0},{128,64},{192,128},{65,1},{129,65},{193,129},{66,2},{130,66... | collective-permute-start | bytes 196616 | tf_op jit(solution)/shard_map/ppermute | solution.py:38
where the time goes:
time: 259 us; the launch traced here: 258 us
  waiting for transfers between devices  132 us (51%)
  matrix products  57.3 us (22%)
  starting transfers between devices  36.3 us (14%)
  local copies, waits for them, and re-layouts  24.4 us (9%)
  other arithmetic  6.92 us (3%)
    ppermute x2, waiting for transfers between devices, extended(): lax.ppermute(head, axis, [((i + 1) % count, i) for i in range(count)])  64.2 us
    ppermute x4, waiting for transfers between devices, shifted(): return lax.ppermute(value, axis, pairs)  43.5 us
    ppermute x2, waiting for transfers between devices, extended(): lax.ppermute(tail, axis, [(i, (i + 1) % count) for i in range(count)])  21.3 us
    ppermute x4, starting transfers between devices, shifted(): return lax.ppermute(value, axis, pairs)  15.7 us
    dot_general x2, matrix products, transpose_aggregate(): jnp.einsum('tbknd,bkw->twnd', pieces, selector, precision=lax.Precision.H...  13.7 us
    dot_general x2, matrix products, forward_pass(): jnp.einsum('tnh,hd->tnd', lifted, outer_weight[layer_index], preferred_el...  11.3 us
    another operation x2, local copies, waits for them, and re-layouts  10.6 us
    dot_general x2, matrix products, adjoint_pass(): jnp.einsum('tnh,dh->tnd', pulled, inner_weight[layer_index], preferred_el...  10.2 us
  transfers between devices with their start and end apart: 11, of which 8 were waited for; matrix products, arithmetic and copies ran while one was open for 2% of the time, Pallas kernels for 0%

commit v1 on v0

v1 whole, which is shorter than its diff:
```python
import jax
import jax.numpy as jnp
from jax import lax
from jax.experimental import pallas as pl
from jax.experimental.pallas import tpu as pltpu
from jax.sharding import PartitionSpec as P

BF = jnp.bfloat16
F32 = jnp.float32
G = 4
NW = 2
B = 128
D = 256
HID = 1024
HC = 256
TM = 4
PARTS = 64
HALF_ROOT = 0.7071067811865476
DENSITY_NORM = 0.3989422804014327


def dot(a, b, ca=1, cb=0):
    return lax.dot_general(a, b, (((ca,), (cb,)), ((), ())), preferred_element_type=F32)


def origin(y, k):
    return lax.rem(y + G - k, G)


def stack(*values):
    return jnp.concatenate(values, axis=0)


def pack_kernel(info, states, inc, *outs):
    y = info[0]
    for k in range(1, G):
        m = lax.rem(y + k, G)
        for w in range(NW):
            outs[k - 1][w, 0] = states[NW * m + w]
            outs[k - 1][w, 1] = inc[NW * m + w].astype(BF)


def fold_kernel(info, slots, states, inc, edges, own, a0, *ext):
    y = info[0]
    for w in range(NW):
        own[w, 0] = states[NW * y + w]
        own[w, 1] = inc[NW * y + w].astype(BF)
    for layer in range(2):
        for slot in range(3):
            total = jnp.zeros((B, B), F32)
            for f in range(4):
                total += jnp.where(slots[0, f] == slot, edges[layer, 0, f].astype(F32), 0.0)
            cols = slice(slot * B, (slot + 1) * B)
            if layer == 0:
                a0[:, cols] = total.astype(BF)
            else:
                for k in range(G):
                    ext[k][:, cols] = total.astype(BF)
    for k in range(G):
        m = lax.rem(y + k + 1, G)
        ext[k][:, 3 * B :] = inc[NW * m].astype(BF)


def edge_kernel(info, r0, r1, r2, r3, send_left, send_right, sems):
    y = info[0]
    for k, r in enumerate((r0, r1, r2, r3)):
        block = origin(y, k)

        @pl.when(block == 0)
        def _():
            pltpu.make_async_copy(r, send_left, sems.at[0]).start()

        @pl.when(block == G - 1)
        def _():
            pltpu.make_async_copy(r, send_right, sems.at[1]).start()

    pltpu.make_async_copy(r0, send_left, sems.at[0]).wait()
    pltpu.make_async_copy(r0, send_right, sems.at[1]).wait()


def sort_edges(y, mats, amat, tmat):
    for k, a in enumerate(mats):
        amat[origin(y, k)] = a[:, : 3 * B]
    for c in range(G):
        for slot in range(3):
            t = jnp.transpose(amat[c, :, slot * B : (slot + 1) * B].astype(F32)).astype(BF)
            to = c + slot - 1
            if 0 <= to < G:
                place = 2 - slot
            else:
                to, place = c, slot
            tmat[to, :, place * B : (place + 1) * B] = t


def pair_matrix(mats, hat):
    hat[0:B, 3 * B :] = jnp.zeros((B, B), BF)
    hat[B:, 0:B] = jnp.zeros((B, B), BF)
    hat[0:B, 0 : 3 * B] = mats[1]
    hat[B:, B:] = mats[2]


def forward_rows(base_sum, tan_sum, win, bias, wout, slope, with_base):
    both = stack(base_sum.astype(BF), tan_sum.astype(BF))
    half = base_sum.shape[0]
    for h in range(HID // HC):
        cols = slice(h * HC, (h + 1) * HC)
        z = dot(both, win[:, cols])
        act = z[:half] + bias[:, cols]
        phi = 0.5 * (1.0 + lax.erf(act * HALF_ROOT))
        slp = phi + act * jnp.exp(-0.5 * act * act) * DENSITY_NORM
        slope[:, cols] = slp.astype(BF)
        lifted = (slp * z[half:]).astype(BF)
        tan_sum = tan_sum + dot(lifted, wout[cols, :])
        if with_base:
            base_sum = base_sum + dot((act * phi).astype(BF), wout[cols, :])
    return base_sum, tan_sum


def adjoint_rows(current, win, wout, slope):
    narrow = current.astype(BF)
    for h in range(HID // HC):
        cols = slice(h * HC, (h + 1) * HC)
        up = dot(narrow, wout[cols, :], 1, 1)
        pulled = (slope[:, cols].astype(F32) * up).astype(BF)
        current = current + dot(pulled, win[:, cols], 1, 1)
    return current


def inner0_kernel(
    info, r0, r1, r2, r3, a0, a1, a2, a3, win, bias, wout,
    field, amat, tmat, base_out, tan_out, slope, hat,
):
    y = info[0]
    sort_edges(y, (a0, a1, a2, a3), amat, tmat)
    pair_matrix(amat, hat)
    for k, r in enumerate((r0, r1, r2, r3)):
        block = origin(y, k)
        rows = pl.ds(pl.multiple_of(block * B, B), B)
        for w in range(NW):
            field[w, rows, 0:D] = r[w, 0]
            field[w, rows, D:] = r[w, 1]
    for w in range(NW):
        agg = dot(hat[...], field[w])
        base_sum = field[w, B : 3 * B, 0:D].astype(F32) + agg[:, 0:D]
        tan_sum = field[w, B : 3 * B, D:].astype(F32) + agg[:, D:]
        base, tan = forward_rows(base_sum, tan_sum, win, bias, wout, slope.at[w], True)
        base_out[w] = base.astype(BF)
        tan_out[w] = tan


def edge0_kernel(
    field, amat, left, right, win, bias, wout,
    send_left, send_right, tan_out, slope,
):
    for w in range(NW):
        lo = stack(jnp.concatenate([left[w, 0], left[w, 1]], axis=1), field[w, 0 : 2 * B])
        hi = stack(field[w, 2 * B :], jnp.concatenate([right[w, 0], right[w, 1]], axis=1))
        agg = stack(dot(amat[0], lo), dot(amat[G - 1], hi))
        own = stack(field[w, 0:B], field[w, 3 * B :]).astype(F32)
        base, tan = forward_rows(
            own[:, 0:D] + agg[:, 0:D], own[:, D:] + agg[:, D:], win, bias, wout, slope.at[w], True
        )
        tan_out[w] = tan
        base, tan = base.astype(BF), tan.astype(BF)
        send_left[w, 0] = base[0:B]
        send_left[w, 1] = tan[0:B]
        send_right[w, 0] = base[B:]
        send_right[w, 1] = tan[B:]


def inner1_kernel(
    info, base_in, tan_in, lo, hi, field, e0, e0r, e1, e2, e3, win, bias, wout,
    amat, tmat, next_out, image, returned, hat, slope, nxt,
):
    y = info[0]
    sort_edges(y, (e0, e1, e2, e3), amat, tmat)
    pair_matrix(amat, hat)
    for k, e in enumerate((e0, e1, e2, e3)):
        value = e[:, 3 * B :]
        if k == 0:
            value = jnp.where(y == G - 1, e0r[:, 3 * B :], value)
        nxt[origin(y, k)] = value
    next_out[0:B] = nxt[0]
    next_out[B:] = nxt[G - 1]
    for w in range(NW):
        base = stack(lo[w, 0], base_in[w], hi[w, 0])
        tan = stack(lo[w, 1], tan_in[w].astype(BF), hi[w, 1])
        base_sum = base_in[w].astype(F32) + dot(hat[...], base)
        tan_sum = tan_in[w] + dot(hat[...], tan)
        _, out = forward_rows(base_sum, tan_sum, win, bias, wout, slope, False)
        image[w] = out.astype(BF)
        if w == 0:
            following = field[1, B : 3 * B, D:].astype(F32)
            current = following - out
        else:
            following = stack(nxt[1], nxt[2]).astype(F32)
            current = jnp.where(info[1] == 1, 0.0, following - out)
        returned[w] = adjoint_rows(current, win, wout, slope)


def edge1_kernel(
    info, lo, hi, tan_edge, base_in, tan_in, left, right, field, next_edge, amat, tmat, image_in, win, bias, wout,
    im0, im1, im2, im3, returned, send_left, send_right, slope, image,
):
    y = info[0]
    for w in range(NW):
        tan_mid = tan_in[w].astype(BF)
        agg = []
        for f, mid in ((0, base_in[w]), (1, tan_mid)):
            agg.append(stack(
                dot(amat[0], stack(left[w, f], lo[w, f], mid[0:B])),
                dot(amat[G - 1], stack(mid[B:], hi[w, f], right[w, f])),
            ))
        base_sum = stack(lo[w, 0], hi[w, 0]).astype(F32) + agg[0]
        _, out = forward_rows(base_sum, tan_edge[w] + agg[1], win, bias, wout, slope, False)
        image[0, w] = out[0:B].astype(BF)
        image[1, w] = image_in[w, 0:B]
        image[2, w] = image_in[w, B:]
        image[3, w] = out[B:].astype(BF)
        if w == 0:
            following = stack(field[1, 0:B, D:], field[1, 3 * B :, D:]).astype(F32)
            current = following - out
        else:
            current = jnp.where(info[1] == 1, 0.0, next_edge[...].astype(F32) - out)
        back = adjoint_rows(current, win, wout, slope)
        returned[w] = back
        send_left[w] = dot(tmat[0, :, 0:B], back[0:B].astype(BF)).astype(BF)
        send_right[w] = dot(tmat[G - 1, :, 2 * B :], back[B:].astype(BF)).astype(BF)
    for k, im in enumerate((im0, im1, im2, im3)):
        im[...] = image[lax.rem(y + k, G)]


def spread_edge(tmat, edge, narrow):
    return edge + stack(
        dot(tmat[0, :, B:], narrow[0 : 2 * B]), dot(tmat[G - 1, :, 0 : 2 * B], narrow[2 * B :])
    )


def inner2_kernel(inner, edge, tmat, slope, win, wout, cur_edge, returned, hat):
    pair_matrix(tmat, hat)
    for w in range(NW):
        narrow = stack(edge[w, 0:B], inner[w], edge[w, B:]).astype(BF)
        cur_edge[w] = spread_edge(tmat, edge[w], narrow)
        current = inner[w] + dot(hat[...], narrow)
        returned[w] = adjoint_rows(current, win, wout, slope.at[w])


def edge2_kernel(cur_edge, left, right, tmat, slope, win, wout, returned, send_left, send_right):
    for w in range(NW):
        current = cur_edge[w] + stack(left[w], right[w]).astype(F32)
        back = adjoint_rows(current, win, wout, slope.at[w])
        returned[w] = back
        send_left[w] = dot(tmat[0, :, 0:B], back[0:B].astype(BF)).astype(BF)
        send_right[w] = dot(tmat[G - 1, :, 2 * B :], back[B:].astype(BF)).astype(BF)


def inner3_kernel(inner, edge, tmat, cur_edge, cur_inner, hat):
    pair_matrix(tmat, hat)
    for w in range(NW):
        narrow = stack(edge[w, 0:B], inner[w], edge[w, B:]).astype(BF)
        cur_edge[w] = spread_edge(tmat, edge[w], narrow)
        cur_inner[w] = (inner[w] + dot(hat[...], narrow)).astype(BF)


def finish_kernel(info, cur_edge, cur_inner, left, right, o0, o1, o2, o3, all_blocks):
    y = info[0]
    for w in range(NW):
        all_blocks[0, w] = (cur_edge[w, 0:B] + left[w].astype(F32)).astype(BF)
        all_blocks[1, w] = cur_inner[w, 0:B]
        all_blocks[2, w] = cur_inner[w, B:]
        all_blocks[3, w] = (cur_edge[w, B:] + right[w].astype(F32)).astype(BF)
    for k, out in enumerate((o0, o1, o2, o3)):
        out[...] = all_blocks[lax.rem(y + k, G)]


def last_image_kernel(info, i0, i1, i2, i3, out, sem):
    y = info[0]
    for k, im in enumerate((i0, i1, i2, i3)):

        @pl.when(origin(y, k) == G - 1)
        def _():
            pltpu.make_async_copy(im.at[NW - 1], out, sem).start()

    pltpu.make_async_copy(i0.at[NW - 1], out, sem).wait()


def misfit_kernel(info, inc, i0, i1, i2, i3, before, misfit):
    y = info[0]
    for k, im in enumerate((i0, i1, i2, i3)):
        m = origin(y, k)
        misfit[NW * m + 1] = inc[NW * m + 1] - im[0].astype(F32)
        even = NW * lax.rem(m + 1, G)
        image = jnp.where(m == G - 1, before[...], im[1])
        misfit[even] = inc[even] - image.astype(F32)


def normal_kernel(info, misfit, p0, p1, p2, p3, normal):
    y = info[0]
    for k, part in enumerate((p0, p1, p2, p3)):
        m = origin(y, k)
        for w in range(NW):
            normal[NW * m + w] = misfit[NW * m + w] - part[w].astype(F32)


SMEM = pl.BlockSpec(memory_space=pltpu.SMEM)
VMEM = pl.BlockSpec(memory_space=pltpu.VMEM)
ANY = pl.BlockSpec(memory_space=pl.ANY)


def sds(shape, dtype=BF):
    return jax.ShapeDtypeStruct(shape, dtype)


def call(kernel, name, ins, outs, scratch=(), smem=0, layers=(), space=VMEM):
    specs = [SMEM] * smem + [space] * (len(ins) - smem)
    for position, layer in layers:
        shape = ins[position].shape
        specs[position] = pl.BlockSpec((None,) + shape[1:], lambda i, layer=layer: (layer, 0, 0))
    return pl.pallas_call(
        kernel,
        name=name,
        grid=(1,),
        out_shape=outs,
        in_specs=specs,
        out_specs=[space] * len(outs),
        scratch_shapes=list(scratch),
        compiler_params=pltpu.CompilerParams(vmem_limit_bytes=60 * 1024 * 1024),
    )(*ins)


def group_pairs(k):
    return [(b, b // G * G + (b + k) % G) for b in range(PARTS)]


def side_pairs(d):
    return [(b, (b + G * d) % PARTS) for b in range(PARTS)]


def next_increment_pairs(k):
    pairs = []
    for t in range(TM):
        for b in range(PARTS):
            m = (b + k) % G
            if k == 0 and m != G - 1:
                continue
            to = (t - 1) % TM if m == G - 1 else t
            pairs.append((t * PARTS + b, to * PARTS + b // G * G + m))
    return pairs


def to_members(sends):
    return [sends[0]] + [lax.ppermute(sends[k], "mesh", group_pairs(k)) for k in range(1, G)]


def swap_sides(send_left, send_right):
    left = lax.ppermute(send_right, "mesh", side_pairs(1))
    right = lax.ppermute(send_left, "mesh", side_pairs(-1))
    return left, right


def local(states, increment, window_slots, edge_weights, inner_weight, inner_bias, outer_weight):
    y = lax.rem(lax.axis_index("mesh"), G).astype(jnp.int32)
    ends = jnp.logical_and(y == G - 1, lax.axis_index("tm") == TM - 1).astype(jnp.int32)
    info = jnp.stack([y, ends])
    bias = inner_bias.reshape(2, 1, HID)

    item = sds((NW, 2, B, D))
    half = sds((NW, B, D))
    pair_bf = sds((NW, 2 * B, D))
    pair = sds((NW, 2 * B, D), F32)
    hidden = sds((NW, 2 * B, HID))
    mats = sds((G, B, 3 * B))
    hat = pltpu.VMEM((2 * B, 4 * B), BF)
    dma = pltpu.SemaphoreType.DMA

    sends = call(pack_kernel, "pack", (info, states, increment), [item] * (G - 1), smem=1)
    own, a0, *ext = call(
        fold_kernel, "fold", (info, window_slots, states, increment, edge_weights),
        [item, sds((B, 3 * B))] + [sds((B, 3 * B + D))] * G, smem=2,
    )
    got = to_members([own, *sends])
    a0 = to_members([a0] * G)
    moved = [lax.ppermute(ext[k], ("tm", "mesh"), next_increment_pairs(k)) for k in range(G)]

    lo, hi = call(
        edge_kernel, "edge", (info, *got), [item, item], (dma((2,)),), smem=1, space=ANY,
    )
    left, right = swap_sides(lo, hi)
    field, amat0, tmat0, base_in, tan_in, slope_in = call(
        inner0_kernel, "inner0", (info, *got, *a0, inner_weight, bias, outer_weight),
        [sds((NW, G * B, 2 * D)), mats, mats, pair_bf, pair, hidden],
        (hat,), smem=1, layers=((9, 0), (10, 0), (11, 0)),
    )
    lo, hi, tan_edge, slope_edge = call(
        edge0_kernel, "edge0", (field, amat0, left, right, inner_weight, bias, outer_weight),
        [item, item, pair, hidden], layers=((4, 0), (5, 0), (6, 0)),
    )

    left, right = swap_sides(lo, hi)
    slope1 = pltpu.VMEM((2 * B, HID), BF)
    amat1, tmat1, next_edge, image_in, inner = call(
        inner1_kernel, "inner1",
        (info, base_in, tan_in, lo, hi, field, ext[0], *moved, inner_weight, bias, outer_weight),
        [mats, mats, sds((2 * B, D)), pair_bf, pair],
        (hat, slope1, pltpu.VMEM((G, B, D), BF)), smem=1, layers=((11, 1), (12, 1), (13, 1)),
    )
    *images, edge, send_left, send_right = call(
        edge1_kernel, "edge1",
        (info, lo, hi, tan_edge, base_in, tan_in, left, right, field, next_edge, amat1, tmat1, image_in,
         inner_weight, bias, outer_weight),
        [half] * G + [pair, half, half],
        (slope1, pltpu.VMEM((G, NW, B, D), BF)), smem=1, layers=((13, 1), (14, 1), (15, 1)),
    )

    left, right = swap_sides(send_left, send_right)
    images = to_members(images)
    cur_edge, inner = call(
        inner2_kernel, "inner2", (inner, edge, tmat1, slope_in, inner_weight, outer_weight),
        [pair, pair], (hat,), layers=((4, 0), (5, 0)),
    )
    edge, send_left, send_right = call(
        edge2_kernel, "edge2", (cur_edge, left, right, tmat0, slope_edge, inner_weight, outer_weight),
        [pair, half, half], layers=((5, 0), (6, 0)),
    )

    left, right = swap_sides(send_left, send_right)
    (last,) = call(
        last_image_kernel, "last_image", (info, *images), [sds((B, D))], (dma,), smem=1, space=ANY,
    )
    before = lax.ppermute(last, "tm", [(t, t + 1) for t in range(TM - 1)])
    cur_edge, cur_inner = call(
        inner3_kernel, "inner3", (inner, edge, tmat0), [pair, pair_bf], (hat,),
    )
    parts = call(
        finish_kernel, "finish", (info, cur_edge, cur_inner, left, right), [half] * G,
        (pltpu.VMEM((G, NW, B, D), BF),), smem=1,
    )
    parts = to_members(parts)
    whole = sds(increment.shape, F32)
    (misfit,) = call(misfit_kernel, "misfit", (info, increment, *images, before), [whole], smem=1)
    (normal,) = call(normal_kernel, "normal", (info, misfit, *parts), [whole], smem=1)
    return misfit, normal


def solution(mesh):
    placed = (
        P("tm", "mesh", None),
        P("tm", "mesh", None),
        P("mesh", None),
        P(None, "mesh", None, None, None),
        P(),
        P(),
        P(),
    )
    return jax.shard_map(
        local,
        mesh=mesh,
        in_specs=placed,
        out_specs=(P("tm", "mesh", None), P("tm", "mesh", None)),
        check_vma=False,
    )
```

time: 259 us -> 150 us (0.58)
  waiting for transfers between devices: 132 us -> 22.7 us
  Pallas kernels: 0 us -> 66.4 us
  matrix products: 57.3 us -> 0 us
  local copies, waits for them, and re-layouts: 24.4 us -> 7.71 us
  starting transfers between devices: 36.3 us -> 50.9 us
  other arithmetic: 6.92 us -> 0.65 us
    ppermute x11 -> x25, waiting for transfers between devices: 132 us -> 22.7 us  [the longest x12 13.2 us: to_members(): lax.ppermute(sends[k], 'mesh', group_pairs(k))]
    pallas_call x0 -> x14, Pallas kernels: none -> 66.4 us  [call(): pl.pallas_call(kernel, name=name, grid=(1,), out_shape=outs, in_specs=spe...]
    dot_general x13 -> x0, matrix products: 57.3 us -> none  [the longest x2 13.7 us: transpose_aggregate(): jnp.einsum('tbknd,bkw->twnd', pieces, selector, precision=lax.Precision.H...]
    ppermute x11 -> x25, starting transfers between devices: 36.3 us -> 50.9 us  [the longest x4 22.7 us: swap_sides(): right = lax.ppermute(send_left, 'mesh', side_pairs(-1))]
    another operation x2 -> x0, local copies, waits for them, and re-layouts: 10.6 us -> none
    gather x2 -> x0, local copies, waits for them, and re-layouts: 5.62 us -> none  [aggregate(): picked = jnp.take(block_view, window_slots.reshape(-1), axis=1)]
    unnamed x38 -> x68, local copies, waits for them, and re-layouts: 1.7 us -> 7.08 us
    concatenate x2 -> x0, local copies, waits for them, and re-layouts: 4.44 us -> none  [the longest x1 2.28 us: local(): jnp.concatenate([previous_field, increment[:windows - 1]], axis=0)]
  transfers between devices with their start and end apart: 11 -> 25, of which waited for: 8 -> 9; matrix products, arithmetic and copies ran while one was open for 2% -> 0% of each run, Pallas kernels for 0% -> 22%
where the time goes in v1:
time: 150 us; the launch traced here: 149 us
  Pallas kernels  66.4 us (44%)
  starting transfers between devices  50.9 us (34%)
  waiting for transfers between devices  22.7 us (15%)
  local copies, waits for them, and re-layouts  7.71 us (5%)
    pallas_call x14, Pallas kernels, call(): pl.pallas_call(kernel, name=name, grid=(1,), out_shape=outs, in_specs=spe...  66.4 us
    ppermute x4, starting transfers between devices, swap_sides(): right = lax.ppermute(send_left, 'mesh', side_pairs(-1))  22.7 us
    ppermute x12, starting transfers between devices, to_members(): lax.ppermute(sends[k], 'mesh', group_pairs(k))  17.6 us
    ppermute x12, waiting for transfers between devices, to_members(): lax.ppermute(sends[k], 'mesh', group_pairs(k))  13.2 us
    ppermute x4, waiting for transfers between devices, local(): lax.ppermute(ext[k], ('tm', 'mesh'), next_increment_pairs(k))  7.2 us
    unnamed x68, local copies, waits for them, and re-layouts  7.08 us
    ppermute x4, starting transfers between devices, local(): lax.ppermute(ext[k], ('tm', 'mesh'), next_increment_pairs(k))  5.48 us
    ppermute x1, starting transfers between devices, local(): before = lax.ppermute(last, 'tm', [(t, t + 1) for t in range(TM - 1)])  3.84 us
  transfers between devices with their start and end apart: 25, of which 9 were waited for; matrix products, arithmetic and copies ran while one was open for 0% of the time, Pallas kernels for 22%

profile of v1, /device:TPU:1, one launch (start us, length us, event | category | flops | bytes accessed | tf_op | source)
XLA Modules:
  0.0 149.3 jit_solution(1636868708610540000)
XLA Ops:
  1.3 2.3 %pack.1 = (bf16[2,2,128,256]{3,2,1,0:T(8,128)(2,1)}, bf16[2,2,128,256]{3,2,1,0:T(8,128)(2,1)}, bf16[2,2,128,256]{3,2,1,0:T(8,128)(2,1)}) custom-call(s32[2]{0:T(128)} %pad_add_fusion.info, bf16[8,128,256]{2,1,0:T(8,128)(2,1)} %states.3, f32[8,128,256]{2,1,0:T(8,128)} %inc.5), custom_call_target="tpu_custom_call" | custom-call | tf_op jit(solution)/shard_map/pack/pallas_call | solution.py:319
  3.6 2.1 %collective-permute-start = (bf16[2,2,128,256]{3,2,1,0:T(8,128)(2,1)}, bf16[2,2,128,256]{3,2,1,0:T(8,128)(2,1)S(1)}, u32[]{:S(2)}, u32[]{:S(2)}) collective-permute-start(bf16[2,2,128,256]{3,2,1,0:T(8,128)(2,1)} %get-tuple-element.47), channel_id=1, source_target_pairs={{0,1},{1,2},{2,3},{3,0},{4,5},{5,6},{6,7},{7,4},{8,9},{9,10},{10,1... | collective-permute-start | bytes 786440 | tf_op jit(solution)/shard_map/ppermute | solution.py:352
  5.7 2.6 %collective-permute-start.1 = (bf16[2,2,128,256]{3,2,1,0:T(8,128)(2,1)}, bf16[2,2,128,256]{3,2,1,0:T(8,128)(2,1)S(1)}, u32[]{:S(2)}, u32[]{:S(2)}) collective-permute-start(bf16[2,2,128,256]{3,2,1,0:T(8,128)(2,1)} %get-tuple-element.48), channel_id=1, source_target_pairs={{0,2},{1,3},{2,0},{3,1},{4,6},{5,7},{6,4},{7,5},{8,10},{9,11},{10,... | collective-permute-start | bytes 786440 | tf_op jit(solution)/shard_map/ppermute | solution.py:352
  9.4 2.6 %fold.1 = (bf16[2,2,128,256]{3,2,1,0:T(8,128)(2,1)}, bf16[128,384]{1,0:T(8,128)(2,1)}, bf16[128,640]{1,0:T(8,128)(2,1)}, bf16[128,640]{1,0:T(8,128)(2,1)}, bf16[...) custom-call(s32[2]{0:T(128)} %pad_add_fusion.info, s32[1,4]{1,0:T(1,128)} %slots.1, bf16[8,128,256]{2,1,0:T(8,128)(2,1)} %states.3, ...), custom_call_target="tpu_custom_call" | custom-call | tf_op jit(solution)/shard_map/fold/pallas_call | solution.py:319
  12.0 7.9 %collective-permute-done.1.r2 = bf16[2,2,128,256]{3,2,1,0:T(8,128)(2,1)S(1)} collective-permute-done((bf16[2,2,128,256]{3,2,1,0:T(8,128)(2,1)}, bf16[2,2,128,256]{3,2,1,0:T(8,128)(2,1)S(1)}, u32[]{:S(2)}, u32[]{:S(2)}) %collective-permute-start.1) | collective-permute-done | bytes 262176 | tf_op jit(solution)/shard_map/ppermute | solution.py:352
  20.7 17.8 %edge.1 = (bf16[2,2,128,256]{3,2,1,0:T(8,128)(2,1)}, bf16[2,2,128,256]{3,2,1,0:T(8,128)(2,1)}) custom-call(s32[2]{0:T(128)} %pad_add_fusion.info, bf16[2,2,128,256]{3,2,1,0:T(8,128)(2,1)} %get-tuple-element.46.r0, bf16[2,2,128,256]{3,2,1,0:T(8,128)(2,1)} %copy-done, bf16[2,2,128,256]{3,2,1,0:T(8,128)(2,1)} %copy-done.1, bf16[2,2,128,256]{3,2,1,0:T(8,128)(2,1)} %copy-done.2), custom_call_target="tpu_custom_call" | custom-call | tf_op jit(solution)/shard_map/edge/pallas_call | solution.py:319
  39.8 7.1 %collective-permute-start.7 = (bf16[2,2,128,256]{3,2,1,0:T(8,128)(2,1)}, bf16[2,2,128,256]{3,2,1,0:T(8,128)(2,1)S(1)}, u32[]{:S(2)}, u32[]{:S(2)}) collective-permute-start(bf16[2,2,128,256]{3,2,1,0:T(8,128)(2,1)} %get-tuple-element.54), channel_id=1, source_target_pairs={{0,60},{1,61},{2,62},{3,63},{4,0},{5,1},{6,2},{7,3},{8,4},{9,5},{1... | collective-permute-start | bytes 786440 | tf_op jit(solution)/shard_map/ppermute | solution.py:357
  46.9 2.7 %collective-permute-start.5 = (bf16[128,384]{1,0:T(8,128)(2,1)S(1)}, bf16[128,384]{1,0:T(8,128)(2,1)S(1)}, u32[]{:S(2)}, u32[]{:S(2)}) collective-permute-start(bf16[128,384]{1,0:T(8,128)(2,1)S(1)} %copy-done.22), channel_id=1, source_target_pairs={{0,3},{1,0},{2,1},{3,2},{4,7},{5,4},{6,5},{7,6},{8,11},{9,8},{10,9... | collective-permute-start | bytes 294920 | tf_op jit(solution)/shard_map/ppermute | solution.py:352
  50.2 2.4 %collective-permute-done.5.a3 = bf16[128,384]{1,0:T(8,128)(2,1)S(1)} collective-permute-done((bf16[128,384]{1,0:T(8,128)(2,1)S(1)}, bf16[128,384]{1,0:T(8,128)(2,1)S(1)}, u32[]{:S(2)}, u32[]{:S(2)}) %collective-permute-start.5) | collective-permute-done | bytes 98336 | tf_op jit(solution)/shard_map/ppermute | solution.py:352
  53.3 1.7 %collective-permute-done.4.a2 = bf16[128,384]{1,0:T(8,128)(2,1)S(1)} collective-permute-done((bf16[128,384]{1,0:T(8,128)(2,1)S(1)}, bf16[128,384]{1,0:T(8,128)(2,1)S(1)}, u32[]{:S(2)}, u32[]{:S(2)}) %collective-permute-start.4) | collective-permute-done | bytes 98336 | tf_op jit(solution)/shard_map/ppermute | solution.py:352
  56.8 4.9 %inner0.1 = (bf16[2,512,512]{2,1,0:T(8,128)(2,1)}, bf16[4,128,384]{2,1,0:T(8,128)(2,1)}, bf16[4,128,384]{2,1,0:T(8,128)(2,1)}, bf16[2,256,256]{2,1,0:T(8,128)(2,...) custom-call(s32[2]{0:T(128)} %pad_add_fusion.info, bf16[2,2,128,256]{3,2,1,0:T(8,128)(2,1)} %get-tuple-element.46.r0, ...), custom_call_target="tpu_custom_call" | custom-call | tf_op jit(solution)/shard_map/inner0/pallas_call | solution.py:319
  62.5 5.0 %edge0.1 = (bf16[2,2,128,256]{3,2,1,0:T(8,128)(2,1)}, bf16[2,2,128,256]{3,2,1,0:T(8,128)(2,1)}, f32[2,256,256]{2,1,0:T(8,128)}, bf16[2,256,1024]{2,1,0:T(8,128)(2,1)}) custom-call(bf16[2,512,512]{2,1,0:T(8,128)(2,1)} %get-tuple-element.51.field, bf16[4,128,384]{2,1,0:T(8,128)(2,1)} %get-tuple-element.52.amat, bf16[2,2,128,256]{3,2,1,0:T(8,128)(2,1)} %copy-done.6, ...), custom_call_target="tpu_custom_call" | custom-call | tf_op jit(solution)/shard_map/edge0/pallas_call | solution.py:319
  67.5 2.9 %collective-permute-start.9 = (bf16[2,2,128,256]{3,2,1,0:T(8,128)(2,1)}, bf16[2,2,128,256]{3,2,1,0:T(8,128)(2,1)S(1)}, u32[]{:S(2)}, u32[]{:S(2)}) collective-permute-start(bf16[2,2,128,256]{3,2,1,0:T(8,128)(2,1)} %get-tuple-element.55.lo), channel_id=1, source_target_pairs={{0,60},{1,61},{2,62},{3,63},{4,0},{5,1},{6,2},{7,3},{8,4},{9,5},{1... | collective-permute-start | bytes 786440 | tf_op jit(solution)/shard_map/ppermute | solution.py:357
  70.5 2.9 %collective-permute-start.12 = (bf16[128,640]{1,0:T(8,128)(2,1)S(1)}, bf16[128,640]{1,0:T(8,128)(2,1)S(1)}, u32[]{:S(2)}, u32[]{:S(2)}) collective-permute-start(bf16[128,640]{1,0:T(8,128)(2,1)S(1)} %copy-done.29), channel_id=1, source_target_pairs={{0,2},{1,195},{2,0},{3,1},{4,6},{5,199},{6,4},{7,5},{8,10},{9,203}... | collective-permute-start | bytes 491528 | tf_op jit(solution)/shard_map/ppermute | solution.py:383
  73.4 1.9 %collective-permute-start.13 = (bf16[128,640]{1,0:T(8,128)(2,1)S(1)}, bf16[128,640]{1,0:T(8,128)(2,1)S(1)}, u32[]{:S(2)}, u32[]{:S(2)}) collective-permute-start(bf16[128,640]{1,0:T(8,128)(2,1)S(1)} %copy-done.28), channel_id=1, source_target_pairs={{0,195},{1,0},{2,1},{3,2},{4,199},{5,4},{6,5},{7,6},{8,203},{9,8},... | collective-permute-start | bytes 491528 | tf_op jit(solution)/shard_map/ppermute | solution.py:383
  76.6 6.6 %collective-permute-done.13.e3 = bf16[128,640]{1,0:T(8,128)(2,1)S(1)} collective-permute-done((bf16[128,640]{1,0:T(8,128)(2,1)S(1)}, bf16[128,640]{1,0:T(8,128)(2,1)S(1)}, u32[]{:S(2)}, u32[]{:S(2)}) %collective-permute-start.13) | collective-permute-done | bytes 163872 | tf_op jit(solution)/shard_map/ppermute | solution.py:383
  83.9 6.0 %inner1.1 = (bf16[4,128,384]{2,1,0:T(8,128)(2,1)}, bf16[4,128,384]{2,1,0:T(8,128)(2,1)}, bf16[256,256]{1,0:T(8,128)(2,1)}, bf16[2,256,256]{2,1,0:T(8,128)(2,1)}, f32[2,256,256]{2,1,0:T(8,128)}) custom-call(s32[2]{0:T(128)} %pad_add_fusion.info, bf16[2,256,256]{2,1,0:T(8,128)(2,1)} %get-tuple-element.58.base_in, f32[2,256,256]{2,1,0:T(8,128)} %get-tuple-element.59.tan_in, ...), custom_call_target="tpu_custom_call" | custom-call | tf_op jit(solution)/shard_map/inner1/pallas_call | solution.py:319
  90.7 6.6 %edge1.1 = (bf16[2,128,256]{2,1,0:T(8,128)(2,1)}, bf16[2,128,256]{2,1,0:T(8,128)(2,1)}, bf16[2,128,256]{2,1,0:T(8,128)(2,1)}, bf16[2,128,256]{2,1,0:T(8,128)(2,1...) custom-call(s32[2]{0:T(128)} %pad_add_fusion.info, ...), custom_call_target="tpu_custom_call" | custom-call | tf_op jit(solution)/shard_map/edge1/pallas_call | solution.py:319
  97.3 6.3 %collective-permute-start.19 = (bf16[2,128,256]{2,1,0:T(8,128)(2,1)}, bf16[2,128,256]{2,1,0:T(8,128)(2,1)S(1)}, u32[]{:S(2)}, u32[]{:S(2)}) collective-permute-start(bf16[2,128,256]{2,1,0:T(8,128)(2,1)} %get-tuple-element.78), channel_id=1, source_target_pairs={{0,60},{1,61},{2,62},{3,63},{4,0},{5,1},{6,2},{7,3},{8,4},{9,5},{1... | collective-permute-start | bytes 393224 | tf_op jit(solution)/shard_map/ppermute | solution.py:357
  103.5 4.1 %inner2.1 = (f32[2,256,256]{2,1,0:T(8,128)}, f32[2,256,256]{2,1,0:T(8,128)}) custom-call(f32[2,256,256]{2,1,0:T(8,128)} %get-tuple-element.72.inner, f32[2,256,256]{2,1,0:T(8,128)} %get-tuple-element.73.edge, bf16[4,128,384]{2,1,0:T(8,128)(2,1)} %get-tuple-element.66.tmat, bf16[2,256,1024]{2,1,0:T(8,128)(2,1)} %get-tuple-element.74.slope, ...), custom_call_target="tpu_custom_call" | custom-call | tf_op jit(solution)/shard_map/inner2/pallas_call | solution.py:319
  109.0 3.9 %edge2.1 = (f32[2,256,256]{2,1,0:T(8,128)}, bf16[2,128,256]{2,1,0:T(8,128)(2,1)}, bf16[2,128,256]{2,1,0:T(8,128)(2,1)}) custom-call(f32[2,256,256]{2,1,0:T(8,128)} %get-tuple-element.76.cur_edge, bf16[2,128,256]{2,1,0:T(8,128)(2,1)} %copy-done.18, bf16[2,128,256]{2,1,0:T(8,128)(2,1)} %copy-done.19, bf16[4,128,384]{2,1,0:T(8,128)(2,1)} %get-tuple-element.79.tmat, ...), custom_call_target="tpu_custom_call" | custom-call | tf_op jit(solution)/shard_map/edge2/pallas_call | solution.py:319
  112.9 6.5 %collective-permute-start.21 = (bf16[2,128,256]{2,1,0:T(8,128)(2,1)}, bf16[2,128,256]{2,1,0:T(8,128)(2,1)S(1)}, u32[]{:S(2)}, u32[]{:S(2)}) collective-permute-start(bf16[2,128,256]{2,1,0:T(8,128)(2,1)} %get-tuple-element.85), channel_id=1, source_target_pairs={{0,60},{1,61},{2,62},{3,63},{4,0},{5,1},{6,2},{7,3},{8,4},{9,5},{1... | collective-permute-start | bytes 393224 | tf_op jit(solution)/shard_map/ppermute | solution.py:357
  119.4 4.6 %collective-permute-start.15 = (bf16[2,128,256]{2,1,0:T(8,128)(2,1)S(1)}, bf16[2,128,256]{2,1,0:T(8,128)(2,1)S(1)}, u32[]{:S(2)}, u32[]{:S(2)}) collective-permute-start(bf16[2,128,256]{2,1,0:T(8,128)(2,1)S(1)} %copy-done.32), channel_id=1, source_target_pairs={{0,2},{1,3},{2,0},{3,1},{4,6},{5,7},{6,4},{7,5},{8,10},{9,11},{10,... | collective-permute-start | bytes 393224 | tf_op jit(solution)/shard_map/ppermute | solution.py:352
  124.0 2.4 %inner3.1 = (f32[2,256,256]{2,1,0:T(8,128)}, bf16[2,256,256]{2,1,0:T(8,128)(2,1)}) custom-call(f32[2,256,256]{2,1,0:T(8,128)} %get-tuple-element.75.inner, f32[2,256,256]{2,1,0:T(8,128)} %get-tuple-element.81.edge, bf16[4,128,384]{2,1,0:T(8,128)(2,1)} %get-tuple-element.79.tmat), custom_call_target="tpu_custom_call" | custom-call | tf_op jit(solution)/shard_map/inner3/pallas_call | solution.py:319
  127.1 2.1 %finish.1 = (bf16[2,128,256]{2,1,0:T(8,128)(2,1)}, bf16[2,128,256]{2,1,0:T(8,128)(2,1)}, bf16[2,128,256]{2,1,0:T(8,128)(2,1)}, bf16[2,128,256]{2,1,0:T(8,128)(2,1)}) custom-call(s32[2]{0:T(128)} %pad_add_fusion.info, f32[2,256,256]{2,1,0:T(8,128)} %get-tuple-element.82.cur_edge, bf16[2,256,256]{2,1,0:T(8,128)(2,1)} %get-tuple-element.83.cur_inner, ...), custom_call_target="tpu_custom_call" | custom-call | tf_op jit(solution)/shard_map/finish/pallas_call | solution.py:319
  129.2 1.5 collective-permute-start.22
  130.7 2.3 %collective-permute-start.24 = (bf16[2,128,256]{2,1,0:T(8,128)(2,1)}, bf16[2,128,256]{2,1,0:T(8,128)(2,1)S(1)}, u32[]{:S(2)}, u32[]{:S(2)}) collective-permute-start(bf16[2,128,256]{2,1,0:T(8,128)(2,1)} %get-tuple-element.89), channel_id=1, source_target_pairs={{0,3},{1,0},{2,1},{3,2},{4,7},{5,4},{6,5},{7,6},{8,11},{9,8},{10,9... | collective-permute-start | bytes 393224 | tf_op jit(solution)/shard_map/ppermute | solution.py:352
  133.8 3.8 %last_image.1 = bf16[128,256]{1,0:T(8,128)(2,1)} custom-call(s32[2]{0:T(128)} %pad_add_fusion.info, bf16[2,128,256]{2,1,0:T(8,128)(2,1)} %get-tuple-element.68.i0, bf16[2,128,256]{2,1,0:T(8,128)(2,1)} %copy-done.3, bf16[2,128,256]{2,1,0:T(8,128)(2,1)} %copy-done.4, bf16[2,128,256]{2,1,0:T(8,128)(2,1)} %copy-done.5), custom_call_target="tpu_custom_call" | custom-call | tf_op jit(solution)/shard_map/last_image/pallas_call | solution.py:319
  137.5 3.8 %collective-permute-start.17 = (bf16[128,256]{1,0:T(8,128)(2,1)}, bf16[128,256]{1,0:T(8,128)(2,1)S(1)}, u32[]{:S(2)}, u32[]{:S(2)}) collective-permute-start(bf16[128,256]{1,0:T(8,128)(2,1)} %last_image.1), channel_id=1, source_target_pairs={{0,64},{64,128},{128,192},{1,65},{65,129},{129,193},{2,66},{66,130... | collective-permute-start | bytes 196616 | tf_op jit(solution)/shard_map/ppermute | solution.py:430
  141.4 1.6 %collective-permute-done.17.before = bf16[128,256]{1,0:T(8,128)(2,1)S(1)} collective-permute-done((bf16[128,256]{1,0:T(8,128)(2,1)}, bf16[128,256]{1,0:T(8,128)(2,1)S(1)}, u32[]{:S(2)}, u32[]{:S(2)}) %collective-permute-start.17) | collective-permute-done | bytes 65568 | tf_op jit(solution)/shard_map/ppermute | solution.py:430
  143.6 2.5 %misfit.1 = f32[8,128,256]{2,1,0:T(8,128)} custom-call(s32[2]{0:T(128)} %pad_add_fusion.info, f32[8,128,256]{2,1,0:T(8,128)} %inc.5, bf16[2,128,256]{2,1,0:T(8,128)(2,1)} %get-tuple-element.68.i0, bf16[2,128,256]{2,1,0:T(8,128)(2,1)} %copy-done.3, bf16[2,128,256]{2,1,0:T(8,128)(2,1)} %copy-done.4, bf16[2,128,256]{2,1,0:T(8,128)(2,1)} %copy-done.5, ...), custom_call_target="tpu_custom_call" | custom-call | tf_op jit(solution)/shard_map/misfit/pallas_call | solution.py:319
  146.8 2.5 %normal.1 = f32[8,128,256]{2,1,0:T(8,128)} custom-call(s32[2]{0:T(128)} %pad_add_fusion.info, f32[8,128,256]{2,1,0:T(8,128)} %misfit.1, bf16[2,128,256]{2,1,0:T(8,128)(2,1)} %get-tuple-element.86.p0, bf16[2,128,256]{2,1,0:T(8,128)(2,1)} %copy-done.15, bf16[2,128,256]{2,1,0:T(8,128)(2,1)} %copy-done.16, bf16[2,128,256]{2,1,0:T(8,128)(2,1)} %copy-done.17), custom_call_target="tpu_custom_call" | custom-call | tf_op jit(solution)/shard_map/normal/pallas_call | solution.py:319
  (102 shorter events, 14.5 us)
Async XLA Ops:
  3.6 8.4 %collective-permute-start = (bf16[2,2,128,256]{3,2,1,0:T(8,128)(2,1)}, bf16[2,2,128,256]{3,2,1,0:T(8,128)(2,1)S(1)}, u32[]{:S(2)}, u32[]{:S(2)}) collective-permute-start(bf16[2,2,128,256]{3,2,1,0:T(8,128)(2,1)} %get-tuple-element.47), channel_id=1, source_target_pairs={{0,1},{1,2},{2,3},{3,0},{4,5},{5,6},{6,7},{7,4},{8,9},{9,10},{10,1... | collective-permute-start | bytes 786440 | tf_op jit(solution)/shard_map/ppermute | solution.py:352
  5.7 14.2 %collective-permute-start.1 = (bf16[2,2,128,256]{3,2,1,0:T(8,128)(2,1)}, bf16[2,2,128,256]{3,2,1,0:T(8,128)(2,1)S(1)}, u32[]{:S(2)}, u32[]{:S(2)}) collective-permute-start(bf16[2,2,128,256]{3,2,1,0:T(8,128)(2,1)} %get-tuple-element.48), channel_id=1, source_target_pairs={{0,2},{1,3},{2,0},{3,1},{4,6},{5,7},{6,4},{7,5},{8,10},{9,11},{10,... | collective-permute-start | bytes 786440 | tf_op jit(solution)/shard_map/ppermute | solution.py:352
  8.3 11.6 %collective-permute-start.2 = (bf16[2,2,128,256]{3,2,1,0:T(8,128)(2,1)}, bf16[2,2,128,256]{3,2,1,0:T(8,128)(2,1)S(1)}, u32[]{:S(2)}, u32[]{:S(2)}) collective-permute-start(bf16[2,2,128,256]{3,2,1,0:T(8,128)(2,1)} %get-tuple-element.49), channel_id=1, source_target_pairs={{0,3},{1,0},{2,1},{3,2},{4,7},{5,4},{6,5},{7,6},{8,11},{9,8},{10,9... | collective-permute-start | bytes 786440 | tf_op jit(solution)/shard_map/ppermute | solution.py:352
  20.7 26.2 %copy-start.22 = (bf16[128,384]{1,0:T(8,128)(2,1)S(1)}, bf16[128,384]{1,0:T(8,128)(2,1)}, u32[]{:S(2)}) copy-start(bf16[128,384]{1,0:T(8,128)(2,1)} %get-tuple-element.50.a0) | copy-start | bytes 294916
  20.7 31.9 %copy-start.30 = (bf16[128,640]{1,0:T(8,128)(2,1)S(1)}, bf16[128,640]{1,0:T(8,128)(2,1)}, u32[]{:S(2)}) copy-start(bf16[128,640]{1,0:T(8,128)(2,1)} %get-tuple-element.61) | copy-start | bytes 491524
  20.7 31.9 %copy-start.27 = (f32[2,1024]{1,0:T(2,128)S(1)}, f32[2,1024]{1,0:T(2,128)}, u32[]{:S(2)}) copy-start(f32[2,1024]{1,0:T(2,128)} %param.12) | copy-start | bytes 24580
  38.5 23.2 %collective-permute-start.6 = (bf16[2,2,128,256]{3,2,1,0:T(8,128)(2,1)}, bf16[2,2,128,256]{3,2,1,0:T(8,128)(2,1)S(1)}, u32[]{:S(2)}, u32[]{:S(2)}) collective-permute-start(bf16[2,2,128,256]{3,2,1,0:T(8,128)(2,1)} %get-tuple-element.53), channel_id=1, source_target_pairs={{0,4},{1,5},{2,6},{3,7},{4,8},{5,9},{6,10},{7,11},{8,12},{9,13},{1... | collective-permute-start | bytes 786440 | tf_op jit(solution)/shard_map/ppermute | solution.py:356
  39.8 21.9 %collective-permute-start.7 = (bf16[2,2,128,256]{3,2,1,0:T(8,128)(2,1)}, bf16[2,2,128,256]{3,2,1,0:T(8,128)(2,1)S(1)}, u32[]{:S(2)}, u32[]{:S(2)}) collective-permute-start(bf16[2,2,128,256]{3,2,1,0:T(8,128)(2,1)} %get-tuple-element.54), channel_id=1, source_target_pairs={{0,60},{1,61},{2,62},{3,63},{4,0},{5,1},{6,2},{7,3},{8,4},{9,5},{1... | collective-permute-start | bytes 786440 | tf_op jit(solution)/shard_map/ppermute | solution.py:357
  46.9 5.7 %collective-permute-start.5 = (bf16[128,384]{1,0:T(8,128)(2,1)S(1)}, bf16[128,384]{1,0:T(8,128)(2,1)S(1)}, u32[]{:S(2)}, u32[]{:S(2)}) collective-permute-start(bf16[128,384]{1,0:T(8,128)(2,1)S(1)} %copy-done.22), channel_id=1, source_target_pairs={{0,3},{1,0},{2,1},{3,2},{4,7},{5,4},{6,5},{7,6},{8,11},{9,8},{10,9... | collective-permute-start | bytes 294920 | tf_op jit(solution)/shard_map/ppermute | solution.py:352
  49.6 5.3 %collective-permute-start.4 = (bf16[128,384]{1,0:T(8,128)(2,1)S(1)}, bf16[128,384]{1,0:T(8,128)(2,1)S(1)}, u32[]{:S(2)}, u32[]{:S(2)}) collective-permute-start(bf16[128,384]{1,0:T(8,128)(2,1)S(1)} %copy-done.22), channel_id=1, source_target_pairs={{0,2},{1,3},{2,0},{3,1},{4,6},{5,7},{6,4},{7,5},{8,10},{9,11},{10,... | collective-permute-start | bytes 294920 | tf_op jit(solution)/shard_map/ppermute | solution.py:352
  49.7 6.4 %collective-permute-start.3 = (bf16[128,384]{1,0:T(8,128)(2,1)S(1)}, bf16[128,384]{1,0:T(8,128)(2,1)S(1)}, u32[]{:S(2)}, u32[]{:S(2)}) collective-permute-start(bf16[128,384]{1,0:T(8,128)(2,1)S(1)} %copy-done.22), channel_id=1, source_target_pairs={{0,1},{1,2},{2,3},{3,0},{4,5},{5,6},{6,7},{7,4},{8,9},{9,10},{10,1... | collective-permute-start | bytes 294920 | tf_op jit(solution)/shard_map/ppermute | solution.py:352
  52.6 22.7 %collective-permute-start.11 = (bf16[128,640]{1,0:T(8,128)(2,1)S(1)}, bf16[128,640]{1,0:T(8,128)(2,1)S(1)}, u32[]{:S(2)}, u32[]{:S(2)}) collective-permute-start(bf16[128,640]{1,0:T(8,128)(2,1)S(1)} %copy-done.30), channel_id=1, source_target_pairs={{0,1},{1,2},{2,195},{3,0},{4,5},{5,6},{6,199},{7,4},{8,9},{9,10},{... | collective-permute-start | bytes 491528 | tf_op jit(solution)/shard_map/ppermute | solution.py:383
  62.5 10.8 %copy-start.28 = (bf16[128,640]{1,0:T(8,128)(2,1)S(1)}, bf16[128,640]{1,0:T(8,128)(2,1)}, u32[]{:S(2)}) copy-start(bf16[128,640]{1,0:T(8,128)(2,1)} %get-tuple-element.63) | copy-start | bytes 491524
  62.5 12.8 %copy-start.10 = (bf16[128,640]{1,0:T(8,128)(2,1)S(1)}, bf16[128,640]{1,0:T(8,128)(2,1)}, u32[]{:S(2)}) copy-start(bf16[128,640]{1,0:T(8,128)(2,1)} %get-tuple-element.60.e0) | copy-start | bytes 491524
  67.5 22.4 %collective-permute-start.9 = (bf16[2,2,128,256]{3,2,1,0:T(8,128)(2,1)}, bf16[2,2,128,256]{3,2,1,0:T(8,128)(2,1)S(1)}, u32[]{:S(2)}, u32[]{:S(2)}) collective-permute-start(bf16[2,2,128,256]{3,2,1,0:T(8,128)(2,1)} %get-tuple-element.55.lo), channel_id=1, source_target_pairs={{0,60},{1,61},{2,62},{3,63},{4,0},{5,1},{6,2},{7,3},{8,4},{9,5},{1... | collective-permute-start | bytes 786440 | tf_op jit(solution)/shard_map/ppermute | solution.py:357
  70.5 19.4 %collective-permute-start.8 = (bf16[2,2,128,256]{3,2,1,0:T(8,128)(2,1)}, bf16[2,2,128,256]{3,2,1,0:T(8,128)(2,1)S(1)}, u32[]{:S(2)}, u32[]{:S(2)}) collective-permute-start(bf16[2,2,128,256]{3,2,1,0:T(8,128)(2,1)} %get-tuple-element.56.hi), channel_id=1, source_target_pairs={{0,4},{1,5},{2,6},{3,7},{4,8},{5,9},{6,10},{7,11},{8,12},{9,13},{1... | collective-permute-start | bytes 786440 | tf_op jit(solution)/shard_map/ppermute | solution.py:356
  70.5 6.1 %collective-permute-start.12 = (bf16[128,640]{1,0:T(8,128)(2,1)S(1)}, bf16[128,640]{1,0:T(8,128)(2,1)S(1)}, u32[]{:S(2)}, u32[]{:S(2)}) collective-permute-start(bf16[128,640]{1,0:T(8,128)(2,1)S(1)} %copy-done.29), channel_id=1, source_target_pairs={{0,2},{1,195},{2,0},{3,1},{4,6},{5,199},{6,4},{7,5},{8,10},{9,203}... | collective-permute-start | bytes 491528 | tf_op jit(solution)/shard_map/ppermute | solution.py:383
  73.4 9.8 %collective-permute-start.13 = (bf16[128,640]{1,0:T(8,128)(2,1)S(1)}, bf16[128,640]{1,0:T(8,128)(2,1)S(1)}, u32[]{:S(2)}, u32[]{:S(2)}) collective-permute-start(bf16[128,640]{1,0:T(8,128)(2,1)S(1)} %copy-done.28), channel_id=1, source_target_pairs={{0,195},{1,0},{2,1},{3,2},{4,199},{5,4},{6,5},{7,6},{8,203},{9,8},... | collective-permute-start | bytes 491528 | tf_op jit(solution)/shard_map/ppermute | solution.py:383
  75.3 7.9 %collective-permute-start.10 = (bf16[128,640]{1,0:T(8,128)(2,1)S(1)}, bf16[128,640]{1,0:T(8,128)(2,1)S(1)}, u32[]{:S(2)}, u32[]{:S(2)}) collective-permute-start(bf16[128,640]{1,0:T(8,128)(2,1)S(1)} %copy-done.10), channel_id=1, source_target_pairs={{3,195},{7,199},{11,203},{15,207},{19,211},{23,215},{27,219},{31,2... | collective-permute-start | bytes 491528 | tf_op jit(solution)/shard_map/ppermute | solution.py:383
  97.3 10.5 %collective-permute-start.18 = (bf16[2,128,256]{2,1,0:T(8,128)(2,1)}, bf16[2,128,256]{2,1,0:T(8,128)(2,1)S(1)}, u32[]{:S(2)}, u32[]{:S(2)}) collective-permute-start(bf16[2,128,256]{2,1,0:T(8,128)(2,1)} %get-tuple-element.77), channel_id=1, source_target_pairs={{0,4},{1,5},{2,6},{3,7},{4,8},{5,9},{6,10},{7,11},{8,12},{9,13},{1... | collective-permute-start | bytes 393224 | tf_op jit(solution)/shard_map/ppermute | solution.py:356
  97.3 11.0 %collective-permute-start.19 = (bf16[2,128,256]{2,1,0:T(8,128)(2,1)}, bf16[2,128,256]{2,1,0:T(8,128)(2,1)S(1)}, u32[]{:S(2)}, u32[]{:S(2)}) collective-permute-start(bf16[2,128,256]{2,1,0:T(8,128)(2,1)} %get-tuple-element.78), channel_id=1, source_target_pairs={{0,60},{1,61},{2,62},{3,63},{4,0},{5,1},{6,2},{7,3},{8,4},{9,5},{1... | collective-permute-start | bytes 393224 | tf_op jit(solution)/shard_map/ppermute | solution.py:357
  109.0 10.4 %copy-start.32 = (bf16[2,128,256]{2,1,0:T(8,128)(2,1)S(1)}, bf16[2,128,256]{2,1,0:T(8,128)(2,1)}, u32[]{:S(2)}) copy-start(bf16[2,128,256]{2,1,0:T(8,128)(2,1)} %get-tuple-element.70) | copy-start | bytes 393220
  109.0 15.0 %copy-start.31 = (bf16[2,128,256]{2,1,0:T(8,128)(2,1)S(1)}, bf16[2,128,256]{2,1,0:T(8,128)(2,1)}, u32[]{:S(2)}) copy-start(bf16[2,128,256]{2,1,0:T(8,128)(2,1)} %get-tuple-element.71) | copy-start | bytes 393220
  112.9 13.5 %collective-permute-start.20 = (bf16[2,128,256]{2,1,0:T(8,128)(2,1)}, bf16[2,128,256]{2,1,0:T(8,128)(2,1)S(1)}, u32[]{:S(2)}, u32[]{:S(2)}) collective-permute-start(bf16[2,128,256]{2,1,0:T(8,128)(2,1)} %get-tuple-element.84), channel_id=1, source_target_pairs={{0,4},{1,5},{2,6},{3,7},{4,8},{5,9},{6,10},{7,11},{8,12},{9,13},{1... | collective-permute-start | bytes 393224 | tf_op jit(solution)/shard_map/ppermute | solution.py:356
  112.9 13.5 %collective-permute-start.21 = (bf16[2,128,256]{2,1,0:T(8,128)(2,1)}, bf16[2,128,256]{2,1,0:T(8,128)(2,1)S(1)}, u32[]{:S(2)}, u32[]{:S(2)}) collective-permute-start(bf16[2,128,256]{2,1,0:T(8,128)(2,1)} %get-tuple-element.85), channel_id=1, source_target_pairs={{0,60},{1,61},{2,62},{3,63},{4,0},{5,1},{6,2},{7,3},{8,4},{9,5},{1... | collective-permute-start | bytes 393224 | tf_op jit(solution)/shard_map/ppermute | solution.py:357
  119.4 11.3 %collective-permute-start.14 = (bf16[2,128,256]{2,1,0:T(8,128)(2,1)S(1)}, bf16[2,128,256]{2,1,0:T(8,128)(2,1)S(1)}, u32[]{:S(2)}, u32[]{:S(2)}) collective-permute-start(bf16[2,128,256]{2,1,0:T(8,128)(2,1)S(1)} %copy-done.33), channel_id=1, source_target_pairs={{0,1},{1,2},{2,3},{3,0},{4,5},{5,6},{6,7},{7,4},{8,9},{9,10},{10,1... | collective-permute-start | bytes 393224 | tf_op jit(solution)/shard_map/ppermute | solution.py:352
  119.4 13.7 %collective-permute-start.15 = (bf16[2,128,256]{2,1,0:T(8,128)(2,1)S(1)}, bf16[2,128,256]{2,1,0:T(8,128)(2,1)S(1)}, u32[]{:S(2)}, u32[]{:S(2)}) collective-permute-start(bf16[2,128,256]{2,1,0:T(8,128)(2,1)S(1)} %copy-done.32), channel_id=1, source_target_pairs={{0,2},{1,3},{2,0},{3,1},{4,6},{5,7},{6,4},{7,5},{8,10},{9,11},{10,... | collective-permute-start | bytes 393224 | tf_op jit(solution)/shard_map/ppermute | solution.py:352
  124.0 9.1 %collective-permute-start.16 = (bf16[2,128,256]{2,1,0:T(8,128)(2,1)S(1)}, bf16[2,128,256]{2,1,0:T(8,128)(2,1)S(1)}, u32[]{:S(2)}, u32[]{:S(2)}) collective-permute-start(bf16[2,128,256]{2,1,0:T(8,128)(2,1)S(1)} %copy-done.31), channel_id=1, source_target_pairs={{0,3},{1,0},{2,1},{3,2},{4,7},{5,4},{6,5},{7,6},{8,11},{9,8},{10,9... | collective-permute-start | bytes 393224 | tf_op jit(solution)/shard_map/ppermute | solution.py:352
  129.2 16.9 %collective-permute-start.22 = (bf16[2,128,256]{2,1,0:T(8,128)(2,1)}, bf16[2,128,256]{2,1,0:T(8,128)(2,1)S(1)}, u32[]{:S(2)}, u32[]{:S(2)}) collective-permute-start(bf16[2,128,256]{2,1,0:T(8,128)(2,1)} %get-tuple-element.87), channel_id=1, source_target_pairs={{0,1},{1,2},{2,3},{3,0},{4,5},{5,6},{6,7},{7,4},{8,9},{9,10},{10,1... | collective-permute-start | bytes 393224 | tf_op jit(solution)/shard_map/ppermute | solution.py:352
  130.6 15.5 %collective-permute-start.23 = (bf16[2,128,256]{2,1,0:T(8,128)(2,1)}, bf16[2,128,256]{2,1,0:T(8,128)(2,1)S(1)}, u32[]{:S(2)}, u32[]{:S(2)}) collective-permute-start(bf16[2,128,256]{2,1,0:T(8,128)(2,1)} %get-tuple-element.88), channel_id=1, source_target_pairs={{0,2},{1,3},{2,0},{3,1},{4,6},{5,7},{6,4},{7,5},{8,10},{9,11},{10,... | collective-permute-start | bytes 393224 | tf_op jit(solution)/shard_map/ppermute | solution.py:352
  130.7 15.4 %collective-permute-start.24 = (bf16[2,128,256]{2,1,0:T(8,128)(2,1)}, bf16[2,128,256]{2,1,0:T(8,128)(2,1)S(1)}, u32[]{:S(2)}, u32[]{:S(2)}) collective-permute-start(bf16[2,128,256]{2,1,0:T(8,128)(2,1)} %get-tuple-element.89), channel_id=1, source_target_pairs={{0,3},{1,0},{2,1},{3,2},{4,7},{5,4},{6,5},{7,6},{8,11},{9,8},{10,9... | collective-permute-start | bytes 393224 | tf_op jit(solution)/shard_map/ppermute | solution.py:352
  137.5 5.5 %collective-permute-start.17 = (bf16[128,256]{1,0:T(8,128)(2,1)}, bf16[128,256]{1,0:T(8,128)(2,1)S(1)}, u32[]{:S(2)}, u32[]{:S(2)}) collective-permute-start(bf16[128,256]{1,0:T(8,128)(2,1)} %last_image.1), channel_id=1, source_target_pairs={{0,64},{64,128},{128,192},{1,65},{65,129},{129,193},{2,66},{66,130... | collective-permute-start | bytes 196616 | tf_op jit(solution)/shard_map/ppermute | solution.py:430
  (27 other events, 61.0 us)

commit v2 on v1

v2 whole, which is shorter than its diff:
```python
import jax
import jax.numpy as jnp
from jax import lax
from jax.experimental import pallas as pl
from jax.experimental.pallas import tpu as pltpu
from jax.sharding import PartitionSpec as P


BF = jnp.bfloat16
F32 = jnp.float32
G = 4
NW = 2
B = 128
D = 256
HID = 1024
HC = 256
TM = 4
PARTS = 64
HALF_ROOT = 0.7071067811865476
DENSITY_NORM = 0.3989422804014327


def dot(a, b, ca=1, cb=0):
    return lax.dot_general(a, b, (((ca,), (cb,)), ((), ())), preferred_element_type=F32)


def member():
    return lax.rem(lax.axis_index("mesh"), G)


def last_member():
    return jnp.logical_and(member() == G - 1, lax.axis_index("tm") == TM - 1)


def origin(y, k):
    return lax.rem(y + G - k, G)


def stack(*values):
    return jnp.concatenate(values, axis=0)


def pack_kernel(states, inc, *outs):
    y = member()
    for k in range(1, G):
        m = lax.rem(y + k, G)
        for w in range(NW):
            outs[k - 1][w, 0] = states[NW * m + w]
            outs[k - 1][w, 1] = inc[NW * m + w].astype(BF)


def fold_kernel(slots, states, inc, edges, own, cross, *ext):
    y = member()
    for w in range(NW):
        own[w, 0] = states[NW * y + w]
        own[w, 1] = inc[NW * y + w].astype(BF)
    for layer in range(2):
        for slot in range(3):
            total = jnp.zeros((B, B), F32)
            for f in range(4):
                total += jnp.where(slots[0, f] == slot, edges[layer, 0, f].astype(F32), 0.0)
            first = (3 * layer + slot) * B
            for k in range(G):
                ext[k][:, first : first + B] = total.astype(BF)
    for k in range(G):
        m = lax.rem(y + k + 1, G)
        value = inc[NW * m].astype(BF)
        ext[k][:, 6 * B :] = value
        if k == 0:
            cross[...] = value


def edge_kernel(r0, r1, r2, r3, send_left, send_right):
    y = member()
    for k, r in enumerate((r0, r1, r2, r3)):
        block = origin(y, k)

        @pl.when(block == 0)
        def _():
            send_left[...] = r[...]

        @pl.when(block == G - 1)
        def _():
            send_right[...] = r[...]


def sort_edges(y, mats, first, amat, tmat):
    for k, a in enumerate(mats):
        amat[origin(y, k)] = a[:, first : first + 3 * B]
    for c in range(G):
        for slot in range(3):
            t = jnp.transpose(amat[c, :, slot * B : (slot + 1) * B].astype(F32)).astype(BF)
            to = c + slot - 1
            if 0 <= to < G:
                place = 2 - slot
            else:
                to, place = c, slot
            tmat[to, :, place * B : (place + 1) * B] = t


def pair_matrix(mats, hat):
    hat[0:B, 3 * B :] = jnp.zeros((B, B), BF)
    hat[B:, 0:B] = jnp.zeros((B, B), BF)
    hat[0:B, 0 : 3 * B] = mats[1]
    hat[B:, B:] = mats[2]


def forward_rows(base_sum, tan_sum, layer, win, bias, wout, slope, with_base):
    both = stack(base_sum.astype(BF), tan_sum.astype(BF))
    half = base_sum.shape[0]
    for h in range(HID // HC):
        cols = slice(h * HC, (h + 1) * HC)
        z = dot(both, win[:, cols])
        act = z[:half] + bias[layer : layer + 1, cols]
        phi = 0.5 * (1.0 + lax.erf(act * HALF_ROOT))
        slp = phi + act * jnp.exp(-0.5 * act * act) * DENSITY_NORM
        slope[:, cols] = slp.astype(BF)
        lifted = (slp * z[half:]).astype(BF)
        tan_sum = tan_sum + dot(lifted, wout[cols, :])
        if with_base:
            base_sum = base_sum + dot((act * phi).astype(BF), wout[cols, :])
    return base_sum, tan_sum


def adjoint_rows(current, win, wout, slope):
    narrow = current.astype(BF)
    for h in range(HID // HC):
        cols = slice(h * HC, (h + 1) * HC)
        up = dot(narrow, wout[cols, :], 1, 1)
        pulled = (slope[:, cols].astype(F32) * up).astype(BF)
        current = current + dot(pulled, win[:, cols], 1, 1)
    return current


def inner0_kernel(
    r0, r1, r2, r3, a0, a1, a2, a3, win, bias, wout,
    field, amat, tmat, base_out, tan_out, slope, hat,
):
    y = member()
    sort_edges(y, (a0, a1, a2, a3), 0, amat, tmat)
    pair_matrix(amat, hat)
    for k, r in enumerate((r0, r1, r2, r3)):
        block = origin(y, k)
        rows = pl.ds(pl.multiple_of(block * B, B), B)
        for w in range(NW):
            field[w, rows, 0:D] = r[w, 0]
            field[w, rows, D:] = r[w, 1]
    for w in range(NW):
        agg = dot(hat[...], field[w])
        base_sum = field[w, B : 3 * B, 0:D].astype(F32) + agg[:, 0:D]
        tan_sum = field[w, B : 3 * B, D:].astype(F32) + agg[:, D:]
        base, tan = forward_rows(base_sum, tan_sum, 0, win, bias, wout, slope.at[w], True)
        base_out[w] = base.astype(BF)
        tan_out[w] = tan


def edge0_kernel(
    field, amat, left, right, win, bias, wout,
    send_left, send_right, tan_out, slope,
):
    for w in range(NW):
        lo = stack(jnp.concatenate([left[w, 0], left[w, 1]], axis=1), field[w, 0 : 2 * B])
        hi = stack(field[w, 2 * B :], jnp.concatenate([right[w, 0], right[w, 1]], axis=1))
        agg = stack(dot(amat[0], lo), dot(amat[G - 1], hi))
        own = stack(field[w, 0:B], field[w, 3 * B :]).astype(F32)
        base, tan = forward_rows(
            own[:, 0:D] + agg[:, 0:D], own[:, D:] + agg[:, D:], 0, win, bias, wout, slope.at[w], True
        )
        tan_out[w] = tan
        base, tan = base.astype(BF), tan.astype(BF)
        send_left[w, 0] = base[0:B]
        send_left[w, 1] = tan[0:B]
        send_right[w, 0] = base[B:]
        send_right[w, 1] = tan[B:]


def inner1_kernel(
    base_in, tan_in, lo, hi, field, e0, e0r, e1, e2, e3, win, bias, wout,
    amat, tmat, next_out, image, returned, hat, slope, nxt,
):
    y = member()
    sort_edges(y, (e0, e1, e2, e3), 3 * B, amat, tmat)
    pair_matrix(amat, hat)
    for k, e in enumerate((e0, e1, e2, e3)):
        value = e[:, 6 * B :]
        if k == 0:
            value = jnp.where(y == G - 1, e0r[...], value)
        nxt[origin(y, k)] = value
    next_out[0:B] = nxt[0]
    next_out[B:] = nxt[G - 1]
    for w in range(NW):
        base = stack(lo[w, 0], base_in[w], hi[w, 0])
        tan = stack(lo[w, 1], tan_in[w].astype(BF), hi[w, 1])
        base_sum = base_in[w].astype(F32) + dot(hat[...], base)
        tan_sum = tan_in[w] + dot(hat[...], tan)
        _, out = forward_rows(base_sum, tan_sum, 1, win, bias, wout, slope, False)
        image[w] = out.astype(BF)
        if w == 0:
            following = field[1, B : 3 * B, D:].astype(F32)
            current = following - out
        else:
            following = stack(nxt[1], nxt[2]).astype(F32)
            current = jnp.where(last_member(), 0.0, following - out)
        returned[w] = adjoint_rows(current, win, wout, slope)


def edge1_kernel(
    lo, hi, tan_edge, base_in, tan_in, left, right, field, next_edge, amat, tmat, image_in, win, bias, wout,
    im0, im1, im2, im3, returned, send_left, send_right, slope, image,
):
    y = member()
    for w in range(NW):
        tan_mid = tan_in[w].astype(BF)
        agg = []
        for f, mid in ((0, base_in[w]), (1, tan_mid)):
            agg.append(stack(
                dot(amat[0], stack(left[w, f], lo[w, f], mid[0:B])),
                dot(amat[G - 1], stack(mid[B:], hi[w, f], right[w, f])),
            ))
        base_sum = stack(lo[w, 0], hi[w, 0]).astype(F32) + agg[0]
        _, out = forward_rows(base_sum, tan_edge[w] + agg[1], 1, win, bias, wout, slope, False)
        image[0, w] = out[0:B].astype(BF)
        image[1, w] = image_in[w, 0:B]
        image[2, w] = image_in[w, B:]
        image[3, w] = out[B:].astype(BF)
        if w == 0:
            following = stack(field[1, 0:B, D:], field[1, 3 * B :, D:]).astype(F32)
            current = following - out
        else:
            current = jnp.where(last_member(), 0.0, next_edge[...].astype(F32) - out)
        back = adjoint_rows(current, win, wout, slope)
        returned[w] = back
        send_left[w] = dot(tmat[0, :, 0:B], back[0:B].astype(BF)).astype(BF)
        send_right[w] = dot(tmat[G - 1, :, 2 * B :], back[B:].astype(BF)).astype(BF)
    for k, im in enumerate((im0, im1, im2, im3)):
        im[...] = image[lax.rem(y + k, G)]


def spread_edge(tmat, edge, narrow):
    return edge + stack(
        dot(tmat[0, :, B:], narrow[0 : 2 * B]), dot(tmat[G - 1, :, 0 : 2 * B], narrow[2 * B :])
    )


def inner2_kernel(inner, edge, tmat, slope, win, wout, cur_edge, returned, hat):
    pair_matrix(tmat, hat)
    for w in range(NW):
        narrow = stack(edge[w, 0:B], inner[w], edge[w, B:]).astype(BF)
        cur_edge[w] = spread_edge(tmat, edge[w], narrow)
        current = inner[w] + dot(hat[...], narrow)
        returned[w] = adjoint_rows(current, win, wout, slope.at[w])


def edge2_kernel(cur_edge, left, right, tmat, slope, win, wout, returned, send_left, send_right):
    for w in range(NW):
        current = cur_edge[w] + stack(left[w], right[w]).astype(F32)
        back = adjoint_rows(current, win, wout, slope.at[w])
        returned[w] = back
        send_left[w] = dot(tmat[0, :, 0:B], back[0:B].astype(BF)).astype(BF)
        send_right[w] = dot(tmat[G - 1, :, 2 * B :], back[B:].astype(BF)).astype(BF)


def inner3_kernel(inner, edge, tmat, i0, i1, i2, i3, cur_edge, cur_inner, last, hat):
    y = member()
    for k, im in enumerate((i0, i1, i2, i3)):

        @pl.when(origin(y, k) == G - 1)
        def _():
            last[...] = im[NW - 1]

    pair_matrix(tmat, hat)
    for w in range(NW):
        narrow = stack(edge[w, 0:B], inner[w], edge[w, B:]).astype(BF)
        cur_edge[w] = spread_edge(tmat, edge[w], narrow)
        cur_inner[w] = (inner[w] + dot(hat[...], narrow)).astype(BF)


def finish_kernel(cur_edge, cur_inner, left, right, o0, o1, o2, o3, all_blocks):
    y = member()
    for w in range(NW):
        all_blocks[0, w] = (cur_edge[w, 0:B] + left[w].astype(F32)).astype(BF)
        all_blocks[1, w] = cur_inner[w, 0:B]
        all_blocks[2, w] = cur_inner[w, B:]
        all_blocks[3, w] = (cur_edge[w, B:] + right[w].astype(F32)).astype(BF)
    for k, out in enumerate((o0, o1, o2, o3)):
        out[...] = all_blocks[lax.rem(y + k, G)]


def misfit_kernel(inc, i0, i1, i2, i3, before, misfit):
    y = member()
    for k, im in enumerate((i0, i1, i2, i3)):
        m = origin(y, k)
        misfit[NW * m + 1] = inc[NW * m + 1] - im[0].astype(F32)
        even = NW * lax.rem(m + 1, G)
        image = jnp.where(m == G - 1, before[...], im[1])
        misfit[even] = inc[even] - image.astype(F32)


def normal_kernel(misfit, p0, p1, p2, p3, normal):
    y = member()
    for k, part in enumerate((p0, p1, p2, p3)):
        m = origin(y, k)
        for w in range(NW):
            normal[NW * m + w] = misfit[NW * m + w] - part[w].astype(F32)


SMEM = pl.BlockSpec(memory_space=pltpu.SMEM)
VMEM = pl.BlockSpec(memory_space=pltpu.VMEM)


def sds(shape, dtype=BF):
    return jax.ShapeDtypeStruct(shape, dtype)


def call(kernel, ins, outs, scratch=(), smem=0, layer=0, weights=()):
    specs = [SMEM] * smem + [VMEM] * (len(ins) - smem)
    for position in weights:
        shape = ins[position].shape
        specs[position] = pl.BlockSpec((None,) + shape[1:], lambda i: (layer, 0, 0))
    return pl.pallas_call(
        kernel,
        grid=(1,),
        out_shape=outs,
        in_specs=specs,
        out_specs=[VMEM] * len(outs),
        scratch_shapes=list(scratch),
        compiler_params=pltpu.CompilerParams(vmem_limit_bytes=60 * 1024 * 1024),
    )(*ins)


def group_pairs(k):
    return [(b, b // G * G + (b + k) % G) for b in range(PARTS)]


def side_pairs(d):
    return [(b, (b + G * d) % PARTS) for b in range(PARTS)]


def next_increment_pairs(k):
    pairs = []
    for t in range(TM):
        for b in range(PARTS):
            m = (b + k) % G
            if k == 0 and m != G - 1:
                continue
            to = (t - 1) % TM if m == G - 1 else t
            pairs.append((t * PARTS + b, to * PARTS + b // G * G + m))
    return pairs


def to_members(sends):
    return [lax.ppermute(sends[k], "mesh", group_pairs(k)) for k in range(1, G)]


def swap_sides(send_left, send_right):
    left = lax.ppermute(send_right, "mesh", side_pairs(1))
    right = lax.ppermute(send_left, "mesh", side_pairs(-1))
    return left, right


def local(states, increment, window_slots, edge_weights, inner_weight, inner_bias, outer_weight):
    bias = inner_bias

    item = sds((NW, 2, B, D))
    half = sds((NW, B, D))
    pair_bf = sds((NW, 2 * B, D))
    pair = sds((NW, 2 * B, D), F32)
    hidden = sds((NW, 2 * B, HID))
    mats = sds((G, B, 3 * B))
    hat = pltpu.VMEM((2 * B, 4 * B), BF)

    sends = call(pack_kernel, (states, increment), [item] * (G - 1))
    got = [None, *to_members([None, *sends])]
    got[0], cross, *ext = call(
        fold_kernel, (window_slots, states, increment, edge_weights),
        [item, sds((B, D))] + [sds((B, 6 * B + D))] * G, smem=1,
    )
    cross = lax.ppermute(cross, ("tm", "mesh"), next_increment_pairs(0))
    ext = [ext[0]] + [lax.ppermute(ext[k], ("tm", "mesh"), next_increment_pairs(k)) for k in range(1, G)]

    lo, hi = call(edge_kernel, got, [item, item])
    left, right = swap_sides(lo, hi)
    field, amat0, tmat0, base_in, tan_in, slope_in = call(
        inner0_kernel, (*got, *ext, inner_weight, bias, outer_weight),
        [sds((NW, G * B, 2 * D)), mats, mats, pair_bf, pair, hidden], (hat,), weights=(8, 10),
    )
    lo, hi, tan_edge, slope_edge = call(
        edge0_kernel, (field, amat0, left, right, inner_weight, bias, outer_weight),
        [item, item, pair, hidden], weights=(4, 6),
    )

    left, right = swap_sides(lo, hi)
    slope1 = pltpu.VMEM((2 * B, HID), BF)
    amat1, tmat1, next_edge, image_in, inner = call(
        inner1_kernel,
        (base_in, tan_in, lo, hi, field, ext[0], cross, *ext[1:], inner_weight, bias, outer_weight),
        [mats, mats, sds((2 * B, D)), pair_bf, pair],
        (hat, slope1, pltpu.VMEM((G, B, D), BF)), layer=1, weights=(10, 12),
    )
    *images, edge, send_left, send_right = call(
        edge1_kernel,
        (lo, hi, tan_edge, base_in, tan_in, left, right, field, next_edge, amat1, tmat1, image_in,
         inner_weight, bias, outer_weight),
        [half] * G + [pair, half, half],
        (slope1, pltpu.VMEM((G, NW, B, D), BF)), layer=1, weights=(12, 14),
    )

    left, right = swap_sides(send_left, send_right)
    images = [images[0], *to_members(images)]
    cur_edge, inner = call(
        inner2_kernel, (inner, edge, tmat1, slope_in, inner_weight, outer_weight),
        [pair, pair], (hat,), weights=(4, 5),
    )
    edge, send_left, send_right = call(
        edge2_kernel, (cur_edge, left, right, tmat0, slope_edge, inner_weight, outer_weight),
        [pair, half, half], weights=(5, 6),
    )

    left, right = swap_sides(send_left, send_right)
    cur_edge, cur_inner, last = call(
        inner3_kernel, (inner, edge, tmat0, *images), [pair, pair_bf, sds((B, D))], (hat,),
    )
    before = lax.ppermute(last, "tm", [(t, t + 1) for t in range(TM - 1)])
    parts = call(
        finish_kernel, (cur_edge, cur_inner, left, right), [half] * G,
        (pltpu.VMEM((G, NW, B, D), BF),),
    )
    parts = [parts[0], *to_members(parts)]
    whole = sds(increment.shape, F32)
    (misfit,) = call(misfit_kernel, (increment, *images, before), [whole])
    (normal,) = call(normal_kernel, (misfit, *parts), [whole])
    return misfit, normal


def solution(mesh):
    placed = (
        P("tm", "mesh", None),
        P("tm", "mesh", None),
        P("mesh", None),
        P(None, "mesh", None, None, None),
        P(),
        P(),
        P(),
    )

    return jax.shard_map(
        local,
        mesh=mesh,
        in_specs=placed,
        out_specs=(P("tm", "mesh", None), P("tm", "mesh", None)),
        check_vma=False,
    )
```

time: 150 us -> 135 us (0.900)
  Pallas kernels: 66.4 us -> 47.6 us
  starting transfers between devices: 50.9 us -> 55.8 us
    pallas_call x14 -> x13, Pallas kernels: 66.4 us -> 47.6 us  [call(): pl.pallas_call(kernel, grid=(1,), out_shape=outs, in_specs=specs, out_spe...]
    ppermute x4 -> x3, waiting for transfers between devices: 7.2 us -> 0.01 us  [local(): lax.ppermute(ext[k], ('tm', 'mesh'), next_increment_pairs(k))]
    ppermute x4, waiting for transfers between devices: 0.12 us -> 6.92 us  [swap_sides(): left = lax.ppermute(send_right, 'mesh', side_pairs(1))]
    ppermute x4, waiting for transfers between devices: 0.56 us -> 5.38 us  [swap_sides(): right = lax.ppermute(send_left, 'mesh', side_pairs(-1))]
    ppermute x12 -> x10, waiting for transfers between devices: 13.2 us -> 8.88 us  [the longest x9 8.88 us: to_members(): return [lax.ppermute(sends[k], 'mesh', group_pairs(k)) for k in range(1, G)]]
    ppermute x4, starting transfers between devices: 22.7 us -> 24.7 us  [swap_sides(): right = lax.ppermute(send_left, 'mesh', side_pairs(-1))]
    ppermute x12 -> x10, starting transfers between devices: 17.6 us -> 19.4 us  [the longest x9 18.8 us: to_members(): return [lax.ppermute(sends[k], 'mesh', group_pairs(k)) for k in range(1, G)]]
    ppermute x4 -> x3, starting transfers between devices: 5.48 us -> 5.8 us  [local(): lax.ppermute(ext[k], ('tm', 'mesh'), next_increment_pairs(k))]
  transfers between devices with their start and end apart: 25 -> 22, of which waited for: 9 -> 8; matrix products, arithmetic and copies ran while one was open for 0% -> 0% of each run, Pallas kernels for 22% -> 22%
where the time goes in v2:
time: 135 us; the launch traced here: 134 us
  starting transfers between devices  55.8 us (41%)
  Pallas kernels  47.6 us (35%)
  waiting for transfers between devices  22.5 us (17%)
  local copies, waits for them, and re-layouts  7.09 us (5%)
    pallas_call x13, Pallas kernels, call(): pl.pallas_call(kernel, grid=(1,), out_shape=outs, in_specs=specs, out_spe...  47.6 us
    ppermute x4, starting transfers between devices, swap_sides(): right = lax.ppermute(send_left, 'mesh', side_pairs(-1))  24.7 us
    ppermute x9, starting transfers between devices, to_members(): return [lax.ppermute(sends[k], 'mesh', group_pairs(k)) for k in range(1, G)]  18.8 us
    ppermute x9, waiting for transfers between devices, to_members(): return [lax.ppermute(sends[k], 'mesh', group_pairs(k)) for k in range(1, G)]  8.88 us
    unnamed x48, local copies, waits for them, and re-layouts  7.09 us
    ppermute x4, waiting for transfers between devices, swap_sides(): left = lax.ppermute(send_right, 'mesh', side_pairs(1))  6.92 us
    ppermute x3, starting transfers between devices, local(): lax.ppermute(ext[k], ('tm', 'mesh'), next_increment_pairs(k))  5.8 us
    ppermute x4, waiting for transfers between devices, swap_sides(): right = lax.ppermute(send_left, 'mesh', side_pairs(-1))  5.38 us
  transfers between devices with their start and end apart: 22, of which 8 were waited for; matrix products, arithmetic and copies ran while one was open for 0% of the time, Pallas kernels for 22%

profile of v2, /device:TPU:1, one launch (start us, length us, event | category | flops | bytes accessed | tf_op | source)
XLA Modules:
  0.0 133.8 jit_solution(2359314773350148215)
XLA Ops:
  0.6 2.3 %shard_map.87 = (bf16[2,2,128,256]{3,2,1,0:T(8,128)(2,1)}, bf16[2,2,128,256]{3,2,1,0:T(8,128)(2,1)}, bf16[2,2,128,256]{3,2,1,0:T(8,128)(2,1)}) custom-call(bf16[8,128,256]{2,1,0:T(8,128)(2,1)} %states.3, f32[8,128,256]{2,1,0:T(8,128)} %inc.5), custom_call_target="tpu_custom_call" | custom-call | tf_op jit(solution)/shard_map/pallas_call | solution.py:320
  3.0 2.1 %collective-permute-start = (bf16[2,2,128,256]{3,2,1,0:T(8,128)(2,1)}, bf16[2,2,128,256]{3,2,1,0:T(8,128)(2,1)S(1)}, u32[]{:S(2)}, u32[]{:S(2)}) collective-permute-start(bf16[2,2,128,256]{3,2,1,0:T(8,128)(2,1)} %get-tuple-element.48), channel_id=1, source_target_pairs={{0,1},{1,2},{2,3},{3,0},{4,5},{5,6},{6,7},{7,4},{8,9},{9,10},{10,1... | collective-permute-start | bytes 786440 | tf_op jit(solution)/shard_map/ppermute | solution.py:352
  5.1 2.6 %collective-permute-start.1 = (bf16[2,2,128,256]{3,2,1,0:T(8,128)(2,1)}, bf16[2,2,128,256]{3,2,1,0:T(8,128)(2,1)S(1)}, u32[]{:S(2)}, u32[]{:S(2)}) collective-permute-start(bf16[2,2,128,256]{3,2,1,0:T(8,128)(2,1)} %get-tuple-element.49), channel_id=1, source_target_pairs={{0,2},{1,3},{2,0},{3,1},{4,6},{5,7},{6,4},{7,5},{8,10},{9,11},{10,... | collective-permute-start | bytes 786440 | tf_op jit(solution)/shard_map/ppermute | solution.py:352
  8.8 2.7 %shard_map.86 = (bf16[2,2,128,256]{3,2,1,0:T(8,128)(2,1)}, bf16[128,256]{1,0:T(8,128)(2,1)}, bf16[128,1024]{1,0:T(8,128)(2,1)}, bf16[128,1024]{1,0:T(8,128)(2,1)...) custom-call(s32[1,4]{1,0:T(1,128)} %slots.1, bf16[8,128,256]{2,1,0:T(8,128)(2,1)} %states.3, f32[8,128,256]{2,1,0:T(8,128)} %inc.5, ...), custom_call_target="tpu_custom_call" | custom-call | tf_op jit(solution)/shard_map/pallas_call | solution.py:320
  11.9 1.9 %collective-permute-start.4 = (bf16[128,1024]{1,0:T(8,128)(2,1)}, bf16[128,1024]{1,0:T(8,128)(2,1)S(1)}, u32[]{:S(2)}, u32[]{:S(2)}) collective-permute-start(bf16[128,1024]{1,0:T(8,128)(2,1)} %get-tuple-element.53), channel_id=1, source_target_pairs={{0,2},{1,195},{2,0},{3,1},{4,6},{5,199},{6,4},{7,5},{8,10},{9,203}... | collective-permute-start | bytes 786440 | tf_op jit(solution)/shard_map/ppermute | solution.py:379
  13.8 3.5 %collective-permute-start.5 = (bf16[128,1024]{1,0:T(8,128)(2,1)}, bf16[128,1024]{1,0:T(8,128)(2,1)S(1)}, u32[]{:S(2)}, u32[]{:S(2)}) collective-permute-start(bf16[128,1024]{1,0:T(8,128)(2,1)} %get-tuple-element.54), channel_id=1, source_target_pairs={{0,195},{1,0},{2,1},{3,2},{4,199},{5,4},{6,5},{7,6},{8,203},{9,8},... | collective-permute-start | bytes 786440 | tf_op jit(solution)/shard_map/ppermute | solution.py:379
  17.3 4.8 %collective-permute-done.1.r2 = bf16[2,2,128,256]{3,2,1,0:T(8,128)(2,1)S(1)} collective-permute-done((bf16[2,2,128,256]{3,2,1,0:T(8,128)(2,1)}, bf16[2,2,128,256]{3,2,1,0:T(8,128)(2,1)S(1)}, u32[]{:S(2)}, u32[]{:S(2)}) %collective-permute-start.1) | collective-permute-done | bytes 262176 | tf_op jit(solution)/shard_map/ppermute | solution.py:352
  22.1 4.1 %collective-permute-done.2.r3 = bf16[2,2,128,256]{3,2,1,0:T(8,128)(2,1)S(1)} collective-permute-done((bf16[2,2,128,256]{3,2,1,0:T(8,128)(2,1)}, bf16[2,2,128,256]{3,2,1,0:T(8,128)(2,1)S(1)}, u32[]{:S(2)}, u32[]{:S(2)}) %collective-permute-start.2) | collective-permute-done | bytes 262176 | tf_op jit(solution)/shard_map/ppermute | solution.py:352
  26.9 2.1 %shard_map.89 = (bf16[2,2,128,256]{3,2,1,0:T(8,128)(2,1)}, bf16[2,2,128,256]{3,2,1,0:T(8,128)(2,1)}) custom-call(bf16[2,2,128,256]{3,2,1,0:T(8,128)(2,1)} %get-tuple-element.47.r0, bf16[2,2,128,256]{3,2,1,0:T(8,128)(2,1)} %copy-done.3, bf16[2,2,128,256]{3,2,1,0:T(8,128)(2,1)} %copy-done.4, bf16[2,2,128,256]{3,2,1,0:T(8,128)(2,1)} %copy-done.5), custom_call_target="tpu_custom_call" | custom-call | tf_op jit(solution)/shard_map/pallas_call | solution.py:320
  28.9 2.1 %collective-permute-start.6 = (bf16[2,2,128,256]{3,2,1,0:T(8,128)(2,1)}, bf16[2,2,128,256]{3,2,1,0:T(8,128)(2,1)S(1)}, u32[]{:S(2)}, u32[]{:S(2)}) collective-permute-start(bf16[2,2,128,256]{3,2,1,0:T(8,128)(2,1)} %get-tuple-element.57), channel_id=1, source_target_pairs={{0,4},{1,5},{2,6},{3,7},{4,8},{5,9},{6,10},{7,11},{8,12},{9,13},{1... | collective-permute-start | bytes 786440 | tf_op jit(solution)/shard_map/ppermute | solution.py:356
  31.0 7.0 %collective-permute-start.7 = (bf16[2,2,128,256]{3,2,1,0:T(8,128)(2,1)}, bf16[2,2,128,256]{3,2,1,0:T(8,128)(2,1)S(1)}, u32[]{:S(2)}, u32[]{:S(2)}) collective-permute-start(bf16[2,2,128,256]{3,2,1,0:T(8,128)(2,1)} %get-tuple-element.58), channel_id=1, source_target_pairs={{0,60},{1,61},{2,62},{3,63},{4,0},{5,1},{6,2},{7,3},{8,4},{9,5},{1... | collective-permute-start | bytes 786440 | tf_op jit(solution)/shard_map/ppermute | solution.py:357
  38.9 5.2 %shard_map.88 = (bf16[2,512,512]{2,1,0:T(8,128)(2,1)}, bf16[4,128,384]{2,1,0:T(8,128)(2,1)}, bf16[4,128,384]{2,1,0:T(8,128)(2,1)}, bf16[2,256,256]{2,1,0:T(8,128...) custom-call(bf16[2,2,128,256]{3,2,1,0:T(8,128)(2,1)} %get-tuple-element.47.r0, ...), custom_call_target="tpu_custom_call" | custom-call | tf_op jit(solution)/shard_map/pallas_call | solution.py:320
  44.1 1.7 %collective-permute-done.6.left = bf16[2,2,128,256]{3,2,1,0:T(8,128)(2,1)S(1)} collective-permute-done((bf16[2,2,128,256]{3,2,1,0:T(8,128)(2,1)}, bf16[2,2,128,256]{3,2,1,0:T(8,128)(2,1)S(1)}, u32[]{:S(2)}, u32[]{:S(2)}) %collective-permute-start.6) | collective-permute-done | bytes 262176 | tf_op jit(solution)/shard_map/ppermute | solution.py:356
  45.8 3.7 %collective-permute-done.7.right = bf16[2,2,128,256]{3,2,1,0:T(8,128)(2,1)S(1)} collective-permute-done((bf16[2,2,128,256]{3,2,1,0:T(8,128)(2,1)}, bf16[2,2,128,256]{3,2,1,0:T(8,128)(2,1)S(1)}, u32[]{:S(2)}, u32[]{:S(2)}) %collective-permute-start.7) | collective-permute-done | bytes 262176 | tf_op jit(solution)/shard_map/ppermute | solution.py:357
  50.2 4.9 %shard_map.90 = (bf16[2,2,128,256]{3,2,1,0:T(8,128)(2,1)}, bf16[2,2,128,256]{3,2,1,0:T(8,128)(2,1)}, f32[2,256,256]{2,1,0:T(8,128)}, bf16[2,256,1024]{2,1,0:T(8,128)(2,1)}) custom-call(bf16[2,512,512]{2,1,0:T(8,128)(2,1)} %get-tuple-element.55.field, bf16[4,128,384]{2,1,0:T(8,128)(2,1)} %get-tuple-element.56.amat, bf16[2,2,128,256]{3,2,1,0:T(8,128)(2,1)} %copy-done.10, ...), custom_call_target="tpu_custom_call" | custom-call | tf_op jit(solution)/shard_map/pallas_call | solution.py:320
  55.2 6.3 %collective-permute-start.9 = (bf16[2,2,128,256]{3,2,1,0:T(8,128)(2,1)}, bf16[2,2,128,256]{3,2,1,0:T(8,128)(2,1)S(1)}, u32[]{:S(2)}, u32[]{:S(2)}) collective-permute-start(bf16[2,2,128,256]{3,2,1,0:T(8,128)(2,1)} %get-tuple-element.59.lo), channel_id=1, source_target_pairs={{0,60},{1,61},{2,62},{3,63},{4,0},{5,1},{6,2},{7,3},{8,4},{9,5},{1... | collective-permute-start | bytes 786440 | tf_op jit(solution)/shard_map/ppermute | solution.py:357
  62.8 6.1 %shard_map.91 = (bf16[4,128,384]{2,1,0:T(8,128)(2,1)}, bf16[4,128,384]{2,1,0:T(8,128)(2,1)}, bf16[256,256]{1,0:T(8,128)(2,1)}, bf16[2,256,256]{2,1,0:T(8,128)(2,1)}, f32[2,256,256]{2,1,0:T(8,128)}) custom-call(bf16[2,256,256]{2,1,0:T(8,128)(2,1)} %get-tuple-element.62.base_in, f32[2,256,256]{2,1,0:T(8,128)} %get-tuple-element.63.tan_in, ...), custom_call_target="tpu_custom_call" | custom-call | tf_op jit(solution)/shard_map/pallas_call | solution.py:320
  68.9 4.0 %collective-permute-done.8.left = bf16[2,2,128,256]{3,2,1,0:T(8,128)(2,1)S(1)} collective-permute-done((bf16[2,2,128,256]{3,2,1,0:T(8,128)(2,1)}, bf16[2,2,128,256]{3,2,1,0:T(8,128)(2,1)S(1)}, u32[]{:S(2)}, u32[]{:S(2)}) %collective-permute-start.8) | collective-permute-done | bytes 262176 | tf_op jit(solution)/shard_map/ppermute | solution.py:356
  73.7 6.6 %shard_map.92 = (bf16[2,128,256]{2,1,0:T(8,128)(2,1)}, bf16[2,128,256]{2,1,0:T(8,128)(2,1)}, bf16[2,128,256]{2,1,0:T(8,128)(2,1)}, bf16[2,128,256]{2,1,0:T(8,128...) custom-call(bf16[2,2,128,256]{3,2,1,0:T(8,128)(2,1)} %get-tuple-element.59.lo, ...), custom_call_target="tpu_custom_call" | custom-call | tf_op jit(solution)/shard_map/pallas_call | solution.py:320
  80.2 5.7 %collective-permute-start.15 = (bf16[2,128,256]{2,1,0:T(8,128)(2,1)}, bf16[2,128,256]{2,1,0:T(8,128)(2,1)S(1)}, u32[]{:S(2)}, u32[]{:S(2)}) collective-permute-start(bf16[2,128,256]{2,1,0:T(8,128)(2,1)} %get-tuple-element.79), channel_id=1, source_target_pairs={{0,60},{1,61},{2,62},{3,63},{4,0},{5,1},{6,2},{7,3},{8,4},{9,5},{1... | collective-permute-start | bytes 393224 | tf_op jit(solution)/shard_map/ppermute | solution.py:357
  85.9 9.1 %collective-permute-start.12 = (bf16[2,128,256]{2,1,0:T(8,128)(2,1)}, bf16[2,128,256]{2,1,0:T(8,128)(2,1)S(1)}, u32[]{:S(2)}, u32[]{:S(2)}) collective-permute-start(bf16[2,128,256]{2,1,0:T(8,128)(2,1)} %get-tuple-element.71), channel_id=1, source_target_pairs={{0,2},{1,3},{2,0},{3,1},{4,6},{5,7},{6,4},{7,5},{8,10},{9,11},{10,... | collective-permute-start | bytes 393224 | tf_op jit(solution)/shard_map/ppermute | solution.py:352
  95.0 4.1 %shard_map.93 = (f32[2,256,256]{2,1,0:T(8,128)}, f32[2,256,256]{2,1,0:T(8,128)}) custom-call(f32[2,256,256]{2,1,0:T(8,128)} %get-tuple-element.73.inner, f32[2,256,256]{2,1,0:T(8,128)} %get-tuple-element.74.edge, bf16[4,128,384]{2,1,0:T(8,128)(2,1)} %get-tuple-element.67.tmat, bf16[2,256,1024]{2,1,0:T(8,128)(2,1)} %get-tuple-element.75.slope, ...), custom_call_target="tpu_custom_call" | custom-call | tf_op jit(solution)/shard_map/pallas_call | solution.py:320
  99.9 3.9 %shard_map.94 = (f32[2,256,256]{2,1,0:T(8,128)}, bf16[2,128,256]{2,1,0:T(8,128)(2,1)}, bf16[2,128,256]{2,1,0:T(8,128)(2,1)}) custom-call(f32[2,256,256]{2,1,0:T(8,128)} %get-tuple-element.77.cur_edge, bf16[2,128,256]{2,1,0:T(8,128)(2,1)} %copy-done.13, bf16[2,128,256]{2,1,0:T(8,128)(2,1)} %copy-done.15, bf16[4,128,384]{2,1,0:T(8,128)(2,1)} %get-tuple-element.80.tmat, ...), custom_call_target="tpu_custom_call" | custom-call | tf_op jit(solution)/shard_map/pallas_call | solution.py:320
  103.8 5.7 %collective-permute-start.18 = (bf16[2,128,256]{2,1,0:T(8,128)(2,1)}, bf16[2,128,256]{2,1,0:T(8,128)(2,1)S(1)}, u32[]{:S(2)}, u32[]{:S(2)}) collective-permute-start(bf16[2,128,256]{2,1,0:T(8,128)(2,1)} %get-tuple-element.87), channel_id=1, source_target_pairs={{0,60},{1,61},{2,62},{3,63},{4,0},{5,1},{6,2},{7,3},{8,4},{9,5},{1... | collective-permute-start | bytes 393224 | tf_op jit(solution)/shard_map/ppermute | solution.py:357
  110.3 2.6 %shard_map.95 = (f32[2,256,256]{2,1,0:T(8,128)}, bf16[2,256,256]{2,1,0:T(8,128)(2,1)}, bf16[128,256]{1,0:T(8,128)(2,1)}) custom-call(f32[2,256,256]{2,1,0:T(8,128)} %get-tuple-element.76.inner, f32[2,256,256]{2,1,0:T(8,128)} %get-tuple-element.82.edge, bf16[4,128,384]{2,1,0:T(8,128)(2,1)} %get-tuple-element.80.tmat, ...), custom_call_target="tpu_custom_call" | custom-call | tf_op jit(solution)/shard_map/pallas_call | solution.py:320
  114.0 1.6 %collective-permute-done.18.right = bf16[2,128,256]{2,1,0:T(8,128)(2,1)S(1)} collective-permute-done((bf16[2,128,256]{2,1,0:T(8,128)(2,1)}, bf16[2,128,256]{2,1,0:T(8,128)(2,1)S(1)}, u32[]{:S(2)}, u32[]{:S(2)}) %collective-permute-start.18) | collective-permute-done | bytes 131104 | tf_op jit(solution)/shard_map/ppermute | solution.py:357
  116.3 2.1 %shard_map.97 = (bf16[2,128,256]{2,1,0:T(8,128)(2,1)}, bf16[2,128,256]{2,1,0:T(8,128)(2,1)}, bf16[2,128,256]{2,1,0:T(8,128)(2,1)}, bf16[2,128,256]{2,1,0:T(8,128)(2,1)}) custom-call(f32[2,256,256]{2,1,0:T(8,128)} %get-tuple-element.84.cur_edge, bf16[2,256,256]{2,1,0:T(8,128)(2,1)} %get-tuple-element.85.cur_inner, bf16[2,128,256]{2,1,0:T(8,128)(2,1)} %copy-done.18, ...), custom_call_target="tpu_custom_call" | custom-call | tf_op jit(solution)/shard_map/pallas_call | solution.py:320
  118.4 1.4 %collective-permute-start.19 = (bf16[2,128,256]{2,1,0:T(8,128)(2,1)}, bf16[2,128,256]{2,1,0:T(8,128)(2,1)S(1)}, u32[]{:S(2)}, u32[]{:S(2)}) collective-permute-start(bf16[2,128,256]{2,1,0:T(8,128)(2,1)} %get-tuple-element.89), channel_id=1, source_target_pairs={{0,1},{1,2},{2,3},{3,0},{4,5},{5,6},{6,7},{7,4},{8,9},{9,10},{10,1... | collective-permute-start | bytes 393224 | tf_op jit(solution)/shard_map/ppermute | solution.py:352
  120.3 2.0 %collective-permute-start.21 = (bf16[2,128,256]{2,1,0:T(8,128)(2,1)}, bf16[2,128,256]{2,1,0:T(8,128)(2,1)S(1)}, u32[]{:S(2)}, u32[]{:S(2)}) collective-permute-start(bf16[2,128,256]{2,1,0:T(8,128)(2,1)} %get-tuple-element.91), channel_id=1, source_target_pairs={{0,3},{1,0},{2,1},{3,2},{4,7},{5,4},{6,5},{7,6},{8,11},{9,8},{10,9... | collective-permute-start | bytes 393224 | tf_op jit(solution)/shard_map/ppermute | solution.py:352
  122.3 3.9 %collective-permute-start.16 = (bf16[128,256]{1,0:T(8,128)(2,1)S(1)}, bf16[128,256]{1,0:T(8,128)(2,1)S(1)}, u32[]{:S(2)}, u32[]{:S(2)}) collective-permute-start(bf16[128,256]{1,0:T(8,128)(2,1)S(1)} %copy-done.23), channel_id=1, source_target_pairs={{0,64},{64,128},{128,192},{1,65},{65,129},{129,193},{2,66},{66,130... | collective-permute-start | bytes 196616 | tf_op jit(solution)/shard_map/ppermute | solution.py:423
  128.1 2.5 %shard_map.96.misfit = f32[8,128,256]{2,1,0:T(8,128)} custom-call(f32[8,128,256]{2,1,0:T(8,128)} %inc.5, bf16[2,128,256]{2,1,0:T(8,128)(2,1)} %get-tuple-element.69.i0, bf16[2,128,256]{2,1,0:T(8,128)(2,1)} %copy-done.6, bf16[2,128,256]{2,1,0:T(8,128)(2,1)} %copy-done.7, bf16[2,128,256]{2,1,0:T(8,128)(2,1)} %copy-done.8, bf16[128,256]{1,0:T(8,128)(2,1)} %copy-done.21), custom_call_target="tpu_custom_call" | custom-call | tf_op jit(solution)/shard_map/pallas_call | solution.py:320
  131.3 2.5 %shard_map.98 = f32[8,128,256]{2,1,0:T(8,128)} custom-call(f32[8,128,256]{2,1,0:T(8,128)} %shard_map.96.misfit, bf16[2,128,256]{2,1,0:T(8,128)(2,1)} %get-tuple-element.88.p0, bf16[2,128,256]{2,1,0:T(8,128)(2,1)} %copy-done.14, bf16[2,128,256]{2,1,0:T(8,128)(2,1)} %copy-done.16, bf16[2,128,256]{2,1,0:T(8,128)(2,1)} %copy-done.17), custom_call_target="tpu_custom_call" | custom-call | tf_op jit(solution)/shard_map/pallas_call | solution.py:320
  (73 shorter events, 12.1 us)
Async XLA Ops:
  3.0 10.8 %collective-permute-start = (bf16[2,2,128,256]{3,2,1,0:T(8,128)(2,1)}, bf16[2,2,128,256]{3,2,1,0:T(8,128)(2,1)S(1)}, u32[]{:S(2)}, u32[]{:S(2)}) collective-permute-start(bf16[2,2,128,256]{3,2,1,0:T(8,128)(2,1)} %get-tuple-element.48), channel_id=1, source_target_pairs={{0,1},{1,2},{2,3},{3,0},{4,5},{5,6},{6,7},{7,4},{8,9},{9,10},{10,1... | collective-permute-start | bytes 786440 | tf_op jit(solution)/shard_map/ppermute | solution.py:352
  5.1 17.0 %collective-permute-start.1 = (bf16[2,2,128,256]{3,2,1,0:T(8,128)(2,1)}, bf16[2,2,128,256]{3,2,1,0:T(8,128)(2,1)S(1)}, u32[]{:S(2)}, u32[]{:S(2)}) collective-permute-start(bf16[2,2,128,256]{3,2,1,0:T(8,128)(2,1)} %get-tuple-element.49), channel_id=1, source_target_pairs={{0,2},{1,3},{2,0},{3,1},{4,6},{5,7},{6,4},{7,5},{8,10},{9,11},{10,... | collective-permute-start | bytes 786440 | tf_op jit(solution)/shard_map/ppermute | solution.py:352
  7.7 18.5 %collective-permute-start.2 = (bf16[2,2,128,256]{3,2,1,0:T(8,128)(2,1)}, bf16[2,2,128,256]{3,2,1,0:T(8,128)(2,1)S(1)}, u32[]{:S(2)}, u32[]{:S(2)}) collective-permute-start(bf16[2,2,128,256]{3,2,1,0:T(8,128)(2,1)} %get-tuple-element.50), channel_id=1, source_target_pairs={{0,3},{1,0},{2,1},{3,2},{4,7},{5,4},{6,5},{7,6},{8,11},{9,8},{10,9... | collective-permute-start | bytes 786440 | tf_op jit(solution)/shard_map/ppermute | solution.py:352
  11.5 26.5 %collective-permute-start.3 = (bf16[128,1024]{1,0:T(8,128)(2,1)}, bf16[128,1024]{1,0:T(8,128)(2,1)S(1)}, u32[]{:S(2)}, u32[]{:S(2)}) collective-permute-start(bf16[128,1024]{1,0:T(8,128)(2,1)} %get-tuple-element.52), channel_id=1, source_target_pairs={{0,1},{1,2},{2,195},{3,0},{4,5},{5,6},{6,199},{7,4},{8,9},{9,10},{... | collective-permute-start | bytes 786440 | tf_op jit(solution)/shard_map/ppermute | solution.py:379
  11.9 26.1 %collective-permute-start.4 = (bf16[128,1024]{1,0:T(8,128)(2,1)}, bf16[128,1024]{1,0:T(8,128)(2,1)S(1)}, u32[]{:S(2)}, u32[]{:S(2)}) collective-permute-start(bf16[128,1024]{1,0:T(8,128)(2,1)} %get-tuple-element.53), channel_id=1, source_target_pairs={{0,2},{1,195},{2,0},{3,1},{4,6},{5,199},{6,4},{7,5},{8,10},{9,203}... | collective-permute-start | bytes 786440 | tf_op jit(solution)/shard_map/ppermute | solution.py:379
  13.8 12.4 %copy-start.3 = (bf16[2,2,128,256]{3,2,1,0:T(8,128)(2,1)}, bf16[2,2,128,256]{3,2,1,0:T(8,128)(2,1)S(1)}, u32[]{:S(2)}) copy-start(bf16[2,2,128,256]{3,2,1,0:T(8,128)(2,1)S(1)} %collective-permute-done.r1) | copy-start | bytes 786436
  13.8 24.2 %collective-permute-start.5 = (bf16[128,1024]{1,0:T(8,128)(2,1)}, bf16[128,1024]{1,0:T(8,128)(2,1)S(1)}, u32[]{:S(2)}, u32[]{:S(2)}) collective-permute-start(bf16[128,1024]{1,0:T(8,128)(2,1)} %get-tuple-element.54), channel_id=1, source_target_pairs={{0,195},{1,0},{2,1},{3,2},{4,199},{5,4},{6,5},{7,6},{8,203},{9,8},... | collective-permute-start | bytes 786440 | tf_op jit(solution)/shard_map/ppermute | solution.py:379
  22.1 4.1 %copy-start.4 = (bf16[2,2,128,256]{3,2,1,0:T(8,128)(2,1)}, bf16[2,2,128,256]{3,2,1,0:T(8,128)(2,1)S(1)}, u32[]{:S(2)}) copy-start(bf16[2,2,128,256]{3,2,1,0:T(8,128)(2,1)S(1)} %collective-permute-done.1.r2) | copy-start | bytes 786436
  28.9 16.8 %collective-permute-start.6 = (bf16[2,2,128,256]{3,2,1,0:T(8,128)(2,1)}, bf16[2,2,128,256]{3,2,1,0:T(8,128)(2,1)S(1)}, u32[]{:S(2)}, u32[]{:S(2)}) collective-permute-start(bf16[2,2,128,256]{3,2,1,0:T(8,128)(2,1)} %get-tuple-element.57), channel_id=1, source_target_pairs={{0,4},{1,5},{2,6},{3,7},{4,8},{5,9},{6,10},{7,11},{8,12},{9,13},{1... | collective-permute-start | bytes 786440 | tf_op jit(solution)/shard_map/ppermute | solution.py:356
  31.0 18.5 %collective-permute-start.7 = (bf16[2,2,128,256]{3,2,1,0:T(8,128)(2,1)}, bf16[2,2,128,256]{3,2,1,0:T(8,128)(2,1)S(1)}, u32[]{:S(2)}, u32[]{:S(2)}) collective-permute-start(bf16[2,2,128,256]{3,2,1,0:T(8,128)(2,1)} %get-tuple-element.58), channel_id=1, source_target_pairs={{0,60},{1,61},{2,62},{3,63},{4,0},{5,1},{6,2},{7,3},{8,4},{9,5},{1... | collective-permute-start | bytes 786440 | tf_op jit(solution)/shard_map/ppermute | solution.py:357
  38.0 0.8 copy-start.1
  38.0 0.9 copy-start.2
  45.8 3.7 %copy-start.10 = (bf16[2,2,128,256]{3,2,1,0:T(8,128)(2,1)}, bf16[2,2,128,256]{3,2,1,0:T(8,128)(2,1)S(1)}, u32[]{:S(2)}) copy-start(bf16[2,2,128,256]{3,2,1,0:T(8,128)(2,1)S(1)} %collective-permute-done.6.left) | copy-start | bytes 786436
  50.2 11.3 %copy-start.22 = (bf16[128,256]{1,0:T(8,128)(2,1)S(1)}, bf16[128,256]{1,0:T(8,128)(2,1)}, u32[]{:S(2)}) copy-start(bf16[128,256]{1,0:T(8,128)(2,1)} %get-tuple-element.64) | copy-start | bytes 196612
  55.2 13.7 %collective-permute-start.9 = (bf16[2,2,128,256]{3,2,1,0:T(8,128)(2,1)}, bf16[2,2,128,256]{3,2,1,0:T(8,128)(2,1)S(1)}, u32[]{:S(2)}, u32[]{:S(2)}) collective-permute-start(bf16[2,2,128,256]{3,2,1,0:T(8,128)(2,1)} %get-tuple-element.59.lo), channel_id=1, source_target_pairs={{0,60},{1,61},{2,62},{3,63},{4,0},{5,1},{6,2},{7,3},{8,4},{9,5},{1... | collective-permute-start | bytes 786440 | tf_op jit(solution)/shard_map/ppermute | solution.py:357
  61.5 11.5 %collective-permute-start.8 = (bf16[2,2,128,256]{3,2,1,0:T(8,128)(2,1)}, bf16[2,2,128,256]{3,2,1,0:T(8,128)(2,1)S(1)}, u32[]{:S(2)}, u32[]{:S(2)}) collective-permute-start(bf16[2,2,128,256]{3,2,1,0:T(8,128)(2,1)} %get-tuple-element.60.hi), channel_id=1, source_target_pairs={{0,4},{1,5},{2,6},{3,7},{4,8},{5,9},{6,10},{7,11},{8,12},{9,13},{1... | collective-permute-start | bytes 786440 | tf_op jit(solution)/shard_map/ppermute | solution.py:356
  61.5 0.7 collective-permute-start.10
  68.9 4.0 %copy-start.9 = (bf16[2,2,128,256]{3,2,1,0:T(8,128)(2,1)}, bf16[2,2,128,256]{3,2,1,0:T(8,128)(2,1)S(1)}, u32[]{:S(2)}) copy-start(bf16[2,2,128,256]{3,2,1,0:T(8,128)(2,1)S(1)} %collective-permute-done.9.right) | copy-start | bytes 786436
  80.2 18.9 %collective-permute-start.14 = (bf16[2,128,256]{2,1,0:T(8,128)(2,1)}, bf16[2,128,256]{2,1,0:T(8,128)(2,1)S(1)}, u32[]{:S(2)}, u32[]{:S(2)}) collective-permute-start(bf16[2,128,256]{2,1,0:T(8,128)(2,1)} %get-tuple-element.78), channel_id=1, source_target_pairs={{0,4},{1,5},{2,6},{3,7},{4,8},{5,9},{6,10},{7,11},{8,12},{9,13},{1... | collective-permute-start | bytes 393224 | tf_op jit(solution)/shard_map/ppermute | solution.py:356
  80.2 18.9 %collective-permute-start.15 = (bf16[2,128,256]{2,1,0:T(8,128)(2,1)}, bf16[2,128,256]{2,1,0:T(8,128)(2,1)S(1)}, u32[]{:S(2)}, u32[]{:S(2)}) collective-permute-start(bf16[2,128,256]{2,1,0:T(8,128)(2,1)} %get-tuple-element.79), channel_id=1, source_target_pairs={{0,60},{1,61},{2,62},{3,63},{4,0},{5,1},{6,2},{7,3},{8,4},{9,5},{1... | collective-permute-start | bytes 393224 | tf_op jit(solution)/shard_map/ppermute | solution.py:357
  85.9 23.6 %collective-permute-start.11 = (bf16[2,128,256]{2,1,0:T(8,128)(2,1)}, bf16[2,128,256]{2,1,0:T(8,128)(2,1)S(1)}, u32[]{:S(2)}, u32[]{:S(2)}) collective-permute-start(bf16[2,128,256]{2,1,0:T(8,128)(2,1)} %get-tuple-element.70), channel_id=1, source_target_pairs={{0,1},{1,2},{2,3},{3,0},{4,5},{5,6},{6,7},{7,4},{8,9},{9,10},{10,1... | collective-permute-start | bytes 393224 | tf_op jit(solution)/shard_map/ppermute | solution.py:352
  85.9 23.6 %collective-permute-start.12 = (bf16[2,128,256]{2,1,0:T(8,128)(2,1)}, bf16[2,128,256]{2,1,0:T(8,128)(2,1)S(1)}, u32[]{:S(2)}, u32[]{:S(2)}) collective-permute-start(bf16[2,128,256]{2,1,0:T(8,128)(2,1)} %get-tuple-element.71), channel_id=1, source_target_pairs={{0,2},{1,3},{2,0},{3,1},{4,6},{5,7},{6,4},{7,5},{8,10},{9,11},{10,... | collective-permute-start | bytes 393224 | tf_op jit(solution)/shard_map/ppermute | solution.py:352
  95.0 14.5 %collective-permute-start.13 = (bf16[2,128,256]{2,1,0:T(8,128)(2,1)}, bf16[2,128,256]{2,1,0:T(8,128)(2,1)S(1)}, u32[]{:S(2)}, u32[]{:S(2)}) collective-permute-start(bf16[2,128,256]{2,1,0:T(8,128)(2,1)} %get-tuple-element.72), channel_id=1, source_target_pairs={{0,3},{1,0},{2,1},{3,2},{4,7},{5,4},{6,5},{7,6},{8,11},{9,8},{10,9... | collective-permute-start | bytes 393224 | tf_op jit(solution)/shard_map/ppermute | solution.py:352
  103.8 10.2 %collective-permute-start.17 = (bf16[2,128,256]{2,1,0:T(8,128)(2,1)}, bf16[2,128,256]{2,1,0:T(8,128)(2,1)S(1)}, u32[]{:S(2)}, u32[]{:S(2)}) collective-permute-start(bf16[2,128,256]{2,1,0:T(8,128)(2,1)} %get-tuple-element.86), channel_id=1, source_target_pairs={{0,4},{1,5},{2,6},{3,7},{4,8},{5,9},{6,10},{7,11},{8,12},{9,13},{1... | collective-permute-start | bytes 393224 | tf_op jit(solution)/shard_map/ppermute | solution.py:356
  103.8 11.9 %collective-permute-start.18 = (bf16[2,128,256]{2,1,0:T(8,128)(2,1)}, bf16[2,128,256]{2,1,0:T(8,128)(2,1)S(1)}, u32[]{:S(2)}, u32[]{:S(2)}) collective-permute-start(bf16[2,128,256]{2,1,0:T(8,128)(2,1)} %get-tuple-element.87), channel_id=1, source_target_pairs={{0,60},{1,61},{2,62},{3,63},{4,0},{5,1},{6,2},{7,3},{8,4},{9,5},{1... | collective-permute-start | bytes 393224 | tf_op jit(solution)/shard_map/ppermute | solution.py:357
  109.5 0.7 copy-start.8
  114.0 1.6 %copy-start.18 = (bf16[2,128,256]{2,1,0:T(8,128)(2,1)}, bf16[2,128,256]{2,1,0:T(8,128)(2,1)S(1)}, u32[]{:S(2)}) copy-start(bf16[2,128,256]{2,1,0:T(8,128)(2,1)S(1)} %collective-permute-done.17.left) | copy-start | bytes 393220
  116.3 5.9 %copy-start.23 = (bf16[128,256]{1,0:T(8,128)(2,1)S(1)}, bf16[128,256]{1,0:T(8,128)(2,1)}, u32[]{:S(2)}) copy-start(bf16[128,256]{1,0:T(8,128)(2,1)} %get-tuple-element.83) | copy-start | bytes 196612
  118.4 12.1 %collective-permute-start.19 = (bf16[2,128,256]{2,1,0:T(8,128)(2,1)}, bf16[2,128,256]{2,1,0:T(8,128)(2,1)S(1)}, u32[]{:S(2)}, u32[]{:S(2)}) collective-permute-start(bf16[2,128,256]{2,1,0:T(8,128)(2,1)} %get-tuple-element.89), channel_id=1, source_target_pairs={{0,1},{1,2},{2,3},{3,0},{4,5},{5,6},{6,7},{7,4},{8,9},{9,10},{10,1... | collective-permute-start | bytes 393224 | tf_op jit(solution)/shard_map/ppermute | solution.py:352
  119.9 10.7 %collective-permute-start.20 = (bf16[2,128,256]{2,1,0:T(8,128)(2,1)}, bf16[2,128,256]{2,1,0:T(8,128)(2,1)S(1)}, u32[]{:S(2)}, u32[]{:S(2)}) collective-permute-start(bf16[2,128,256]{2,1,0:T(8,128)(2,1)} %get-tuple-element.90), channel_id=1, source_target_pairs={{0,2},{1,3},{2,0},{3,1},{4,6},{5,7},{6,4},{7,5},{8,10},{9,11},{10,... | collective-permute-start | bytes 393224 | tf_op jit(solution)/shard_map/ppermute | solution.py:352
  120.3 10.3 %collective-permute-start.21 = (bf16[2,128,256]{2,1,0:T(8,128)(2,1)}, bf16[2,128,256]{2,1,0:T(8,128)(2,1)S(1)}, u32[]{:S(2)}, u32[]{:S(2)}) collective-permute-start(bf16[2,128,256]{2,1,0:T(8,128)(2,1)} %get-tuple-element.91), channel_id=1, source_target_pairs={{0,3},{1,0},{2,1},{3,2},{4,7},{5,4},{6,5},{7,6},{8,11},{9,8},{10,9... | collective-permute-start | bytes 393224 | tf_op jit(solution)/shard_map/ppermute | solution.py:352
  122.3 5.2 %collective-permute-start.16 = (bf16[128,256]{1,0:T(8,128)(2,1)S(1)}, bf16[128,256]{1,0:T(8,128)(2,1)S(1)}, u32[]{:S(2)}, u32[]{:S(2)}) collective-permute-start(bf16[128,256]{1,0:T(8,128)(2,1)S(1)} %copy-done.23), channel_id=1, source_target_pairs={{0,64},{64,128},{128,192},{1,65},{65,129},{129,193},{2,66},{66,130... | collective-permute-start | bytes 196616 | tf_op jit(solution)/shard_map/ppermute | solution.py:423
  (14 other events, 9.6 us)

commit v3 on v2

--- a/solution.py
+++ b/solution.py
@@ -110,25 +110,25 @@
     half = base_sum.shape[0]
     for h in range(HID // HC):
         cols = slice(h * HC, (h + 1) * HC)
-        z = dot(both, win[:, cols])
+        z = dot(both, win[layer, :, cols])
         act = z[:half] + bias[layer : layer + 1, cols]
         phi = 0.5 * (1.0 + lax.erf(act * HALF_ROOT))
         slp = phi + act * jnp.exp(-0.5 * act * act) * DENSITY_NORM
         slope[:, cols] = slp.astype(BF)
         lifted = (slp * z[half:]).astype(BF)
-        tan_sum = tan_sum + dot(lifted, wout[cols, :])
+        tan_sum = tan_sum + dot(lifted, wout[layer, cols, :])
         if with_base:
-            base_sum = base_sum + dot((act * phi).astype(BF), wout[cols, :])
+            base_sum = base_sum + dot((act * phi).astype(BF), wout[layer, cols, :])
     return base_sum, tan_sum
 
 
-def adjoint_rows(current, win, wout, slope):
+def adjoint_rows(current, layer, win, wout, slope):
     narrow = current.astype(BF)
     for h in range(HID // HC):
         cols = slice(h * HC, (h + 1) * HC)
-        up = dot(narrow, wout[cols, :], 1, 1)
+        up = dot(narrow, wout[layer, cols, :], 1, 1)
         pulled = (slope[:, cols].astype(F32) * up).astype(BF)
-        current = current + dot(pulled, win[:, cols], 1, 1)
+        current = current + dot(pulled, win[layer, :, cols], 1, 1)
     return current
 
 
@@ -201,7 +201,7 @@
         else:
             following = stack(nxt[1], nxt[2]).astype(F32)
             current = jnp.where(last_member(), 0.0, following - out)
-        returned[w] = adjoint_rows(current, win, wout, slope)
+        returned[w] = adjoint_rows(current, 1, win, wout, slope)
 
 
 def edge1_kernel(
@@ -228,7 +228,7 @@
             current = following - out
         else:
             current = jnp.where(last_member(), 0.0, next_edge[...].astype(F32) - out)
-        back = adjoint_rows(current, win, wout, slope)
+        back = adjoint_rows(current, 1, win, wout, slope)
         returned[w] = back
         send_left[w] = dot(tmat[0, :, 0:B], back[0:B].astype(BF)).astype(BF)
         send_right[w] = dot(tmat[G - 1, :, 2 * B :], back[B:].astype(BF)).astype(BF)
@@ -248,13 +248,13 @@
         narrow = stack(edge[w, 0:B], inner[w], edge[w, B:]).astype(BF)
         cur_edge[w] = spread_edge(tmat, edge[w], narrow)
         current = inner[w] + dot(hat[...], narrow)
-        returned[w] = adjoint_rows(current, win, wout, slope.at[w])
+        returned[w] = adjoint_rows(current, 0, win, wout, slope.at[w])
 
 
 def edge2_kernel(cur_edge, left, right, tmat, slope, win, wout, returned, send_left, send_right):
     for w in range(NW):
         current = cur_edge[w] + stack(left[w], right[w]).astype(F32)
-        back = adjoint_rows(current, win, wout, slope.at[w])
+        back = adjoint_rows(current, 0, win, wout, slope.at[w])
         returned[w] = back
         send_left[w] = dot(tmat[0, :, 0:B], back[0:B].astype(BF)).astype(BF)
         send_right[w] = dot(tmat[G - 1, :, 2 * B :], back[B:].astype(BF)).astype(BF)
@@ -286,24 +286,29 @@
         out[...] = all_blocks[lax.rem(y + k, G)]
 
 
-def misfit_kernel(inc, i0, i1, i2, i3, before, misfit):
+def misfit_kernel(inc, i0, i1, i2, i3, before, misfit, kept):
     y = member()
     for k, im in enumerate((i0, i1, i2, i3)):
         m = origin(y, k)
-        misfit[NW * m + 1] = inc[NW * m + 1] - im[0].astype(F32)
+        value = inc[NW * m + 1] - im[0].astype(F32)
+        misfit[NW * m + 1] = value
+        kept[NW * m + 1] = value
         even = NW * lax.rem(m + 1, G)
         image = jnp.where(m == G - 1, before[...], im[1])
-        misfit[even] = inc[even] - image.astype(F32)
-
-
-def normal_kernel(misfit, p0, p1, p2, p3, normal):
+        value = inc[even] - image.astype(F32)
+        misfit[even] = value
+        kept[even] = value
+
+
+def normal_kernel(kept, p0, p1, p2, p3, normal):
     y = member()
     for k, part in enumerate((p0, p1, p2, p3)):
         m = origin(y, k)
         for w in range(NW):
-            normal[NW * m + w] = misfit[NW * m + w] - part[w].astype(F32)
-
-
+            normal[NW * m + w] = kept[NW * m + w] - part[w].astype(F32)
+
+
+VMEM_LIMIT = 16 * 1024 * 1024
 SMEM = pl.BlockSpec(memory_space=pltpu.SMEM)
 VMEM = pl.BlockSpec(memory_space=pltpu.VMEM)
 
@@ -312,19 +317,14 @@
     return jax.ShapeDtypeStruct(shape, dtype)
 
 
-def call(kernel, ins, outs, scratch=(), smem=0, layer=0, weights=()):
-    specs = [SMEM] * smem + [VMEM] * (len(ins) - smem)
-    for position in weights:
-        shape = ins[position].shape
-        specs[position] = pl.BlockSpec((None,) + shape[1:], lambda i: (layer, 0, 0))
+def call(kernel, ins, outs, scratch=(), smem=0):
     return pl.pallas_call(
         kernel,
-        grid=(1,),
         out_shape=outs,
-        in_specs=specs,
+        in_specs=[SMEM] * smem + [VMEM] * (len(ins) - smem),
         out_specs=[VMEM] * len(outs),
         scratch_shapes=list(scratch),
-        compiler_params=pltpu.CompilerParams(vmem_limit_bytes=60 * 1024 * 1024),
+        compiler_params=pltpu.CompilerParams(vmem_limit_bytes=VMEM_LIMIT),
     )(*ins)
 
 
@@ -382,11 +382,11 @@
     left, right = swap_sides(lo, hi)
     field, amat0, tmat0, base_in, tan_in, slope_in = call(
         inner0_kernel, (*got, *ext, inner_weight, bias, outer_weight),
-        [sds((NW, G * B, 2 * D)), mats, mats, pair_bf, pair, hidden], (hat,), weights=(8, 10),
+        [sds((NW, G * B, 2 * D)), mats, mats, pair_bf, pair, hidden], (hat,)
     )
     lo, hi, tan_edge, slope_edge = call(
         edge0_kernel, (field, amat0, left, right, inner_weight, bias, outer_weight),
-        [item, item, pair, hidden], weights=(4, 6),
+        [item, item, pair, hidden]
     )
 
     left, right = swap_sides(lo, hi)
@@ -395,25 +395,25 @@
         inner1_kernel,
         (base_in, tan_in, lo, hi, field, ext[0], cross, *ext[1:], inner_weight, bias, outer_weight),
         [mats, mats, sds((2 * B, D)), pair_bf, pair],
-        (hat, slope1, pltpu.VMEM((G, B, D), BF)), layer=1, weights=(10, 12),
+        (hat, slope1, pltpu.VMEM((G, B, D), BF))
     )
     *images, edge, send_left, send_right = call(
         edge1_kernel,
         (lo, hi, tan_edge, base_in, tan_in, left, right, field, next_edge, amat1, tmat1, image_in,
          inner_weight, bias, outer_weight),
         [half] * G + [pair, half, half],
-        (slope1, pltpu.VMEM((G, NW, B, D), BF)), layer=1, weights=(12, 14),
+        (slope1, pltpu.VMEM((G, NW, B, D), BF))
     )
 
     left, right = swap_sides(send_left, send_right)
     images = [images[0], *to_members(images)]
     cur_edge, inner = call(
         inner2_kernel, (inner, edge, tmat1, slope_in, inner_weight, outer_weight),
-        [pair, pair], (hat,), weights=(4, 5),
+        [pair, pair], (hat,)
     )
     edge, send_left, send_right = call(
         edge2_kernel, (cur_edge, left, right, tmat0, slope_edge, inner_weight, outer_weight),
-        [pair, half, half], weights=(5, 6),
+        [pair, half, half]
     )
 
     left, right = swap_sides(send_left, send_right)
@@ -427,8 +427,8 @@
     )
     parts = [parts[0], *to_members(parts)]
     whole = sds(increment.shape, F32)
-    (misfit,) = call(misfit_kernel, (increment, *images, before), [whole])
-    (normal,) = call(normal_kernel, (misfit, *parts), [whole])
+    misfit, kept = call(misfit_kernel, (increment, *images, before), [whole, whole])
+    (normal,) = call(normal_kernel, (kept, *parts), [whole])
     return misfit, normal
 
 

time: 135 us -> 110 us (0.81)
  Pallas kernels: 47.6 us -> 17 us
  waiting for transfers between devices: 22.5 us -> 29.7 us
  local copies, waits for them, and re-layouts: 7.09 us -> 3.23 us
  starting transfers between devices: 55.8 us -> 59.3 us
    pallas_call x13, Pallas kernels: 47.6 us -> 17 us  [call(): pl.pallas_call(kernel, out_shape=outs, in_specs=[SMEM] * smem + [VMEM] *...]
    ppermute x4, waiting for transfers between devices: 6.92 us -> 15.2 us  [swap_sides(): left = lax.ppermute(send_right, 'mesh', side_pairs(1))]
    unnamed x48 -> x18, local copies, waits for them, and re-layouts: 7.09 us -> 3.23 us
    ppermute x3, starting transfers between devices: 5.8 us -> 8.58 us  [local(): lax.ppermute(ext[k], ('tm', 'mesh'), next_increment_pairs(k))]
    ppermute x9, waiting for transfers between devices: 8.88 us -> 7.46 us  [to_members(): return [lax.ppermute(sends[k], 'mesh', group_pairs(k)) for k in range(1, G)]]
  transfers between devices with their start and end apart: 22 -> 22, of which waited for: 8 -> 8; matrix products, arithmetic and copies ran while one was open for 0% -> 0% of each run, Pallas kernels for 22% -> 9%
where the time goes in v3:
time: 110 us
  starting transfers between devices  59.3 us (54%)
  waiting for transfers between devices  29.7 us (27%)
  Pallas kernels  17 us (15%)
  local copies, waits for them, and re-layouts  3.23 us (3%)
    ppermute x4, starting transfers between devices, swap_sides(): right = lax.ppermute(send_left, 'mesh', side_pairs(-1))  25.1 us
    ppermute x9, starting transfers between devices, to_members(): return [lax.ppermute(sends[k], 'mesh', group_pairs(k)) for k in range(1, G)]  18.3 us
    pallas_call x13, Pallas kernels, call(): pl.pallas_call(kernel, out_shape=outs, in_specs=[SMEM] * smem + [VMEM] *...  17 us
    ppermute x4, waiting for transfers between devices, swap_sides(): left = lax.ppermute(send_right, 'mesh', side_pairs(1))  15.2 us
    ppermute x3, starting transfers between devices, local(): lax.ppermute(ext[k], ('tm', 'mesh'), next_increment_pairs(k))  8.58 us
    ppermute x9, waiting for transfers between devices, to_members(): return [lax.ppermute(sends[k], 'mesh', group_pairs(k)) for k in range(1, G)]  7.46 us
    ppermute x4, waiting for transfers between devices, swap_sides(): right = lax.ppermute(send_left, 'mesh', side_pairs(-1))  5.74 us
    ppermute x1, starting transfers between devices, local(): before = lax.ppermute(last, 'tm', [(t, t + 1) for t in range(TM - 1)])  4.88 us
  transfers between devices with their start and end apart: 22, of which 8 were waited for; matrix products, arithmetic and copies ran while one was open for 0% of the time, Pallas kernels for 9%

profile of v3, /device:TPU:1, one launch (start us, length us, event | category | flops | bytes accessed | tf_op | source)
XLA Modules:
  0.0 110.1 jit_solution(5891847117328046556)
XLA Ops:
  0.6 1.2 %copy-done.2 = f32[8,128,256]{2,1,0:T(8,128)S(1)} copy-done((f32[8,128,256]{2,1,0:T(8,128)S(1)}, f32[8,128,256]{2,1,0:T(8,128)}, u32[]{:S(2)}) %copy-start.2) | copy-done | bytes 1048600
  1.9 1.0 copy-done.4
  3.0 2.2 %collective-permute-start = (bf16[2,2,128,256]{3,2,1,0:T(8,128)(2,1)S(1)}, bf16[2,2,128,256]{3,2,1,0:T(8,128)(2,1)S(1)}, u32[]{:S(2)}, u32[]{:S(2)}) collective-permute-start(bf16[2,2,128,256]{3,2,1,0:T(8,128)(2,1)S(1)} %get-tuple-element.50), channel_id=1, source_target_pairs={{0,1},{1,2},{2,3},{3,0},{4,5},{5,6},{6,7},{7,4},{8,9},{9,10},{10,1... | collective-permute-start | bytes 786440 | tf_op jit(solution)/shard_map/ppermute | solution.py:352
  5.2 2.6 %collective-permute-start.1 = (bf16[2,2,128,256]{3,2,1,0:T(8,128)(2,1)S(1)}, bf16[2,2,128,256]{3,2,1,0:T(8,128)(2,1)S(1)}, u32[]{:S(2)}, u32[]{:S(2)}) collective-permute-start(bf16[2,2,128,256]{3,2,1,0:T(8,128)(2,1)S(1)} %get-tuple-element.51), channel_id=1, source_target_pairs={{0,2},{1,3},{2,0},{3,1},{4,6},{5,7},{6,4},{7,5},{8,10},{9,11},{10,... | collective-permute-start | bytes 786440 | tf_op jit(solution)/shard_map/ppermute | solution.py:352
  7.8 1.1 collective-permute-start.2
  11.0 2.1 %collective-permute-start.4 = (bf16[128,1024]{1,0:T(8,128)(2,1)S(1)}, bf16[128,1024]{1,0:T(8,128)(2,1)S(1)}, u32[]{:S(2)}, u32[]{:S(2)}) collective-permute-start(bf16[128,1024]{1,0:T(8,128)(2,1)S(1)} %get-tuple-element.55), channel_id=1, source_target_pairs={{0,2},{1,195},{2,0},{3,1},{4,6},{5,199},{6,4},{7,5},{8,10},{9,203}... | collective-permute-start | bytes 786440 | tf_op jit(solution)/shard_map/ppermute | solution.py:379
  13.2 6.0 %collective-permute-start.5 = (bf16[128,1024]{1,0:T(8,128)(2,1)S(1)}, bf16[128,1024]{1,0:T(8,128)(2,1)S(1)}, u32[]{:S(2)}, u32[]{:S(2)}) collective-permute-start(bf16[128,1024]{1,0:T(8,128)(2,1)S(1)} %get-tuple-element.56), channel_id=1, source_target_pairs={{0,195},{1,0},{2,1},{3,2},{4,199},{5,4},{6,5},{7,6},{8,203},{9,8},... | collective-permute-start | bytes 786440 | tf_op jit(solution)/shard_map/ppermute | solution.py:379
  19.1 2.8 %collective-permute-done.1.r2 = bf16[2,2,128,256]{3,2,1,0:T(8,128)(2,1)S(1)} collective-permute-done((bf16[2,2,128,256]{3,2,1,0:T(8,128)(2,1)S(1)}, bf16[2,2,128,256]{3,2,1,0:T(8,128)(2,1)S(1)}, u32[]{:S(2)}, u32[]{:S(2)}) %collective-permute-start.1) | collective-permute-done | bytes 262176 | tf_op jit(solution)/shard_map/ppermute | solution.py:352
  22.0 4.6 %collective-permute-done.2.r3 = bf16[2,2,128,256]{3,2,1,0:T(8,128)(2,1)S(1)} collective-permute-done((bf16[2,2,128,256]{3,2,1,0:T(8,128)(2,1)S(1)}, bf16[2,2,128,256]{3,2,1,0:T(8,128)(2,1)S(1)}, u32[]{:S(2)}, u32[]{:S(2)}) %collective-permute-start.2) | collective-permute-done | bytes 262176 | tf_op jit(solution)/shard_map/ppermute | solution.py:352
  26.7 1.6 %collective-permute-start.6 = (bf16[2,2,128,256]{3,2,1,0:T(8,128)(2,1)S(1)}, bf16[2,2,128,256]{3,2,1,0:T(8,128)(2,1)S(1)}, u32[]{:S(2)}, u32[]{:S(2)}) collective-permute-start(bf16[2,2,128,256]{3,2,1,0:T(8,128)(2,1)S(1)} %get-tuple-element.59), channel_id=1, source_target_pairs={{0,4},{1,5},{2,6},{3,7},{4,8},{5,9},{6,10},{7,11},{8,12},{9,13},{1... | collective-permute-start | bytes 786440 | tf_op jit(solution)/shard_map/ppermute | solution.py:356
  28.3 7.1 %collective-permute-start.7 = (bf16[2,2,128,256]{3,2,1,0:T(8,128)(2,1)S(1)}, bf16[2,2,128,256]{3,2,1,0:T(8,128)(2,1)S(1)}, u32[]{:S(2)}, u32[]{:S(2)}) collective-permute-start(bf16[2,2,128,256]{3,2,1,0:T(8,128)(2,1)S(1)} %get-tuple-element.60), channel_id=1, source_target_pairs={{0,60},{1,61},{2,62},{3,63},{4,0},{5,1},{6,2},{7,3},{8,4},{9,5},{1... | collective-permute-start | bytes 786440 | tf_op jit(solution)/shard_map/ppermute | solution.py:357
  35.4 2.2 %shard_map.88 = (bf16[2,512,512]{2,1,0:T(8,128)(2,1)S(1)}, bf16[4,128,384]{2,1,0:T(8,128)(2,1)S(1)}, bf16[4,128,384]{2,1,0:T(8,128)(2,1)S(1)}, bf16[2,256,256]{2...) custom-call(bf16[2,2,128,256]{3,2,1,0:T(8,128)(2,1)S(1)} %get-tuple-element.49.r0, ...), custom_call_target="tpu_custom_call" | custom-call | tf_op jit(solution)/shard_map/pallas_call | solution.py:321
  37.7 5.2 %collective-permute-done.6.left = bf16[2,2,128,256]{3,2,1,0:T(8,128)(2,1)S(1)} collective-permute-done((bf16[2,2,128,256]{3,2,1,0:T(8,128)(2,1)S(1)}, bf16[2,2,128,256]{3,2,1,0:T(8,128)(2,1)S(1)}, u32[]{:S(2)}, u32[]{:S(2)}) %collective-permute-start.6) | collective-permute-done | bytes 262176 | tf_op jit(solution)/shard_map/ppermute | solution.py:356
  42.9 3.5 %collective-permute-done.7.right = bf16[2,2,128,256]{3,2,1,0:T(8,128)(2,1)S(1)} collective-permute-done((bf16[2,2,128,256]{3,2,1,0:T(8,128)(2,1)S(1)}, bf16[2,2,128,256]{3,2,1,0:T(8,128)(2,1)S(1)}, u32[]{:S(2)}, u32[]{:S(2)}) %collective-permute-start.7) | collective-permute-done | bytes 262176 | tf_op jit(solution)/shard_map/ppermute | solution.py:357
  46.4 2.1 %shard_map.90 = (bf16[2,2,128,256]{3,2,1,0:T(8,128)(2,1)S(1)}, bf16[2,2,128,256]{3,2,1,0:T(8,128)(2,1)S(1)}, f32[2,256,256]{2,1,0:T(8,128)S(1)}, bf16[2,256,1024]{2,1,0:T(8,128)(2,1)S(1)}) custom-call(bf16[2,512,512]{2,1,0:T(8,128)(2,1)S(1)} %get-tuple-element.57.field, bf16[4,128,384]{2,1,0:T(8,128)(2,1)S(1)} %get-tuple-element.58.amat, ...), custom_call_target="tpu_custom_call" | custom-call | tf_op jit(solution)/shard_map/pallas_call | solution.py:321
  48.5 6.7 %collective-permute-start.9 = (bf16[2,2,128,256]{3,2,1,0:T(8,128)(2,1)S(1)}, bf16[2,2,128,256]{3,2,1,0:T(8,128)(2,1)S(1)}, u32[]{:S(2)}, u32[]{:S(2)}) collective-permute-start(bf16[2,2,128,256]{3,2,1,0:T(8,128)(2,1)S(1)} %get-tuple-element.61.lo), channel_id=1, source_target_pairs={{0,60},{1,61},{2,62},{3,63},{4,0},{5,1},{6,2},{7,3},{8,4},{9,5},{1... | collective-permute-start | bytes 786440 | tf_op jit(solution)/shard_map/ppermute | solution.py:357
  55.8 3.1 %shard_map.91 = (bf16[4,128,384]{2,1,0:T(8,128)(2,1)S(1)}, bf16[4,128,384]{2,1,0:T(8,128)(2,1)S(1)}, bf16[256,256]{1,0:T(8,128)(2,1)S(1)}, bf16[2,256,256]{2,1,0:T(8,128)(2,1)S(1)}, f32[2,256,256]{2,1,0:T(8,128)S(1)}) custom-call(bf16[2,256,256]{2,1,0:T(8,128)(2,1)S(1)} %get-tuple-element.64.base_in, f32[2,256,256]{2,1,0:T(8,128)S(1)} %get-tuple-element.65.tan_in, ...), custom_call_target="tpu_custom_call" | custom-call | tf_op jit(solution)/shard_map/pallas_call | solution.py:321
  58.9 2.2 %collective-permute-done.9.right = bf16[2,2,128,256]{3,2,1,0:T(8,128)(2,1)S(1)} collective-permute-done((bf16[2,2,128,256]{3,2,1,0:T(8,128)(2,1)S(1)}, bf16[2,2,128,256]{3,2,1,0:T(8,128)(2,1)S(1)}, u32[]{:S(2)}, u32[]{:S(2)}) %collective-permute-start.9) | collective-permute-done | bytes 262176 | tf_op jit(solution)/shard_map/ppermute | solution.py:357
  61.2 5.2 %collective-permute-done.8.left = bf16[2,2,128,256]{3,2,1,0:T(8,128)(2,1)S(1)} collective-permute-done((bf16[2,2,128,256]{3,2,1,0:T(8,128)(2,1)S(1)}, bf16[2,2,128,256]{3,2,1,0:T(8,128)(2,1)S(1)}, u32[]{:S(2)}, u32[]{:S(2)}) %collective-permute-start.8) | collective-permute-done | bytes 262176 | tf_op jit(solution)/shard_map/ppermute | solution.py:356
  66.3 3.3 %shard_map.92 = (bf16[2,128,256]{2,1,0:T(8,128)(2,1)S(1)}, bf16[2,128,256]{2,1,0:T(8,128)(2,1)S(1)}, bf16[2,128,256]{2,1,0:T(8,128)(2,1)S(1)}, bf16[2,128,256]{2...) custom-call(bf16[2,2,128,256]{3,2,1,0:T(8,128)(2,1)S(1)} %get-tuple-, ...), custom_call_target="tpu_custom_call" | custom-call | tf_op jit(solution)/shard_map/pallas_call | solution.py:321
  69.8 5.7 %collective-permute-start.15 = (bf16[2,128,256]{2,1,0:T(8,128)(2,1)S(1)}, bf16[2,128,256]{2,1,0:T(8,128)(2,1)S(1)}, u32[]{:S(2)}, u32[]{:S(2)}) collective-permute-start(bf16[2,128,256]{2,1,0:T(8,128)(2,1)S(1)} %get-tuple-element.81), channel_id=1, source_target_pairs={{0,60},{1,61},{2,62},{3,63},{4,0},{5,1},{6,2},{7,3},{8,4},{9,5},{1... | collective-permute-start | bytes 393224 | tf_op jit(solution)/shard_map/ppermute | solution.py:357
  75.4 7.8 %collective-permute-start.12 = (bf16[2,128,256]{2,1,0:T(8,128)(2,1)S(1)}, bf16[2,128,256]{2,1,0:T(8,128)(2,1)S(1)}, u32[]{:S(2)}, u32[]{:S(2)}) collective-permute-start(bf16[2,128,256]{2,1,0:T(8,128)(2,1)S(1)} %get-tuple-element.73), channel_id=1, source_target_pairs={{0,2},{1,3},{2,0},{3,1},{4,6},{5,7},{6,4},{7,5},{8,10},{9,11},{10,... | collective-permute-start | bytes 393224 | tf_op jit(solution)/shard_map/ppermute | solution.py:352
  83.2 1.4 %shard_map.93 = (f32[2,256,256]{2,1,0:T(8,128)S(1)}, f32[2,256,256]{2,1,0:T(8,128)S(1)}) custom-call(f32[2,256,256]{2,1,0:T(8,128)S(1)} %get-tuple-element.75.inner, f32[2,256,256]{2,1,0:T(8,128)S(1)} %get-tuple-element.76.edge, bf16[4,128,384]{2,1,0:T(8,128)(2,1)S(1)} %get-tuple-element.69.tmat, bf16[2,256,1024]{2,1,0:T(8,128)(2,1)S(1)} %get-tuple-element.77.slope, ...), custom_call_target="tpu_custom_call" | custom-call | tf_op jit(solution)/shard_map/pallas_call | solution.py:321
  84.6 1.3 %shard_map.94 = (f32[2,256,256]{2,1,0:T(8,128)S(1)}, bf16[2,128,256]{2,1,0:T(8,128)(2,1)S(1)}, bf16[2,128,256]{2,1,0:T(8,128)(2,1)S(1)}) custom-call(f32[2,256,256]{2,1,0:T(8,128)S(1)} %get-tuple-element.79.cur_edge, bf16[2,128,256]{2,1,0:T(8,128)(2,1)S(1)} %collective-permute-done.14.left, bf16[2,128,256]{2,1,0:T(8,128)(2,1)S(1)} %collective-permute-done.15.right, ...), custom_call_target="tpu_custom_call" | custom-call | tf_op jit(solution)/shard_map/pallas_call | solution.py:321
  86.0 5.7 %collective-permute-start.18 = (bf16[2,128,256]{2,1,0:T(8,128)(2,1)S(1)}, bf16[2,128,256]{2,1,0:T(8,128)(2,1)S(1)}, u32[]{:S(2)}, u32[]{:S(2)}) collective-permute-start(bf16[2,128,256]{2,1,0:T(8,128)(2,1)S(1)} %get-tuple-element.91), channel_id=1, source_target_pairs={{0,60},{1,61},{2,62},{3,63},{4,0},{5,1},{6,2},{7,3},{8,4},{9,5},{1... | collective-permute-start | bytes 393224 | tf_op jit(solution)/shard_map/ppermute | solution.py:357
  92.2 4.8 %collective-permute-done.17.left = bf16[2,128,256]{2,1,0:T(8,128)(2,1)S(1)} collective-permute-done((bf16[2,128,256]{2,1,0:T(8,128)(2,1)S(1)}, bf16[2,128,256]{2,1,0:T(8,128)(2,1)S(1)}, u32[]{:S(2)}, u32[]{:S(2)}) %collective-permute-start.17) | collective-permute-done | bytes 131104 | tf_op jit(solution)/shard_map/ppermute | solution.py:356
  97.0 1.1 collective-permute-start.19
  98.1 3.6 %collective-permute-start.20 = (bf16[2,128,256]{2,1,0:T(8,128)(2,1)S(1)}, bf16[2,128,256]{2,1,0:T(8,128)(2,1)S(1)}, u32[]{:S(2)}, u32[]{:S(2)}) collective-permute-start(bf16[2,128,256]{2,1,0:T(8,128)(2,1)S(1)} %get-tuple-element.94), channel_id=1, source_target_pairs={{0,2},{1,3},{2,0},{3,1},{4,6},{5,7},{6,4},{7,5},{8,10},{9,11},{10,... | collective-permute-start | bytes 393224 | tf_op jit(solution)/shard_map/ppermute | solution.py:352
  101.6 4.9 %collective-permute-start.16 = (bf16[128,256]{1,0:T(8,128)(2,1)S(1)}, bf16[128,256]{1,0:T(8,128)(2,1)S(1)}, u32[]{:S(2)}, u32[]{:S(2)}) collective-permute-start(bf16[128,256]{1,0:T(8,128)(2,1)S(1)} %get-tuple-element.85), channel_id=1, source_target_pairs={{0,64},{64,128},{128,192},{1,65},{65,129},{129,193},{2,66},{66,130... | collective-permute-start | bytes 196616 | tf_op jit(solution)/shard_map/ppermute | solution.py:423
  106.5 1.3 %collective-permute-done.16.before = bf16[128,256]{1,0:T(8,128)(2,1)S(1)} collective-permute-done((bf16[128,256]{1,0:T(8,128)(2,1)S(1)}, bf16[128,256]{1,0:T(8,128)(2,1)S(1)}, u32[]{:S(2)}, u32[]{:S(2)}) %collective-permute-start.16) | collective-permute-done | bytes 65568 | tf_op jit(solution)/shard_map/ppermute | solution.py:423
  107.9 1.1 %shard_map.96 = (f32[8,128,256]{2,1,0:T(8,128)}, f32[8,128,256]{2,1,0:T(8,128)S(1)}) custom-call(f32[8,128,256]{2,1,0:T(8,128)S(1)} %copy-done.3, bf16[2,128,256]{2,1,0:T(8,128)(2,1)S(1)} %get-tuple-element.71.i0, bf16[2,128,256]{2,1,0:T(8,128)(2,1)S(1)} %collective-permute-done.11.i1, bf16[2,128,256]{2,1,0:T(8,128)(2,1)S(1)} %collective-permute-done.12.i2, ...), custom_call_target="tpu_custom_call" | custom-call | tf_op jit(solution)/shard_map/pallas_call | solution.py:321
  109.0 1.1 shard_map.98
  (43 shorter events, 3.7 us)
Async XLA Ops:
  0.6 1.2 %copy-start.2 = (f32[8,128,256]{2,1,0:T(8,128)S(1)}, f32[8,128,256]{2,1,0:T(8,128)}, u32[]{:S(2)}) copy-start(f32[8,128,256]{2,1,0:T(8,128)} %inc.5) | copy-start | bytes 3145732
  1.9 1.0 copy-start.4
  2.9 6.0 %copy-start.3 = (f32[8,128,256]{2,1,0:T(8,128)S(1)}, f32[8,128,256]{2,1,0:T(8,128)}, u32[]{:S(2)}) copy-start(f32[8,128,256]{2,1,0:T(8,128)} %inc.5) | copy-start | bytes 3145732
  2.9 6.0 %copy-start.5 = (bf16[8,128,256]{2,1,0:T(8,128)(2,1)S(1)}, bf16[8,128,256]{2,1,0:T(8,128)(2,1)}, u32[]{:S(2)}) copy-start(bf16[8,128,256]{2,1,0:T(8,128)(2,1)} %states.3) | copy-start | bytes 1572868
  3.0 10.2 %collective-permute-start = (bf16[2,2,128,256]{3,2,1,0:T(8,128)(2,1)S(1)}, bf16[2,2,128,256]{3,2,1,0:T(8,128)(2,1)S(1)}, u32[]{:S(2)}, u32[]{:S(2)}) collective-permute-start(bf16[2,2,128,256]{3,2,1,0:T(8,128)(2,1)S(1)} %get-tuple-element.50), channel_id=1, source_target_pairs={{0,1},{1,2},{2,3},{3,0},{4,5},{5,6},{6,7},{7,4},{8,9},{9,10},{10,1... | collective-permute-start | bytes 786440 | tf_op jit(solution)/shard_map/ppermute | solution.py:352
  5.2 3.7 %copy-start.8 = (s32[1,4]{1,0:T(1,128)S(1)}, s32[1,4]{1,0:T(1,128)}, u32[]{:S(2)}) copy-start(s32[1,4]{1,0:T(1,128)} %slots.1) | copy-start | bytes 52
  5.2 16.8 %collective-permute-start.1 = (bf16[2,2,128,256]{3,2,1,0:T(8,128)(2,1)S(1)}, bf16[2,2,128,256]{3,2,1,0:T(8,128)(2,1)S(1)}, u32[]{:S(2)}, u32[]{:S(2)}) collective-permute-start(bf16[2,2,128,256]{3,2,1,0:T(8,128)(2,1)S(1)} %get-tuple-element.51), channel_id=1, source_target_pairs={{0,2},{1,3},{2,0},{3,1},{4,6},{5,7},{6,4},{7,5},{8,10},{9,11},{10,... | collective-permute-start | bytes 786440 | tf_op jit(solution)/shard_map/ppermute | solution.py:352
  7.8 27.6 %copy-start = (bf16[2,256,1024]{2,1,0:T(8,128)(2,1)S(1)}, bf16[2,256,1024]{2,1,0:T(8,128)(2,1)}, u32[]{:S(2)}) copy-start(bf16[2,256,1024]{2,1,0:T(8,128)(2,1)} %win.11) | copy-start | bytes 3145732
  7.8 27.6 %copy-start.1 = (bf16[2,1024,256]{2,1,0:T(8,128)(2,1)S(1)}, bf16[2,1024,256]{2,1,0:T(8,128)(2,1)}, u32[]{:S(2)}) copy-start(bf16[2,1024,256]{2,1,0:T(8,128)(2,1)} %wout.11) | copy-start | bytes 3145732
  7.8 18.8 %collective-permute-start.2 = (bf16[2,2,128,256]{3,2,1,0:T(8,128)(2,1)S(1)}, bf16[2,2,128,256]{3,2,1,0:T(8,128)(2,1)S(1)}, u32[]{:S(2)}, u32[]{:S(2)}) collective-permute-start(bf16[2,2,128,256]{3,2,1,0:T(8,128)(2,1)S(1)} %get-tuple-element.52), channel_id=1, source_target_pairs={{0,3},{1,0},{2,1},{3,2},{4,7},{5,4},{6,5},{7,6},{8,11},{9,8},{10,9... | collective-permute-start | bytes 786440 | tf_op jit(solution)/shard_map/ppermute | solution.py:352
  8.9 1.0 copy-start.6
  10.6 24.8 %collective-permute-start.3 = (bf16[128,1024]{1,0:T(8,128)(2,1)S(1)}, bf16[128,1024]{1,0:T(8,128)(2,1)S(1)}, u32[]{:S(2)}, u32[]{:S(2)}) collective-permute-start(bf16[128,1024]{1,0:T(8,128)(2,1)S(1)} %get-tuple-element.54), channel_id=1, source_target_pairs={{0,1},{1,2},{2,195},{3,0},{4,5},{5,6},{6,199},{7,4},{8,9},{9,10},{... | collective-permute-start | bytes 786440 | tf_op jit(solution)/shard_map/ppermute | solution.py:379
  11.0 24.4 %collective-permute-start.4 = (bf16[128,1024]{1,0:T(8,128)(2,1)S(1)}, bf16[128,1024]{1,0:T(8,128)(2,1)S(1)}, u32[]{:S(2)}, u32[]{:S(2)}) collective-permute-start(bf16[128,1024]{1,0:T(8,128)(2,1)S(1)} %get-tuple-element.55), channel_id=1, source_target_pairs={{0,2},{1,195},{2,0},{3,1},{4,6},{5,199},{6,4},{7,5},{8,10},{9,203}... | collective-permute-start | bytes 786440 | tf_op jit(solution)/shard_map/ppermute | solution.py:379
  13.2 22.2 %collective-permute-start.5 = (bf16[128,1024]{1,0:T(8,128)(2,1)S(1)}, bf16[128,1024]{1,0:T(8,128)(2,1)S(1)}, u32[]{:S(2)}, u32[]{:S(2)}) collective-permute-start(bf16[128,1024]{1,0:T(8,128)(2,1)S(1)} %get-tuple-element.56), channel_id=1, source_target_pairs={{0,195},{1,0},{2,1},{3,2},{4,199},{5,4},{6,5},{7,6},{8,203},{9,8},... | collective-permute-start | bytes 786440 | tf_op jit(solution)/shard_map/ppermute | solution.py:379
  26.6 8.8 %copy-start.7 = (f32[2,1024]{1,0:T(2,128)S(1)}, f32[2,1024]{1,0:T(2,128)}, u32[]{:S(2)}) copy-start(f32[2,1024]{1,0:T(2,128)} %bias.7) | copy-start | bytes 24580
  26.7 16.2 %collective-permute-start.6 = (bf16[2,2,128,256]{3,2,1,0:T(8,128)(2,1)S(1)}, bf16[2,2,128,256]{3,2,1,0:T(8,128)(2,1)S(1)}, u32[]{:S(2)}, u32[]{:S(2)}) collective-permute-start(bf16[2,2,128,256]{3,2,1,0:T(8,128)(2,1)S(1)} %get-tuple-element.59), channel_id=1, source_target_pairs={{0,4},{1,5},{2,6},{3,7},{4,8},{5,9},{6,10},{7,11},{8,12},{9,13},{1... | collective-permute-start | bytes 786440 | tf_op jit(solution)/shard_map/ppermute | solution.py:356
  28.3 18.1 %collective-permute-start.7 = (bf16[2,2,128,256]{3,2,1,0:T(8,128)(2,1)S(1)}, bf16[2,2,128,256]{3,2,1,0:T(8,128)(2,1)S(1)}, u32[]{:S(2)}, u32[]{:S(2)}) collective-permute-start(bf16[2,2,128,256]{3,2,1,0:T(8,128)(2,1)S(1)} %get-tuple-element.60), channel_id=1, source_target_pairs={{0,60},{1,61},{2,62},{3,63},{4,0},{5,1},{6,2},{7,3},{8,4},{9,5},{1... | collective-permute-start | bytes 786440 | tf_op jit(solution)/shard_map/ppermute | solution.py:357
  48.5 12.7 %collective-permute-start.9 = (bf16[2,2,128,256]{3,2,1,0:T(8,128)(2,1)S(1)}, bf16[2,2,128,256]{3,2,1,0:T(8,128)(2,1)S(1)}, u32[]{:S(2)}, u32[]{:S(2)}) collective-permute-start(bf16[2,2,128,256]{3,2,1,0:T(8,128)(2,1)S(1)} %get-tuple-element.61.lo), channel_id=1, source_target_pairs={{0,60},{1,61},{2,62},{3,63},{4,0},{5,1},{6,2},{7,3},{8,4},{9,5},{1... | collective-permute-start | bytes 786440 | tf_op jit(solution)/shard_map/ppermute | solution.py:357
  55.2 11.2 %collective-permute-start.8 = (bf16[2,2,128,256]{3,2,1,0:T(8,128)(2,1)S(1)}, bf16[2,2,128,256]{3,2,1,0:T(8,128)(2,1)S(1)}, u32[]{:S(2)}, u32[]{:S(2)}) collective-permute-start(bf16[2,2,128,256]{3,2,1,0:T(8,128)(2,1)S(1)} %get-tuple-element.62.hi), channel_id=1, source_target_pairs={{0,4},{1,5},{2,6},{3,7},{4,8},{5,9},{6,10},{7,11},{8,12},{9,13},{1... | collective-permute-start | bytes 786440 | tf_op jit(solution)/shard_map/ppermute | solution.py:356
  55.2 0.7 collective-permute-start.10
  69.7 14.9 %collective-permute-start.14 = (bf16[2,128,256]{2,1,0:T(8,128)(2,1)S(1)}, bf16[2,128,256]{2,1,0:T(8,128)(2,1)S(1)}, u32[]{:S(2)}, u32[]{:S(2)}) collective-permute-start(bf16[2,128,256]{2,1,0:T(8,128)(2,1)S(1)} %get-tuple-element.80), channel_id=1, source_target_pairs={{0,4},{1,5},{2,6},{3,7},{4,8},{5,9},{6,10},{7,11},{8,12},{9,13},{1... | collective-permute-start | bytes 393224 | tf_op jit(solution)/shard_map/ppermute | solution.py:356
  69.8 14.9 %collective-permute-start.15 = (bf16[2,128,256]{2,1,0:T(8,128)(2,1)S(1)}, bf16[2,128,256]{2,1,0:T(8,128)(2,1)S(1)}, u32[]{:S(2)}, u32[]{:S(2)}) collective-permute-start(bf16[2,128,256]{2,1,0:T(8,128)(2,1)S(1)} %get-tuple-element.81), channel_id=1, source_target_pairs={{0,60},{1,61},{2,62},{3,63},{4,0},{5,1},{6,2},{7,3},{8,4},{9,5},{1... | collective-permute-start | bytes 393224 | tf_op jit(solution)/shard_map/ppermute | solution.py:357
  75.4 16.3 %collective-permute-start.11 = (bf16[2,128,256]{2,1,0:T(8,128)(2,1)S(1)}, bf16[2,128,256]{2,1,0:T(8,128)(2,1)S(1)}, u32[]{:S(2)}, u32[]{:S(2)}) collective-permute-start(bf16[2,128,256]{2,1,0:T(8,128)(2,1)S(1)} %get-tuple-element.72), channel_id=1, source_target_pairs={{0,1},{1,2},{2,3},{3,0},{4,5},{5,6},{6,7},{7,4},{8,9},{9,10},{10,1... | collective-permute-start | bytes 393224 | tf_op jit(solution)/shard_map/ppermute | solution.py:352
  75.4 16.3 %collective-permute-start.12 = (bf16[2,128,256]{2,1,0:T(8,128)(2,1)S(1)}, bf16[2,128,256]{2,1,0:T(8,128)(2,1)S(1)}, u32[]{:S(2)}, u32[]{:S(2)}) collective-permute-start(bf16[2,128,256]{2,1,0:T(8,128)(2,1)S(1)} %get-tuple-element.73), channel_id=1, source_target_pairs={{0,2},{1,3},{2,0},{3,1},{4,6},{5,7},{6,4},{7,5},{8,10},{9,11},{10,... | collective-permute-start | bytes 393224 | tf_op jit(solution)/shard_map/ppermute | solution.py:352
  83.2 8.5 %collective-permute-start.13 = (bf16[2,128,256]{2,1,0:T(8,128)(2,1)S(1)}, bf16[2,128,256]{2,1,0:T(8,128)(2,1)S(1)}, u32[]{:S(2)}, u32[]{:S(2)}) collective-permute-start(bf16[2,128,256]{2,1,0:T(8,128)(2,1)S(1)} %get-tuple-element.74), channel_id=1, source_target_pairs={{0,3},{1,0},{2,1},{3,2},{4,7},{5,4},{6,5},{7,6},{8,11},{9,8},{10,9... | collective-permute-start | bytes 393224 | tf_op jit(solution)/shard_map/ppermute | solution.py:352
  85.9 11.0 %collective-permute-start.17 = (bf16[2,128,256]{2,1,0:T(8,128)(2,1)S(1)}, bf16[2,128,256]{2,1,0:T(8,128)(2,1)S(1)}, u32[]{:S(2)}, u32[]{:S(2)}) collective-permute-start(bf16[2,128,256]{2,1,0:T(8,128)(2,1)S(1)} %get-tuple-element.90), channel_id=1, source_target_pairs={{0,4},{1,5},{2,6},{3,7},{4,8},{5,9},{6,10},{7,11},{8,12},{9,13},{1... | collective-permute-start | bytes 393224 | tf_op jit(solution)/shard_map/ppermute | solution.py:356
  86.0 10.9 %collective-permute-start.18 = (bf16[2,128,256]{2,1,0:T(8,128)(2,1)S(1)}, bf16[2,128,256]{2,1,0:T(8,128)(2,1)S(1)}, u32[]{:S(2)}, u32[]{:S(2)}) collective-permute-start(bf16[2,128,256]{2,1,0:T(8,128)(2,1)S(1)} %get-tuple-element.91), channel_id=1, source_target_pairs={{0,60},{1,61},{2,62},{3,63},{4,0},{5,1},{6,2},{7,3},{8,4},{9,5},{1... | collective-permute-start | bytes 393224 | tf_op jit(solution)/shard_map/ppermute | solution.py:357
  97.0 12.0 %collective-permute-start.19 = (bf16[2,128,256]{2,1,0:T(8,128)(2,1)S(1)}, bf16[2,128,256]{2,1,0:T(8,128)(2,1)S(1)}, u32[]{:S(2)}, u32[]{:S(2)}) collective-permute-start(bf16[2,128,256]{2,1,0:T(8,128)(2,1)S(1)} %get-tuple-element.93), channel_id=1, source_target_pairs={{0,1},{1,2},{2,3},{3,0},{4,5},{5,6},{6,7},{7,4},{8,9},{9,10},{10,1... | collective-permute-start | bytes 393224 | tf_op jit(solution)/shard_map/ppermute | solution.py:352
  98.1 10.9 %collective-permute-start.20 = (bf16[2,128,256]{2,1,0:T(8,128)(2,1)S(1)}, bf16[2,128,256]{2,1,0:T(8,128)(2,1)S(1)}, u32[]{:S(2)}, u32[]{:S(2)}) collective-permute-start(bf16[2,128,256]{2,1,0:T(8,128)(2,1)S(1)} %get-tuple-element.94), channel_id=1, source_target_pairs={{0,2},{1,3},{2,0},{3,1},{4,6},{5,7},{6,4},{7,5},{8,10},{9,11},{10,... | collective-permute-start | bytes 393224 | tf_op jit(solution)/shard_map/ppermute | solution.py:352
  101.6 7.3 %collective-permute-start.21 = (bf16[2,128,256]{2,1,0:T(8,128)(2,1)S(1)}, bf16[2,128,256]{2,1,0:T(8,128)(2,1)S(1)}, u32[]{:S(2)}, u32[]{:S(2)}) collective-permute-start(bf16[2,128,256]{2,1,0:T(8,128)(2,1)S(1)} %get-tuple-element.95), channel_id=1, source_target_pairs={{0,3},{1,0},{2,1},{3,2},{4,7},{5,4},{6,5},{7,6},{8,11},{9,8},{10,9... | collective-permute-start | bytes 393224 | tf_op jit(solution)/shard_map/ppermute | solution.py:352
  101.6 6.2 %collective-permute-start.16 = (bf16[128,256]{1,0:T(8,128)(2,1)S(1)}, bf16[128,256]{1,0:T(8,128)(2,1)S(1)}, u32[]{:S(2)}, u32[]{:S(2)}) collective-permute-start(bf16[128,256]{1,0:T(8,128)(2,1)S(1)} %get-tuple-element.85), channel_id=1, source_target_pairs={{0,64},{64,128},{128,192},{1,65},{65,129},{129,193},{2,66},{66,130... | collective-permute-start | bytes 196616 | tf_op jit(solution)/shard_map/ppermute | solution.py:423

commit v4 on v3

--- a/solution.py
+++ b/solution.py
@@ -1,3 +1,5 @@
+import functools
+
 import jax
 import jax.numpy as jnp
 from jax import lax
@@ -42,30 +44,33 @@
 
 def pack_kernel(states, inc, *outs):
     y = member()
-    for k in range(1, G):
-        m = lax.rem(y + k, G)
-        for w in range(NW):
-            outs[k - 1][w, 0] = states[NW * m + w]
-            outs[k - 1][w, 1] = inc[NW * m + w].astype(BF)
-
-
-def fold_kernel(slots, states, inc, edges, own, cross, *ext):
-    y = member()
-    for w in range(NW):
-        own[w, 0] = states[NW * y + w]
-        own[w, 1] = inc[NW * y + w].astype(BF)
+    for w in range(NW):
+        for k in range(1, G):
+            m = lax.rem(y + k, G)
+            outs[w * (G - 1) + k - 1][0] = states[NW * m + w]
+            outs[w * (G - 1) + k - 1][1] = inc[NW * m + w].astype(BF)
+
+
+def fold_kernel(slots, states, inc, edges, own0, own1, a0, cross, *ext):
+    y = member()
+    for w, own in enumerate((own0, own1)):
+        own[0] = states[NW * y + w]
+        own[1] = inc[NW * y + w].astype(BF)
     for layer in range(2):
         for slot in range(3):
             total = jnp.zeros((B, B), F32)
             for f in range(4):
                 total += jnp.where(slots[0, f] == slot, edges[layer, 0, f].astype(F32), 0.0)
-            first = (3 * layer + slot) * B
-            for k in range(G):
-                ext[k][:, first : first + B] = total.astype(BF)
+            cols = slice(slot * B, (slot + 1) * B)
+            if layer == 0:
+                a0[:, cols] = total.astype(BF)
+            else:
+                for k in range(G):
+                    ext[k][:, cols] = total.astype(BF)
     for k in range(G):
         m = lax.rem(y + k + 1, G)
         value = inc[NW * m].astype(BF)
-        ext[k][:, 6 * B :] = value
+        ext[k][:, 3 * B :] = value
         if k == 0:
             cross[...] = value
 
@@ -84,9 +89,9 @@
             send_right[...] = r[...]
 
 
-def sort_edges(y, mats, first, amat, tmat):
+def sort_edges(y, mats, amat, tmat):
     for k, a in enumerate(mats):
-        amat[origin(y, k)] = a[:, first : first + 3 * B]
+        amat[origin(y, k)] = a[:, : 3 * B]
     for c in range(G):
         for slot in range(3):
             t = jnp.transpose(amat[c, :, slot * B : (slot + 1) * B].astype(F32)).astype(BF)
@@ -133,18 +138,17 @@
 
 
 def inner0_kernel(
-    r0, r1, r2, r3, a0, a1, a2, a3, win, bias, wout,
+    r00, r01, r02, r03, r10, r11, r12, r13, a0, a1, a2, a3, win, bias, wout,
     field, amat, tmat, base_out, tan_out, slope, hat,
 ):
     y = member()
-    sort_edges(y, (a0, a1, a2, a3), 0, amat, tmat)
+    sort_edges(y, (a0, a1, a2, a3), amat, tmat)
     pair_matrix(amat, hat)
-    for k, r in enumerate((r0, r1, r2, r3)):
-        block = origin(y, k)
-        rows = pl.ds(pl.multiple_of(block * B, B), B)
-        for w in range(NW):
-            field[w, rows, 0:D] = r[w, 0]
-            field[w, rows, D:] = r[w, 1]
+    for w, got in enumerate(((r00, r01, r02, r03), (r10, r11, r12, r13))):
+        for k, r in enumerate(got):
+            rows = pl.ds(pl.multiple_of(origin(y, k) * B, B), B)
+            field[w, rows, 0:D] = r[0]
+            field[w, rows, D:] = r[1]
     for w in range(NW):
         agg = dot(hat[...], field[w])
         base_sum = field[w, B : 3 * B, 0:D].astype(F32) + agg[:, 0:D]
@@ -155,42 +159,42 @@
 
 
 def edge0_kernel(
-    field, amat, left, right, win, bias, wout,
+    w, field, amat, left, right, win, bias, wout,
     send_left, send_right, tan_out, slope,
 ):
-    for w in range(NW):
-        lo = stack(jnp.concatenate([left[w, 0], left[w, 1]], axis=1), field[w, 0 : 2 * B])
-        hi = stack(field[w, 2 * B :], jnp.concatenate([right[w, 0], right[w, 1]], axis=1))
-        agg = stack(dot(amat[0], lo), dot(amat[G - 1], hi))
-        own = stack(field[w, 0:B], field[w, 3 * B :]).astype(F32)
-        base, tan = forward_rows(
-            own[:, 0:D] + agg[:, 0:D], own[:, D:] + agg[:, D:], 0, win, bias, wout, slope.at[w], True
-        )
-        tan_out[w] = tan
-        base, tan = base.astype(BF), tan.astype(BF)
-        send_left[w, 0] = base[0:B]
-        send_left[w, 1] = tan[0:B]
-        send_right[w, 0] = base[B:]
-        send_right[w, 1] = tan[B:]
+    lo = stack(jnp.concatenate([left[0], left[1]], axis=1), field[w, 0 : 2 * B])
+    hi = stack(field[w, 2 * B :], jnp.concatenate([right[0], right[1]], axis=1))
+    agg = stack(dot(amat[0], lo), dot(amat[G - 1], hi))
+    own = stack(field[w, 0:B], field[w, 3 * B :]).astype(F32)
+    base, tan = forward_rows(
+        own[:, 0:D] + agg[:, 0:D], own[:, D:] + agg[:, D:], 0, win, bias, wout, slope, True
+    )
+    tan_out[...] = tan
+    base, tan = base.astype(BF), tan.astype(BF)
+    send_left[0] = base[0:B]
+    send_left[1] = tan[0:B]
+    send_right[0] = base[B:]
+    send_right[1] = tan[B:]
 
 
 def inner1_kernel(
-    base_in, tan_in, lo, hi, field, e0, e0r, e1, e2, e3, win, bias, wout,
+    base_in, tan_in, lo0, lo1, hi0, hi1, field, e0, e0r, e1, e2, e3, win, bias, wout,
     amat, tmat, next_out, image, returned, hat, slope, nxt,
 ):
     y = member()
-    sort_edges(y, (e0, e1, e2, e3), 3 * B, amat, tmat)
+    sort_edges(y, (e0, e1, e2, e3), amat, tmat)
     pair_matrix(amat, hat)
     for k, e in enumerate((e0, e1, e2, e3)):
-        value = e[:, 6 * B :]
+        value = e[:, 3 * B :]
         if k == 0:
             value = jnp.where(y == G - 1, e0r[...], value)
         nxt[origin(y, k)] = value
     next_out[0:B] = nxt[0]
     next_out[B:] = nxt[G - 1]
     for w in range(NW):
-        base = stack(lo[w, 0], base_in[w], hi[w, 0])
-        tan = stack(lo[w, 1], tan_in[w].astype(BF), hi[w, 1])
+        lo, hi = (lo0, lo1)[w], (hi0, hi1)[w]
+        base = stack(lo[0], base_in[w], hi[0])
+        tan = stack(lo[1], tan_in[w].astype(BF), hi[1])
         base_sum = base_in[w].astype(F32) + dot(hat[...], base)
         tan_sum = tan_in[w] + dot(hat[...], tan)
         _, out = forward_rows(base_sum, tan_sum, 1, win, bias, wout, slope, False)
@@ -205,20 +209,22 @@
 
 
 def edge1_kernel(
-    lo, hi, tan_edge, base_in, tan_in, left, right, field, next_edge, amat, tmat, image_in, win, bias, wout,
+    lo0, lo1, hi0, hi1, tan0, tan1, left0, left1, right0, right1, base_in, tan_in, field, next_edge, amat, tmat, image_in, win, bias, wout,
     im0, im1, im2, im3, returned, send_left, send_right, slope, image,
 ):
     y = member()
     for w in range(NW):
+        lo, hi, tan_edge = (lo0, lo1)[w], (hi0, hi1)[w], (tan0, tan1)[w]
+        left, right = (left0, left1)[w], (right0, right1)[w]
         tan_mid = tan_in[w].astype(BF)
         agg = []
         for f, mid in ((0, base_in[w]), (1, tan_mid)):
             agg.append(stack(
-                dot(amat[0], stack(left[w, f], lo[w, f], mid[0:B])),
-                dot(amat[G - 1], stack(mid[B:], hi[w, f], right[w, f])),
+                dot(amat[0], stack(left[f], lo[f], mid[0:B])),
+                dot(amat[G - 1], stack(mid[B:], hi[f], right[f])),
             ))
-        base_sum = stack(lo[w, 0], hi[w, 0]).astype(F32) + agg[0]
-        _, out = forward_rows(base_sum, tan_edge[w] + agg[1], 1, win, bias, wout, slope, False)
+        base_sum = stack(lo[0], hi[0]).astype(F32) + agg[0]
+        _, out = forward_rows(base_sum, tan_edge[...] + agg[1], 1, win, bias, wout, slope, False)
         image[0, w] = out[0:B].astype(BF)
         image[1, w] = image_in[w, 0:B]
         image[2, w] = image_in[w, B:]
@@ -251,10 +257,10 @@
         returned[w] = adjoint_rows(current, 0, win, wout, slope.at[w])
 
 
-def edge2_kernel(cur_edge, left, right, tmat, slope, win, wout, returned, send_left, send_right):
+def edge2_kernel(cur_edge, left, right, tmat, slope0, slope1, win, wout, returned, send_left, send_right):
     for w in range(NW):
         current = cur_edge[w] + stack(left[w], right[w]).astype(F32)
-        back = adjoint_rows(current, 0, win, wout, slope.at[w])
+        back = adjoint_rows(current, 0, win, wout, (slope0, slope1)[w])
         returned[w] = back
         send_left[w] = dot(tmat[0, :, 0:B], back[0:B].astype(BF)).astype(BF)
         send_right[w] = dot(tmat[G - 1, :, 2 * B :], back[B:].astype(BF)).astype(BF)
@@ -359,50 +365,58 @@
 
 
 def local(states, increment, window_slots, edge_weights, inner_weight, inner_bias, outer_weight):
-    bias = inner_bias
-
-    item = sds((NW, 2, B, D))
+
+    item = sds((2, B, D))
     half = sds((NW, B, D))
     pair_bf = sds((NW, 2 * B, D))
     pair = sds((NW, 2 * B, D), F32)
     hidden = sds((NW, 2 * B, HID))
     mats = sds((G, B, 3 * B))
     hat = pltpu.VMEM((2 * B, 4 * B), BF)
-
-    sends = call(pack_kernel, (states, increment), [item] * (G - 1))
-    got = [None, *to_members([None, *sends])]
-    got[0], cross, *ext = call(
+    weights = (inner_weight, inner_bias, outer_weight)
+    both = ("tm", "mesh")
+
+    sends = call(pack_kernel, (states, increment), [item] * (NW * (G - 1)))
+    got = [to_members([None, *sends[w * (G - 1) : (w + 1) * (G - 1)]]) for w in range(NW)]
+    *own, a0, cross, ext, ext1, ext2, ext3 = call(
         fold_kernel, (window_slots, states, increment, edge_weights),
-        [item, sds((B, D))] + [sds((B, 6 * B + D))] * G, smem=1,
-    )
-    cross = lax.ppermute(cross, ("tm", "mesh"), next_increment_pairs(0))
-    ext = [ext[0]] + [lax.ppermute(ext[k], ("tm", "mesh"), next_increment_pairs(k)) for k in range(1, G)]
-
-    lo, hi = call(edge_kernel, got, [item, item])
-    left, right = swap_sides(lo, hi)
+        [item] * NW + [sds((B, 3 * B)), sds((B, D))] + [sds((B, 3 * B + D))] * G, smem=1,
+    )
+    a0 = [a0, *to_members([a0] * G)]
+    cross = lax.ppermute(cross, both, next_increment_pairs(0))
+    ext = [ext, cross] + [
+        lax.ppermute(e, both, next_increment_pairs(k + 1)) for k, e in enumerate((ext1, ext2, ext3))
+    ]
+
+    got = [[own[w], *got[w]] for w in range(NW)]
+    halo = []
+    for w in range(NW):
+        lo, hi = call(edge_kernel, got[w], [item, item])
+        halo.append(swap_sides(lo, hi))
     field, amat0, tmat0, base_in, tan_in, slope_in = call(
-        inner0_kernel, (*got, *ext, inner_weight, bias, outer_weight),
-        [sds((NW, G * B, 2 * D)), mats, mats, pair_bf, pair, hidden], (hat,)
-    )
-    lo, hi, tan_edge, slope_edge = call(
-        edge0_kernel, (field, amat0, left, right, inner_weight, bias, outer_weight),
-        [item, item, pair, hidden]
-    )
-
-    left, right = swap_sides(lo, hi)
+        inner0_kernel, (*got[0], *got[1], *a0, *weights),
+        [sds((NW, G * B, 2 * D)), mats, mats, pair_bf, pair, hidden], (hat,),
+    )
+    lo, hi, tan_edge, slope_edge, left, right = [], [], [], [], [], []
+    for w in range(NW):
+        out = call(
+            functools.partial(edge0_kernel, w), (field, amat0, *halo[w], *weights),
+            [item, item, sds((2 * B, D), F32), sds((2 * B, HID))],
+        )
+        for values, value in zip((lo, hi, tan_edge, slope_edge), out):
+            values.append(value)
+        for values, value in zip((left, right), swap_sides(out[0], out[1])):
+            values.append(value)
+
     slope1 = pltpu.VMEM((2 * B, HID), BF)
     amat1, tmat1, next_edge, image_in, inner = call(
-        inner1_kernel,
-        (base_in, tan_in, lo, hi, field, ext[0], cross, *ext[1:], inner_weight, bias, outer_weight),
-        [mats, mats, sds((2 * B, D)), pair_bf, pair],
-        (hat, slope1, pltpu.VMEM((G, B, D), BF))
+        inner1_kernel, (base_in, tan_in, *lo, *hi, field, *ext, *weights),
+        [mats, mats, sds((2 * B, D)), pair_bf, pair], (hat, slope1, pltpu.VMEM((G, B, D), BF)),
     )
     *images, edge, send_left, send_right = call(
         edge1_kernel,
-        (lo, hi, tan_edge, base_in, tan_in, left, right, field, next_edge, amat1, tmat1, image_in,
-         inner_weight, bias, outer_weight),
-        [half] * G + [pair, half, half],
-        (slope1, pltpu.VMEM((G, NW, B, D), BF))
+        (*lo, *hi, *tan_edge, *left, *right, base_in, tan_in, field, next_edge, amat1, tmat1, image_in, *weights),
+        [half] * G + [pair, half, half], (slope1, pltpu.VMEM((G, NW, B, D), BF)),
     )
 
     left, right = swap_sides(send_left, send_right)
@@ -412,7 +426,7 @@
         [pair, pair], (hat,)
     )
     edge, send_left, send_right = call(
-        edge2_kernel, (cur_edge, left, right, tmat0, slope_edge, inner_weight, outer_weight),
+        edge2_kernel, (cur_edge, left, right, tmat0, *slope_edge, inner_weight, outer_weight),
         [pair, half, half]
     )
 

time: 110 us -> 108 us (0.982)
  waiting for transfers between devices: 29.7 us -> 12.6 us
  starting transfers between devices: 59.3 us -> 74.4 us
    ppermute x4 -> x6, starting transfers between devices: 25.1 us -> 32.4 us  [swap_sides(): right = lax.ppermute(send_left, 'mesh', side_pairs(-1))]
    ppermute x4 -> x6, waiting for transfers between devices: 15.2 us -> 8.54 us  [swap_sides(): left = lax.ppermute(send_right, 'mesh', side_pairs(1))]
    ppermute x4 -> x6, waiting for transfers between devices: 5.74 us -> 0.02 us  [swap_sides(): right = lax.ppermute(send_left, 'mesh', side_pairs(-1))]
    ppermute x9 -> x15, waiting for transfers between devices: 7.46 us -> 2.74 us  [to_members(): return [lax.ppermute(sends[k], 'mesh', group_pairs(k)) for k in range(1, G)]]
    ppermute x4, starting transfers between devices: 9.23 us -> 12.9 us  [the longest x3 12.2 us: local(): lax.ppermute(e, both, next_increment_pairs(k + 1))]
    ppermute x1, starting transfers between devices: 4.88 us -> 6.97 us  [local(): before = lax.ppermute(last, 'tm', [(t, t + 1) for t in range(TM - 1)])]
    ppermute x4 -> x6, starting transfers between devices: 1.8 us -> 2.83 us  [swap_sides(): left = lax.ppermute(send_right, 'mesh', side_pairs(1))]
    ppermute x9 -> x15, starting transfers between devices: 18.3 us -> 19.2 us  [to_members(): return [lax.ppermute(sends[k], 'mesh', group_pairs(k)) for k in range(1, G)]]
  transfers between devices with their start and end apart: 22 -> 32, of which waited for: 8 -> 9; matrix products, arithmetic and copies ran while one was open for 0% -> 0% of each run, Pallas kernels for 9% -> 12%
where the time goes in v4:
time: 108 us
  starting transfers between devices  74.4 us (69%)
  Pallas kernels  17.2 us (16%)
  waiting for transfers between devices  12.6 us (12%)
  local copies, waits for them, and re-layouts  3.23 us (3%)
    ppermute x6, starting transfers between devices, swap_sides(): right = lax.ppermute(send_left, 'mesh', side_pairs(-1))  32.4 us
    ppermute x15, starting transfers between devices, to_members(): return [lax.ppermute(sends[k], 'mesh', group_pairs(k)) for k in range(1, G)]  19.2 us
    pallas_call x15, Pallas kernels, call(): pl.pallas_call(kernel, out_shape=outs, in_specs=[SMEM] * smem + [VMEM] *...  17.2 us
    ppermute x3, starting transfers between devices, local(): lax.ppermute(e, both, next_increment_pairs(k + 1))  12.2 us
    ppermute x6, waiting for transfers between devices, swap_sides(): left = lax.ppermute(send_right, 'mesh', side_pairs(1))  8.54 us
    ppermute x1, starting transfers between devices, local(): before = lax.ppermute(last, 'tm', [(t, t + 1) for t in range(TM - 1)])  6.97 us
    unnamed x18, local copies, waits for them, and re-layouts  3.23 us
    ppermute x6, starting transfers between devices, swap_sides(): left = lax.ppermute(send_right, 'mesh', side_pairs(1))  2.83 us
  transfers between devices with their start and end apart: 32, of which 9 were waited for; matrix products, arithmetic and copies ran while one was open for 0% of the time, Pallas kernels for 12%

profile of v4, /device:TPU:1, one launch (start us, length us, event | category | flops | bytes accessed | tf_op | source)
XLA Modules:
  0.0 108.2 jit_solution(10378947064188216239)
XLA Ops:
  0.6 1.2 %copy-done.2 = f32[8,128,256]{2,1,0:T(8,128)S(1)} copy-done((f32[8,128,256]{2,1,0:T(8,128)S(1)}, f32[8,128,256]{2,1,0:T(8,128)}, u32[]{:S(2)}) %copy-start.2) | copy-done | bytes 1048600
  3.0 2.2 %collective-permute-start = (bf16[2,128,256]{2,1,0:T(8,128)(2,1)S(1)}, bf16[2,128,256]{2,1,0:T(8,128)(2,1)S(1)}, u32[]{:S(2)}, u32[]{:S(2)}) collective-permute-start(bf16[2,128,256]{2,1,0:T(8,128)(2,1)S(1)} %get-tuple-element.61), channel_id=1, source_target_pairs={{0,1},{1,2},{2,3},{3,0},{4,5},{5,6},{6,7},{7,4},{8,9},{9,10},{10,1... | collective-permute-start | bytes 393224 | tf_op jit(solution)/shard_map/ppermute | solution.py:358
  5.2 2.6 %collective-permute-start.1 = (bf16[2,128,256]{2,1,0:T(8,128)(2,1)S(1)}, bf16[2,128,256]{2,1,0:T(8,128)(2,1)S(1)}, u32[]{:S(2)}, u32[]{:S(2)}) collective-permute-start(bf16[2,128,256]{2,1,0:T(8,128)(2,1)S(1)} %get-tuple-element.62), channel_id=1, source_target_pairs={{0,2},{1,3},{2,0},{3,1},{4,6},{5,7},{6,4},{7,5},{8,10},{9,11},{10,... | collective-permute-start | bytes 393224 | tf_op jit(solution)/shard_map/ppermute | solution.py:358
  10.0 1.7 %collective-permute-start.5 = (bf16[2,128,256]{2,1,0:T(8,128)(2,1)S(1)}, bf16[2,128,256]{2,1,0:T(8,128)(2,1)S(1)}, u32[]{:S(2)}, u32[]{:S(2)}) collective-permute-start(bf16[2,128,256]{2,1,0:T(8,128)(2,1)S(1)} %get-tuple-element.67), channel_id=1, source_target_pairs={{0,3},{1,0},{2,1},{3,2},{4,7},{5,4},{6,5},{7,6},{8,11},{9,8},{10,9... | collective-permute-start | bytes 393224 | tf_op jit(solution)/shard_map/ppermute | solution.py:358
  13.6 1.3 %collective-permute-start.9 = (bf16[2,128,256]{2,1,0:T(8,128)(2,1)S(1)}, bf16[2,128,256]{2,1,0:T(8,128)(2,1)S(1)}, u32[]{:S(2)}, u32[]{:S(2)}) collective-permute-start(bf16[2,128,256]{2,1,0:T(8,128)(2,1)S(1)} %get-tuple-element.71), channel_id=1, source_target_pairs={{0,4},{1,5},{2,6},{3,7},{4,8},{5,9},{6,10},{7,11},{8,12},{9,13},{1... | collective-permute-start | bytes 393224 | tf_op jit(solution)/shard_map/ppermute | solution.py:362
  14.9 2.2 %collective-permute-start.8 = (bf16[128,384]{1,0:T(8,128)(2,1)S(1)}, bf16[128,384]{1,0:T(8,128)(2,1)S(1)}, u32[]{:S(2)}, u32[]{:S(2)}) collective-permute-start(bf16[128,384]{1,0:T(8,128)(2,1)S(1)} %get-tuple-element.68.a0), channel_id=1, source_target_pairs={{0,3},{1,0},{2,1},{3,2},{4,7},{5,4},{6,5},{7,6},{8,11},{9,8},{10,9... | collective-permute-start | bytes 294920 | tf_op jit(solution)/shard_map/ppermute | solution.py:358
  19.2 1.3 %collective-permute-start.11 = (bf16[2,128,256]{2,1,0:T(8,128)(2,1)S(1)}, bf16[2,128,256]{2,1,0:T(8,128)(2,1)S(1)}, u32[]{:S(2)}, u32[]{:S(2)}) collective-permute-start(bf16[2,128,256]{2,1,0:T(8,128)(2,1)S(1)} %get-tuple-element.74), channel_id=1, source_target_pairs={{0,4},{1,5},{2,6},{3,7},{4,8},{5,9},{6,10},{7,11},{8,12},{9,13},{1... | collective-permute-start | bytes 393224 | tf_op jit(solution)/shard_map/ppermute | solution.py:362
  21.1 7.5 %collective-permute-start.12 = (bf16[2,128,256]{2,1,0:T(8,128)(2,1)S(1)}, bf16[2,128,256]{2,1,0:T(8,128)(2,1)S(1)}, u32[]{:S(2)}, u32[]{:S(2)}) collective-permute-start(bf16[2,128,256]{2,1,0:T(8,128)(2,1)S(1)} %get-tuple-element.75), channel_id=1, source_target_pairs={{0,60},{1,61},{2,62},{3,63},{4,0},{5,1},{6,2},{7,3},{8,4},{9,5},{1... | collective-permute-start | bytes 393224 | tf_op jit(solution)/shard_map/ppermute | solution.py:363
  28.6 2.2 %collective-permute-start.18 = (bf16[128,640]{1,0:T(8,128)(2,1)S(1)}, bf16[128,640]{1,0:T(8,128)(2,1)S(1)}, u32[]{:S(2)}, u32[]{:S(2)}) collective-permute-start(bf16[128,640]{1,0:T(8,128)(2,1)S(1)} %get-tuple-element.85), channel_id=1, source_target_pairs={{0,1},{1,2},{2,195},{3,0},{4,5},{5,6},{6,199},{7,4},{8,9},{9,10},{... | collective-permute-start | bytes 491528 | tf_op jit(solution)/shard_map/ppermute | solution.py:388
  30.8 5.9 %collective-permute-start.19 = (bf16[128,640]{1,0:T(8,128)(2,1)S(1)}, bf16[128,640]{1,0:T(8,128)(2,1)S(1)}, u32[]{:S(2)}, u32[]{:S(2)}) collective-permute-start(bf16[128,640]{1,0:T(8,128)(2,1)S(1)} %get-tuple-element.86), channel_id=1, source_target_pairs={{0,2},{1,195},{2,0},{3,1},{4,6},{5,199},{6,4},{7,5},{8,10},{9,203}... | collective-permute-start | bytes 491528 | tf_op jit(solution)/shard_map/ppermute | solution.py:388
  36.7 1.4 %collective-permute-start.10 = (bf16[2,128,256]{2,1,0:T(8,128)(2,1)S(1)}, bf16[2,128,256]{2,1,0:T(8,128)(2,1)S(1)}, u32[]{:S(2)}, u32[]{:S(2)}) collective-permute-start(bf16[2,128,256]{2,1,0:T(8,128)(2,1)S(1)} %get-tuple-element.72), channel_id=1, source_target_pairs={{0,60},{1,61},{2,62},{3,63},{4,0},{5,1},{6,2},{7,3},{8,4},{9,5},{1... | collective-permute-start | bytes 393224 | tf_op jit(solution)/shard_map/ppermute | solution.py:363
  38.8 4.1 %collective-permute-start.20 = (bf16[128,640]{1,0:T(8,128)(2,1)S(1)}, bf16[128,640]{1,0:T(8,128)(2,1)S(1)}, u32[]{:S(2)}, u32[]{:S(2)}) collective-permute-start(bf16[128,640]{1,0:T(8,128)(2,1)S(1)} %get-tuple-element.87), channel_id=1, source_target_pairs={{0,195},{1,0},{2,1},{3,2},{4,199},{5,4},{6,5},{7,6},{8,203},{9,8},... | collective-permute-start | bytes 491528 | tf_op jit(solution)/shard_map/ppermute | solution.py:388
  43.0 2.2 %shard_map.88 = (bf16[2,512,512]{2,1,0:T(8,128)(2,1)S(1)}, bf16[4,128,384]{2,1,0:T(8,128)(2,1)S(1)}, bf16[4,128,384]{2,1,0:T(8,128)(2,1)S(1)}, bf16[2,256,256]{2...) custom-call(bf16[2,128,256]{2,1,0:T(8,128)(2,1)S(1)} %get-tuple-element.60.r00.r0, ...), custom_call_target="tpu_custom_call" | custom-call | tf_op jit(solution)/shard_map/pallas_call | solution.py:327
  45.2 1.1 %shard_map.92 = (bf16[2,128,256]{2,1,0:T(8,128)(2,1)S(1)}, bf16[2,128,256]{2,1,0:T(8,128)(2,1)S(1)}, f32[256,256]{1,0:T(8,128)S(1)}, bf16[256,1024]{1,0:T(8,128)(2,1)S(1)}) custom-call(bf16[2,512,512]{2,1,0:T(8,128)(2,1)S(1)} %get-tuple-element.69.field, bf16[4,128,384]{2,1,0:T(8,128)(2,1)S(1)} %get-tuple-element.70.amat, ...), custom_call_target="tpu_custom_call" | custom-call | tf_op jit(solution)/shard_map/pallas_call | solution.py:327
  46.4 6.5 %collective-permute-start.16 = (bf16[2,128,256]{2,1,0:T(8,128)(2,1)S(1)}, bf16[2,128,256]{2,1,0:T(8,128)(2,1)S(1)}, u32[]{:S(2)}, u32[]{:S(2)}) collective-permute-start(bf16[2,128,256]{2,1,0:T(8,128)(2,1)S(1)} %get-tuple-element.76.lo1), channel_id=1, source_target_pairs={{0,60},{1,61},{2,62},{3,63},{4,0},{5,1},{6,2},{7,3},{8,4},{9,5},{1... | collective-permute-start | bytes 393224 | tf_op jit(solution)/shard_map/ppermute | solution.py:363
  52.8 1.1 %shard_map.90 = (bf16[2,128,256]{2,1,0:T(8,128)(2,1)S(1)}, bf16[2,128,256]{2,1,0:T(8,128)(2,1)S(1)}, f32[256,256]{1,0:T(8,128)S(1)}, bf16[256,1024]{1,0:T(8,128)(2,1)S(1)}) custom-call(bf16[2,512,512]{2,1,0:T(8,128)(2,1)S(1)} %get-tuple-element.69.field, bf16[4,128,384]{2,1,0:T(8,128)(2,1)S(1)} %get-tuple-element.70.amat, ...), custom_call_target="tpu_custom_call" | custom-call | tf_op jit(solution)/shard_map/pallas_call | solution.py:327
  54.1 5.7 %collective-permute-start.15 = (bf16[2,128,256]{2,1,0:T(8,128)(2,1)S(1)}, bf16[2,128,256]{2,1,0:T(8,128)(2,1)S(1)}, u32[]{:S(2)}, u32[]{:S(2)}) collective-permute-start(bf16[2,128,256]{2,1,0:T(8,128)(2,1)S(1)} %get-tuple-element.73.lo0), channel_id=1, source_target_pairs={{0,60},{1,61},{2,62},{3,63},{4,0},{5,1},{6,2},{7,3},{8,4},{9,5},{1... | collective-permute-start | bytes 393224 | tf_op jit(solution)/shard_map/ppermute | solution.py:363
  59.8 3.0 %shard_map.93 = (bf16[4,128,384]{2,1,0:T(8,128)(2,1)S(1)}, bf16[4,128,384]{2,1,0:T(8,128)(2,1)S(1)}, bf16[256,256]{1,0:T(8,128)(2,1)S(1)}, bf16[2,256,256]{2,1,0:T(8,128)(2,1)S(1)}, f32[2,256,256]{2,1,0:T(8,128)S(1)}) custom-call(bf16[2,256,256]{2,1,0:T(8,128)(2,1)S(1)} %get-tuple-element.81.base_in, f32[2,256,256]{2,1,0:T(8,128)S(1)} %get-tuple-element.82.tan_in, ...), custom_call_target="tpu_custom_call" | custom-call | tf_op jit(solution)/shard_map/pallas_call | solution.py:327
  62.8 2.3 %collective-permute-done.14.left1 = bf16[2,128,256]{2,1,0:T(8,128)(2,1)S(1)} collective-permute-done((bf16[2,128,256]{2,1,0:T(8,128)(2,1)S(1)}, bf16[2,128,256]{2,1,0:T(8,128)(2,1)S(1)}, u32[]{:S(2)}, u32[]{:S(2)}) %collective-permute-start.14) | collective-permute-done | bytes 131104 | tf_op jit(solution)/shard_map/ppermute | solution.py:362
  65.1 3.1 %collective-permute-done.13.left0 = bf16[2,128,256]{2,1,0:T(8,128)(2,1)S(1)} collective-permute-done((bf16[2,128,256]{2,1,0:T(8,128)(2,1)S(1)}, bf16[2,128,256]{2,1,0:T(8,128)(2,1)S(1)}, u32[]{:S(2)}, u32[]{:S(2)}) %collective-permute-start.13) | collective-permute-done | bytes 131104 | tf_op jit(solution)/shard_map/ppermute | solution.py:362
  68.2 3.3 %shard_map.94 = (bf16[2,128,256]{2,1,0:T(8,128)(2,1)S(1)}, bf16[2,128,256]{2,1,0:T(8,128)(2,1)S(1)}, bf16[2,128,256]{2,1,0:T(8,128)(2,1)S(1)}, bf16[2,128,256]{2...) custom-call(bf16[2,128,256]{2,1,0:T(8,128)(2,1)S(1)} %get-tuple-elem, ...), custom_call_target="tpu_custom_call" | custom-call | tf_op jit(solution)/shard_map/pallas_call | solution.py:327
  71.6 5.7 %collective-permute-start.25 = (bf16[2,128,256]{2,1,0:T(8,128)(2,1)S(1)}, bf16[2,128,256]{2,1,0:T(8,128)(2,1)S(1)}, u32[]{:S(2)}, u32[]{:S(2)}) collective-permute-start(bf16[2,128,256]{2,1,0:T(8,128)(2,1)S(1)} %get-tuple-element.102), channel_id=1, source_target_pairs={{0,60},{1,61},{2,62},{3,63},{4,0},{5,1},{6,2},{7,3},{8,4},{9,5},{1... | collective-permute-start | bytes 393224 | tf_op jit(solution)/shard_map/ppermute | solution.py:363
  77.3 2.7 %collective-permute-start.23 = (bf16[2,128,256]{2,1,0:T(8,128)(2,1)S(1)}, bf16[2,128,256]{2,1,0:T(8,128)(2,1)S(1)}, u32[]{:S(2)}, u32[]{:S(2)}) collective-permute-start(bf16[2,128,256]{2,1,0:T(8,128)(2,1)S(1)} %get-tuple-element.95), channel_id=1, source_target_pairs={{0,3},{1,0},{2,1},{3,2},{4,7},{5,4},{6,5},{7,6},{8,11},{9,8},{10,9... | collective-permute-start | bytes 393224 | tf_op jit(solution)/shard_map/ppermute | solution.py:358
  80.0 1.4 %shard_map.95 = (f32[2,256,256]{2,1,0:T(8,128)S(1)}, f32[2,256,256]{2,1,0:T(8,128)S(1)}) custom-call(f32[2,256,256]{2,1,0:T(8,128)S(1)} %get-tuple-element.96.inner, f32[2,256,256]{2,1,0:T(8,128)S(1)} %get-tuple-element.97.edge, bf16[4,128,384]{2,1,0:T(8,128)(2,1)S(1)} %get-tuple-element.90.tmat, bf16[2,256,1024]{2,1,0:T(8,128)(2,1)S(1)} %get-tuple-element.98.slope, ...), custom_call_target="tpu_custom_call" | custom-call | tf_op jit(solution)/shard_map/pallas_call | solution.py:327
  82.3 1.3 %shard_map.96 = (f32[2,256,256]{2,1,0:T(8,128)S(1)}, bf16[2,128,256]{2,1,0:T(8,128)(2,1)S(1)}, bf16[2,128,256]{2,1,0:T(8,128)(2,1)S(1)}) custom-call(f32[2,256,256]{2,1,0:T(8,128)S(1)} %get-tuple-element.100.cur_edge, bf16[2,128,256]{2,1,0:T(8,128)(2,1)S(1)} %collective-permute-done.24.left, bf16[2,128,256]{2,1,0:T(8,128)(2,1)S(1)} %collective-permute-done.25.right, ...), custom_call_target="tpu_custom_call" | custom-call | tf_op jit(solution)/shard_map/pallas_call | solution.py:327
  83.7 5.7 %collective-permute-start.28 = (bf16[2,128,256]{2,1,0:T(8,128)(2,1)S(1)}, bf16[2,128,256]{2,1,0:T(8,128)(2,1)S(1)}, u32[]{:S(2)}, u32[]{:S(2)}) collective-permute-start(bf16[2,128,256]{2,1,0:T(8,128)(2,1)S(1)} %get-tuple-element.113), channel_id=1, source_target_pairs={{0,60},{1,61},{2,62},{3,63},{4,0},{5,1},{6,2},{7,3},{8,4},{9,5},{1... | collective-permute-start | bytes 393224 | tf_op jit(solution)/shard_map/ppermute | solution.py:363
  89.8 2.2 %collective-permute-done.27.left = bf16[2,128,256]{2,1,0:T(8,128)(2,1)S(1)} collective-permute-done((bf16[2,128,256]{2,1,0:T(8,128)(2,1)S(1)}, bf16[2,128,256]{2,1,0:T(8,128)(2,1)S(1)}, u32[]{:S(2)}, u32[]{:S(2)}) %collective-permute-start.27) | collective-permute-done | bytes 131104 | tf_op jit(solution)/shard_map/ppermute | solution.py:362
  93.1 2.6 %collective-permute-start.30 = (bf16[2,128,256]{2,1,0:T(8,128)(2,1)S(1)}, bf16[2,128,256]{2,1,0:T(8,128)(2,1)S(1)}, u32[]{:S(2)}, u32[]{:S(2)}) collective-permute-start(bf16[2,128,256]{2,1,0:T(8,128)(2,1)S(1)} %get-tuple-element.116), channel_id=1, source_target_pairs={{0,2},{1,3},{2,0},{3,1},{4,6},{5,7},{6,4},{7,5},{8,10},{9,11},{10,... | collective-permute-start | bytes 393224 | tf_op jit(solution)/shard_map/ppermute | solution.py:358
  95.8 2.0 %collective-permute-start.31 = (bf16[2,128,256]{2,1,0:T(8,128)(2,1)S(1)}, bf16[2,128,256]{2,1,0:T(8,128)(2,1)S(1)}, u32[]{:S(2)}, u32[]{:S(2)}) collective-permute-start(bf16[2,128,256]{2,1,0:T(8,128)(2,1)S(1)} %get-tuple-element.117), channel_id=1, source_target_pairs={{0,3},{1,0},{2,1},{3,2},{4,7},{5,4},{6,5},{7,6},{8,11},{9,8},{10,9... | collective-permute-start | bytes 393224 | tf_op jit(solution)/shard_map/ppermute | solution.py:358
  97.7 7.0 %collective-permute-start.26 = (bf16[128,256]{1,0:T(8,128)(2,1)S(1)}, bf16[128,256]{1,0:T(8,128)(2,1)S(1)}, u32[]{:S(2)}, u32[]{:S(2)}) collective-permute-start(bf16[128,256]{1,0:T(8,128)(2,1)S(1)} %get-tuple-element.107), channel_id=1, source_target_pairs={{0,64},{64,128},{128,192},{1,65},{65,129},{129,193},{2,66},{66,130... | collective-permute-start | bytes 196616 | tf_op jit(solution)/shard_map/ppermute | solution.py:437
  104.7 1.3 %collective-permute-done.26.before = bf16[128,256]{1,0:T(8,128)(2,1)S(1)} collective-permute-done((bf16[128,256]{1,0:T(8,128)(2,1)S(1)}, bf16[128,256]{1,0:T(8,128)(2,1)S(1)}, u32[]{:S(2)}, u32[]{:S(2)}) %collective-permute-start.26) | collective-permute-done | bytes 65568 | tf_op jit(solution)/shard_map/ppermute | solution.py:437
  106.0 1.1 %shard_map.98 = (f32[8,128,256]{2,1,0:T(8,128)}, f32[8,128,256]{2,1,0:T(8,128)S(1)}) custom-call(f32[8,128,256]{2,1,0:T(8,128)S(1)} %copy-done.3, bf16[2,128,256]{2,1,0:T(8,128)(2,1)S(1)} %get-tuple-element.92.i0, bf16[2,128,256]{2,1,0:T(8,128)(2,1)S(1)} %collective-permute-done.21.i1, bf16[2,128,256]{2,1,0:T(8,128)(2,1)S(1)} %collective-permute-done.22.i2, ...), custom_call_target="tpu_custom_call" | custom-call | tf_op jit(solution)/shard_map/pallas_call | solution.py:327
  (65 shorter events, 12.4 us)
Async XLA Ops:
  3.0 7.1 %collective-permute-start = (bf16[2,128,256]{2,1,0:T(8,128)(2,1)S(1)}, bf16[2,128,256]{2,1,0:T(8,128)(2,1)S(1)}, u32[]{:S(2)}, u32[]{:S(2)}) collective-permute-start(bf16[2,128,256]{2,1,0:T(8,128)(2,1)S(1)} %get-tuple-element.61), channel_id=1, source_target_pairs={{0,1},{1,2},{2,3},{3,0},{4,5},{5,6},{6,7},{7,4},{8,9},{9,10},{10,1... | collective-permute-start | bytes 393224 | tf_op jit(solution)/shard_map/ppermute | solution.py:358
  5.2 8.3 %collective-permute-start.1 = (bf16[2,128,256]{2,1,0:T(8,128)(2,1)S(1)}, bf16[2,128,256]{2,1,0:T(8,128)(2,1)S(1)}, u32[]{:S(2)}, u32[]{:S(2)}) collective-permute-start(bf16[2,128,256]{2,1,0:T(8,128)(2,1)S(1)} %get-tuple-element.62), channel_id=1, source_target_pairs={{0,2},{1,3},{2,0},{3,1},{4,6},{5,7},{6,4},{7,5},{8,10},{9,11},{10,... | collective-permute-start | bytes 393224 | tf_op jit(solution)/shard_map/ppermute | solution.py:358
  7.8 5.7 %collective-permute-start.2 = (bf16[2,128,256]{2,1,0:T(8,128)(2,1)S(1)}, bf16[2,128,256]{2,1,0:T(8,128)(2,1)S(1)}, u32[]{:S(2)}, u32[]{:S(2)}) collective-permute-start(bf16[2,128,256]{2,1,0:T(8,128)(2,1)S(1)} %get-tuple-element.63), channel_id=1, source_target_pairs={{0,3},{1,0},{2,1},{3,2},{4,7},{5,4},{6,5},{7,6},{8,11},{9,8},{10,9... | collective-permute-start | bytes 393224 | tf_op jit(solution)/shard_map/ppermute | solution.py:358
  8.9 9.3 %collective-permute-start.3 = (bf16[2,128,256]{2,1,0:T(8,128)(2,1)S(1)}, bf16[2,128,256]{2,1,0:T(8,128)(2,1)S(1)}, u32[]{:S(2)}, u32[]{:S(2)}) collective-permute-start(bf16[2,128,256]{2,1,0:T(8,128)(2,1)S(1)} %get-tuple-element.65), channel_id=1, source_target_pairs={{0,1},{1,2},{2,3},{3,0},{4,5},{5,6},{6,7},{7,4},{8,9},{9,10},{10,1... | collective-permute-start | bytes 393224 | tf_op jit(solution)/shard_map/ppermute | solution.py:358
  9.3 9.9 %collective-permute-start.4 = (bf16[2,128,256]{2,1,0:T(8,128)(2,1)S(1)}, bf16[2,128,256]{2,1,0:T(8,128)(2,1)S(1)}, u32[]{:S(2)}, u32[]{:S(2)}) collective-permute-start(bf16[2,128,256]{2,1,0:T(8,128)(2,1)S(1)} %get-tuple-element.66), channel_id=1, source_target_pairs={{0,2},{1,3},{2,0},{3,1},{4,6},{5,7},{6,4},{7,5},{8,10},{9,11},{10,... | collective-permute-start | bytes 393224 | tf_op jit(solution)/shard_map/ppermute | solution.py:358
  10.0 9.1 %collective-permute-start.5 = (bf16[2,128,256]{2,1,0:T(8,128)(2,1)S(1)}, bf16[2,128,256]{2,1,0:T(8,128)(2,1)S(1)}, u32[]{:S(2)}, u32[]{:S(2)}) collective-permute-start(bf16[2,128,256]{2,1,0:T(8,128)(2,1)S(1)} %get-tuple-element.67), channel_id=1, source_target_pairs={{0,3},{1,0},{2,1},{3,2},{4,7},{5,4},{6,5},{7,6},{8,11},{9,8},{10,9... | collective-permute-start | bytes 393224 | tf_op jit(solution)/shard_map/ppermute | solution.py:358
  13.6 23.2 %collective-permute-start.9 = (bf16[2,128,256]{2,1,0:T(8,128)(2,1)S(1)}, bf16[2,128,256]{2,1,0:T(8,128)(2,1)S(1)}, u32[]{:S(2)}, u32[]{:S(2)}) collective-permute-start(bf16[2,128,256]{2,1,0:T(8,128)(2,1)S(1)} %get-tuple-element.71), channel_id=1, source_target_pairs={{0,4},{1,5},{2,6},{3,7},{4,8},{5,9},{6,10},{7,11},{8,12},{9,13},{1... | collective-permute-start | bytes 393224 | tf_op jit(solution)/shard_map/ppermute | solution.py:362
  14.9 6.2 %collective-permute-start.8 = (bf16[128,384]{1,0:T(8,128)(2,1)S(1)}, bf16[128,384]{1,0:T(8,128)(2,1)S(1)}, u32[]{:S(2)}, u32[]{:S(2)}) collective-permute-start(bf16[128,384]{1,0:T(8,128)(2,1)S(1)} %get-tuple-element.68.a0), channel_id=1, source_target_pairs={{0,3},{1,0},{2,1},{3,2},{4,7},{5,4},{6,5},{7,6},{8,11},{9,8},{10,9... | collective-permute-start | bytes 294920 | tf_op jit(solution)/shard_map/ppermute | solution.py:358
  18.1 10.5 %collective-permute-start.7 = (bf16[128,384]{1,0:T(8,128)(2,1)S(1)}, bf16[128,384]{1,0:T(8,128)(2,1)S(1)}, u32[]{:S(2)}, u32[]{:S(2)}) collective-permute-start(bf16[128,384]{1,0:T(8,128)(2,1)S(1)} %get-tuple-element.68.a0), channel_id=1, source_target_pairs={{0,2},{1,3},{2,0},{3,1},{4,6},{5,7},{6,4},{7,5},{8,10},{9,11},{10,... | collective-permute-start | bytes 294920 | tf_op jit(solution)/shard_map/ppermute | solution.py:358
  19.1 11.7 %collective-permute-start.6 = (bf16[128,384]{1,0:T(8,128)(2,1)S(1)}, bf16[128,384]{1,0:T(8,128)(2,1)S(1)}, u32[]{:S(2)}, u32[]{:S(2)}) collective-permute-start(bf16[128,384]{1,0:T(8,128)(2,1)S(1)} %get-tuple-element.68.a0), channel_id=1, source_target_pairs={{0,1},{1,2},{2,3},{3,0},{4,5},{5,6},{6,7},{7,4},{8,9},{9,10},{10,1... | collective-permute-start | bytes 294920 | tf_op jit(solution)/shard_map/ppermute | solution.py:358
  19.2 19.0 %collective-permute-start.11 = (bf16[2,128,256]{2,1,0:T(8,128)(2,1)S(1)}, bf16[2,128,256]{2,1,0:T(8,128)(2,1)S(1)}, u32[]{:S(2)}, u32[]{:S(2)}) collective-permute-start(bf16[2,128,256]{2,1,0:T(8,128)(2,1)S(1)} %get-tuple-element.74), channel_id=1, source_target_pairs={{0,4},{1,5},{2,6},{3,7},{4,8},{5,9},{6,10},{7,11},{8,12},{9,13},{1... | collective-permute-start | bytes 393224 | tf_op jit(solution)/shard_map/ppermute | solution.py:362
  21.1 17.8 %collective-permute-start.12 = (bf16[2,128,256]{2,1,0:T(8,128)(2,1)S(1)}, bf16[2,128,256]{2,1,0:T(8,128)(2,1)S(1)}, u32[]{:S(2)}, u32[]{:S(2)}) collective-permute-start(bf16[2,128,256]{2,1,0:T(8,128)(2,1)S(1)} %get-tuple-element.75), channel_id=1, source_target_pairs={{0,60},{1,61},{2,62},{3,63},{4,0},{5,1},{6,2},{7,3},{8,4},{9,5},{1... | collective-permute-start | bytes 393224 | tf_op jit(solution)/shard_map/ppermute | solution.py:363
  28.6 25.5 %collective-permute-start.18 = (bf16[128,640]{1,0:T(8,128)(2,1)S(1)}, bf16[128,640]{1,0:T(8,128)(2,1)S(1)}, u32[]{:S(2)}, u32[]{:S(2)}) collective-permute-start(bf16[128,640]{1,0:T(8,128)(2,1)S(1)} %get-tuple-element.85), channel_id=1, source_target_pairs={{0,1},{1,2},{2,195},{3,0},{4,5},{5,6},{6,199},{7,4},{8,9},{9,10},{... | collective-permute-start | bytes 491528 | tf_op jit(solution)/shard_map/ppermute | solution.py:388
  30.8 28.9 %collective-permute-start.19 = (bf16[128,640]{1,0:T(8,128)(2,1)S(1)}, bf16[128,640]{1,0:T(8,128)(2,1)S(1)}, u32[]{:S(2)}, u32[]{:S(2)}) collective-permute-start(bf16[128,640]{1,0:T(8,128)(2,1)S(1)} %get-tuple-element.86), channel_id=1, source_target_pairs={{0,2},{1,195},{2,0},{3,1},{4,6},{5,199},{6,4},{7,5},{8,10},{9,203}... | collective-permute-start | bytes 491528 | tf_op jit(solution)/shard_map/ppermute | solution.py:388
  36.7 9.6 %collective-permute-start.10 = (bf16[2,128,256]{2,1,0:T(8,128)(2,1)S(1)}, bf16[2,128,256]{2,1,0:T(8,128)(2,1)S(1)}, u32[]{:S(2)}, u32[]{:S(2)}) collective-permute-start(bf16[2,128,256]{2,1,0:T(8,128)(2,1)S(1)} %get-tuple-element.72), channel_id=1, source_target_pairs={{0,60},{1,61},{2,62},{3,63},{4,0},{5,1},{6,2},{7,3},{8,4},{9,5},{1... | collective-permute-start | bytes 393224 | tf_op jit(solution)/shard_map/ppermute | solution.py:363
  38.2 15.8 %collective-permute-start.17 = (bf16[128,256]{1,0:T(8,128)(2,1)S(1)}, bf16[128,256]{1,0:T(8,128)(2,1)S(1)}, u32[]{:S(2)}, u32[]{:S(2)}) collective-permute-start(bf16[128,256]{1,0:T(8,128)(2,1)S(1)} %get-tuple-element.84), channel_id=1, source_target_pairs={{3,195},{7,199},{11,203},{15,207},{19,211},{23,215},{27,219},{31,2... | collective-permute-start | bytes 196616 | tf_op jit(solution)/shard_map/ppermute | solution.py:386
  38.8 20.9 %collective-permute-start.20 = (bf16[128,640]{1,0:T(8,128)(2,1)S(1)}, bf16[128,640]{1,0:T(8,128)(2,1)S(1)}, u32[]{:S(2)}, u32[]{:S(2)}) collective-permute-start(bf16[128,640]{1,0:T(8,128)(2,1)S(1)} %get-tuple-element.87), channel_id=1, source_target_pairs={{0,195},{1,0},{2,1},{3,2},{4,199},{5,4},{6,5},{7,6},{8,203},{9,8},... | collective-permute-start | bytes 491528 | tf_op jit(solution)/shard_map/ppermute | solution.py:388
  46.4 16.4 %collective-permute-start.16 = (bf16[2,128,256]{2,1,0:T(8,128)(2,1)S(1)}, bf16[2,128,256]{2,1,0:T(8,128)(2,1)S(1)}, u32[]{:S(2)}, u32[]{:S(2)}) collective-permute-start(bf16[2,128,256]{2,1,0:T(8,128)(2,1)S(1)} %get-tuple-element.76.lo1), channel_id=1, source_target_pairs={{0,60},{1,61},{2,62},{3,63},{4,0},{5,1},{6,2},{7,3},{8,4},{9,5},{1... | collective-permute-start | bytes 393224 | tf_op jit(solution)/shard_map/ppermute | solution.py:363
  54.0 11.1 %collective-permute-start.14 = (bf16[2,128,256]{2,1,0:T(8,128)(2,1)S(1)}, bf16[2,128,256]{2,1,0:T(8,128)(2,1)S(1)}, u32[]{:S(2)}, u32[]{:S(2)}) collective-permute-start(bf16[2,128,256]{2,1,0:T(8,128)(2,1)S(1)} %get-tuple-element.78.hi1), channel_id=1, source_target_pairs={{0,4},{1,5},{2,6},{3,7},{4,8},{5,9},{6,10},{7,11},{8,12},{9,13},{1... | collective-permute-start | bytes 393224 | tf_op jit(solution)/shard_map/ppermute | solution.py:362
  54.1 11.1 %collective-permute-start.15 = (bf16[2,128,256]{2,1,0:T(8,128)(2,1)S(1)}, bf16[2,128,256]{2,1,0:T(8,128)(2,1)S(1)}, u32[]{:S(2)}, u32[]{:S(2)}) collective-permute-start(bf16[2,128,256]{2,1,0:T(8,128)(2,1)S(1)} %get-tuple-element.73.lo0), channel_id=1, source_target_pairs={{0,60},{1,61},{2,62},{3,63},{4,0},{5,1},{6,2},{7,3},{8,4},{9,5},{1... | collective-permute-start | bytes 393224 | tf_op jit(solution)/shard_map/ppermute | solution.py:363
  59.8 8.5 %collective-permute-start.13 = (bf16[2,128,256]{2,1,0:T(8,128)(2,1)S(1)}, bf16[2,128,256]{2,1,0:T(8,128)(2,1)S(1)}, u32[]{:S(2)}, u32[]{:S(2)}) collective-permute-start(bf16[2,128,256]{2,1,0:T(8,128)(2,1)S(1)} %get-tuple-element.77.hi0), channel_id=1, source_target_pairs={{0,4},{1,5},{2,6},{3,7},{4,8},{5,9},{6,10},{7,11},{8,12},{9,13},{1... | collective-permute-start | bytes 393224 | tf_op jit(solution)/shard_map/ppermute | solution.py:362
  71.5 10.7 %collective-permute-start.24 = (bf16[2,128,256]{2,1,0:T(8,128)(2,1)S(1)}, bf16[2,128,256]{2,1,0:T(8,128)(2,1)S(1)}, u32[]{:S(2)}, u32[]{:S(2)}) collective-permute-start(bf16[2,128,256]{2,1,0:T(8,128)(2,1)S(1)} %get-tuple-element.101), channel_id=1, source_target_pairs={{0,4},{1,5},{2,6},{3,7},{4,8},{5,9},{6,10},{7,11},{8,12},{9,13},{1... | collective-permute-start | bytes 393224 | tf_op jit(solution)/shard_map/ppermute | solution.py:362
  71.6 10.7 %collective-permute-start.25 = (bf16[2,128,256]{2,1,0:T(8,128)(2,1)S(1)}, bf16[2,128,256]{2,1,0:T(8,128)(2,1)S(1)}, u32[]{:S(2)}, u32[]{:S(2)}) collective-permute-start(bf16[2,128,256]{2,1,0:T(8,128)(2,1)S(1)} %get-tuple-element.102), channel_id=1, source_target_pairs={{0,60},{1,61},{2,62},{3,63},{4,0},{5,1},{6,2},{7,3},{8,4},{9,5},{1... | collective-permute-start | bytes 393224 | tf_op jit(solution)/shard_map/ppermute | solution.py:363
  77.3 12.1 %collective-permute-start.21 = (bf16[2,128,256]{2,1,0:T(8,128)(2,1)S(1)}, bf16[2,128,256]{2,1,0:T(8,128)(2,1)S(1)}, u32[]{:S(2)}, u32[]{:S(2)}) collective-permute-start(bf16[2,128,256]{2,1,0:T(8,128)(2,1)S(1)} %get-tuple-element.93), channel_id=1, source_target_pairs={{0,1},{1,2},{2,3},{3,0},{4,5},{5,6},{6,7},{7,4},{8,9},{9,10},{10,1... | collective-permute-start | bytes 393224 | tf_op jit(solution)/shard_map/ppermute | solution.py:358
  77.3 12.1 %collective-permute-start.22 = (bf16[2,128,256]{2,1,0:T(8,128)(2,1)S(1)}, bf16[2,128,256]{2,1,0:T(8,128)(2,1)S(1)}, u32[]{:S(2)}, u32[]{:S(2)}) collective-permute-start(bf16[2,128,256]{2,1,0:T(8,128)(2,1)S(1)} %get-tuple-element.94), channel_id=1, source_target_pairs={{0,2},{1,3},{2,0},{3,1},{4,6},{5,7},{6,4},{7,5},{8,10},{9,11},{10,... | collective-permute-start | bytes 393224 | tf_op jit(solution)/shard_map/ppermute | solution.py:358
  77.3 12.1 %collective-permute-start.23 = (bf16[2,128,256]{2,1,0:T(8,128)(2,1)S(1)}, bf16[2,128,256]{2,1,0:T(8,128)(2,1)S(1)}, u32[]{:S(2)}, u32[]{:S(2)}) collective-permute-start(bf16[2,128,256]{2,1,0:T(8,128)(2,1)S(1)} %get-tuple-element.95), channel_id=1, source_target_pairs={{0,3},{1,0},{2,1},{3,2},{4,7},{5,4},{6,5},{7,6},{8,11},{9,8},{10,9... | collective-permute-start | bytes 393224 | tf_op jit(solution)/shard_map/ppermute | solution.py:358
  83.6 8.4 %collective-permute-start.27 = (bf16[2,128,256]{2,1,0:T(8,128)(2,1)S(1)}, bf16[2,128,256]{2,1,0:T(8,128)(2,1)S(1)}, u32[]{:S(2)}, u32[]{:S(2)}) collective-permute-start(bf16[2,128,256]{2,1,0:T(8,128)(2,1)S(1)} %get-tuple-element.112), channel_id=1, source_target_pairs={{0,4},{1,5},{2,6},{3,7},{4,8},{5,9},{6,10},{7,11},{8,12},{9,13},{1... | collective-permute-start | bytes 393224 | tf_op jit(solution)/shard_map/ppermute | solution.py:362
  83.7 8.3 %collective-permute-start.28 = (bf16[2,128,256]{2,1,0:T(8,128)(2,1)S(1)}, bf16[2,128,256]{2,1,0:T(8,128)(2,1)S(1)}, u32[]{:S(2)}, u32[]{:S(2)}) collective-permute-start(bf16[2,128,256]{2,1,0:T(8,128)(2,1)S(1)} %get-tuple-element.113), channel_id=1, source_target_pairs={{0,60},{1,61},{2,62},{3,63},{4,0},{5,1},{6,2},{7,3},{8,4},{9,5},{1... | collective-permute-start | bytes 393224 | tf_op jit(solution)/shard_map/ppermute | solution.py:363
  92.1 15.0 %collective-permute-start.29 = (bf16[2,128,256]{2,1,0:T(8,128)(2,1)S(1)}, bf16[2,128,256]{2,1,0:T(8,128)(2,1)S(1)}, u32[]{:S(2)}, u32[]{:S(2)}) collective-permute-start(bf16[2,128,256]{2,1,0:T(8,128)(2,1)S(1)} %get-tuple-element.115), channel_id=1, source_target_pairs={{0,1},{1,2},{2,3},{3,0},{4,5},{5,6},{6,7},{7,4},{8,9},{9,10},{10,1... | collective-permute-start | bytes 393224 | tf_op jit(solution)/shard_map/ppermute | solution.py:358
  93.1 14.0 %collective-permute-start.30 = (bf16[2,128,256]{2,1,0:T(8,128)(2,1)S(1)}, bf16[2,128,256]{2,1,0:T(8,128)(2,1)S(1)}, u32[]{:S(2)}, u32[]{:S(2)}) collective-permute-start(bf16[2,128,256]{2,1,0:T(8,128)(2,1)S(1)} %get-tuple-element.116), channel_id=1, source_target_pairs={{0,2},{1,3},{2,0},{3,1},{4,6},{5,7},{6,4},{7,5},{8,10},{9,11},{10,... | collective-permute-start | bytes 393224 | tf_op jit(solution)/shard_map/ppermute | solution.py:358
  95.8 11.4 %collective-permute-start.31 = (bf16[2,128,256]{2,1,0:T(8,128)(2,1)S(1)}, bf16[2,128,256]{2,1,0:T(8,128)(2,1)S(1)}, u32[]{:S(2)}, u32[]{:S(2)}) collective-permute-start(bf16[2,128,256]{2,1,0:T(8,128)(2,1)S(1)} %get-tuple-element.117), channel_id=1, source_target_pairs={{0,3},{1,0},{2,1},{3,2},{4,7},{5,4},{6,5},{7,6},{8,11},{9,8},{10,9... | collective-permute-start | bytes 393224 | tf_op jit(solution)/shard_map/ppermute | solution.py:358
  97.7 8.3 %collective-permute-start.26 = (bf16[128,256]{1,0:T(8,128)(2,1)S(1)}, bf16[128,256]{1,0:T(8,128)(2,1)S(1)}, u32[]{:S(2)}, u32[]{:S(2)}) collective-permute-start(bf16[128,256]{1,0:T(8,128)(2,1)S(1)} %get-tuple-element.107), channel_id=1, source_target_pairs={{0,64},{64,128},{128,192},{1,65},{65,129},{129,193},{2,66},{66,130... | collective-permute-start | bytes 196616 | tf_op jit(solution)/shard_map/ppermute | solution.py:437
  (9 other events, 112.9 us)

commit v5 on v4

--- a/solution.py
+++ b/solution.py
@@ -51,7 +51,7 @@
             outs[w * (G - 1) + k - 1][1] = inc[NW * m + w].astype(BF)
 
 
-def fold_kernel(slots, states, inc, edges, own0, own1, a0, cross, *ext):
+def fold_kernel(slots, states, inc, edges, own0, own1, folded):
     y = member()
     for w, own in enumerate((own0, own1)):
         own[0] = states[NW * y + w]
@@ -61,24 +61,16 @@
             total = jnp.zeros((B, B), F32)
             for f in range(4):
                 total += jnp.where(slots[0, f] == slot, edges[layer, 0, f].astype(F32), 0.0)
-            cols = slice(slot * B, (slot + 1) * B)
-            if layer == 0:
-                a0[:, cols] = total.astype(BF)
-            else:
-                for k in range(G):
-                    ext[k][:, cols] = total.astype(BF)
-    for k in range(G):
-        m = lax.rem(y + k + 1, G)
-        value = inc[NW * m].astype(BF)
-        ext[k][:, 3 * B :] = value
-        if k == 0:
-            cross[...] = value
-
-
-def edge_kernel(r0, r1, r2, r3, send_left, send_right):
+            first = (3 * layer + slot) * B
+            folded[:, first : first + B] = total.astype(BF)
+
+
+def edge_kernel(r0, r1, r2, r3, send_left, send_right, inc=None):
     y = member()
     for k, r in enumerate((r0, r1, r2, r3)):
         block = origin(y, k)
+        if inc is not None:
+            inc[block] = r[1]
 
         @pl.when(block == 0)
         def _():
@@ -89,9 +81,9 @@
             send_right[...] = r[...]
 
 
-def sort_edges(y, mats, amat, tmat):
+def sort_edges(y, mats, layer, amat, tmat):
     for k, a in enumerate(mats):
-        amat[origin(y, k)] = a[:, : 3 * B]
+        amat[origin(y, k)] = a[:, 3 * layer * B : 3 * (layer + 1) * B]
     for c in range(G):
         for slot in range(3):
             t = jnp.transpose(amat[c, :, slot * B : (slot + 1) * B].astype(F32)).astype(BF)
@@ -142,7 +134,7 @@
     field, amat, tmat, base_out, tan_out, slope, hat,
 ):
     y = member()
-    sort_edges(y, (a0, a1, a2, a3), amat, tmat)
+    sort_edges(y, (a0, a1, a2, a3), 0, amat, tmat)
     pair_matrix(amat, hat)
     for w, got in enumerate(((r00, r01, r02, r03), (r10, r11, r12, r13))):
         for k, r in enumerate(got):
@@ -178,19 +170,12 @@
 
 
 def inner1_kernel(
-    base_in, tan_in, lo0, lo1, hi0, hi1, field, e0, e0r, e1, e2, e3, win, bias, wout,
-    amat, tmat, next_out, image, returned, hat, slope, nxt,
+    base_in, tan_in, lo0, lo1, hi0, hi1, field, a0, a1, a2, a3, nxt, win, bias, wout,
+    amat, tmat, image, returned, hat, slope,
 ):
     y = member()
-    sort_edges(y, (e0, e1, e2, e3), amat, tmat)
+    sort_edges(y, (a0, a1, a2, a3), 1, amat, tmat)
     pair_matrix(amat, hat)
-    for k, e in enumerate((e0, e1, e2, e3)):
-        value = e[:, 3 * B :]
-        if k == 0:
-            value = jnp.where(y == G - 1, e0r[...], value)
-        nxt[origin(y, k)] = value
-    next_out[0:B] = nxt[0]
-    next_out[B:] = nxt[G - 1]
     for w in range(NW):
         lo, hi = (lo0, lo1)[w], (hi0, hi1)[w]
         base = stack(lo[0], base_in[w], hi[0])
@@ -209,7 +194,7 @@
 
 
 def edge1_kernel(
-    lo0, lo1, hi0, hi1, tan0, tan1, left0, left1, right0, right1, base_in, tan_in, field, next_edge, amat, tmat, image_in, win, bias, wout,
+    lo0, lo1, hi0, hi1, tan0, tan1, left0, left1, right0, right1, base_in, tan_in, field, nxt, amat, tmat, image_in, win, bias, wout,
     im0, im1, im2, im3, returned, send_left, send_right, slope, image,
 ):
     y = member()
@@ -233,7 +218,7 @@
             following = stack(field[1, 0:B, D:], field[1, 3 * B :, D:]).astype(F32)
             current = following - out
         else:
-            current = jnp.where(last_member(), 0.0, next_edge[...].astype(F32) - out)
+            current = jnp.where(last_member(), 0.0, stack(nxt[0], nxt[G - 1]).astype(F32) - out)
         back = adjoint_rows(current, 1, win, wout, slope)
         returned[w] = back
         send_left[w] = dot(tmat[0, :, 0:B], back[0:B].astype(BF)).astype(BF)
@@ -342,15 +327,12 @@
     return [(b, (b + G * d) % PARTS) for b in range(PARTS)]
 
 
-def next_increment_pairs(k):
+def next_increment_pairs():
     pairs = []
     for t in range(TM):
         for b in range(PARTS):
-            m = (b + k) % G
-            if k == 0 and m != G - 1:
-                continue
-            to = (t - 1) % TM if m == G - 1 else t
-            pairs.append((t * PARTS + b, to * PARTS + b // G * G + m))
+            to = (t - 1) % TM if b % G == 0 else t
+            pairs.append((t * PARTS + b, to * PARTS + b // G * G + (b - 1) % G))
     return pairs
 
 
@@ -374,27 +356,23 @@
     mats = sds((G, B, 3 * B))
     hat = pltpu.VMEM((2 * B, 4 * B), BF)
     weights = (inner_weight, inner_bias, outer_weight)
-    both = ("tm", "mesh")
 
     sends = call(pack_kernel, (states, increment), [item] * (NW * (G - 1)))
     got = [to_members([None, *sends[w * (G - 1) : (w + 1) * (G - 1)]]) for w in range(NW)]
-    *own, a0, cross, ext, ext1, ext2, ext3 = call(
+    *own, folded = call(
         fold_kernel, (window_slots, states, increment, edge_weights),
-        [item] * NW + [sds((B, 3 * B)), sds((B, D))] + [sds((B, 3 * B + D))] * G, smem=1,
-    )
-    a0 = [a0, *to_members([a0] * G)]
-    cross = lax.ppermute(cross, both, next_increment_pairs(0))
-    ext = [ext, cross] + [
-        lax.ppermute(e, both, next_increment_pairs(k + 1)) for k, e in enumerate((ext1, ext2, ext3))
-    ]
+        [item] * NW + [sds((B, 6 * B))], smem=1,
+    )
+    folded = [folded, *to_members([folded] * G)]
 
     got = [[own[w], *got[w]] for w in range(NW)]
-    halo = []
-    for w in range(NW):
-        lo, hi = call(edge_kernel, got[w], [item, item])
-        halo.append(swap_sides(lo, hi))
+    lo, hi, nxt = call(edge_kernel, got[0], [item, item, sds((G, B, D))])
+    halo = [swap_sides(lo, hi)]
+    lo, hi = call(edge_kernel, got[1], [item, item])
+    halo.append(swap_sides(lo, hi))
+    nxt = lax.ppermute(nxt, ("tm", "mesh"), next_increment_pairs())
     field, amat0, tmat0, base_in, tan_in, slope_in = call(
-        inner0_kernel, (*got[0], *got[1], *a0, *weights),
+        inner0_kernel, (*got[0], *got[1], *folded, *weights),
         [sds((NW, G * B, 2 * D)), mats, mats, pair_bf, pair, hidden], (hat,),
     )
     lo, hi, tan_edge, slope_edge, left, right = [], [], [], [], [], []
@@ -409,13 +387,13 @@
             values.append(value)
 
     slope1 = pltpu.VMEM((2 * B, HID), BF)
-    amat1, tmat1, next_edge, image_in, inner = call(
-        inner1_kernel, (base_in, tan_in, *lo, *hi, field, *ext, *weights),
-        [mats, mats, sds((2 * B, D)), pair_bf, pair], (hat, slope1, pltpu.VMEM((G, B, D), BF)),
+    amat1, tmat1, image_in, inner = call(
+        inner1_kernel, (base_in, tan_in, *lo, *hi, field, *folded, nxt, *weights),
+        [mats, mats, pair_bf, pair], (hat, slope1),
     )
     *images, edge, send_left, send_right = call(
         edge1_kernel,
-        (*lo, *hi, *tan_edge, *left, *right, base_in, tan_in, field, next_edge, amat1, tmat1, image_in, *weights),
+        (*lo, *hi, *tan_edge, *left, *right, base_in, tan_in, field, nxt, amat1, tmat1, image_in, *weights),
         [half] * G + [pair, half, half], (slope1, pltpu.VMEM((G, NW, B, D), BF)),
     )
 

time: 108 us -> 108 us (level)
  starting transfers between devices: 74.4 us -> 60.9 us
  waiting for transfers between devices: 12.6 us -> 26 us
    ppermute x15, waiting for transfers between devices: 2.74 us -> 13.8 us  [to_members(): return [lax.ppermute(sends[k], 'mesh', group_pairs(k)) for k in range(1, G)]]
    ppermute x4 -> x1, starting transfers between devices: 12.9 us -> 4.6 us  [local(): nxt = lax.ppermute(nxt, ('tm', 'mesh'), next_increment_pairs())]
    ppermute x6, waiting for transfers between devices: 0.02 us -> 2.75 us  [swap_sides(): right = lax.ppermute(send_left, 'mesh', side_pairs(-1))]
    ppermute x1, starting transfers between devices: 6.97 us -> 4.71 us  [local(): before = lax.ppermute(last, 'tm', [(t, t + 1) for t in range(TM - 1)])]
    ppermute x15, starting transfers between devices: 19.2 us -> 17.3 us  [to_members(): return [lax.ppermute(sends[k], 'mesh', group_pairs(k)) for k in range(1, G)]]
  transfers between devices with their start and end apart: 32 -> 29, of which waited for: 9 -> 7; matrix products, arithmetic and copies ran while one was open for 0% -> 0% of each run, Pallas kernels for 12% -> 12%
where the time goes in v5:
time: 108 us
  starting transfers between devices  60.9 us (56%)
  waiting for transfers between devices  26 us (24%)
  Pallas kernels  17.1 us (16%)
  local copies, waits for them, and re-layouts  3.23 us (3%)
    ppermute x6, starting transfers between devices, swap_sides(): right = lax.ppermute(send_left, 'mesh', side_pairs(-1))  31.5 us
    ppermute x15, starting transfers between devices, to_members(): return [lax.ppermute(sends[k], 'mesh', group_pairs(k)) for k in range(1, G)]  17.3 us
    pallas_call x15, Pallas kernels, call(): pl.pallas_call(kernel, out_shape=outs, in_specs=[SMEM] * smem + [VMEM] *...  17.1 us
    ppermute x15, waiting for transfers between devices, to_members(): return [lax.ppermute(sends[k], 'mesh', group_pairs(k)) for k in range(1, G)]  13.8 us
    ppermute x6, waiting for transfers between devices, swap_sides(): left = lax.ppermute(send_right, 'mesh', side_pairs(1))  8.16 us
    ppermute x1, starting transfers between devices, local(): before = lax.ppermute(last, 'tm', [(t, t + 1) for t in range(TM - 1)])  4.71 us
    ppermute x1, starting transfers between devices, local(): nxt = lax.ppermute(nxt, ('tm', 'mesh'), next_increment_pairs())  4.6 us
    unnamed x18, local copies, waits for them, and re-layouts  3.23 us
  transfers between devices with their start and end apart: 29, of which 7 were waited for; matrix products, arithmetic and copies ran while one was open for 0% of the time, Pallas kernels for 12%

profile of v5, /device:TPU:1, one launch (start us, length us, event | category | flops | bytes accessed | tf_op | source)
XLA Modules:
  0.0 108.1 jit_solution(14965397864496207145)
XLA Ops:
  0.6 1.2 %copy-done.2 = f32[8,128,256]{2,1,0:T(8,128)S(1)} copy-done((f32[8,128,256]{2,1,0:T(8,128)S(1)}, f32[8,128,256]{2,1,0:T(8,128)}, u32[]{:S(2)}) %copy-start.2) | copy-done | bytes 1048600
  3.0 2.2 %collective-permute-start = (bf16[2,128,256]{2,1,0:T(8,128)(2,1)S(1)}, bf16[2,128,256]{2,1,0:T(8,128)(2,1)S(1)}, u32[]{:S(2)}, u32[]{:S(2)}) collective-permute-start(bf16[2,128,256]{2,1,0:T(8,128)(2,1)S(1)} %get-tuple-element.56), channel_id=1, source_target_pairs={{0,1},{1,2},{2,3},{3,0},{4,5},{5,6},{6,7},{7,4},{8,9},{9,10},{10,1... | collective-permute-start | bytes 393224 | tf_op jit(solution)/shard_map/ppermute | solution.py:340
  5.2 1.3 %collective-permute-start.3 = (bf16[2,128,256]{2,1,0:T(8,128)(2,1)S(1)}, bf16[2,128,256]{2,1,0:T(8,128)(2,1)S(1)}, u32[]{:S(2)}, u32[]{:S(2)}) collective-permute-start(bf16[2,128,256]{2,1,0:T(8,128)(2,1)S(1)} %get-tuple-element.60), channel_id=1, source_target_pairs={{0,1},{1,2},{2,3},{3,0},{4,5},{5,6},{6,7},{7,4},{8,9},{9,10},{10,1... | collective-permute-start | bytes 393224 | tf_op jit(solution)/shard_map/ppermute | solution.py:340
  6.5 1.4 %collective-permute-start.4 = (bf16[2,128,256]{2,1,0:T(8,128)(2,1)S(1)}, bf16[2,128,256]{2,1,0:T(8,128)(2,1)S(1)}, u32[]{:S(2)}, u32[]{:S(2)}) collective-permute-start(bf16[2,128,256]{2,1,0:T(8,128)(2,1)S(1)} %get-tuple-element.61), channel_id=1, source_target_pairs={{0,2},{1,3},{2,0},{3,1},{4,6},{5,7},{6,4},{7,5},{8,10},{9,11},{10,... | collective-permute-start | bytes 393224 | tf_op jit(solution)/shard_map/ppermute | solution.py:340
  7.9 2.0 %collective-permute-start.5 = (bf16[2,128,256]{2,1,0:T(8,128)(2,1)S(1)}, bf16[2,128,256]{2,1,0:T(8,128)(2,1)S(1)}, u32[]{:S(2)}, u32[]{:S(2)}) collective-permute-start(bf16[2,128,256]{2,1,0:T(8,128)(2,1)S(1)} %get-tuple-element.62), channel_id=1, source_target_pairs={{0,3},{1,0},{2,1},{3,2},{4,7},{5,4},{6,5},{7,6},{8,11},{9,8},{10,9... | collective-permute-start | bytes 393224 | tf_op jit(solution)/shard_map/ppermute | solution.py:340
  11.8 1.1 %collective-permute-start.7 = (bf16[128,768]{1,0:T(8,128)(2,1)S(1)}, bf16[128,768]{1,0:T(8,128)(2,1)S(1)}, u32[]{:S(2)}, u32[]{:S(2)}) collective-permute-start(bf16[128,768]{1,0:T(8,128)(2,1)S(1)} %get-tuple-element.63.a0), channel_id=1, source_target_pairs={{0,2},{1,3},{2,0},{3,1},{4,6},{5,7},{6,4},{7,5},{8,10},{9,11},{10,... | collective-permute-start | bytes 589832 | tf_op jit(solution)/shard_map/ppermute | solution.py:340
  13.2 3.1 %collective-permute-done.4.r12.r2 = bf16[2,128,256]{2,1,0:T(8,128)(2,1)S(1)} collective-permute-done((bf16[2,128,256]{2,1,0:T(8,128)(2,1)S(1)}, bf16[2,128,256]{2,1,0:T(8,128)(2,1)S(1)}, u32[]{:S(2)}, u32[]{:S(2)}) %collective-permute-start.4) | collective-permute-done | bytes 131104 | tf_op jit(solution)/shard_map/ppermute | solution.py:340
  17.0 10.6 %collective-permute-done.1.r02.r2 = bf16[2,128,256]{2,1,0:T(8,128)(2,1)S(1)} collective-permute-done((bf16[2,128,256]{2,1,0:T(8,128)(2,1)S(1)}, bf16[2,128,256]{2,1,0:T(8,128)(2,1)S(1)}, u32[]{:S(2)}, u32[]{:S(2)}) %collective-permute-start.1) | collective-permute-done | bytes 131104 | tf_op jit(solution)/shard_map/ppermute | solution.py:340
  27.6 1.2 %collective-permute-start.11 = (bf16[2,128,256]{2,1,0:T(8,128)(2,1)S(1)}, bf16[2,128,256]{2,1,0:T(8,128)(2,1)S(1)}, u32[]{:S(2)}, u32[]{:S(2)}) collective-permute-start(bf16[2,128,256]{2,1,0:T(8,128)(2,1)S(1)} %get-tuple-element.69), channel_id=1, source_target_pairs={{0,4},{1,5},{2,6},{3,7},{4,8},{5,9},{6,10},{7,11},{8,12},{9,13},{1... | collective-permute-start | bytes 393224 | tf_op jit(solution)/shard_map/ppermute | solution.py:344
  28.8 7.5 %collective-permute-start.12 = (bf16[2,128,256]{2,1,0:T(8,128)(2,1)S(1)}, bf16[2,128,256]{2,1,0:T(8,128)(2,1)S(1)}, u32[]{:S(2)}, u32[]{:S(2)}) collective-permute-start(bf16[2,128,256]{2,1,0:T(8,128)(2,1)S(1)} %get-tuple-element.70), channel_id=1, source_target_pairs={{0,60},{1,61},{2,62},{3,63},{4,0},{5,1},{6,2},{7,3},{8,4},{9,5},{1... | collective-permute-start | bytes 393224 | tf_op jit(solution)/shard_map/ppermute | solution.py:345
  36.5 4.6 %collective-permute-start.17 = (bf16[4,128,256]{2,1,0:T(8,128)(2,1)S(1)}, bf16[4,128,256]{2,1,0:T(8,128)(2,1)S(1)}, u32[]{:S(2)}, u32[]{:S(2)}) collective-permute-start(bf16[4,128,256]{2,1,0:T(8,128)(2,1)S(1)} %get-tuple-element.78), channel_id=1, source_target_pairs={{0,195},{1,0},{2,1},{3,2},{4,199},{5,4},{6,5},{7,6},{8,203},{9,8},... | collective-permute-start | bytes 786440 | tf_op jit(solution)/shard_map/ppermute | solution.py:373
  41.1 5.9 %collective-permute-start.10 = (bf16[2,128,256]{2,1,0:T(8,128)(2,1)S(1)}, bf16[2,128,256]{2,1,0:T(8,128)(2,1)S(1)}, u32[]{:S(2)}, u32[]{:S(2)}) collective-permute-start(bf16[2,128,256]{2,1,0:T(8,128)(2,1)S(1)} %get-tuple-element.67), channel_id=1, source_target_pairs={{0,60},{1,61},{2,62},{3,63},{4,0},{5,1},{6,2},{7,3},{8,4},{9,5},{1... | collective-permute-start | bytes 393224 | tf_op jit(solution)/shard_map/ppermute | solution.py:345
  46.9 2.2 %shard_map.88 = (bf16[2,512,512]{2,1,0:T(8,128)(2,1)S(1)}, bf16[4,128,384]{2,1,0:T(8,128)(2,1)S(1)}, bf16[4,128,384]{2,1,0:T(8,128)(2,1)S(1)}, bf16[2,256,256]{2...) custom-call(bf16[2,128,256]{2,1,0:T(8,128)(2,1)S(1)} %get-tuple-element.55.r00.r0, ...), custom_call_target="tpu_custom_call" | custom-call | tf_op jit(solution)/shard_map/pallas_call | solution.py:312
  49.2 1.1 %shard_map.92 = (bf16[2,128,256]{2,1,0:T(8,128)(2,1)S(1)}, bf16[2,128,256]{2,1,0:T(8,128)(2,1)S(1)}, f32[256,256]{1,0:T(8,128)S(1)}, bf16[256,1024]{1,0:T(8,128)(2,1)S(1)}) custom-call(bf16[2,512,512]{2,1,0:T(8,128)(2,1)S(1)} %get-tuple-element.64.field, bf16[4,128,384]{2,1,0:T(8,128)(2,1)S(1)} %get-tuple-element.65.amat, ...), custom_call_target="tpu_custom_call" | custom-call | tf_op jit(solution)/shard_map/pallas_call | solution.py:312
  50.4 1.4 %collective-permute-start.14 = (bf16[2,128,256]{2,1,0:T(8,128)(2,1)S(1)}, bf16[2,128,256]{2,1,0:T(8,128)(2,1)S(1)}, u32[]{:S(2)}, u32[]{:S(2)}) collective-permute-start(bf16[2,128,256]{2,1,0:T(8,128)(2,1)S(1)} %get-tuple-element.73.hi1), channel_id=1, source_target_pairs={{0,4},{1,5},{2,6},{3,7},{4,8},{5,9},{6,10},{7,11},{8,12},{9,13},{1... | collective-permute-start | bytes 393224 | tf_op jit(solution)/shard_map/ppermute | solution.py:344
  51.9 2.6 %collective-permute-done.10.right = bf16[2,128,256]{2,1,0:T(8,128)(2,1)S(1)} collective-permute-done((bf16[2,128,256]{2,1,0:T(8,128)(2,1)S(1)}, bf16[2,128,256]{2,1,0:T(8,128)(2,1)S(1)}, u32[]{:S(2)}, u32[]{:S(2)}) %collective-permute-start.10) | collective-permute-done | bytes 131104 | tf_op jit(solution)/shard_map/ppermute | solution.py:345
  54.5 1.1 %shard_map.90 = (bf16[2,128,256]{2,1,0:T(8,128)(2,1)S(1)}, bf16[2,128,256]{2,1,0:T(8,128)(2,1)S(1)}, f32[256,256]{1,0:T(8,128)S(1)}, bf16[256,1024]{1,0:T(8,128)(2,1)S(1)}) custom-call(bf16[2,512,512]{2,1,0:T(8,128)(2,1)S(1)} %get-tuple-element.64.field, bf16[4,128,384]{2,1,0:T(8,128)(2,1)S(1)} %get-tuple-element.65.amat, ...), custom_call_target="tpu_custom_call" | custom-call | tf_op jit(solution)/shard_map/pallas_call | solution.py:312
  55.6 6.5 %collective-permute-start.15 = (bf16[2,128,256]{2,1,0:T(8,128)(2,1)S(1)}, bf16[2,128,256]{2,1,0:T(8,128)(2,1)S(1)}, u32[]{:S(2)}, u32[]{:S(2)}) collective-permute-start(bf16[2,128,256]{2,1,0:T(8,128)(2,1)S(1)} %get-tuple-element.68.lo0), channel_id=1, source_target_pairs={{0,60},{1,61},{2,62},{3,63},{4,0},{5,1},{6,2},{7,3},{8,4},{9,5},{1... | collective-permute-start | bytes 393224 | tf_op jit(solution)/shard_map/ppermute | solution.py:345
  62.1 3.0 %shard_map.93 = (bf16[4,128,384]{2,1,0:T(8,128)(2,1)S(1)}, bf16[4,128,384]{2,1,0:T(8,128)(2,1)S(1)}, bf16[2,256,256]{2,1,0:T(8,128)(2,1)S(1)}, f32[2,256,256]{2,1,0:T(8,128)S(1)}) custom-call(bf16[2,256,256]{2,1,0:T(8,128)(2,1)S(1)} %get-tuple-element.76.base_in, f32[2,256,256]{2,1,0:T(8,128)S(1)} %get-tuple-element.77.tan_in, ...), custom_call_target="tpu_custom_call" | custom-call | tf_op jit(solution)/shard_map/pallas_call | solution.py:312
  65.3 6.4 %collective-permute-done.13.left0 = bf16[2,128,256]{2,1,0:T(8,128)(2,1)S(1)} collective-permute-done((bf16[2,128,256]{2,1,0:T(8,128)(2,1)S(1)}, bf16[2,128,256]{2,1,0:T(8,128)(2,1)S(1)}, u32[]{:S(2)}, u32[]{:S(2)}) %collective-permute-start.13) | collective-permute-done | bytes 131104 | tf_op jit(solution)/shard_map/ppermute | solution.py:344
  71.7 3.3 %shard_map.94 = (bf16[2,128,256]{2,1,0:T(8,128)(2,1)S(1)}, bf16[2,128,256]{2,1,0:T(8,128)(2,1)S(1)}, bf16[2,128,256]{2,1,0:T(8,128)(2,1)S(1)}, bf16[2,128,256]{2...) custom-call(bf16[2,128,256]{2,1,0:T(8,128)(2,1)S(1)} %get-tuple-elem, ...), custom_call_target="tpu_custom_call" | custom-call | tf_op jit(solution)/shard_map/pallas_call | solution.py:312
  75.1 5.7 %collective-permute-start.22 = (bf16[2,128,256]{2,1,0:T(8,128)(2,1)S(1)}, bf16[2,128,256]{2,1,0:T(8,128)(2,1)S(1)}, u32[]{:S(2)}, u32[]{:S(2)}) collective-permute-start(bf16[2,128,256]{2,1,0:T(8,128)(2,1)S(1)} %get-tuple-element.92), channel_id=1, source_target_pairs={{0,60},{1,61},{2,62},{3,63},{4,0},{5,1},{6,2},{7,3},{8,4},{9,5},{1... | collective-permute-start | bytes 393224 | tf_op jit(solution)/shard_map/ppermute | solution.py:345
  80.8 2.7 %collective-permute-start.20 = (bf16[2,128,256]{2,1,0:T(8,128)(2,1)S(1)}, bf16[2,128,256]{2,1,0:T(8,128)(2,1)S(1)}, u32[]{:S(2)}, u32[]{:S(2)}) collective-permute-start(bf16[2,128,256]{2,1,0:T(8,128)(2,1)S(1)} %get-tuple-element.85), channel_id=1, source_target_pairs={{0,3},{1,0},{2,1},{3,2},{4,7},{5,4},{6,5},{7,6},{8,11},{9,8},{10,9... | collective-permute-start | bytes 393224 | tf_op jit(solution)/shard_map/ppermute | solution.py:340
  83.5 1.4 %shard_map.95 = (f32[2,256,256]{2,1,0:T(8,128)S(1)}, f32[2,256,256]{2,1,0:T(8,128)S(1)}) custom-call(f32[2,256,256]{2,1,0:T(8,128)S(1)} %get-tuple-element.86.inner, f32[2,256,256]{2,1,0:T(8,128)S(1)} %get-tuple-element.87.edge, bf16[4,128,384]{2,1,0:T(8,128)(2,1)S(1)} %get-tuple-element.80.tmat, bf16[2,256,1024]{2,1,0:T(8,128)(2,1)S(1)} %get-tuple-element.88.slope, ...), custom_call_target="tpu_custom_call" | custom-call | tf_op jit(solution)/shard_map/pallas_call | solution.py:312
  84.9 1.3 %shard_map.96 = (f32[2,256,256]{2,1,0:T(8,128)S(1)}, bf16[2,128,256]{2,1,0:T(8,128)(2,1)S(1)}, bf16[2,128,256]{2,1,0:T(8,128)(2,1)S(1)}) custom-call(f32[2,256,256]{2,1,0:T(8,128)S(1)} %get-tuple-element.90.cur_edge, bf16[2,128,256]{2,1,0:T(8,128)(2,1)S(1)} %collective-permute-done.21.left, bf16[2,128,256]{2,1,0:T(8,128)(2,1)S(1)} %collective-permute-done.22.right, ...), custom_call_target="tpu_custom_call" | custom-call | tf_op jit(solution)/shard_map/pallas_call | solution.py:312
  86.3 5.9 %collective-permute-start.25 = (bf16[2,128,256]{2,1,0:T(8,128)(2,1)S(1)}, bf16[2,128,256]{2,1,0:T(8,128)(2,1)S(1)}, u32[]{:S(2)}, u32[]{:S(2)}) collective-permute-start(bf16[2,128,256]{2,1,0:T(8,128)(2,1)S(1)} %get-tuple-element.103), channel_id=1, source_target_pairs={{0,60},{1,61},{2,62},{3,63},{4,0},{5,1},{6,2},{7,3},{8,4},{9,5},{1... | collective-permute-start | bytes 393224 | tf_op jit(solution)/shard_map/ppermute | solution.py:345
  92.6 1.7 %collective-permute-done.24.left = bf16[2,128,256]{2,1,0:T(8,128)(2,1)S(1)} collective-permute-done((bf16[2,128,256]{2,1,0:T(8,128)(2,1)S(1)}, bf16[2,128,256]{2,1,0:T(8,128)(2,1)S(1)}, u32[]{:S(2)}, u32[]{:S(2)}) %collective-permute-start.24) | collective-permute-done | bytes 131104 | tf_op jit(solution)/shard_map/ppermute | solution.py:344
  95.1 2.8 %collective-permute-start.27 = (bf16[2,128,256]{2,1,0:T(8,128)(2,1)S(1)}, bf16[2,128,256]{2,1,0:T(8,128)(2,1)S(1)}, u32[]{:S(2)}, u32[]{:S(2)}) collective-permute-start(bf16[2,128,256]{2,1,0:T(8,128)(2,1)S(1)} %get-tuple-element.106), channel_id=1, source_target_pairs={{0,2},{1,3},{2,0},{3,1},{4,6},{5,7},{6,4},{7,5},{8,10},{9,11},{10,... | collective-permute-start | bytes 393224 | tf_op jit(solution)/shard_map/ppermute | solution.py:340
  97.9 2.0 %collective-permute-start.28 = (bf16[2,128,256]{2,1,0:T(8,128)(2,1)S(1)}, bf16[2,128,256]{2,1,0:T(8,128)(2,1)S(1)}, u32[]{:S(2)}, u32[]{:S(2)}) collective-permute-start(bf16[2,128,256]{2,1,0:T(8,128)(2,1)S(1)} %get-tuple-element.107), channel_id=1, source_target_pairs={{0,3},{1,0},{2,1},{3,2},{4,7},{5,4},{6,5},{7,6},{8,11},{9,8},{10,9... | collective-permute-start | bytes 393224 | tf_op jit(solution)/shard_map/ppermute | solution.py:340
  99.9 4.7 %collective-permute-start.23 = (bf16[128,256]{1,0:T(8,128)(2,1)S(1)}, bf16[128,256]{1,0:T(8,128)(2,1)S(1)}, u32[]{:S(2)}, u32[]{:S(2)}) collective-permute-start(bf16[128,256]{1,0:T(8,128)(2,1)S(1)} %get-tuple-element.97), channel_id=1, source_target_pairs={{0,64},{64,128},{128,192},{1,65},{65,129},{129,193},{2,66},{66,130... | collective-permute-start | bytes 196616 | tf_op jit(solution)/shard_map/ppermute | solution.py:415
  104.6 1.3 %collective-permute-done.23.before = bf16[128,256]{1,0:T(8,128)(2,1)S(1)} collective-permute-done((bf16[128,256]{1,0:T(8,128)(2,1)S(1)}, bf16[128,256]{1,0:T(8,128)(2,1)S(1)}, u32[]{:S(2)}, u32[]{:S(2)}) %collective-permute-start.23) | collective-permute-done | bytes 65568 | tf_op jit(solution)/shard_map/ppermute | solution.py:415
  105.9 1.1 %shard_map.98 = (f32[8,128,256]{2,1,0:T(8,128)}, f32[8,128,256]{2,1,0:T(8,128)S(1)}) custom-call(f32[8,128,256]{2,1,0:T(8,128)S(1)} %copy-done.3, bf16[2,128,256]{2,1,0:T(8,128)(2,1)S(1)} %get-tuple-element.82.i0, bf16[2,128,256]{2,1,0:T(8,128)(2,1)S(1)} %collective-permute-done.18.i1, bf16[2,128,256]{2,1,0:T(8,128)(2,1)S(1)} %collective-permute-done.19.i2, ...), custom_call_target="tpu_custom_call" | custom-call | tf_op jit(solution)/shard_map/pallas_call | solution.py:312
  (59 shorter events, 6.9 us)
Async XLA Ops:
  3.0 8.8 %collective-permute-start = (bf16[2,128,256]{2,1,0:T(8,128)(2,1)S(1)}, bf16[2,128,256]{2,1,0:T(8,128)(2,1)S(1)}, u32[]{:S(2)}, u32[]{:S(2)}) collective-permute-start(bf16[2,128,256]{2,1,0:T(8,128)(2,1)S(1)} %get-tuple-element.56), channel_id=1, source_target_pairs={{0,1},{1,2},{2,3},{3,0},{4,5},{5,6},{6,7},{7,4},{8,9},{9,10},{10,1... | collective-permute-start | bytes 393224 | tf_op jit(solution)/shard_map/ppermute | solution.py:340
  5.2 7.7 %collective-permute-start.3 = (bf16[2,128,256]{2,1,0:T(8,128)(2,1)S(1)}, bf16[2,128,256]{2,1,0:T(8,128)(2,1)S(1)}, u32[]{:S(2)}, u32[]{:S(2)}) collective-permute-start(bf16[2,128,256]{2,1,0:T(8,128)(2,1)S(1)} %get-tuple-element.60), channel_id=1, source_target_pairs={{0,1},{1,2},{2,3},{3,0},{4,5},{5,6},{6,7},{7,4},{8,9},{9,10},{10,1... | collective-permute-start | bytes 393224 | tf_op jit(solution)/shard_map/ppermute | solution.py:340
  6.5 9.9 %collective-permute-start.4 = (bf16[2,128,256]{2,1,0:T(8,128)(2,1)S(1)}, bf16[2,128,256]{2,1,0:T(8,128)(2,1)S(1)}, u32[]{:S(2)}, u32[]{:S(2)}) collective-permute-start(bf16[2,128,256]{2,1,0:T(8,128)(2,1)S(1)} %get-tuple-element.61), channel_id=1, source_target_pairs={{0,2},{1,3},{2,0},{3,1},{4,6},{5,7},{6,4},{7,5},{8,10},{9,11},{10,... | collective-permute-start | bytes 393224 | tf_op jit(solution)/shard_map/ppermute | solution.py:340
  7.9 39.1 %copy-start = (bf16[2,256,1024]{2,1,0:T(8,128)(2,1)S(1)}, bf16[2,256,1024]{2,1,0:T(8,128)(2,1)}, u32[]{:S(2)}) copy-start(bf16[2,256,1024]{2,1,0:T(8,128)(2,1)} %win.13) | copy-start | bytes 3145732
  7.9 39.1 %copy-start.1 = (bf16[2,1024,256]{2,1,0:T(8,128)(2,1)S(1)}, bf16[2,1024,256]{2,1,0:T(8,128)(2,1)}, u32[]{:S(2)}) copy-start(bf16[2,1024,256]{2,1,0:T(8,128)(2,1)} %wout.13) | copy-start | bytes 3145732
  7.9 8.8 %collective-permute-start.5 = (bf16[2,128,256]{2,1,0:T(8,128)(2,1)S(1)}, bf16[2,128,256]{2,1,0:T(8,128)(2,1)S(1)}, u32[]{:S(2)}, u32[]{:S(2)}) collective-permute-start(bf16[2,128,256]{2,1,0:T(8,128)(2,1)S(1)} %get-tuple-element.62), channel_id=1, source_target_pairs={{0,3},{1,0},{2,1},{3,2},{4,7},{5,4},{6,5},{7,6},{8,11},{9,8},{10,9... | collective-permute-start | bytes 393224 | tf_op jit(solution)/shard_map/ppermute | solution.py:340
  11.5 24.8 %collective-permute-start.8 = (bf16[128,768]{1,0:T(8,128)(2,1)S(1)}, bf16[128,768]{1,0:T(8,128)(2,1)S(1)}, u32[]{:S(2)}, u32[]{:S(2)}) collective-permute-start(bf16[128,768]{1,0:T(8,128)(2,1)S(1)} %get-tuple-element.63.a0), channel_id=1, source_target_pairs={{0,3},{1,0},{2,1},{3,2},{4,7},{5,4},{6,5},{7,6},{8,11},{9,8},{10,9... | collective-permute-start | bytes 589832 | tf_op jit(solution)/shard_map/ppermute | solution.py:340
  11.8 24.7 %collective-permute-start.7 = (bf16[128,768]{1,0:T(8,128)(2,1)S(1)}, bf16[128,768]{1,0:T(8,128)(2,1)S(1)}, u32[]{:S(2)}, u32[]{:S(2)}) collective-permute-start(bf16[128,768]{1,0:T(8,128)(2,1)S(1)} %get-tuple-element.63.a0), channel_id=1, source_target_pairs={{0,2},{1,3},{2,0},{3,1},{4,6},{5,7},{6,4},{7,5},{8,10},{9,11},{10,... | collective-permute-start | bytes 589832 | tf_op jit(solution)/shard_map/ppermute | solution.py:340
  12.9 28.2 %collective-permute-start.6 = (bf16[128,768]{1,0:T(8,128)(2,1)S(1)}, bf16[128,768]{1,0:T(8,128)(2,1)S(1)}, u32[]{:S(2)}, u32[]{:S(2)}) collective-permute-start(bf16[128,768]{1,0:T(8,128)(2,1)S(1)} %get-tuple-element.63.a0), channel_id=1, source_target_pairs={{0,1},{1,2},{2,3},{3,0},{4,5},{5,6},{6,7},{7,4},{8,9},{9,10},{10,1... | collective-permute-start | bytes 589832 | tf_op jit(solution)/shard_map/ppermute | solution.py:340
  16.3 11.3 %collective-permute-start.1 = (bf16[2,128,256]{2,1,0:T(8,128)(2,1)S(1)}, bf16[2,128,256]{2,1,0:T(8,128)(2,1)S(1)}, u32[]{:S(2)}, u32[]{:S(2)}) collective-permute-start(bf16[2,128,256]{2,1,0:T(8,128)(2,1)S(1)} %get-tuple-element.57), channel_id=1, source_target_pairs={{0,2},{1,3},{2,0},{3,1},{4,6},{5,7},{6,4},{7,5},{8,10},{9,11},{10,... | collective-permute-start | bytes 393224 | tf_op jit(solution)/shard_map/ppermute | solution.py:340
  16.7 12.1 %collective-permute-start.2 = (bf16[2,128,256]{2,1,0:T(8,128)(2,1)S(1)}, bf16[2,128,256]{2,1,0:T(8,128)(2,1)S(1)}, u32[]{:S(2)}, u32[]{:S(2)}) collective-permute-start(bf16[2,128,256]{2,1,0:T(8,128)(2,1)S(1)} %get-tuple-element.58), channel_id=1, source_target_pairs={{0,3},{1,0},{2,1},{3,2},{4,7},{5,4},{6,5},{7,6},{8,11},{9,8},{10,9... | collective-permute-start | bytes 393224 | tf_op jit(solution)/shard_map/ppermute | solution.py:340
  27.6 21.6 %collective-permute-start.11 = (bf16[2,128,256]{2,1,0:T(8,128)(2,1)S(1)}, bf16[2,128,256]{2,1,0:T(8,128)(2,1)S(1)}, u32[]{:S(2)}, u32[]{:S(2)}) collective-permute-start(bf16[2,128,256]{2,1,0:T(8,128)(2,1)S(1)} %get-tuple-element.69), channel_id=1, source_target_pairs={{0,4},{1,5},{2,6},{3,7},{4,8},{5,9},{6,10},{7,11},{8,12},{9,13},{1... | collective-permute-start | bytes 393224 | tf_op jit(solution)/shard_map/ppermute | solution.py:344
  28.8 20.4 %collective-permute-start.12 = (bf16[2,128,256]{2,1,0:T(8,128)(2,1)S(1)}, bf16[2,128,256]{2,1,0:T(8,128)(2,1)S(1)}, u32[]{:S(2)}, u32[]{:S(2)}) collective-permute-start(bf16[2,128,256]{2,1,0:T(8,128)(2,1)S(1)} %get-tuple-element.70), channel_id=1, source_target_pairs={{0,60},{1,61},{2,62},{3,63},{4,0},{5,1},{6,2},{7,3},{8,4},{9,5},{1... | collective-permute-start | bytes 393224 | tf_op jit(solution)/shard_map/ppermute | solution.py:345
  36.3 10.7 %copy-start.7 = (f32[2,1024]{1,0:T(2,128)S(1)}, f32[2,1024]{1,0:T(2,128)}, u32[]{:S(2)}) copy-start(f32[2,1024]{1,0:T(2,128)} %bias.9) | copy-start | bytes 24580
  36.4 15.5 %collective-permute-start.9 = (bf16[2,128,256]{2,1,0:T(8,128)(2,1)S(1)}, bf16[2,128,256]{2,1,0:T(8,128)(2,1)S(1)}, u32[]{:S(2)}, u32[]{:S(2)}) collective-permute-start(bf16[2,128,256]{2,1,0:T(8,128)(2,1)S(1)} %get-tuple-element.66), channel_id=1, source_target_pairs={{0,4},{1,5},{2,6},{3,7},{4,8},{5,9},{6,10},{7,11},{8,12},{9,13},{1... | collective-permute-start | bytes 393224 | tf_op jit(solution)/shard_map/ppermute | solution.py:344
  36.5 25.7 %collective-permute-start.17 = (bf16[4,128,256]{2,1,0:T(8,128)(2,1)S(1)}, bf16[4,128,256]{2,1,0:T(8,128)(2,1)S(1)}, u32[]{:S(2)}, u32[]{:S(2)}) collective-permute-start(bf16[4,128,256]{2,1,0:T(8,128)(2,1)S(1)} %get-tuple-element.78), channel_id=1, source_target_pairs={{0,195},{1,0},{2,1},{3,2},{4,199},{5,4},{6,5},{7,6},{8,203},{9,8},... | collective-permute-start | bytes 786440 | tf_op jit(solution)/shard_map/ppermute | solution.py:373
  41.1 13.4 %collective-permute-start.10 = (bf16[2,128,256]{2,1,0:T(8,128)(2,1)S(1)}, bf16[2,128,256]{2,1,0:T(8,128)(2,1)S(1)}, u32[]{:S(2)}, u32[]{:S(2)}) collective-permute-start(bf16[2,128,256]{2,1,0:T(8,128)(2,1)S(1)} %get-tuple-element.67), channel_id=1, source_target_pairs={{0,60},{1,61},{2,62},{3,63},{4,0},{5,1},{6,2},{7,3},{8,4},{9,5},{1... | collective-permute-start | bytes 393224 | tf_op jit(solution)/shard_map/ppermute | solution.py:345
  50.3 14.8 %collective-permute-start.16 = (bf16[2,128,256]{2,1,0:T(8,128)(2,1)S(1)}, bf16[2,128,256]{2,1,0:T(8,128)(2,1)S(1)}, u32[]{:S(2)}, u32[]{:S(2)}) collective-permute-start(bf16[2,128,256]{2,1,0:T(8,128)(2,1)S(1)} %get-tuple-element.71.lo1), channel_id=1, source_target_pairs={{0,60},{1,61},{2,62},{3,63},{4,0},{5,1},{6,2},{7,3},{8,4},{9,5},{1... | collective-permute-start | bytes 393224 | tf_op jit(solution)/shard_map/ppermute | solution.py:345
  50.4 14.7 %collective-permute-start.14 = (bf16[2,128,256]{2,1,0:T(8,128)(2,1)S(1)}, bf16[2,128,256]{2,1,0:T(8,128)(2,1)S(1)}, u32[]{:S(2)}, u32[]{:S(2)}) collective-permute-start(bf16[2,128,256]{2,1,0:T(8,128)(2,1)S(1)} %get-tuple-element.73.hi1), channel_id=1, source_target_pairs={{0,4},{1,5},{2,6},{3,7},{4,8},{5,9},{6,10},{7,11},{8,12},{9,13},{1... | collective-permute-start | bytes 393224 | tf_op jit(solution)/shard_map/ppermute | solution.py:344
  55.6 9.7 %collective-permute-start.15 = (bf16[2,128,256]{2,1,0:T(8,128)(2,1)S(1)}, bf16[2,128,256]{2,1,0:T(8,128)(2,1)S(1)}, u32[]{:S(2)}, u32[]{:S(2)}) collective-permute-start(bf16[2,128,256]{2,1,0:T(8,128)(2,1)S(1)} %get-tuple-element.68.lo0), channel_id=1, source_target_pairs={{0,60},{1,61},{2,62},{3,63},{4,0},{5,1},{6,2},{7,3},{8,4},{9,5},{1... | collective-permute-start | bytes 393224 | tf_op jit(solution)/shard_map/ppermute | solution.py:345
  62.1 9.6 %collective-permute-start.13 = (bf16[2,128,256]{2,1,0:T(8,128)(2,1)S(1)}, bf16[2,128,256]{2,1,0:T(8,128)(2,1)S(1)}, u32[]{:S(2)}, u32[]{:S(2)}) collective-permute-start(bf16[2,128,256]{2,1,0:T(8,128)(2,1)S(1)} %get-tuple-element.72.hi0), channel_id=1, source_target_pairs={{0,4},{1,5},{2,6},{3,7},{4,8},{5,9},{6,10},{7,11},{8,12},{9,13},{1... | collective-permute-start | bytes 393224 | tf_op jit(solution)/shard_map/ppermute | solution.py:344
  75.0 9.8 %collective-permute-start.21 = (bf16[2,128,256]{2,1,0:T(8,128)(2,1)S(1)}, bf16[2,128,256]{2,1,0:T(8,128)(2,1)S(1)}, u32[]{:S(2)}, u32[]{:S(2)}) collective-permute-start(bf16[2,128,256]{2,1,0:T(8,128)(2,1)S(1)} %get-tuple-element.91), channel_id=1, source_target_pairs={{0,4},{1,5},{2,6},{3,7},{4,8},{5,9},{6,10},{7,11},{8,12},{9,13},{1... | collective-permute-start | bytes 393224 | tf_op jit(solution)/shard_map/ppermute | solution.py:344
  75.1 9.8 %collective-permute-start.22 = (bf16[2,128,256]{2,1,0:T(8,128)(2,1)S(1)}, bf16[2,128,256]{2,1,0:T(8,128)(2,1)S(1)}, u32[]{:S(2)}, u32[]{:S(2)}) collective-permute-start(bf16[2,128,256]{2,1,0:T(8,128)(2,1)S(1)} %get-tuple-element.92), channel_id=1, source_target_pairs={{0,60},{1,61},{2,62},{3,63},{4,0},{5,1},{6,2},{7,3},{8,4},{9,5},{1... | collective-permute-start | bytes 393224 | tf_op jit(solution)/shard_map/ppermute | solution.py:345
  80.8 11.3 %collective-permute-start.18 = (bf16[2,128,256]{2,1,0:T(8,128)(2,1)S(1)}, bf16[2,128,256]{2,1,0:T(8,128)(2,1)S(1)}, u32[]{:S(2)}, u32[]{:S(2)}) collective-permute-start(bf16[2,128,256]{2,1,0:T(8,128)(2,1)S(1)} %get-tuple-element.83), channel_id=1, source_target_pairs={{0,1},{1,2},{2,3},{3,0},{4,5},{5,6},{6,7},{7,4},{8,9},{9,10},{10,1... | collective-permute-start | bytes 393224 | tf_op jit(solution)/shard_map/ppermute | solution.py:340
  80.8 11.3 %collective-permute-start.19 = (bf16[2,128,256]{2,1,0:T(8,128)(2,1)S(1)}, bf16[2,128,256]{2,1,0:T(8,128)(2,1)S(1)}, u32[]{:S(2)}, u32[]{:S(2)}) collective-permute-start(bf16[2,128,256]{2,1,0:T(8,128)(2,1)S(1)} %get-tuple-element.84), channel_id=1, source_target_pairs={{0,2},{1,3},{2,0},{3,1},{4,6},{5,7},{6,4},{7,5},{8,10},{9,11},{10,... | collective-permute-start | bytes 393224 | tf_op jit(solution)/shard_map/ppermute | solution.py:340
  80.8 11.3 %collective-permute-start.20 = (bf16[2,128,256]{2,1,0:T(8,128)(2,1)S(1)}, bf16[2,128,256]{2,1,0:T(8,128)(2,1)S(1)}, u32[]{:S(2)}, u32[]{:S(2)}) collective-permute-start(bf16[2,128,256]{2,1,0:T(8,128)(2,1)S(1)} %get-tuple-element.85), channel_id=1, source_target_pairs={{0,3},{1,0},{2,1},{3,2},{4,7},{5,4},{6,5},{7,6},{8,11},{9,8},{10,9... | collective-permute-start | bytes 393224 | tf_op jit(solution)/shard_map/ppermute | solution.py:340
  86.2 8.1 %collective-permute-start.24 = (bf16[2,128,256]{2,1,0:T(8,128)(2,1)S(1)}, bf16[2,128,256]{2,1,0:T(8,128)(2,1)S(1)}, u32[]{:S(2)}, u32[]{:S(2)}) collective-permute-start(bf16[2,128,256]{2,1,0:T(8,128)(2,1)S(1)} %get-tuple-element.102), channel_id=1, source_target_pairs={{0,4},{1,5},{2,6},{3,7},{4,8},{5,9},{6,10},{7,11},{8,12},{9,13},{1... | collective-permute-start | bytes 393224 | tf_op jit(solution)/shard_map/ppermute | solution.py:344
  86.3 8.0 %collective-permute-start.25 = (bf16[2,128,256]{2,1,0:T(8,128)(2,1)S(1)}, bf16[2,128,256]{2,1,0:T(8,128)(2,1)S(1)}, u32[]{:S(2)}, u32[]{:S(2)}) collective-permute-start(bf16[2,128,256]{2,1,0:T(8,128)(2,1)S(1)} %get-tuple-element.103), channel_id=1, source_target_pairs={{0,60},{1,61},{2,62},{3,63},{4,0},{5,1},{6,2},{7,3},{8,4},{9,5},{1... | collective-permute-start | bytes 393224 | tf_op jit(solution)/shard_map/ppermute | solution.py:345
  94.4 12.6 %collective-permute-start.26 = (bf16[2,128,256]{2,1,0:T(8,128)(2,1)S(1)}, bf16[2,128,256]{2,1,0:T(8,128)(2,1)S(1)}, u32[]{:S(2)}, u32[]{:S(2)}) collective-permute-start(bf16[2,128,256]{2,1,0:T(8,128)(2,1)S(1)} %get-tuple-element.105), channel_id=1, source_target_pairs={{0,1},{1,2},{2,3},{3,0},{4,5},{5,6},{6,7},{7,4},{8,9},{9,10},{10,1... | collective-permute-start | bytes 393224 | tf_op jit(solution)/shard_map/ppermute | solution.py:340
  95.1 11.9 %collective-permute-start.27 = (bf16[2,128,256]{2,1,0:T(8,128)(2,1)S(1)}, bf16[2,128,256]{2,1,0:T(8,128)(2,1)S(1)}, u32[]{:S(2)}, u32[]{:S(2)}) collective-permute-start(bf16[2,128,256]{2,1,0:T(8,128)(2,1)S(1)} %get-tuple-element.106), channel_id=1, source_target_pairs={{0,2},{1,3},{2,0},{3,1},{4,6},{5,7},{6,4},{7,5},{8,10},{9,11},{10,... | collective-permute-start | bytes 393224 | tf_op jit(solution)/shard_map/ppermute | solution.py:340
  97.9 9.1 %collective-permute-start.28 = (bf16[2,128,256]{2,1,0:T(8,128)(2,1)S(1)}, bf16[2,128,256]{2,1,0:T(8,128)(2,1)S(1)}, u32[]{:S(2)}, u32[]{:S(2)}) collective-permute-start(bf16[2,128,256]{2,1,0:T(8,128)(2,1)S(1)} %get-tuple-element.107), channel_id=1, source_target_pairs={{0,3},{1,0},{2,1},{3,2},{4,7},{5,4},{6,5},{7,6},{8,11},{9,8},{10,9... | collective-permute-start | bytes 393224 | tf_op jit(solution)/shard_map/ppermute | solution.py:340
  99.9 6.0 %collective-permute-start.23 = (bf16[128,256]{1,0:T(8,128)(2,1)S(1)}, bf16[128,256]{1,0:T(8,128)(2,1)S(1)}, u32[]{:S(2)}, u32[]{:S(2)}) collective-permute-start(bf16[128,256]{1,0:T(8,128)(2,1)S(1)} %get-tuple-element.97), channel_id=1, source_target_pairs={{0,64},{64,128},{128,192},{1,65},{65,129},{129,193},{2,66},{66,130... | collective-permute-start | bytes 196616 | tf_op jit(solution)/shard_map/ppermute | solution.py:415
  (6 other events, 20.6 us)

commit v6 on v5

--- a/solution.py
+++ b/solution.py
@@ -195,9 +195,8 @@
 
 def edge1_kernel(
     lo0, lo1, hi0, hi1, tan0, tan1, left0, left1, right0, right1, base_in, tan_in, field, nxt, amat, tmat, image_in, win, bias, wout,
-    im0, im1, im2, im3, returned, send_left, send_right, slope, image,
+    image0, image1, returned, send_left, send_right, slope,
 ):
-    y = member()
     for w in range(NW):
         lo, hi, tan_edge = (lo0, lo1)[w], (hi0, hi1)[w], (tan0, tan1)[w]
         left, right = (left0, left1)[w], (right0, right1)[w]
@@ -210,10 +209,11 @@
             ))
         base_sum = stack(lo[0], hi[0]).astype(F32) + agg[0]
         _, out = forward_rows(base_sum, tan_edge[...] + agg[1], 1, win, bias, wout, slope, False)
-        image[0, w] = out[0:B].astype(BF)
-        image[1, w] = image_in[w, 0:B]
-        image[2, w] = image_in[w, B:]
-        image[3, w] = out[B:].astype(BF)
+        image = (image0, image1)[w]
+        image[0] = out[0:B].astype(BF)
+        image[1] = image_in[w, 0:B]
+        image[2] = image_in[w, B:]
+        image[3] = out[B:].astype(BF)
         if w == 0:
             following = stack(field[1, 0:B, D:], field[1, 3 * B :, D:]).astype(F32)
             current = following - out
@@ -223,8 +223,6 @@
         returned[w] = back
         send_left[w] = dot(tmat[0, :, 0:B], back[0:B].astype(BF)).astype(BF)
         send_right[w] = dot(tmat[G - 1, :, 2 * B :], back[B:].astype(BF)).astype(BF)
-    for k, im in enumerate((im0, im1, im2, im3)):
-        im[...] = image[lax.rem(y + k, G)]
 
 
 def spread_edge(tmat, edge, narrow):
@@ -251,14 +249,14 @@
         send_right[w] = dot(tmat[G - 1, :, 2 * B :], back[B:].astype(BF)).astype(BF)
 
 
-def inner3_kernel(inner, edge, tmat, i0, i1, i2, i3, cur_edge, cur_inner, last, hat):
-    y = member()
-    for k, im in enumerate((i0, i1, i2, i3)):
-
-        @pl.when(origin(y, k) == G - 1)
-        def _():
-            last[...] = im[NW - 1]
-
+def inner3_kernel(
+    inner, edge, tmat, image0, image1, before, cur_edge, cur_inner, im0, im1, im2, im3, hat
+):
+    y = member()
+    for k, im in enumerate((im0, im1, im2, im3)):
+        block = lax.rem(y + k, G)
+        im[0] = image0[block]
+        im[1] = jnp.where(y == G - 1, before[block], image1[block])
     pair_matrix(tmat, hat)
     for w in range(NW):
         narrow = stack(edge[w, 0:B], inner[w], edge[w, B:]).astype(BF)
@@ -277,7 +275,7 @@
         out[...] = all_blocks[lax.rem(y + k, G)]
 
 
-def misfit_kernel(inc, i0, i1, i2, i3, before, misfit, kept):
+def misfit_kernel(inc, i0, i1, i2, i3, misfit, kept):
     y = member()
     for k, im in enumerate((i0, i1, i2, i3)):
         m = origin(y, k)
@@ -285,8 +283,7 @@
         misfit[NW * m + 1] = value
         kept[NW * m + 1] = value
         even = NW * lax.rem(m + 1, G)
-        image = jnp.where(m == G - 1, before[...], im[1])
-        value = inc[even] - image.astype(F32)
+        value = inc[even] - im[1].astype(F32)
         misfit[even] = value
         kept[even] = value
 
@@ -336,6 +333,13 @@
     return pairs
 
 
+def last_image_pairs():
+    return [
+        (t * PARTS + b, (t + 1) * PARTS + b)
+        for t in range(TM - 1) for b in range(PARTS) if b % G == G - 1
+    ]
+
+
 def to_members(sends):
     return [lax.ppermute(sends[k], "mesh", group_pairs(k)) for k in range(1, G)]
 
@@ -367,10 +371,10 @@
 
     got = [[own[w], *got[w]] for w in range(NW)]
     lo, hi, nxt = call(edge_kernel, got[0], [item, item, sds((G, B, D))])
+    nxt = lax.ppermute(nxt, ("tm", "mesh"), next_increment_pairs())
     halo = [swap_sides(lo, hi)]
     lo, hi = call(edge_kernel, got[1], [item, item])
     halo.append(swap_sides(lo, hi))
-    nxt = lax.ppermute(nxt, ("tm", "mesh"), next_increment_pairs())
     field, amat0, tmat0, base_in, tan_in, slope_in = call(
         inner0_kernel, (*got[0], *got[1], *folded, *weights),
         [sds((NW, G * B, 2 * D)), mats, mats, pair_bf, pair, hidden], (hat,),
@@ -391,14 +395,14 @@
         inner1_kernel, (base_in, tan_in, *lo, *hi, field, *folded, nxt, *weights),
         [mats, mats, pair_bf, pair], (hat, slope1),
     )
-    *images, edge, send_left, send_right = call(
+    image0, image1, edge, send_left, send_right = call(
         edge1_kernel,
         (*lo, *hi, *tan_edge, *left, *right, base_in, tan_in, field, nxt, amat1, tmat1, image_in, *weights),
-        [half] * G + [pair, half, half], (slope1, pltpu.VMEM((G, NW, B, D), BF)),
+        [sds((G, B, D))] * NW + [pair, half, half], (slope1,),
     )
 
     left, right = swap_sides(send_left, send_right)
-    images = [images[0], *to_members(images)]
+    before = lax.ppermute(image1, ("tm", "mesh"), last_image_pairs())
     cur_edge, inner = call(
         inner2_kernel, (inner, edge, tmat1, slope_in, inner_weight, outer_weight),
         [pair, pair], (hat,)
@@ -409,17 +413,18 @@
     )
 
     left, right = swap_sides(send_left, send_right)
-    cur_edge, cur_inner, last = call(
-        inner3_kernel, (inner, edge, tmat0, *images), [pair, pair_bf, sds((B, D))], (hat,),
-    )
-    before = lax.ppermute(last, "tm", [(t, t + 1) for t in range(TM - 1)])
+    cur_edge, cur_inner, *images = call(
+        inner3_kernel, (inner, edge, tmat0, image0, image1, before),
+        [pair, pair_bf] + [half] * G, (hat,),
+    )
+    images = [images[0], *to_members(images)]
     parts = call(
         finish_kernel, (cur_edge, cur_inner, left, right), [half] * G,
         (pltpu.VMEM((G, NW, B, D), BF),),
     )
     parts = [parts[0], *to_members(parts)]
     whole = sds(increment.shape, F32)
-    misfit, kept = call(misfit_kernel, (increment, *images, before), [whole, whole])
+    misfit, kept = call(misfit_kernel, (increment, *images), [whole, whole])
     (normal,) = call(normal_kernel, (kept, *parts), [whole])
     return misfit, normal
 

time: 108 us -> 109 us (level)
  waiting for transfers between devices: 26 us -> 32.3 us
  starting transfers between devices: 60.9 us -> 55.8 us
    ppermute x15, waiting for transfers between devices: 13.8 us -> 20.6 us  [to_members(): return [lax.ppermute(sends[k], 'mesh', group_pairs(k)) for k in range(1, G)]]
    ppermute x1, starting transfers between devices: 4.71 us -> 0.68 us  [local(): before = lax.ppermute(image1, ('tm', 'mesh'), last_image_pairs())]
    ppermute x1, waiting for transfers between devices: 1.31 us -> 0.01 us  [local(): before = lax.ppermute(image1, ('tm', 'mesh'), last_image_pairs())]
  transfers between devices with their start and end apart: 29 -> 29, of which waited for: 7 -> 9; matrix products, arithmetic and copies ran while one was open for 0% -> 0% of each run, Pallas kernels for 12% -> 12%
where the time goes in v6:
time: 109 us
  starting transfers between devices  55.8 us (51%)
  waiting for transfers between devices  32.3 us (30%)
  Pallas kernels  17 us (16%)
  local copies, waits for them, and re-layouts  3.23 us (3%)
    ppermute x6, starting transfers between devices, swap_sides(): right = lax.ppermute(send_left, 'mesh', side_pairs(-1))  31.3 us
    ppermute x15, waiting for transfers between devices, to_members(): return [lax.ppermute(sends[k], 'mesh', group_pairs(k)) for k in range(1, G)]  20.6 us
    pallas_call x15, Pallas kernels, call(): pl.pallas_call(kernel, out_shape=outs, in_specs=[SMEM] * smem + [VMEM] *...  17 us
    ppermute x15, starting transfers between devices, to_members(): return [lax.ppermute(sends[k], 'mesh', group_pairs(k)) for k in range(1, G)]  16.3 us
    ppermute x6, waiting for transfers between devices, swap_sides(): left = lax.ppermute(send_right, 'mesh', side_pairs(1))  8.96 us
    ppermute x1, starting transfers between devices, local(): nxt = lax.ppermute(nxt, ('tm', 'mesh'), next_increment_pairs())  4.6 us
    unnamed x18, local copies, waits for them, and re-layouts  3.23 us
    ppermute x6, starting transfers between devices, swap_sides(): left = lax.ppermute(send_right, 'mesh', side_pairs(1))  2.91 us
  transfers between devices with their start and end apart: 29, of which 9 were waited for; matrix products, arithmetic and copies ran while one was open for 0% of the time, Pallas kernels for 12%

profile of v6, /device:TPU:1, one launch (start us, length us, event | category | flops | bytes accessed | tf_op | source)
XLA Modules:
  0.0 109.2 jit_solution(14065021648358812721)
XLA Ops:
  0.6 1.2 %copy-done.2 = f32[8,128,256]{2,1,0:T(8,128)S(1)} copy-done((f32[8,128,256]{2,1,0:T(8,128)S(1)}, f32[8,128,256]{2,1,0:T(8,128)}, u32[]{:S(2)}) %copy-start.2) | copy-done | bytes 1048600
  3.0 2.2 %collective-permute-start = (bf16[2,128,256]{2,1,0:T(8,128)(2,1)S(1)}, bf16[2,128,256]{2,1,0:T(8,128)(2,1)S(1)}, u32[]{:S(2)}, u32[]{:S(2)}) collective-permute-start(bf16[2,128,256]{2,1,0:T(8,128)(2,1)S(1)} %get-tuple-element.57), channel_id=1, source_target_pairs={{0,1},{1,2},{2,3},{3,0},{4,5},{5,6},{6,7},{7,4},{8,9},{9,10},{10,1... | collective-permute-start | bytes 393224 | tf_op jit(solution)/shard_map/ppermute | solution.py:344
  5.2 1.3 %collective-permute-start.3 = (bf16[2,128,256]{2,1,0:T(8,128)(2,1)S(1)}, bf16[2,128,256]{2,1,0:T(8,128)(2,1)S(1)}, u32[]{:S(2)}, u32[]{:S(2)}) collective-permute-start(bf16[2,128,256]{2,1,0:T(8,128)(2,1)S(1)} %get-tuple-element.61), channel_id=1, source_target_pairs={{0,1},{1,2},{2,3},{3,0},{4,5},{5,6},{6,7},{7,4},{8,9},{9,10},{10,1... | collective-permute-start | bytes 393224 | tf_op jit(solution)/shard_map/ppermute | solution.py:344
  6.5 1.4 %collective-permute-start.4 = (bf16[2,128,256]{2,1,0:T(8,128)(2,1)S(1)}, bf16[2,128,256]{2,1,0:T(8,128)(2,1)S(1)}, u32[]{:S(2)}, u32[]{:S(2)}) collective-permute-start(bf16[2,128,256]{2,1,0:T(8,128)(2,1)S(1)} %get-tuple-element.62), channel_id=1, source_target_pairs={{0,2},{1,3},{2,0},{3,1},{4,6},{5,7},{6,4},{7,5},{8,10},{9,11},{10,... | collective-permute-start | bytes 393224 | tf_op jit(solution)/shard_map/ppermute | solution.py:344
  7.9 2.0 %collective-permute-start.5 = (bf16[2,128,256]{2,1,0:T(8,128)(2,1)S(1)}, bf16[2,128,256]{2,1,0:T(8,128)(2,1)S(1)}, u32[]{:S(2)}, u32[]{:S(2)}) collective-permute-start(bf16[2,128,256]{2,1,0:T(8,128)(2,1)S(1)} %get-tuple-element.63), channel_id=1, source_target_pairs={{0,3},{1,0},{2,1},{3,2},{4,7},{5,4},{6,5},{7,6},{8,11},{9,8},{10,9... | collective-permute-start | bytes 393224 | tf_op jit(solution)/shard_map/ppermute | solution.py:344
  13.2 3.1 %collective-permute-done.4.r12.r2 = bf16[2,128,256]{2,1,0:T(8,128)(2,1)S(1)} collective-permute-done((bf16[2,128,256]{2,1,0:T(8,128)(2,1)S(1)}, bf16[2,128,256]{2,1,0:T(8,128)(2,1)S(1)}, u32[]{:S(2)}, u32[]{:S(2)}) %collective-permute-start.4) | collective-permute-done | bytes 131104 | tf_op jit(solution)/shard_map/ppermute | solution.py:344
  17.0 10.6 %collective-permute-done.1.r02.r2 = bf16[2,128,256]{2,1,0:T(8,128)(2,1)S(1)} collective-permute-done((bf16[2,128,256]{2,1,0:T(8,128)(2,1)S(1)}, bf16[2,128,256]{2,1,0:T(8,128)(2,1)S(1)}, u32[]{:S(2)}, u32[]{:S(2)}) %collective-permute-start.1) | collective-permute-done | bytes 131104 | tf_op jit(solution)/shard_map/ppermute | solution.py:344
  27.6 1.2 %collective-permute-start.11 = (bf16[2,128,256]{2,1,0:T(8,128)(2,1)S(1)}, bf16[2,128,256]{2,1,0:T(8,128)(2,1)S(1)}, u32[]{:S(2)}, u32[]{:S(2)}) collective-permute-start(bf16[2,128,256]{2,1,0:T(8,128)(2,1)S(1)} %get-tuple-element.72), channel_id=1, source_target_pairs={{0,4},{1,5},{2,6},{3,7},{4,8},{5,9},{6,10},{7,11},{8,12},{9,13},{1... | collective-permute-start | bytes 393224 | tf_op jit(solution)/shard_map/ppermute | solution.py:348
  28.8 7.5 %collective-permute-start.12 = (bf16[2,128,256]{2,1,0:T(8,128)(2,1)S(1)}, bf16[2,128,256]{2,1,0:T(8,128)(2,1)S(1)}, u32[]{:S(2)}, u32[]{:S(2)}) collective-permute-start(bf16[2,128,256]{2,1,0:T(8,128)(2,1)S(1)} %get-tuple-element.73), channel_id=1, source_target_pairs={{0,60},{1,61},{2,62},{3,63},{4,0},{5,1},{6,2},{7,3},{8,4},{9,5},{1... | collective-permute-start | bytes 393224 | tf_op jit(solution)/shard_map/ppermute | solution.py:349
  36.5 4.6 %collective-permute-start.13 = (bf16[4,128,256]{2,1,0:T(8,128)(2,1)S(1)}, bf16[4,128,256]{2,1,0:T(8,128)(2,1)S(1)}, u32[]{:S(2)}, u32[]{:S(2)}) collective-permute-start(bf16[4,128,256]{2,1,0:T(8,128)(2,1)S(1)} %get-tuple-element.77), channel_id=1, source_target_pairs={{0,195},{1,0},{2,1},{3,2},{4,199},{5,4},{6,5},{7,6},{8,203},{9,8},... | collective-permute-start | bytes 786440 | tf_op jit(solution)/shard_map/ppermute | solution.py:374
  41.1 5.9 %collective-permute-start.10 = (bf16[2,128,256]{2,1,0:T(8,128)(2,1)S(1)}, bf16[2,128,256]{2,1,0:T(8,128)(2,1)S(1)}, u32[]{:S(2)}, u32[]{:S(2)}) collective-permute-start(bf16[2,128,256]{2,1,0:T(8,128)(2,1)S(1)} %get-tuple-element.70), channel_id=1, source_target_pairs={{0,60},{1,61},{2,62},{3,63},{4,0},{5,1},{6,2},{7,3},{8,4},{9,5},{1... | collective-permute-start | bytes 393224 | tf_op jit(solution)/shard_map/ppermute | solution.py:349
  46.9 2.2 %shard_map.88 = (bf16[2,512,512]{2,1,0:T(8,128)(2,1)S(1)}, bf16[4,128,384]{2,1,0:T(8,128)(2,1)S(1)}, bf16[4,128,384]{2,1,0:T(8,128)(2,1)S(1)}, bf16[2,256,256]{2...) custom-call(bf16[2,128,256]{2,1,0:T(8,128)(2,1)S(1)} %get-tuple-element.56.r00.r0, ...), custom_call_target="tpu_custom_call" | custom-call | tf_op jit(solution)/shard_map/pallas_call | solution.py:309
  49.2 1.1 %shard_map.92 = (bf16[2,128,256]{2,1,0:T(8,128)(2,1)S(1)}, bf16[2,128,256]{2,1,0:T(8,128)(2,1)S(1)}, f32[256,256]{1,0:T(8,128)S(1)}, bf16[256,1024]{1,0:T(8,128)(2,1)S(1)}) custom-call(bf16[2,512,512]{2,1,0:T(8,128)(2,1)S(1)} %get-tuple-element.67.field, bf16[4,128,384]{2,1,0:T(8,128)(2,1)S(1)} %get-tuple-element.68.amat, ...), custom_call_target="tpu_custom_call" | custom-call | tf_op jit(solution)/shard_map/pallas_call | solution.py:309
  50.4 1.4 %collective-permute-start.15 = (bf16[2,128,256]{2,1,0:T(8,128)(2,1)S(1)}, bf16[2,128,256]{2,1,0:T(8,128)(2,1)S(1)}, u32[]{:S(2)}, u32[]{:S(2)}) collective-permute-start(bf16[2,128,256]{2,1,0:T(8,128)(2,1)S(1)} %get-tuple-element.76.hi1), channel_id=1, source_target_pairs={{0,4},{1,5},{2,6},{3,7},{4,8},{5,9},{6,10},{7,11},{8,12},{9,13},{1... | collective-permute-start | bytes 393224 | tf_op jit(solution)/shard_map/ppermute | solution.py:348
  51.9 2.6 %collective-permute-done.10.right = bf16[2,128,256]{2,1,0:T(8,128)(2,1)S(1)} collective-permute-done((bf16[2,128,256]{2,1,0:T(8,128)(2,1)S(1)}, bf16[2,128,256]{2,1,0:T(8,128)(2,1)S(1)}, u32[]{:S(2)}, u32[]{:S(2)}) %collective-permute-start.10) | collective-permute-done | bytes 131104 | tf_op jit(solution)/shard_map/ppermute | solution.py:349
  54.5 1.1 %shard_map.90 = (bf16[2,128,256]{2,1,0:T(8,128)(2,1)S(1)}, bf16[2,128,256]{2,1,0:T(8,128)(2,1)S(1)}, f32[256,256]{1,0:T(8,128)S(1)}, bf16[256,1024]{1,0:T(8,128)(2,1)S(1)}) custom-call(bf16[2,512,512]{2,1,0:T(8,128)(2,1)S(1)} %get-tuple-element.67.field, bf16[4,128,384]{2,1,0:T(8,128)(2,1)S(1)} %get-tuple-element.68.amat, ...), custom_call_target="tpu_custom_call" | custom-call | tf_op jit(solution)/shard_map/pallas_call | solution.py:309
  55.6 6.5 %collective-permute-start.16 = (bf16[2,128,256]{2,1,0:T(8,128)(2,1)S(1)}, bf16[2,128,256]{2,1,0:T(8,128)(2,1)S(1)}, u32[]{:S(2)}, u32[]{:S(2)}) collective-permute-start(bf16[2,128,256]{2,1,0:T(8,128)(2,1)S(1)} %get-tuple-element.71.lo0), channel_id=1, source_target_pairs={{0,60},{1,61},{2,62},{3,63},{4,0},{5,1},{6,2},{7,3},{8,4},{9,5},{1... | collective-permute-start | bytes 393224 | tf_op jit(solution)/shard_map/ppermute | solution.py:349
  62.1 3.0 %shard_map.93 = (bf16[4,128,384]{2,1,0:T(8,128)(2,1)S(1)}, bf16[4,128,384]{2,1,0:T(8,128)(2,1)S(1)}, bf16[2,256,256]{2,1,0:T(8,128)(2,1)S(1)}, f32[2,256,256]{2,1,0:T(8,128)S(1)}) custom-call(bf16[2,256,256]{2,1,0:T(8,128)(2,1)S(1)} %get-tuple-element.65.base_in, f32[2,256,256]{2,1,0:T(8,128)S(1)} %get-tuple-element.66.tan_in, ...), custom_call_target="tpu_custom_call" | custom-call | tf_op jit(solution)/shard_map/pallas_call | solution.py:309
  65.3 6.4 %collective-permute-done.14.left0 = bf16[2,128,256]{2,1,0:T(8,128)(2,1)S(1)} collective-permute-done((bf16[2,128,256]{2,1,0:T(8,128)(2,1)S(1)}, bf16[2,128,256]{2,1,0:T(8,128)(2,1)S(1)}, u32[]{:S(2)}, u32[]{:S(2)}) %collective-permute-start.14) | collective-permute-done | bytes 131104 | tf_op jit(solution)/shard_map/ppermute | solution.py:348
  71.7 3.2 %shard_map.94 = (bf16[4,128,256]{2,1,0:T(8,128)(2,1)S(1)}, bf16[4,128,256]{2,1,0:T(8,128)(2,1)S(1)}, f32[2,256,256]{2,1,0:T(8,128)S(1)}, bf16[2,128,256]{2,1,0:T(8,128)(2,1)S(1)}, bf16[2,128,256]{2,1,0:T(8,128)(2,1)S(1)}) custom-call(bf16[2,128,256]{2,1,0:T(8,128)(2,1)S(1)} %get-tuple-element.71.lo0, bf16[2,128,256]{2,1,0:T(8,128)(2,1)S(1)} %get-tuple-element.74.lo1, ...), custom_call_target="tpu_custom_call" | custom-call | tf_op jit(solution)/shard_map/pallas_call | solution.py:309
  75.8 5.7 %collective-permute-start.19 = (bf16[2,128,256]{2,1,0:T(8,128)(2,1)S(1)}, bf16[2,128,256]{2,1,0:T(8,128)(2,1)S(1)}, u32[]{:S(2)}, u32[]{:S(2)}) collective-permute-start(bf16[2,128,256]{2,1,0:T(8,128)(2,1)S(1)} %get-tuple-element.89), channel_id=1, source_target_pairs={{0,60},{1,61},{2,62},{3,63},{4,0},{5,1},{6,2},{7,3},{8,4},{9,5},{1... | collective-permute-start | bytes 393224 | tf_op jit(solution)/shard_map/ppermute | solution.py:349
  81.4 1.4 %shard_map.95 = (f32[2,256,256]{2,1,0:T(8,128)S(1)}, f32[2,256,256]{2,1,0:T(8,128)S(1)}) custom-call(f32[2,256,256]{2,1,0:T(8,128)S(1)} %get-tuple-element.78.inner, f32[2,256,256]{2,1,0:T(8,128)S(1)} %get-tuple-element.84.edge, bf16[4,128,384]{2,1,0:T(8,128)(2,1)S(1)} %get-tuple-element.82.tmat, bf16[2,256,1024]{2,1,0:T(8,128)(2,1)S(1)} %get-tuple-element.85.slope, ...), custom_call_target="tpu_custom_call" | custom-call | tf_op jit(solution)/shard_map/pallas_call | solution.py:309
  82.8 2.5 %collective-permute-done.18.left = bf16[2,128,256]{2,1,0:T(8,128)(2,1)S(1)} collective-permute-done((bf16[2,128,256]{2,1,0:T(8,128)(2,1)S(1)}, bf16[2,128,256]{2,1,0:T(8,128)(2,1)S(1)}, u32[]{:S(2)}, u32[]{:S(2)}) %collective-permute-start.18) | collective-permute-done | bytes 131104 | tf_op jit(solution)/shard_map/ppermute | solution.py:348
  85.3 1.3 %shard_map.96 = (f32[2,256,256]{2,1,0:T(8,128)S(1)}, bf16[2,128,256]{2,1,0:T(8,128)(2,1)S(1)}, bf16[2,128,256]{2,1,0:T(8,128)(2,1)S(1)}) custom-call(f32[2,256,256]{2,1,0:T(8,128)S(1)} %get-tuple-element.87.cur_edge, bf16[2,128,256]{2,1,0:T(8,128)(2,1)S(1)} %collective-permute-done.18.left, bf16[2,128,256]{2,1,0:T(8,128)(2,1)S(1)} %collective-permute-done.19.right, ...), custom_call_target="tpu_custom_call" | custom-call | tf_op jit(solution)/shard_map/pallas_call | solution.py:309
  86.7 5.7 %collective-permute-start.25 = (bf16[2,128,256]{2,1,0:T(8,128)(2,1)S(1)}, bf16[2,128,256]{2,1,0:T(8,128)(2,1)S(1)}, u32[]{:S(2)}, u32[]{:S(2)}) collective-permute-start(bf16[2,128,256]{2,1,0:T(8,128)(2,1)S(1)} %get-tuple-element.105), channel_id=1, source_target_pairs={{0,60},{1,61},{2,62},{3,63},{4,0},{5,1},{6,2},{7,3},{8,4},{9,5},{1... | collective-permute-start | bytes 393224 | tf_op jit(solution)/shard_map/ppermute | solution.py:349
  92.9 3.1 %collective-permute-start.22 = (bf16[2,128,256]{2,1,0:T(8,128)(2,1)S(1)}, bf16[2,128,256]{2,1,0:T(8,128)(2,1)S(1)}, u32[]{:S(2)}, u32[]{:S(2)}) collective-permute-start(bf16[2,128,256]{2,1,0:T(8,128)(2,1)S(1)} %get-tuple-element.98), channel_id=1, source_target_pairs={{0,2},{1,3},{2,0},{3,1},{4,6},{5,7},{6,4},{7,5},{8,10},{9,11},{10,... | collective-permute-start | bytes 393224 | tf_op jit(solution)/shard_map/ppermute | solution.py:344
  96.2 1.5 %collective-permute-start.26 = (bf16[2,128,256]{2,1,0:T(8,128)(2,1)S(1)}, bf16[2,128,256]{2,1,0:T(8,128)(2,1)S(1)}, u32[]{:S(2)}, u32[]{:S(2)}) collective-permute-start(bf16[2,128,256]{2,1,0:T(8,128)(2,1)S(1)} %get-tuple-element.107), channel_id=1, source_target_pairs={{0,1},{1,2},{2,3},{3,0},{4,5},{5,6},{6,7},{7,4},{8,9},{9,10},{10,1... | collective-permute-start | bytes 393224 | tf_op jit(solution)/shard_map/ppermute | solution.py:344
  97.7 1.9 %collective-permute-start.27 = (bf16[2,128,256]{2,1,0:T(8,128)(2,1)S(1)}, bf16[2,128,256]{2,1,0:T(8,128)(2,1)S(1)}, u32[]{:S(2)}, u32[]{:S(2)}) collective-permute-start(bf16[2,128,256]{2,1,0:T(8,128)(2,1)S(1)} %get-tuple-element.108), channel_id=1, source_target_pairs={{0,2},{1,3},{2,0},{3,1},{4,6},{5,7},{6,4},{7,5},{8,10},{9,11},{10,... | collective-permute-start | bytes 393224 | tf_op jit(solution)/shard_map/ppermute | solution.py:344
  100.2 2.3 %collective-permute-done.22.i2 = bf16[2,128,256]{2,1,0:T(8,128)(2,1)S(1)} collective-permute-done((bf16[2,128,256]{2,1,0:T(8,128)(2,1)S(1)}, bf16[2,128,256]{2,1,0:T(8,128)(2,1)S(1)}, u32[]{:S(2)}, u32[]{:S(2)}) %collective-permute-start.22) | collective-permute-done | bytes 131104 | tf_op jit(solution)/shard_map/ppermute | solution.py:344
  102.5 1.1 %shard_map.98 = (f32[8,128,256]{2,1,0:T(8,128)}, f32[8,128,256]{2,1,0:T(8,128)S(1)}) custom-call(f32[8,128,256]{2,1,0:T(8,128)S(1)} %copy-done.3, bf16[2,128,256]{2,1,0:T(8,128)(2,1)S(1)} %get-tuple-element.96.i0, bf16[2,128,256]{2,1,0:T(8,128)(2,1)S(1)} %collective-permute-done.21.i1, bf16[2,128,256]{2,1,0:T(8,128)(2,1)S(1)} %collective-permute-done.22.i2, ...), custom_call_target="tpu_custom_call" | custom-call | tf_op jit(solution)/shard_map/pallas_call | solution.py:309
  103.7 1.4 %collective-permute-done.26.p1 = bf16[2,128,256]{2,1,0:T(8,128)(2,1)S(1)} collective-permute-done((bf16[2,128,256]{2,1,0:T(8,128)(2,1)S(1)}, bf16[2,128,256]{2,1,0:T(8,128)(2,1)S(1)}, u32[]{:S(2)}, u32[]{:S(2)}) %collective-permute-start.26) | collective-permute-done | bytes 131104 | tf_op jit(solution)/shard_map/ppermute | solution.py:344
  105.1 3.1 %collective-permute-done.27.p2 = bf16[2,128,256]{2,1,0:T(8,128)(2,1)S(1)} collective-permute-done((bf16[2,128,256]{2,1,0:T(8,128)(2,1)S(1)}, bf16[2,128,256]{2,1,0:T(8,128)(2,1)S(1)}, u32[]{:S(2)}, u32[]{:S(2)}) %collective-permute-start.27) | collective-permute-done | bytes 131104 | tf_op jit(solution)/shard_map/ppermute | solution.py:344
  (59 shorter events, 8.6 us)
Async XLA Ops:
  3.0 8.8 %collective-permute-start = (bf16[2,128,256]{2,1,0:T(8,128)(2,1)S(1)}, bf16[2,128,256]{2,1,0:T(8,128)(2,1)S(1)}, u32[]{:S(2)}, u32[]{:S(2)}) collective-permute-start(bf16[2,128,256]{2,1,0:T(8,128)(2,1)S(1)} %get-tuple-element.57), channel_id=1, source_target_pairs={{0,1},{1,2},{2,3},{3,0},{4,5},{5,6},{6,7},{7,4},{8,9},{9,10},{10,1... | collective-permute-start | bytes 393224 | tf_op jit(solution)/shard_map/ppermute | solution.py:344
  5.2 7.7 %collective-permute-start.3 = (bf16[2,128,256]{2,1,0:T(8,128)(2,1)S(1)}, bf16[2,128,256]{2,1,0:T(8,128)(2,1)S(1)}, u32[]{:S(2)}, u32[]{:S(2)}) collective-permute-start(bf16[2,128,256]{2,1,0:T(8,128)(2,1)S(1)} %get-tuple-element.61), channel_id=1, source_target_pairs={{0,1},{1,2},{2,3},{3,0},{4,5},{5,6},{6,7},{7,4},{8,9},{9,10},{10,1... | collective-permute-start | bytes 393224 | tf_op jit(solution)/shard_map/ppermute | solution.py:344
  6.5 9.9 %collective-permute-start.4 = (bf16[2,128,256]{2,1,0:T(8,128)(2,1)S(1)}, bf16[2,128,256]{2,1,0:T(8,128)(2,1)S(1)}, u32[]{:S(2)}, u32[]{:S(2)}) collective-permute-start(bf16[2,128,256]{2,1,0:T(8,128)(2,1)S(1)} %get-tuple-element.62), channel_id=1, source_target_pairs={{0,2},{1,3},{2,0},{3,1},{4,6},{5,7},{6,4},{7,5},{8,10},{9,11},{10,... | collective-permute-start | bytes 393224 | tf_op jit(solution)/shard_map/ppermute | solution.py:344
  7.9 39.1 %copy-start = (bf16[2,256,1024]{2,1,0:T(8,128)(2,1)S(1)}, bf16[2,256,1024]{2,1,0:T(8,128)(2,1)}, u32[]{:S(2)}) copy-start(bf16[2,256,1024]{2,1,0:T(8,128)(2,1)} %win.13) | copy-start | bytes 3145732
  7.9 39.1 %copy-start.1 = (bf16[2,1024,256]{2,1,0:T(8,128)(2,1)S(1)}, bf16[2,1024,256]{2,1,0:T(8,128)(2,1)}, u32[]{:S(2)}) copy-start(bf16[2,1024,256]{2,1,0:T(8,128)(2,1)} %wout.13) | copy-start | bytes 3145732
  7.9 8.8 %collective-permute-start.5 = (bf16[2,128,256]{2,1,0:T(8,128)(2,1)S(1)}, bf16[2,128,256]{2,1,0:T(8,128)(2,1)S(1)}, u32[]{:S(2)}, u32[]{:S(2)}) collective-permute-start(bf16[2,128,256]{2,1,0:T(8,128)(2,1)S(1)} %get-tuple-element.63), channel_id=1, source_target_pairs={{0,3},{1,0},{2,1},{3,2},{4,7},{5,4},{6,5},{7,6},{8,11},{9,8},{10,9... | collective-permute-start | bytes 393224 | tf_op jit(solution)/shard_map/ppermute | solution.py:344
  11.5 24.8 %collective-permute-start.8 = (bf16[128,768]{1,0:T(8,128)(2,1)S(1)}, bf16[128,768]{1,0:T(8,128)(2,1)S(1)}, u32[]{:S(2)}, u32[]{:S(2)}) collective-permute-start(bf16[128,768]{1,0:T(8,128)(2,1)S(1)} %get-tuple-element.64.a0), channel_id=1, source_target_pairs={{0,3},{1,0},{2,1},{3,2},{4,7},{5,4},{6,5},{7,6},{8,11},{9,8},{10,9... | collective-permute-start | bytes 589832 | tf_op jit(solution)/shard_map/ppermute | solution.py:344
  11.8 24.7 %collective-permute-start.7 = (bf16[128,768]{1,0:T(8,128)(2,1)S(1)}, bf16[128,768]{1,0:T(8,128)(2,1)S(1)}, u32[]{:S(2)}, u32[]{:S(2)}) collective-permute-start(bf16[128,768]{1,0:T(8,128)(2,1)S(1)} %get-tuple-element.64.a0), channel_id=1, source_target_pairs={{0,2},{1,3},{2,0},{3,1},{4,6},{5,7},{6,4},{7,5},{8,10},{9,11},{10,... | collective-permute-start | bytes 589832 | tf_op jit(solution)/shard_map/ppermute | solution.py:344
  12.9 28.2 %collective-permute-start.6 = (bf16[128,768]{1,0:T(8,128)(2,1)S(1)}, bf16[128,768]{1,0:T(8,128)(2,1)S(1)}, u32[]{:S(2)}, u32[]{:S(2)}) collective-permute-start(bf16[128,768]{1,0:T(8,128)(2,1)S(1)} %get-tuple-element.64.a0), channel_id=1, source_target_pairs={{0,1},{1,2},{2,3},{3,0},{4,5},{5,6},{6,7},{7,4},{8,9},{9,10},{10,1... | collective-permute-start | bytes 589832 | tf_op jit(solution)/shard_map/ppermute | solution.py:344
  16.3 11.3 %collective-permute-start.1 = (bf16[2,128,256]{2,1,0:T(8,128)(2,1)S(1)}, bf16[2,128,256]{2,1,0:T(8,128)(2,1)S(1)}, u32[]{:S(2)}, u32[]{:S(2)}) collective-permute-start(bf16[2,128,256]{2,1,0:T(8,128)(2,1)S(1)} %get-tuple-element.58), channel_id=1, source_target_pairs={{0,2},{1,3},{2,0},{3,1},{4,6},{5,7},{6,4},{7,5},{8,10},{9,11},{10,... | collective-permute-start | bytes 393224 | tf_op jit(solution)/shard_map/ppermute | solution.py:344
  16.7 12.1 %collective-permute-start.2 = (bf16[2,128,256]{2,1,0:T(8,128)(2,1)S(1)}, bf16[2,128,256]{2,1,0:T(8,128)(2,1)S(1)}, u32[]{:S(2)}, u32[]{:S(2)}) collective-permute-start(bf16[2,128,256]{2,1,0:T(8,128)(2,1)S(1)} %get-tuple-element.59), channel_id=1, source_target_pairs={{0,3},{1,0},{2,1},{3,2},{4,7},{5,4},{6,5},{7,6},{8,11},{9,8},{10,9... | collective-permute-start | bytes 393224 | tf_op jit(solution)/shard_map/ppermute | solution.py:344
  27.6 21.6 %collective-permute-start.11 = (bf16[2,128,256]{2,1,0:T(8,128)(2,1)S(1)}, bf16[2,128,256]{2,1,0:T(8,128)(2,1)S(1)}, u32[]{:S(2)}, u32[]{:S(2)}) collective-permute-start(bf16[2,128,256]{2,1,0:T(8,128)(2,1)S(1)} %get-tuple-element.72), channel_id=1, source_target_pairs={{0,4},{1,5},{2,6},{3,7},{4,8},{5,9},{6,10},{7,11},{8,12},{9,13},{1... | collective-permute-start | bytes 393224 | tf_op jit(solution)/shard_map/ppermute | solution.py:348
  28.8 20.4 %collective-permute-start.12 = (bf16[2,128,256]{2,1,0:T(8,128)(2,1)S(1)}, bf16[2,128,256]{2,1,0:T(8,128)(2,1)S(1)}, u32[]{:S(2)}, u32[]{:S(2)}) collective-permute-start(bf16[2,128,256]{2,1,0:T(8,128)(2,1)S(1)} %get-tuple-element.73), channel_id=1, source_target_pairs={{0,60},{1,61},{2,62},{3,63},{4,0},{5,1},{6,2},{7,3},{8,4},{9,5},{1... | collective-permute-start | bytes 393224 | tf_op jit(solution)/shard_map/ppermute | solution.py:349
  36.3 10.7 %copy-start.7 = (f32[2,1024]{1,0:T(2,128)S(1)}, f32[2,1024]{1,0:T(2,128)}, u32[]{:S(2)}) copy-start(f32[2,1024]{1,0:T(2,128)} %bias.9) | copy-start | bytes 24580
  36.4 15.5 %collective-permute-start.9 = (bf16[2,128,256]{2,1,0:T(8,128)(2,1)S(1)}, bf16[2,128,256]{2,1,0:T(8,128)(2,1)S(1)}, u32[]{:S(2)}, u32[]{:S(2)}) collective-permute-start(bf16[2,128,256]{2,1,0:T(8,128)(2,1)S(1)} %get-tuple-element.69), channel_id=1, source_target_pairs={{0,4},{1,5},{2,6},{3,7},{4,8},{5,9},{6,10},{7,11},{8,12},{9,13},{1... | collective-permute-start | bytes 393224 | tf_op jit(solution)/shard_map/ppermute | solution.py:348
  36.5 25.7 %collective-permute-start.13 = (bf16[4,128,256]{2,1,0:T(8,128)(2,1)S(1)}, bf16[4,128,256]{2,1,0:T(8,128)(2,1)S(1)}, u32[]{:S(2)}, u32[]{:S(2)}) collective-permute-start(bf16[4,128,256]{2,1,0:T(8,128)(2,1)S(1)} %get-tuple-element.77), channel_id=1, source_target_pairs={{0,195},{1,0},{2,1},{3,2},{4,199},{5,4},{6,5},{7,6},{8,203},{9,8},... | collective-permute-start | bytes 786440 | tf_op jit(solution)/shard_map/ppermute | solution.py:374
  41.1 13.4 %collective-permute-start.10 = (bf16[2,128,256]{2,1,0:T(8,128)(2,1)S(1)}, bf16[2,128,256]{2,1,0:T(8,128)(2,1)S(1)}, u32[]{:S(2)}, u32[]{:S(2)}) collective-permute-start(bf16[2,128,256]{2,1,0:T(8,128)(2,1)S(1)} %get-tuple-element.70), channel_id=1, source_target_pairs={{0,60},{1,61},{2,62},{3,63},{4,0},{5,1},{6,2},{7,3},{8,4},{9,5},{1... | collective-permute-start | bytes 393224 | tf_op jit(solution)/shard_map/ppermute | solution.py:349
  50.3 14.8 %collective-permute-start.17 = (bf16[2,128,256]{2,1,0:T(8,128)(2,1)S(1)}, bf16[2,128,256]{2,1,0:T(8,128)(2,1)S(1)}, u32[]{:S(2)}, u32[]{:S(2)}) collective-permute-start(bf16[2,128,256]{2,1,0:T(8,128)(2,1)S(1)} %get-tuple-element.74.lo1), channel_id=1, source_target_pairs={{0,60},{1,61},{2,62},{3,63},{4,0},{5,1},{6,2},{7,3},{8,4},{9,5},{1... | collective-permute-start | bytes 393224 | tf_op jit(solution)/shard_map/ppermute | solution.py:349
  50.4 14.7 %collective-permute-start.15 = (bf16[2,128,256]{2,1,0:T(8,128)(2,1)S(1)}, bf16[2,128,256]{2,1,0:T(8,128)(2,1)S(1)}, u32[]{:S(2)}, u32[]{:S(2)}) collective-permute-start(bf16[2,128,256]{2,1,0:T(8,128)(2,1)S(1)} %get-tuple-element.76.hi1), channel_id=1, source_target_pairs={{0,4},{1,5},{2,6},{3,7},{4,8},{5,9},{6,10},{7,11},{8,12},{9,13},{1... | collective-permute-start | bytes 393224 | tf_op jit(solution)/shard_map/ppermute | solution.py:348
  55.6 9.7 %collective-permute-start.16 = (bf16[2,128,256]{2,1,0:T(8,128)(2,1)S(1)}, bf16[2,128,256]{2,1,0:T(8,128)(2,1)S(1)}, u32[]{:S(2)}, u32[]{:S(2)}) collective-permute-start(bf16[2,128,256]{2,1,0:T(8,128)(2,1)S(1)} %get-tuple-element.71.lo0), channel_id=1, source_target_pairs={{0,60},{1,61},{2,62},{3,63},{4,0},{5,1},{6,2},{7,3},{8,4},{9,5},{1... | collective-permute-start | bytes 393224 | tf_op jit(solution)/shard_map/ppermute | solution.py:349
  62.1 9.6 %collective-permute-start.14 = (bf16[2,128,256]{2,1,0:T(8,128)(2,1)S(1)}, bf16[2,128,256]{2,1,0:T(8,128)(2,1)S(1)}, u32[]{:S(2)}, u32[]{:S(2)}) collective-permute-start(bf16[2,128,256]{2,1,0:T(8,128)(2,1)S(1)} %get-tuple-element.75.hi0), channel_id=1, source_target_pairs={{0,4},{1,5},{2,6},{3,7},{4,8},{5,9},{6,10},{7,11},{8,12},{9,13},{1... | collective-permute-start | bytes 393224 | tf_op jit(solution)/shard_map/ppermute | solution.py:348
  75.0 17.4 %collective-permute-start.20 = (bf16[4,128,256]{2,1,0:T(8,128)(2,1)S(1)}, bf16[4,128,256]{2,1,0:T(8,128)(2,1)S(1)}, u32[]{:S(2)}, u32[]{:S(2)}) collective-permute-start(bf16[4,128,256]{2,1,0:T(8,128)(2,1)S(1)} %get-tuple-element.95.image1), channel_id=1, source_target_pairs={{3,67},{7,71},{11,75},{15,79},{19,83},{23,87},{27,91},{31,95},{35,... | collective-permute-start | bytes 786440 | tf_op jit(solution)/shard_map/ppermute | solution.py:405
  75.7 9.7 %collective-permute-start.18 = (bf16[2,128,256]{2,1,0:T(8,128)(2,1)S(1)}, bf16[2,128,256]{2,1,0:T(8,128)(2,1)S(1)}, u32[]{:S(2)}, u32[]{:S(2)}) collective-permute-start(bf16[2,128,256]{2,1,0:T(8,128)(2,1)S(1)} %get-tuple-element.88), channel_id=1, source_target_pairs={{0,4},{1,5},{2,6},{3,7},{4,8},{5,9},{6,10},{7,11},{8,12},{9,13},{1... | collective-permute-start | bytes 393224 | tf_op jit(solution)/shard_map/ppermute | solution.py:348
  75.8 9.6 %collective-permute-start.19 = (bf16[2,128,256]{2,1,0:T(8,128)(2,1)S(1)}, bf16[2,128,256]{2,1,0:T(8,128)(2,1)S(1)}, u32[]{:S(2)}, u32[]{:S(2)}) collective-permute-start(bf16[2,128,256]{2,1,0:T(8,128)(2,1)S(1)} %get-tuple-element.89), channel_id=1, source_target_pairs={{0,60},{1,61},{2,62},{3,63},{4,0},{5,1},{6,2},{7,3},{8,4},{9,5},{1... | collective-permute-start | bytes 393224 | tf_op jit(solution)/shard_map/ppermute | solution.py:349
  86.6 9.4 %collective-permute-start.24 = (bf16[2,128,256]{2,1,0:T(8,128)(2,1)S(1)}, bf16[2,128,256]{2,1,0:T(8,128)(2,1)S(1)}, u32[]{:S(2)}, u32[]{:S(2)}) collective-permute-start(bf16[2,128,256]{2,1,0:T(8,128)(2,1)S(1)} %get-tuple-element.104), channel_id=1, source_target_pairs={{0,4},{1,5},{2,6},{3,7},{4,8},{5,9},{6,10},{7,11},{8,12},{9,13},{1... | collective-permute-start | bytes 393224 | tf_op jit(solution)/shard_map/ppermute | solution.py:348
  86.7 9.3 %collective-permute-start.25 = (bf16[2,128,256]{2,1,0:T(8,128)(2,1)S(1)}, bf16[2,128,256]{2,1,0:T(8,128)(2,1)S(1)}, u32[]{:S(2)}, u32[]{:S(2)}) collective-permute-start(bf16[2,128,256]{2,1,0:T(8,128)(2,1)S(1)} %get-tuple-element.105), channel_id=1, source_target_pairs={{0,60},{1,61},{2,62},{3,63},{4,0},{5,1},{6,2},{7,3},{8,4},{9,5},{1... | collective-permute-start | bytes 393224 | tf_op jit(solution)/shard_map/ppermute | solution.py:349
  92.8 6.8 %collective-permute-start.21 = (bf16[2,128,256]{2,1,0:T(8,128)(2,1)S(1)}, bf16[2,128,256]{2,1,0:T(8,128)(2,1)S(1)}, u32[]{:S(2)}, u32[]{:S(2)}) collective-permute-start(bf16[2,128,256]{2,1,0:T(8,128)(2,1)S(1)} %get-tuple-element.97), channel_id=1, source_target_pairs={{0,1},{1,2},{2,3},{3,0},{4,5},{5,6},{6,7},{7,4},{8,9},{9,10},{10,1... | collective-permute-start | bytes 393224 | tf_op jit(solution)/shard_map/ppermute | solution.py:344
  92.9 9.6 %collective-permute-start.22 = (bf16[2,128,256]{2,1,0:T(8,128)(2,1)S(1)}, bf16[2,128,256]{2,1,0:T(8,128)(2,1)S(1)}, u32[]{:S(2)}, u32[]{:S(2)}) collective-permute-start(bf16[2,128,256]{2,1,0:T(8,128)(2,1)S(1)} %get-tuple-element.98), channel_id=1, source_target_pairs={{0,2},{1,3},{2,0},{3,1},{4,6},{5,7},{6,4},{7,5},{8,10},{9,11},{10,... | collective-permute-start | bytes 393224 | tf_op jit(solution)/shard_map/ppermute | solution.py:344
  96.1 6.5 %collective-permute-start.23 = (bf16[2,128,256]{2,1,0:T(8,128)(2,1)S(1)}, bf16[2,128,256]{2,1,0:T(8,128)(2,1)S(1)}, u32[]{:S(2)}, u32[]{:S(2)}) collective-permute-start(bf16[2,128,256]{2,1,0:T(8,128)(2,1)S(1)} %get-tuple-element.99), channel_id=1, source_target_pairs={{0,3},{1,0},{2,1},{3,2},{4,7},{5,4},{6,5},{7,6},{8,11},{9,8},{10,9... | collective-permute-start | bytes 393224 | tf_op jit(solution)/shard_map/ppermute | solution.py:344
  96.2 8.9 %collective-permute-start.26 = (bf16[2,128,256]{2,1,0:T(8,128)(2,1)S(1)}, bf16[2,128,256]{2,1,0:T(8,128)(2,1)S(1)}, u32[]{:S(2)}, u32[]{:S(2)}) collective-permute-start(bf16[2,128,256]{2,1,0:T(8,128)(2,1)S(1)} %get-tuple-element.107), channel_id=1, source_target_pairs={{0,1},{1,2},{2,3},{3,0},{4,5},{5,6},{6,7},{7,4},{8,9},{9,10},{10,1... | collective-permute-start | bytes 393224 | tf_op jit(solution)/shard_map/ppermute | solution.py:344
  97.7 10.4 %collective-permute-start.27 = (bf16[2,128,256]{2,1,0:T(8,128)(2,1)S(1)}, bf16[2,128,256]{2,1,0:T(8,128)(2,1)S(1)}, u32[]{:S(2)}, u32[]{:S(2)}) collective-permute-start(bf16[2,128,256]{2,1,0:T(8,128)(2,1)S(1)} %get-tuple-element.108), channel_id=1, source_target_pairs={{0,2},{1,3},{2,0},{3,1},{4,6},{5,7},{6,4},{7,5},{8,10},{9,11},{10,... | collective-permute-start | bytes 393224 | tf_op jit(solution)/shard_map/ppermute | solution.py:344
  99.6 8.5 %collective-permute-start.28 = (bf16[2,128,256]{2,1,0:T(8,128)(2,1)S(1)}, bf16[2,128,256]{2,1,0:T(8,128)(2,1)S(1)}, u32[]{:S(2)}, u32[]{:S(2)}) collective-permute-start(bf16[2,128,256]{2,1,0:T(8,128)(2,1)S(1)} %get-tuple-element.109), channel_id=1, source_target_pairs={{0,3},{1,0},{2,1},{3,2},{4,7},{5,4},{6,5},{7,6},{8,11},{9,8},{10,9... | collective-permute-start | bytes 393224 | tf_op jit(solution)/shard_map/ppermute | solution.py:344
  (6 other events, 20.6 us)

commit v7 on v5

--- a/solution.py
+++ b/solution.py
@@ -34,6 +34,15 @@
     return jnp.logical_and(member() == G - 1, lax.axis_index("tm") == TM - 1)
 
 
+def even_group():
+    return lax.rem(lax.div(lax.axis_index("mesh"), G), 2) == 0
+
+
+def swap(first, second):
+    even = even_group()
+    return jnp.where(even, first, second), jnp.where(even, second, first)
+
+
 def origin(y, k):
     return lax.rem(y + G - k, G)
 
@@ -65,20 +74,21 @@
             folded[:, first : first + B] = total.astype(BF)
 
 
-def edge_kernel(r0, r1, r2, r3, send_left, send_right, inc=None):
-    y = member()
+def edge_kernel(r0, r1, r2, r3, far, near, inc=None):
+    y = member()
+    far_block = jnp.where(even_group(), 0, G - 1)
     for k, r in enumerate((r0, r1, r2, r3)):
         block = origin(y, k)
         if inc is not None:
             inc[block] = r[1]
 
-        @pl.when(block == 0)
+        @pl.when(block == far_block)
         def _():
-            send_left[...] = r[...]
-
-        @pl.when(block == G - 1)
+            far[...] = r[...]
+
+        @pl.when(block == G - 1 - far_block)
         def _():
-            send_right[...] = r[...]
+            near[...] = r[...]
 
 
 def sort_edges(y, mats, layer, amat, tmat):
@@ -151,9 +161,10 @@
 
 
 def edge0_kernel(
-    w, field, amat, left, right, win, bias, wout,
-    send_left, send_right, tan_out, slope,
+    w, field, amat, far, near, win, bias, wout,
+    send_far, send_near, tan_out, slope,
 ):
+    left, right = zip(*(swap(far[f], near[f]) for f in range(2)))
     lo = stack(jnp.concatenate([left[0], left[1]], axis=1), field[w, 0 : 2 * B])
     hi = stack(field[w, 2 * B :], jnp.concatenate([right[0], right[1]], axis=1))
     agg = stack(dot(amat[0], lo), dot(amat[G - 1], hi))
@@ -163,21 +174,20 @@
     )
     tan_out[...] = tan
     base, tan = base.astype(BF), tan.astype(BF)
-    send_left[0] = base[0:B]
-    send_left[1] = tan[0:B]
-    send_right[0] = base[B:]
-    send_right[1] = tan[B:]
+    send_far[0], send_near[0] = swap(base[0:B], base[B:])
+    send_far[1], send_near[1] = swap(tan[0:B], tan[B:])
 
 
 def inner1_kernel(
-    base_in, tan_in, lo0, lo1, hi0, hi1, field, a0, a1, a2, a3, nxt, win, bias, wout,
+    base_in, tan_in, far0, far1, near0, near1, field, a0, a1, a2, a3, nxt, win, bias, wout,
     amat, tmat, image, returned, hat, slope,
 ):
     y = member()
     sort_edges(y, (a0, a1, a2, a3), 1, amat, tmat)
     pair_matrix(amat, hat)
     for w in range(NW):
-        lo, hi = (lo0, lo1)[w], (hi0, hi1)[w]
+        far, near = (far0, far1)[w], (near0, near1)[w]
+        lo, hi = zip(*(swap(far[f], near[f]) for f in range(2)))
         base = stack(lo[0], base_in[w], hi[0])
         tan = stack(lo[1], tan_in[w].astype(BF), hi[1])
         base_sum = base_in[w].astype(F32) + dot(hat[...], base)
@@ -194,13 +204,15 @@
 
 
 def edge1_kernel(
-    lo0, lo1, hi0, hi1, tan0, tan1, left0, left1, right0, right1, base_in, tan_in, field, nxt, amat, tmat, image_in, win, bias, wout,
-    im0, im1, im2, im3, returned, send_left, send_right, slope, image,
+    far0, far1, near0, near1, tan0, tan1, got_far0, got_far1, got_near0, got_near1, base_in, tan_in, field, nxt, amat, tmat, image_in, win, bias, wout,
+    im0, im1, im2, im3, returned, send_far, send_near, slope, image,
 ):
     y = member()
     for w in range(NW):
-        lo, hi, tan_edge = (lo0, lo1)[w], (hi0, hi1)[w], (tan0, tan1)[w]
-        left, right = (left0, left1)[w], (right0, right1)[w]
+        far, near, tan_edge = (far0, far1)[w], (near0, near1)[w], (tan0, tan1)[w]
+        lo, hi = zip(*(swap(far[f], near[f]) for f in range(2)))
+        far, near = (got_far0, got_far1)[w], (got_near0, got_near1)[w]
+        left, right = zip(*(swap(far[f], near[f]) for f in range(2)))
         tan_mid = tan_in[w].astype(BF)
         agg = []
         for f, mid in ((0, base_in[w]), (1, tan_mid)):
@@ -221,8 +233,10 @@
             current = jnp.where(last_member(), 0.0, stack(nxt[0], nxt[G - 1]).astype(F32) - out)
         back = adjoint_rows(current, 1, win, wout, slope)
         returned[w] = back
-        send_left[w] = dot(tmat[0, :, 0:B], back[0:B].astype(BF)).astype(BF)
-        send_right[w] = dot(tmat[G - 1, :, 2 * B :], back[B:].astype(BF)).astype(BF)
+        send_far[w], send_near[w] = swap(
+            dot(tmat[0, :, 0:B], back[0:B].astype(BF)).astype(BF),
+            dot(tmat[G - 1, :, 2 * B :], back[B:].astype(BF)).astype(BF),
+        )
     for k, im in enumerate((im0, im1, im2, im3)):
         im[...] = image[lax.rem(y + k, G)]
 
@@ -242,13 +256,15 @@
         returned[w] = adjoint_rows(current, 0, win, wout, slope.at[w])
 
 
-def edge2_kernel(cur_edge, left, right, tmat, slope0, slope1, win, wout, returned, send_left, send_right):
-    for w in range(NW):
-        current = cur_edge[w] + stack(left[w], right[w]).astype(F32)
+def edge2_kernel(cur_edge, far, near, tmat, slope0, slope1, win, wout, returned, send_far, send_near):
+    for w in range(NW):
+        current = cur_edge[w] + stack(*swap(far[w], near[w])).astype(F32)
         back = adjoint_rows(current, 0, win, wout, (slope0, slope1)[w])
         returned[w] = back
-        send_left[w] = dot(tmat[0, :, 0:B], back[0:B].astype(BF)).astype(BF)
-        send_right[w] = dot(tmat[G - 1, :, 2 * B :], back[B:].astype(BF)).astype(BF)
+        send_far[w], send_near[w] = swap(
+            dot(tmat[0, :, 0:B], back[0:B].astype(BF)).astype(BF),
+            dot(tmat[G - 1, :, 2 * B :], back[B:].astype(BF)).astype(BF),
+        )
 
 
 def inner3_kernel(inner, edge, tmat, i0, i1, i2, i3, cur_edge, cur_inner, last, hat):
@@ -266,13 +282,14 @@
         cur_inner[w] = (inner[w] + dot(hat[...], narrow)).astype(BF)
 
 
-def finish_kernel(cur_edge, cur_inner, left, right, o0, o1, o2, o3, all_blocks):
-    y = member()
-    for w in range(NW):
-        all_blocks[0, w] = (cur_edge[w, 0:B] + left[w].astype(F32)).astype(BF)
+def finish_kernel(cur_edge, cur_inner, far, near, o0, o1, o2, o3, all_blocks):
+    y = member()
+    for w in range(NW):
+        left, right = swap(far[w], near[w])
+        all_blocks[0, w] = (cur_edge[w, 0:B] + left.astype(F32)).astype(BF)
         all_blocks[1, w] = cur_inner[w, 0:B]
         all_blocks[2, w] = cur_inner[w, B:]
-        all_blocks[3, w] = (cur_edge[w, B:] + right[w].astype(F32)).astype(BF)
+        all_blocks[3, w] = (cur_edge[w, B:] + right.astype(F32)).astype(BF)
     for k, out in enumerate((o0, o1, o2, o3)):
         out[...] = all_blocks[lax.rem(y + k, G)]
 
@@ -323,8 +340,12 @@
     return [(b, b // G * G + (b + k) % G) for b in range(PARTS)]
 
 
-def side_pairs(d):
-    return [(b, (b + G * d) % PARTS) for b in range(PARTS)]
+def side_pairs(near):
+    pairs = []
+    for b in range(PARTS):
+        step = G if (b // G % 2 == 0) == near else -G
+        pairs.append((b, (b + step) % PARTS))
+    return pairs
 
 
 def next_increment_pairs():
@@ -340,10 +361,10 @@
     return [lax.ppermute(sends[k], "mesh", group_pairs(k)) for k in range(1, G)]
 
 
-def swap_sides(send_left, send_right):
-    left = lax.ppermute(send_right, "mesh", side_pairs(1))
-    right = lax.ppermute(send_left, "mesh", side_pairs(-1))
-    return left, right
+def swap_sides(far, near):
+    far = lax.ppermute(far, "mesh", side_pairs(False))
+    near = lax.ppermute(near, "mesh", side_pairs(True))
+    return far, near
 
 
 def local(states, increment, window_slots, edge_weights, inner_weight, inner_bias, outer_weight):

time: 108 us -> 100 us (0.926)
  starting transfers between devices: 60.9 us -> 50.7 us
  waiting for transfers between devices: 26 us -> 27.8 us
    ppermute x12, starting transfers between devices: 34.4 us -> 22.6 us  [the longest x6 22.6 us: swap_sides(): far = lax.ppermute(far, 'mesh', side_pairs(False))]
    ppermute x1, starting transfers between devices: 4.71 us -> 6.63 us  [local(): before = lax.ppermute(last, 'tm', [(t, t + 1) for t in range(TM - 1)])]
    ppermute x12, waiting for transfers between devices: 10.9 us -> 12.7 us  [the longest x6 12.7 us: swap_sides(): far = lax.ppermute(far, 'mesh', side_pairs(False))]
  transfers between devices with their start and end apart: 29 -> 29, of which waited for: 7 -> 7; matrix products, arithmetic and copies ran while one was open for 0% -> 0% of each run, Pallas kernels for 12% -> 13%
where the time goes in v7:
time: 100 us; the launch traced here: 99.8 us
  starting transfers between devices  50.7 us (51%)
  waiting for transfers between devices  27.8 us (28%)
  Pallas kernels  17.2 us (17%)
  local copies, waits for them, and re-layouts  3.23 us (3%)
    ppermute x6, starting transfers between devices, swap_sides(): far = lax.ppermute(far, 'mesh', side_pairs(False))  22.6 us
    pallas_call x15, Pallas kernels, call(): pl.pallas_call(kernel, out_shape=outs, in_specs=[SMEM] * smem + [VMEM] *...  17.2 us
    ppermute x15, starting transfers between devices, to_members(): return [lax.ppermute(sends[k], 'mesh', group_pairs(k)) for k in range(1, G)]  16.7 us
    ppermute x15, waiting for transfers between devices, to_members(): return [lax.ppermute(sends[k], 'mesh', group_pairs(k)) for k in range(1, G)]  13.8 us
    ppermute x6, waiting for transfers between devices, swap_sides(): far = lax.ppermute(far, 'mesh', side_pairs(False))  12.7 us
    ppermute x1, starting transfers between devices, local(): before = lax.ppermute(last, 'tm', [(t, t + 1) for t in range(TM - 1)])  6.63 us
    ppermute x1, starting transfers between devices, local(): nxt = lax.ppermute(nxt, ('tm', 'mesh'), next_increment_pairs())  4.8 us
    unnamed x18, local copies, waits for them, and re-layouts  3.23 us
  transfers between devices with their start and end apart: 29, of which 7 were waited for; matrix products, arithmetic and copies ran while one was open for 0% of the time, Pallas kernels for 13%

profile of v7, /device:TPU:1, one launch (start us, length us, event | category | flops | bytes accessed | tf_op | source)
XLA Modules:
  0.0 99.8 jit_solution(15198656183821784981)
XLA Ops:
  0.6 1.2 %copy-done.2 = f32[8,128,256]{2,1,0:T(8,128)S(1)} copy-done((f32[8,128,256]{2,1,0:T(8,128)S(1)}, f32[8,128,256]{2,1,0:T(8,128)}, u32[]{:S(2)}) %copy-start.2) | copy-done | bytes 1048600
  3.0 2.2 %collective-permute-start = (bf16[2,128,256]{2,1,0:T(8,128)(2,1)S(1)}, bf16[2,128,256]{2,1,0:T(8,128)(2,1)S(1)}, u32[]{:S(2)}, u32[]{:S(2)}) collective-permute-start(bf16[2,128,256]{2,1,0:T(8,128)(2,1)S(1)} %get-tuple-element.56), channel_id=1, source_target_pairs={{0,1},{1,2},{2,3},{3,0},{4,5},{5,6},{6,7},{7,4},{8,9},{9,10},{10,1... | collective-permute-start | bytes 393224 | tf_op jit(solution)/shard_map/ppermute | solution.py:361
  5.2 1.3 %collective-permute-start.3 = (bf16[2,128,256]{2,1,0:T(8,128)(2,1)S(1)}, bf16[2,128,256]{2,1,0:T(8,128)(2,1)S(1)}, u32[]{:S(2)}, u32[]{:S(2)}) collective-permute-start(bf16[2,128,256]{2,1,0:T(8,128)(2,1)S(1)} %get-tuple-element.60), channel_id=1, source_target_pairs={{0,1},{1,2},{2,3},{3,0},{4,5},{5,6},{6,7},{7,4},{8,9},{9,10},{10,1... | collective-permute-start | bytes 393224 | tf_op jit(solution)/shard_map/ppermute | solution.py:361
  6.5 1.4 %collective-permute-start.4 = (bf16[2,128,256]{2,1,0:T(8,128)(2,1)S(1)}, bf16[2,128,256]{2,1,0:T(8,128)(2,1)S(1)}, u32[]{:S(2)}, u32[]{:S(2)}) collective-permute-start(bf16[2,128,256]{2,1,0:T(8,128)(2,1)S(1)} %get-tuple-element.61), channel_id=1, source_target_pairs={{0,2},{1,3},{2,0},{3,1},{4,6},{5,7},{6,4},{7,5},{8,10},{9,11},{10,... | collective-permute-start | bytes 393224 | tf_op jit(solution)/shard_map/ppermute | solution.py:361
  7.9 2.0 %collective-permute-start.5 = (bf16[2,128,256]{2,1,0:T(8,128)(2,1)S(1)}, bf16[2,128,256]{2,1,0:T(8,128)(2,1)S(1)}, u32[]{:S(2)}, u32[]{:S(2)}) collective-permute-start(bf16[2,128,256]{2,1,0:T(8,128)(2,1)S(1)} %get-tuple-element.62), channel_id=1, source_target_pairs={{0,3},{1,0},{2,1},{3,2},{4,7},{5,4},{6,5},{7,6},{8,11},{9,8},{10,9... | collective-permute-start | bytes 393224 | tf_op jit(solution)/shard_map/ppermute | solution.py:361
  11.8 1.1 %collective-permute-start.7 = (bf16[128,768]{1,0:T(8,128)(2,1)S(1)}, bf16[128,768]{1,0:T(8,128)(2,1)S(1)}, u32[]{:S(2)}, u32[]{:S(2)}) collective-permute-start(bf16[128,768]{1,0:T(8,128)(2,1)S(1)} %get-tuple-element.63.a0), channel_id=1, source_target_pairs={{0,2},{1,3},{2,0},{3,1},{4,6},{5,7},{6,4},{7,5},{8,10},{9,11},{10,... | collective-permute-start | bytes 589832 | tf_op jit(solution)/shard_map/ppermute | solution.py:361
  13.2 3.1 %collective-permute-done.4.r12.r2 = bf16[2,128,256]{2,1,0:T(8,128)(2,1)S(1)} collective-permute-done((bf16[2,128,256]{2,1,0:T(8,128)(2,1)S(1)}, bf16[2,128,256]{2,1,0:T(8,128)(2,1)S(1)}, u32[]{:S(2)}, u32[]{:S(2)}) %collective-permute-start.4) | collective-permute-done | bytes 131104 | tf_op jit(solution)/shard_map/ppermute | solution.py:361
  17.0 10.6 %collective-permute-done.1.r02.r2 = bf16[2,128,256]{2,1,0:T(8,128)(2,1)S(1)} collective-permute-done((bf16[2,128,256]{2,1,0:T(8,128)(2,1)S(1)}, bf16[2,128,256]{2,1,0:T(8,128)(2,1)S(1)}, u32[]{:S(2)}, u32[]{:S(2)}) %collective-permute-start.1) | collective-permute-done | bytes 131104 | tf_op jit(solution)/shard_map/ppermute | solution.py:361
  27.6 8.2 %collective-permute-start.11 = (bf16[2,128,256]{2,1,0:T(8,128)(2,1)S(1)}, bf16[2,128,256]{2,1,0:T(8,128)(2,1)S(1)}, u32[]{:S(2)}, u32[]{:S(2)}) collective-permute-start(bf16[2,128,256]{2,1,0:T(8,128)(2,1)S(1)} %get-tuple-element.69), channel_id=1, source_target_pairs={{0,60},{1,61},{2,62},{3,63},{4,8},{5,9},{6,10},{7,11},{8,4},{9,5},... | collective-permute-start | bytes 393224 | tf_op jit(solution)/shard_map/ppermute | solution.py:365
  35.9 1.1 %collective-permute-start.9 = (bf16[2,128,256]{2,1,0:T(8,128)(2,1)S(1)}, bf16[2,128,256]{2,1,0:T(8,128)(2,1)S(1)}, u32[]{:S(2)}, u32[]{:S(2)}) collective-permute-start(bf16[2,128,256]{2,1,0:T(8,128)(2,1)S(1)} %get-tuple-element.66), channel_id=1, source_target_pairs={{0,60},{1,61},{2,62},{3,63},{4,8},{5,9},{6,10},{7,11},{8,4},{9,5},... | collective-permute-start | bytes 393224 | tf_op jit(solution)/shard_map/ppermute | solution.py:365
  37.0 4.8 %collective-permute-start.17 = (bf16[4,128,256]{2,1,0:T(8,128)(2,1)S(1)}, bf16[4,128,256]{2,1,0:T(8,128)(2,1)S(1)}, u32[]{:S(2)}, u32[]{:S(2)}) collective-permute-start(bf16[4,128,256]{2,1,0:T(8,128)(2,1)S(1)} %get-tuple-element.78), channel_id=1, source_target_pairs={{0,195},{1,0},{2,1},{3,2},{4,199},{5,4},{6,5},{7,6},{8,203},{9,8},... | collective-permute-start | bytes 786440 | tf_op jit(solution)/shard_map/ppermute | solution.py:394
  41.8 2.2 %shard_map.88 = (bf16[2,512,512]{2,1,0:T(8,128)(2,1)S(1)}, bf16[4,128,384]{2,1,0:T(8,128)(2,1)S(1)}, bf16[4,128,384]{2,1,0:T(8,128)(2,1)S(1)}, bf16[2,256,256]{2...) custom-call(bf16[2,128,256]{2,1,0:T(8,128)(2,1)S(1)} %get-tuple-element.55.r00.r0, ...), custom_call_target="tpu_custom_call" | custom-call | tf_op jit(solution)/shard_map/pallas_call | solution.py:329
  44.1 1.2 %shard_map.92 = (bf16[2,128,256]{2,1,0:T(8,128)(2,1)S(1)}, bf16[2,128,256]{2,1,0:T(8,128)(2,1)S(1)}, f32[256,256]{1,0:T(8,128)S(1)}, bf16[256,1024]{1,0:T(8,128)(2,1)S(1)}) custom-call(bf16[2,512,512]{2,1,0:T(8,128)(2,1)S(1)} %get-tuple-element.64.field, bf16[4,128,384]{2,1,0:T(8,128)(2,1)S(1)} %get-tuple-element.65.amat, ...), custom_call_target="tpu_custom_call" | custom-call | tf_op jit(solution)/shard_map/pallas_call | solution.py:329
  45.2 3.5 %collective-permute-start.14 = (bf16[2,128,256]{2,1,0:T(8,128)(2,1)S(1)}, bf16[2,128,256]{2,1,0:T(8,128)(2,1)S(1)}, u32[]{:S(2)}, u32[]{:S(2)}) collective-permute-start(bf16[2,128,256]{2,1,0:T(8,128)(2,1)S(1)} %get-tuple-element.71.far1), channel_id=1, source_target_pairs={{0,60},{1,61},{2,62},{3,63},{4,8},{5,9},{6,10},{7,11},{8,4},{9,5},... | collective-permute-start | bytes 393224 | tf_op jit(solution)/shard_map/ppermute | solution.py:365
  48.7 1.2 %shard_map.90 = (bf16[2,128,256]{2,1,0:T(8,128)(2,1)S(1)}, bf16[2,128,256]{2,1,0:T(8,128)(2,1)S(1)}, f32[256,256]{1,0:T(8,128)S(1)}, bf16[256,1024]{1,0:T(8,128)(2,1)S(1)}) custom-call(bf16[2,512,512]{2,1,0:T(8,128)(2,1)S(1)} %get-tuple-element.64.field, bf16[4,128,384]{2,1,0:T(8,128)(2,1)S(1)} %get-tuple-element.65.amat, ...), custom_call_target="tpu_custom_call" | custom-call | tf_op jit(solution)/shard_map/pallas_call | solution.py:329
  49.9 3.6 %collective-permute-start.13 = (bf16[2,128,256]{2,1,0:T(8,128)(2,1)S(1)}, bf16[2,128,256]{2,1,0:T(8,128)(2,1)S(1)}, u32[]{:S(2)}, u32[]{:S(2)}) collective-permute-start(bf16[2,128,256]{2,1,0:T(8,128)(2,1)S(1)} %get-tuple-element.68.far0), channel_id=1, source_target_pairs={{0,60},{1,61},{2,62},{3,63},{4,8},{5,9},{6,10},{7,11},{8,4},{9,5},... | collective-permute-start | bytes 393224 | tf_op jit(solution)/shard_map/ppermute | solution.py:365
  53.5 3.1 %shard_map.93 = (bf16[4,128,384]{2,1,0:T(8,128)(2,1)S(1)}, bf16[4,128,384]{2,1,0:T(8,128)(2,1)S(1)}, bf16[2,256,256]{2,1,0:T(8,128)(2,1)S(1)}, f32[2,256,256]{2,1,0:T(8,128)S(1)}) custom-call(bf16[2,256,256]{2,1,0:T(8,128)(2,1)S(1)} %get-tuple-element.76.base_in, f32[2,256,256]{2,1,0:T(8,128)S(1)} %get-tuple-element.77.tan_in, ...), custom_call_target="tpu_custom_call" | custom-call | tf_op jit(solution)/shard_map/pallas_call | solution.py:329
  57.2 4.7 %collective-permute-done.13.got_far0 = bf16[2,128,256]{2,1,0:T(8,128)(2,1)S(1)} collective-permute-done((bf16[2,128,256]{2,1,0:T(8,128)(2,1)S(1)}, bf16[2,128,256]{2,1,0:T(8,128)(2,1)S(1)}, u32[]{:S(2)}, u32[]{:S(2)}) %collective-permute-start.13) | collective-permute-done | bytes 131104 | tf_op jit(solution)/shard_map/ppermute | solution.py:365
  61.8 3.3 %shard_map.94 = (bf16[2,128,256]{2,1,0:T(8,128)(2,1)S(1)}, bf16[2,128,256]{2,1,0:T(8,128)(2,1)S(1)}, bf16[2,128,256]{2,1,0:T(8,128)(2,1)S(1)}, bf16[2,128,256]{2...) custom-call(bf16[2,128,256]{2,1,0:T(8,128)(2,1)S(1)} %get-tuple-elem, ...), custom_call_target="tpu_custom_call" | custom-call | tf_op jit(solution)/shard_map/pallas_call | solution.py:329
  65.2 4.1 %collective-permute-start.21 = (bf16[2,128,256]{2,1,0:T(8,128)(2,1)S(1)}, bf16[2,128,256]{2,1,0:T(8,128)(2,1)S(1)}, u32[]{:S(2)}, u32[]{:S(2)}) collective-permute-start(bf16[2,128,256]{2,1,0:T(8,128)(2,1)S(1)} %get-tuple-element.91), channel_id=1, source_target_pairs={{0,60},{1,61},{2,62},{3,63},{4,8},{5,9},{6,10},{7,11},{8,4},{9,5},... | collective-permute-start | bytes 393224 | tf_op jit(solution)/shard_map/ppermute | solution.py:365
  69.3 1.8 %collective-permute-start.19 = (bf16[2,128,256]{2,1,0:T(8,128)(2,1)S(1)}, bf16[2,128,256]{2,1,0:T(8,128)(2,1)S(1)}, u32[]{:S(2)}, u32[]{:S(2)}) collective-permute-start(bf16[2,128,256]{2,1,0:T(8,128)(2,1)S(1)} %get-tuple-element.84), channel_id=1, source_target_pairs={{0,2},{1,3},{2,0},{3,1},{4,6},{5,7},{6,4},{7,5},{8,10},{9,11},{10,... | collective-permute-start | bytes 393224 | tf_op jit(solution)/shard_map/ppermute | solution.py:361
  71.0 2.1 %collective-permute-start.20 = (bf16[2,128,256]{2,1,0:T(8,128)(2,1)S(1)}, bf16[2,128,256]{2,1,0:T(8,128)(2,1)S(1)}, u32[]{:S(2)}, u32[]{:S(2)}) collective-permute-start(bf16[2,128,256]{2,1,0:T(8,128)(2,1)S(1)} %get-tuple-element.85), channel_id=1, source_target_pairs={{0,3},{1,0},{2,1},{3,2},{4,7},{5,4},{6,5},{7,6},{8,11},{9,8},{10,9... | collective-permute-start | bytes 393224 | tf_op jit(solution)/shard_map/ppermute | solution.py:361
  73.1 1.4 %shard_map.95 = (f32[2,256,256]{2,1,0:T(8,128)S(1)}, f32[2,256,256]{2,1,0:T(8,128)S(1)}) custom-call(f32[2,256,256]{2,1,0:T(8,128)S(1)} %get-tuple-element.86.inner, f32[2,256,256]{2,1,0:T(8,128)S(1)} %get-tuple-element.87.edge, bf16[4,128,384]{2,1,0:T(8,128)(2,1)S(1)} %get-tuple-element.80.tmat, bf16[2,256,1024]{2,1,0:T(8,128)(2,1)S(1)} %get-tuple-element.88.slope, ...), custom_call_target="tpu_custom_call" | custom-call | tf_op jit(solution)/shard_map/pallas_call | solution.py:329
  75.3 1.3 %shard_map.96 = (f32[2,256,256]{2,1,0:T(8,128)S(1)}, bf16[2,128,256]{2,1,0:T(8,128)(2,1)S(1)}, bf16[2,128,256]{2,1,0:T(8,128)(2,1)S(1)}) custom-call(f32[2,256,256]{2,1,0:T(8,128)S(1)} %get-tuple-element.90.cur_edge, bf16[2,128,256]{2,1,0:T(8,128)(2,1)S(1)} %collective-permute-done.21.far, bf16[2,128,256]{2,1,0:T(8,128)(2,1)S(1)} %collective-permute-done.22.near, ...), custom_call_target="tpu_custom_call" | custom-call | tf_op jit(solution)/shard_map/pallas_call | solution.py:329
  76.6 2.1 %collective-permute-start.24 = (bf16[2,128,256]{2,1,0:T(8,128)(2,1)S(1)}, bf16[2,128,256]{2,1,0:T(8,128)(2,1)S(1)}, u32[]{:S(2)}, u32[]{:S(2)}) collective-permute-start(bf16[2,128,256]{2,1,0:T(8,128)(2,1)S(1)} %get-tuple-element.102), channel_id=1, source_target_pairs={{0,60},{1,61},{2,62},{3,63},{4,8},{5,9},{6,10},{7,11},{8,4},{9,5},... | collective-permute-start | bytes 393224 | tf_op jit(solution)/shard_map/ppermute | solution.py:365
  79.1 6.6 %collective-permute-done.24.far = bf16[2,128,256]{2,1,0:T(8,128)(2,1)S(1)} collective-permute-done((bf16[2,128,256]{2,1,0:T(8,128)(2,1)S(1)}, bf16[2,128,256]{2,1,0:T(8,128)(2,1)S(1)}, u32[]{:S(2)}, u32[]{:S(2)}) %collective-permute-start.24) | collective-permute-done | bytes 131104 | tf_op jit(solution)/shard_map/ppermute | solution.py:365
  86.0 1.7 %collective-permute-start.27 = (bf16[2,128,256]{2,1,0:T(8,128)(2,1)S(1)}, bf16[2,128,256]{2,1,0:T(8,128)(2,1)S(1)}, u32[]{:S(2)}, u32[]{:S(2)}) collective-permute-start(bf16[2,128,256]{2,1,0:T(8,128)(2,1)S(1)} %get-tuple-element.106), channel_id=1, source_target_pairs={{0,2},{1,3},{2,0},{3,1},{4,6},{5,7},{6,4},{7,5},{8,10},{9,11},{10,... | collective-permute-start | bytes 393224 | tf_op jit(solution)/shard_map/ppermute | solution.py:361
  87.7 2.0 %collective-permute-start.28 = (bf16[2,128,256]{2,1,0:T(8,128)(2,1)S(1)}, bf16[2,128,256]{2,1,0:T(8,128)(2,1)S(1)}, u32[]{:S(2)}, u32[]{:S(2)}) collective-permute-start(bf16[2,128,256]{2,1,0:T(8,128)(2,1)S(1)} %get-tuple-element.107), channel_id=1, source_target_pairs={{0,3},{1,0},{2,1},{3,2},{4,7},{5,4},{6,5},{7,6},{8,11},{9,8},{10,9... | collective-permute-start | bytes 393224 | tf_op jit(solution)/shard_map/ppermute | solution.py:361
  89.7 6.6 %collective-permute-start.23 = (bf16[128,256]{1,0:T(8,128)(2,1)S(1)}, bf16[128,256]{1,0:T(8,128)(2,1)S(1)}, u32[]{:S(2)}, u32[]{:S(2)}) collective-permute-start(bf16[128,256]{1,0:T(8,128)(2,1)S(1)} %get-tuple-element.97), channel_id=1, source_target_pairs={{0,64},{64,128},{128,192},{1,65},{65,129},{129,193},{2,66},{66,130... | collective-permute-start | bytes 196616 | tf_op jit(solution)/shard_map/ppermute | solution.py:436
  96.3 1.3 %collective-permute-done.23.before = bf16[128,256]{1,0:T(8,128)(2,1)S(1)} collective-permute-done((bf16[128,256]{1,0:T(8,128)(2,1)S(1)}, bf16[128,256]{1,0:T(8,128)(2,1)S(1)}, u32[]{:S(2)}, u32[]{:S(2)}) %collective-permute-start.23) | collective-permute-done | bytes 65568 | tf_op jit(solution)/shard_map/ppermute | solution.py:436
  97.6 1.1 %shard_map.98 = (f32[8,128,256]{2,1,0:T(8,128)}, f32[8,128,256]{2,1,0:T(8,128)S(1)}) custom-call(f32[8,128,256]{2,1,0:T(8,128)S(1)} %copy-done.3, bf16[2,128,256]{2,1,0:T(8,128)(2,1)S(1)} %get-tuple-element.82.i0, bf16[2,128,256]{2,1,0:T(8,128)(2,1)S(1)} %collective-permute-done.18.i1, bf16[2,128,256]{2,1,0:T(8,128)(2,1)S(1)} %collective-permute-done.19.i2, ...), custom_call_target="tpu_custom_call" | custom-call | tf_op jit(solution)/shard_map/pallas_call | solution.py:329
  98.8 1.1 %shard_map.100 = f32[8,128,256]{2,1,0:T(8,128)} custom-call(f32[8,128,256]{2,1,0:T(8,128)S(1)} %get-tuple-element.99.kept, bf16[2,128,256]{2,1,0:T(8,128)(2,1)S(1)} %get-tuple-element.104.p0, bf16[2,128,256]{2,1,0:T(8,128)(2,1)S(1)} %collective-permute-done.26.p1, bf16[2,128,256]{2,1,0:T(8,128)(2,1)S(1)} %collective-permute-done.27.p2, ...), custom_call_target="tpu_custom_call" | custom-call | tf_op jit(solution)/shard_map/pallas_call | solution.py:329
  (59 shorter events, 6.1 us)
Async XLA Ops:
  2.9 7.0 %copy-start.5 = (bf16[8,128,256]{2,1,0:T(8,128)(2,1)S(1)}, bf16[8,128,256]{2,1,0:T(8,128)(2,1)}, u32[]{:S(2)}) copy-start(bf16[8,128,256]{2,1,0:T(8,128)(2,1)} %states.3) | copy-start | bytes 1572868
  3.0 8.8 %collective-permute-start = (bf16[2,128,256]{2,1,0:T(8,128)(2,1)S(1)}, bf16[2,128,256]{2,1,0:T(8,128)(2,1)S(1)}, u32[]{:S(2)}, u32[]{:S(2)}) collective-permute-start(bf16[2,128,256]{2,1,0:T(8,128)(2,1)S(1)} %get-tuple-element.56), channel_id=1, source_target_pairs={{0,1},{1,2},{2,3},{3,0},{4,5},{5,6},{6,7},{7,4},{8,9},{9,10},{10,1... | collective-permute-start | bytes 393224 | tf_op jit(solution)/shard_map/ppermute | solution.py:361
  5.2 7.7 %collective-permute-start.3 = (bf16[2,128,256]{2,1,0:T(8,128)(2,1)S(1)}, bf16[2,128,256]{2,1,0:T(8,128)(2,1)S(1)}, u32[]{:S(2)}, u32[]{:S(2)}) collective-permute-start(bf16[2,128,256]{2,1,0:T(8,128)(2,1)S(1)} %get-tuple-element.60), channel_id=1, source_target_pairs={{0,1},{1,2},{2,3},{3,0},{4,5},{5,6},{6,7},{7,4},{8,9},{9,10},{10,1... | collective-permute-start | bytes 393224 | tf_op jit(solution)/shard_map/ppermute | solution.py:361
  6.5 9.9 %collective-permute-start.4 = (bf16[2,128,256]{2,1,0:T(8,128)(2,1)S(1)}, bf16[2,128,256]{2,1,0:T(8,128)(2,1)S(1)}, u32[]{:S(2)}, u32[]{:S(2)}) collective-permute-start(bf16[2,128,256]{2,1,0:T(8,128)(2,1)S(1)} %get-tuple-element.61), channel_id=1, source_target_pairs={{0,2},{1,3},{2,0},{3,1},{4,6},{5,7},{6,4},{7,5},{8,10},{9,11},{10,... | collective-permute-start | bytes 393224 | tf_op jit(solution)/shard_map/ppermute | solution.py:361
  7.9 33.9 %copy-start = (bf16[2,256,1024]{2,1,0:T(8,128)(2,1)S(1)}, bf16[2,256,1024]{2,1,0:T(8,128)(2,1)}, u32[]{:S(2)}) copy-start(bf16[2,256,1024]{2,1,0:T(8,128)(2,1)} %win.13) | copy-start | bytes 3145732
  7.9 33.9 %copy-start.1 = (bf16[2,1024,256]{2,1,0:T(8,128)(2,1)S(1)}, bf16[2,1024,256]{2,1,0:T(8,128)(2,1)}, u32[]{:S(2)}) copy-start(bf16[2,1024,256]{2,1,0:T(8,128)(2,1)} %wout.13) | copy-start | bytes 3145732
  7.9 8.8 %collective-permute-start.5 = (bf16[2,128,256]{2,1,0:T(8,128)(2,1)S(1)}, bf16[2,128,256]{2,1,0:T(8,128)(2,1)S(1)}, u32[]{:S(2)}, u32[]{:S(2)}) collective-permute-start(bf16[2,128,256]{2,1,0:T(8,128)(2,1)S(1)} %get-tuple-element.62), channel_id=1, source_target_pairs={{0,3},{1,0},{2,1},{3,2},{4,7},{5,4},{6,5},{7,6},{8,11},{9,8},{10,9... | collective-permute-start | bytes 393224 | tf_op jit(solution)/shard_map/ppermute | solution.py:361
  11.5 24.4 %collective-permute-start.8 = (bf16[128,768]{1,0:T(8,128)(2,1)S(1)}, bf16[128,768]{1,0:T(8,128)(2,1)S(1)}, u32[]{:S(2)}, u32[]{:S(2)}) collective-permute-start(bf16[128,768]{1,0:T(8,128)(2,1)S(1)} %get-tuple-element.63.a0), channel_id=1, source_target_pairs={{0,3},{1,0},{2,1},{3,2},{4,7},{5,4},{6,5},{7,6},{8,11},{9,8},{10,9... | collective-permute-start | bytes 589832 | tf_op jit(solution)/shard_map/ppermute | solution.py:361
  11.8 25.2 %collective-permute-start.7 = (bf16[128,768]{1,0:T(8,128)(2,1)S(1)}, bf16[128,768]{1,0:T(8,128)(2,1)S(1)}, u32[]{:S(2)}, u32[]{:S(2)}) collective-permute-start(bf16[128,768]{1,0:T(8,128)(2,1)S(1)} %get-tuple-element.63.a0), channel_id=1, source_target_pairs={{0,2},{1,3},{2,0},{3,1},{4,6},{5,7},{6,4},{7,5},{8,10},{9,11},{10,... | collective-permute-start | bytes 589832 | tf_op jit(solution)/shard_map/ppermute | solution.py:361
  12.9 28.9 %collective-permute-start.6 = (bf16[128,768]{1,0:T(8,128)(2,1)S(1)}, bf16[128,768]{1,0:T(8,128)(2,1)S(1)}, u32[]{:S(2)}, u32[]{:S(2)}) collective-permute-start(bf16[128,768]{1,0:T(8,128)(2,1)S(1)} %get-tuple-element.63.a0), channel_id=1, source_target_pairs={{0,1},{1,2},{2,3},{3,0},{4,5},{5,6},{6,7},{7,4},{8,9},{9,10},{10,1... | collective-permute-start | bytes 589832 | tf_op jit(solution)/shard_map/ppermute | solution.py:361
  16.3 11.3 %collective-permute-start.1 = (bf16[2,128,256]{2,1,0:T(8,128)(2,1)S(1)}, bf16[2,128,256]{2,1,0:T(8,128)(2,1)S(1)}, u32[]{:S(2)}, u32[]{:S(2)}) collective-permute-start(bf16[2,128,256]{2,1,0:T(8,128)(2,1)S(1)} %get-tuple-element.57), channel_id=1, source_target_pairs={{0,2},{1,3},{2,0},{3,1},{4,6},{5,7},{6,4},{7,5},{8,10},{9,11},{10,... | collective-permute-start | bytes 393224 | tf_op jit(solution)/shard_map/ppermute | solution.py:361
  16.7 19.1 %collective-permute-start.2 = (bf16[2,128,256]{2,1,0:T(8,128)(2,1)S(1)}, bf16[2,128,256]{2,1,0:T(8,128)(2,1)S(1)}, u32[]{:S(2)}, u32[]{:S(2)}) collective-permute-start(bf16[2,128,256]{2,1,0:T(8,128)(2,1)S(1)} %get-tuple-element.58), channel_id=1, source_target_pairs={{0,3},{1,0},{2,1},{3,2},{4,7},{5,4},{6,5},{7,6},{8,11},{9,8},{10,9... | collective-permute-start | bytes 393224 | tf_op jit(solution)/shard_map/ppermute | solution.py:361
  27.6 16.5 %collective-permute-start.11 = (bf16[2,128,256]{2,1,0:T(8,128)(2,1)S(1)}, bf16[2,128,256]{2,1,0:T(8,128)(2,1)S(1)}, u32[]{:S(2)}, u32[]{:S(2)}) collective-permute-start(bf16[2,128,256]{2,1,0:T(8,128)(2,1)S(1)} %get-tuple-element.69), channel_id=1, source_target_pairs={{0,60},{1,61},{2,62},{3,63},{4,8},{5,9},{6,10},{7,11},{8,4},{9,5},... | collective-permute-start | bytes 393224 | tf_op jit(solution)/shard_map/ppermute | solution.py:365
  35.8 8.3 %collective-permute-start.12 = (bf16[2,128,256]{2,1,0:T(8,128)(2,1)S(1)}, bf16[2,128,256]{2,1,0:T(8,128)(2,1)S(1)}, u32[]{:S(2)}, u32[]{:S(2)}) collective-permute-start(bf16[2,128,256]{2,1,0:T(8,128)(2,1)S(1)} %get-tuple-element.70), channel_id=1, source_target_pairs={{0,4},{1,5},{2,6},{3,7},{4,0},{5,1},{6,2},{7,3},{8,12},{9,13},{10,... | collective-permute-start | bytes 393224 | tf_op jit(solution)/shard_map/ppermute | solution.py:366
  35.9 12.8 %collective-permute-start.9 = (bf16[2,128,256]{2,1,0:T(8,128)(2,1)S(1)}, bf16[2,128,256]{2,1,0:T(8,128)(2,1)S(1)}, u32[]{:S(2)}, u32[]{:S(2)}) collective-permute-start(bf16[2,128,256]{2,1,0:T(8,128)(2,1)S(1)} %get-tuple-element.66), channel_id=1, source_target_pairs={{0,60},{1,61},{2,62},{3,63},{4,8},{5,9},{6,10},{7,11},{8,4},{9,5},... | collective-permute-start | bytes 393224 | tf_op jit(solution)/shard_map/ppermute | solution.py:365
  37.0 16.5 %collective-permute-start.17 = (bf16[4,128,256]{2,1,0:T(8,128)(2,1)S(1)}, bf16[4,128,256]{2,1,0:T(8,128)(2,1)S(1)}, u32[]{:S(2)}, u32[]{:S(2)}) collective-permute-start(bf16[4,128,256]{2,1,0:T(8,128)(2,1)S(1)} %get-tuple-element.78), channel_id=1, source_target_pairs={{0,195},{1,0},{2,1},{3,2},{4,199},{5,4},{6,5},{7,6},{8,203},{9,8},... | collective-permute-start | bytes 786440 | tf_op jit(solution)/shard_map/ppermute | solution.py:394
  41.8 6.9 %collective-permute-start.10 = (bf16[2,128,256]{2,1,0:T(8,128)(2,1)S(1)}, bf16[2,128,256]{2,1,0:T(8,128)(2,1)S(1)}, u32[]{:S(2)}, u32[]{:S(2)}) collective-permute-start(bf16[2,128,256]{2,1,0:T(8,128)(2,1)S(1)} %get-tuple-element.67), channel_id=1, source_target_pairs={{0,4},{1,5},{2,6},{3,7},{4,0},{5,1},{6,2},{7,3},{8,12},{9,13},{10,... | collective-permute-start | bytes 393224 | tf_op jit(solution)/shard_map/ppermute | solution.py:366
  45.2 11.9 %collective-permute-start.14 = (bf16[2,128,256]{2,1,0:T(8,128)(2,1)S(1)}, bf16[2,128,256]{2,1,0:T(8,128)(2,1)S(1)}, u32[]{:S(2)}, u32[]{:S(2)}) collective-permute-start(bf16[2,128,256]{2,1,0:T(8,128)(2,1)S(1)} %get-tuple-element.71.far1), channel_id=1, source_target_pairs={{0,60},{1,61},{2,62},{3,63},{4,8},{5,9},{6,10},{7,11},{8,4},{9,5},... | collective-permute-start | bytes 393224 | tf_op jit(solution)/shard_map/ppermute | solution.py:365
  48.7 8.4 %collective-permute-start.16 = (bf16[2,128,256]{2,1,0:T(8,128)(2,1)S(1)}, bf16[2,128,256]{2,1,0:T(8,128)(2,1)S(1)}, u32[]{:S(2)}, u32[]{:S(2)}) collective-permute-start(bf16[2,128,256]{2,1,0:T(8,128)(2,1)S(1)} %get-tuple-element.73.near1), channel_id=1, source_target_pairs={{0,4},{1,5},{2,6},{3,7},{4,0},{5,1},{6,2},{7,3},{8,12},{9,13},{10,... | collective-permute-start | bytes 393224 | tf_op jit(solution)/shard_map/ppermute | solution.py:366
  49.9 11.9 %collective-permute-start.13 = (bf16[2,128,256]{2,1,0:T(8,128)(2,1)S(1)}, bf16[2,128,256]{2,1,0:T(8,128)(2,1)S(1)}, u32[]{:S(2)}, u32[]{:S(2)}) collective-permute-start(bf16[2,128,256]{2,1,0:T(8,128)(2,1)S(1)} %get-tuple-element.68.far0), channel_id=1, source_target_pairs={{0,60},{1,61},{2,62},{3,63},{4,8},{5,9},{6,10},{7,11},{8,4},{9,5},... | collective-permute-start | bytes 393224 | tf_op jit(solution)/shard_map/ppermute | solution.py:365
  53.5 8.3 %collective-permute-start.15 = (bf16[2,128,256]{2,1,0:T(8,128)(2,1)S(1)}, bf16[2,128,256]{2,1,0:T(8,128)(2,1)S(1)}, u32[]{:S(2)}, u32[]{:S(2)}) collective-permute-start(bf16[2,128,256]{2,1,0:T(8,128)(2,1)S(1)} %get-tuple-element.72.near0), channel_id=1, source_target_pairs={{0,4},{1,5},{2,6},{3,7},{4,0},{5,1},{6,2},{7,3},{8,12},{9,13},{10,... | collective-permute-start | bytes 393224 | tf_op jit(solution)/shard_map/ppermute | solution.py:366
  65.2 10.1 %collective-permute-start.21 = (bf16[2,128,256]{2,1,0:T(8,128)(2,1)S(1)}, bf16[2,128,256]{2,1,0:T(8,128)(2,1)S(1)}, u32[]{:S(2)}, u32[]{:S(2)}) collective-permute-start(bf16[2,128,256]{2,1,0:T(8,128)(2,1)S(1)} %get-tuple-element.91), channel_id=1, source_target_pairs={{0,60},{1,61},{2,62},{3,63},{4,8},{5,9},{6,10},{7,11},{8,4},{9,5},... | collective-permute-start | bytes 393224 | tf_op jit(solution)/shard_map/ppermute | solution.py:365
  69.3 6.1 %collective-permute-start.22 = (bf16[2,128,256]{2,1,0:T(8,128)(2,1)S(1)}, bf16[2,128,256]{2,1,0:T(8,128)(2,1)S(1)}, u32[]{:S(2)}, u32[]{:S(2)}) collective-permute-start(bf16[2,128,256]{2,1,0:T(8,128)(2,1)S(1)} %get-tuple-element.92), channel_id=1, source_target_pairs={{0,4},{1,5},{2,6},{3,7},{4,0},{5,1},{6,2},{7,3},{8,12},{9,13},{10,... | collective-permute-start | bytes 393224 | tf_op jit(solution)/shard_map/ppermute | solution.py:366
  69.3 9.4 %collective-permute-start.18 = (bf16[2,128,256]{2,1,0:T(8,128)(2,1)S(1)}, bf16[2,128,256]{2,1,0:T(8,128)(2,1)S(1)}, u32[]{:S(2)}, u32[]{:S(2)}) collective-permute-start(bf16[2,128,256]{2,1,0:T(8,128)(2,1)S(1)} %get-tuple-element.83), channel_id=1, source_target_pairs={{0,1},{1,2},{2,3},{3,0},{4,5},{5,6},{6,7},{7,4},{8,9},{9,10},{10,1... | collective-permute-start | bytes 393224 | tf_op jit(solution)/shard_map/ppermute | solution.py:361
  69.3 9.4 %collective-permute-start.19 = (bf16[2,128,256]{2,1,0:T(8,128)(2,1)S(1)}, bf16[2,128,256]{2,1,0:T(8,128)(2,1)S(1)}, u32[]{:S(2)}, u32[]{:S(2)}) collective-permute-start(bf16[2,128,256]{2,1,0:T(8,128)(2,1)S(1)} %get-tuple-element.84), channel_id=1, source_target_pairs={{0,2},{1,3},{2,0},{3,1},{4,6},{5,7},{6,4},{7,5},{8,10},{9,11},{10,... | collective-permute-start | bytes 393224 | tf_op jit(solution)/shard_map/ppermute | solution.py:361
  71.0 7.7 %collective-permute-start.20 = (bf16[2,128,256]{2,1,0:T(8,128)(2,1)S(1)}, bf16[2,128,256]{2,1,0:T(8,128)(2,1)S(1)}, u32[]{:S(2)}, u32[]{:S(2)}) collective-permute-start(bf16[2,128,256]{2,1,0:T(8,128)(2,1)S(1)} %get-tuple-element.85), channel_id=1, source_target_pairs={{0,3},{1,0},{2,1},{3,2},{4,7},{5,4},{6,5},{7,6},{8,11},{9,8},{10,9... | collective-permute-start | bytes 393224 | tf_op jit(solution)/shard_map/ppermute | solution.py:361
  76.6 9.2 %collective-permute-start.24 = (bf16[2,128,256]{2,1,0:T(8,128)(2,1)S(1)}, bf16[2,128,256]{2,1,0:T(8,128)(2,1)S(1)}, u32[]{:S(2)}, u32[]{:S(2)}) collective-permute-start(bf16[2,128,256]{2,1,0:T(8,128)(2,1)S(1)} %get-tuple-element.102), channel_id=1, source_target_pairs={{0,60},{1,61},{2,62},{3,63},{4,8},{5,9},{6,10},{7,11},{8,4},{9,5},... | collective-permute-start | bytes 393224 | tf_op jit(solution)/shard_map/ppermute | solution.py:365
  78.7 7.1 %collective-permute-start.25 = (bf16[2,128,256]{2,1,0:T(8,128)(2,1)S(1)}, bf16[2,128,256]{2,1,0:T(8,128)(2,1)S(1)}, u32[]{:S(2)}, u32[]{:S(2)}) collective-permute-start(bf16[2,128,256]{2,1,0:T(8,128)(2,1)S(1)} %get-tuple-element.103), channel_id=1, source_target_pairs={{0,4},{1,5},{2,6},{3,7},{4,0},{5,1},{6,2},{7,3},{8,12},{9,13},{10,... | collective-permute-start | bytes 393224 | tf_op jit(solution)/shard_map/ppermute | solution.py:366
  85.9 12.9 %collective-permute-start.26 = (bf16[2,128,256]{2,1,0:T(8,128)(2,1)S(1)}, bf16[2,128,256]{2,1,0:T(8,128)(2,1)S(1)}, u32[]{:S(2)}, u32[]{:S(2)}) collective-permute-start(bf16[2,128,256]{2,1,0:T(8,128)(2,1)S(1)} %get-tuple-element.105), channel_id=1, source_target_pairs={{0,1},{1,2},{2,3},{3,0},{4,5},{5,6},{6,7},{7,4},{8,9},{9,10},{10,1... | collective-permute-start | bytes 393224 | tf_op jit(solution)/shard_map/ppermute | solution.py:361
  86.0 12.8 %collective-permute-start.27 = (bf16[2,128,256]{2,1,0:T(8,128)(2,1)S(1)}, bf16[2,128,256]{2,1,0:T(8,128)(2,1)S(1)}, u32[]{:S(2)}, u32[]{:S(2)}) collective-permute-start(bf16[2,128,256]{2,1,0:T(8,128)(2,1)S(1)} %get-tuple-element.106), channel_id=1, source_target_pairs={{0,2},{1,3},{2,0},{3,1},{4,6},{5,7},{6,4},{7,5},{8,10},{9,11},{10,... | collective-permute-start | bytes 393224 | tf_op jit(solution)/shard_map/ppermute | solution.py:361
  87.7 11.0 %collective-permute-start.28 = (bf16[2,128,256]{2,1,0:T(8,128)(2,1)S(1)}, bf16[2,128,256]{2,1,0:T(8,128)(2,1)S(1)}, u32[]{:S(2)}, u32[]{:S(2)}) collective-permute-start(bf16[2,128,256]{2,1,0:T(8,128)(2,1)S(1)} %get-tuple-element.107), channel_id=1, source_target_pairs={{0,3},{1,0},{2,1},{3,2},{4,7},{5,4},{6,5},{7,6},{8,11},{9,8},{10,9... | collective-permute-start | bytes 393224 | tf_op jit(solution)/shard_map/ppermute | solution.py:361
  89.7 7.9 %collective-permute-start.23 = (bf16[128,256]{1,0:T(8,128)(2,1)S(1)}, bf16[128,256]{1,0:T(8,128)(2,1)S(1)}, u32[]{:S(2)}, u32[]{:S(2)}) collective-permute-start(bf16[128,256]{1,0:T(8,128)(2,1)S(1)} %get-tuple-element.97), channel_id=1, source_target_pairs={{0,64},{64,128},{128,192},{1,65},{65,129},{129,193},{2,66},{66,130... | collective-permute-start | bytes 196616 | tf_op jit(solution)/shard_map/ppermute | solution.py:436
  (6 other events, 19.6 us)
